TPU v7x, 128 devices: a whole 4x4x4 slice. The times are simulated.
128 devices in a mesh: req: 4 (over y), kv: 32 (over x, z, core).
Axes of the slice: x: 4, y: 4, z: 4, core: 2. Of those that a mesh axis runs over, the one named last changes fastest.
Arguments:
- stream: bfloat16 [16384, 2048], P(('req', 'kv')), may hold values from -40 to 40
- projections: bfloat16 [16384, 6144], P(('req', 'kv')), may hold values from -32 to 32
- key_cache: bfloat16 [131072, 2048], P(('req', 'kv')), may hold values from -12 to 12
- value_cache: bfloat16 [131072, 2048], P(('req', 'kv')), may hold values from -6 to 6
- cache_range: int32 [16, 2], replicated, may hold values from 0 to 8192, as said below
- norm_gain: float32 [2048], replicated, may hold values from 0.5 to 1.5
- out_weight: bfloat16 [2048, 2048], P(('req', 'kv')), may hold values from -0.125 to 0.125
- up_weight: bfloat16 [8192, 2048], P(('req', 'kv')), may hold values from -0.125 to 0.125
- down_weight: bfloat16 [8192, 2048], P(('req', 'kv')), may hold values from -0.0625 to 0.0625
Outputs:
- layer_out: bfloat16 [16384, 2048], P(('req', 'kv'))
Inputs may be any that keep to these rules, and one draw needn't show every extreme that they name: `cache_range`: row r holds the first and the end of the cached positions that request r attends to: 0 <= first < 2048, first < end <= 8192, and end = 8192 for some request.
All inputs are finite; a program needn't handle non-finite values.
Results may differ from a plain program's by a relative error of at most 0.011.
Values may be sent and summed in bfloat16 or wider, within the bound.
No kernel may reach another device: no remote copies, remote signals or barrier semaphores. Data moves between devices by JAX's collectives and lax.ppermute only.
A program may use at most 192 MiB of HBM per device.

v0:
```python
import math

import jax
import jax.numpy as jnp
from jax import lax
from jax.sharding import PartitionSpec as P

HD = 256
SPAN = 8


NEG_FILL = -1e30
NORM_EPS = 1e-05


def partner_2(value, axis, stride):
    mask = 2**stride
    pairs = [(source, source ^ mask) for source in range(lax.axis_size(axis))]
    return lax.ppermute(value, axis, pairs)


def shortened(array):

    def short(part):
        return part.astype(jnp.bfloat16) if part.dtype == jnp.float32 else part

    return jax.tree.map(short, array)


def layer_norm(stream, norm_gain):
    values = stream.astype(jnp.float32)
    centred = values - jnp.mean(values, axis=-1, keepdims=True)
    spread = jnp.mean(centred * centred, axis=-1, keepdims=True)
    return (centred * lax.rsqrt(spread + NORM_EPS) * norm_gain).astype(jnp.bfloat16)


def attend_block(query_block, key_rows, value_rows, visible):
    head_count = key_rows.shape[1]
    head_size = key_rows.shape[2]
    scores = jnp.einsum(
        "qhd,khd->hqk", query_block, key_rows, preferred_element_type=jnp.float32
    ) * (1.0 / math.sqrt(head_size))
    scores = jnp.where(visible[None], scores, NEG_FILL)
    row_max = jnp.max(scores, axis=-1)
    weights = jnp.where(visible[None], jnp.exp(scores - row_max[..., None]), 0.0)
    denominator = jnp.sum(weights, axis=-1)
    numerator = jnp.einsum(
        "hqk,khd->qhd", weights.astype(jnp.bfloat16), value_rows, preferred_element_type=jnp.float32
    )
    return (
        numerator.reshape(query_block.shape[0], head_count * head_size),
        row_max.T,
        denominator.T,
    )


def combine_partials(earlier, later):
    numerator_one, maximum_one, denominator_one = earlier
    numerator_two, maximum_two, denominator_two = later
    joint_max = jnp.maximum(maximum_one, maximum_two)
    factor_one = jnp.exp(maximum_one - joint_max)
    factor_two = jnp.exp(maximum_two - joint_max)
    row_count, head_count = maximum_one.shape
    merged = (
        numerator_one.reshape(row_count, head_count, -1) * factor_one[..., None]
        + numerator_two.reshape(row_count, head_count, -1) * factor_two[..., None]
    )
    return (
        merged.reshape(row_count, -1),
        joint_max,
        denominator_one * factor_one + denominator_two * factor_two,
    )


def unit_adder(inputs, pieces):
    gates = lax.dot_general(
        inputs, pieces[0], (((1,), (1,)), ((), ())), preferred_element_type=jnp.float32
    )
    hidden = jax.nn.gelu(gates, approximate=False).astype(jnp.bfloat16)
    return jnp.dot(hidden, pieces[1], preferred_element_type=jnp.float32)


def on_device(
    stream,
    projections,
    key_cache,
    value_cache,
    cache_range,
    norm_gain,
    out_weight,
    up_weight,
    down_weight,
):
    token_count, model_width = stream.shape
    cache_rows = key_cache.shape[0]
    head_size = HD
    head_count = model_width // head_size
    group_size = SPAN
    levels = group_size.bit_length() - 1
    kv_count = lax.axis_size("kv")
    kv_place = lax.axis_index("kv")
    req_place = lax.axis_index("req")
    member = kv_place % group_size
    request = (req_place * kv_count + kv_place) // group_size
    queries = projections[:, :model_width]
    for level in range(levels):
        partner = partner_2(queries, "kv", level)
        lower = kv_place >> level & 1 == 0
        queries = jnp.where(
            lower, jnp.concatenate([queries, partner], 0), jnp.concatenate([partner, queries], 0)
        )
    new_total = queries.shape[0]
    block_rows = min(512, new_total)
    block_count = new_total // block_rows
    query_blocks = queries.reshape(block_count, block_rows, head_count, head_size)
    block_starts = jnp.arange(block_count, dtype=jnp.int32) * block_rows
    pick = (jnp.arange(cache_range.shape[0], dtype=jnp.int32) == request)[:, None]
    bounds = jnp.sum(jnp.where(pick, cache_range, 0), axis=0)
    positions = member * cache_rows + jnp.arange(cache_rows, dtype=jnp.int32)
    cache_visible = (positions >= bounds[0]) & (positions < bounds[1])
    new_positions = member * token_count + jnp.arange(token_count, dtype=jnp.int32)
    new_keys = projections[:, model_width : 2 * model_width].reshape(
        token_count, head_count, head_size
    )
    new_values = projections[:, 2 * model_width :].reshape(token_count, head_count, head_size)
    cached_keys = key_cache.reshape(cache_rows, head_count, head_size)
    cached_values = value_cache.reshape(cache_rows, head_count, head_size)

    def new_visible(offset):
        query_positions = offset + jnp.arange(block_rows, dtype=jnp.int32)
        return new_positions[None, :] <= query_positions[:, None]

    all_keys = jnp.concatenate([cached_keys, new_keys], 0)
    all_values = jnp.concatenate([cached_values, new_values], 0)

    def one_block(item):
        query_block, offset = item
        visible = jnp.concatenate(
            [
                jnp.broadcast_to(cache_visible[None, :], (block_rows, cache_rows)),
                new_visible(offset),
            ],
            1,
        )
        return attend_block(query_block, all_keys, all_values, visible)

    partial_sums = lax.map(one_block, (query_blocks, block_starts))
    numerator = partial_sums[0].reshape(new_total, model_width)
    row_max = partial_sums[1].reshape(new_total, head_count)
    denominator = partial_sums[2].reshape(new_total, head_count)
    row_count = new_total
    for level in reversed(range(levels)):
        half_rows = row_count // 2
        upper = kv_place >> level & 1
        kept = tuple(
            (
                lax.dynamic_slice_in_dim(member_part, upper * half_rows, half_rows, 0)
                for member_part in (numerator, row_max, denominator)
            )
        )
        given = tuple(
            (
                lax.dynamic_slice_in_dim(member_part, (1 - upper) * half_rows, half_rows, 0)
                for member_part in (numerator, row_max, denominator)
            )
        )
        received = partner_2(
            (shortened(given[0]), shortened(given[1]), shortened(given[2])), "kv", level
        )
        numerator, row_max, denominator = combine_partials(kept, received)
        row_count = half_rows
    attention = (
        (numerator.reshape(token_count, head_count, head_size) / denominator[..., None])
        .reshape(token_count, model_width)
        .astype(jnp.bfloat16)
    )
    normed = layer_norm(stream, norm_gain)
    head_part = lax.all_to_all(attention, "req", split_axis=1, concat_axis=0, tiled=True)
    projected = jnp.dot(
        head_part,
        lax.all_gather(out_weight, "kv", axis=0, tiled=True),
        preferred_element_type=jnp.float32,
    )
    row_inputs = lax.all_gather(normed, "req", axis=0, tiled=True)
    units = unit_adder(
        row_inputs,
        (
            lax.all_gather(up_weight, "kv", axis=0, tiled=True),
            lax.all_gather(down_weight, "kv", axis=0, tiled=True),
        ),
    )
    summed = lax.psum_scatter(
        projected.astype(jnp.bfloat16), "req", scatter_dimension=0, tiled=True
    ).astype(jnp.float32) + lax.psum_scatter(
        units.astype(jnp.bfloat16), "req", scatter_dimension=0, tiled=True
    ).astype(
        jnp.float32
    )
    return (stream.astype(jnp.float32) + summed).astype(jnp.bfloat16)


def solution(mesh):
    in_specs = (
        P(("req", "kv"), None),
        P(("req", "kv"), None),
        P(("req", "kv"), None),
        P(("req", "kv"), None),
        P(),
        P(),
        P(("req", "kv"), None),
        P(("req", "kv"), None),
        P(("req", "kv"), None),
    )
    out_specs = P(("req", "kv"), None)
    return jax.shard_map(
        on_device, mesh=mesh, in_specs=in_specs, out_specs=out_specs, check_vma=False
    )
```

profile of v0, /device:TPU:1, one launch (start us, length us, event | category | flops | bytes accessed | tf_op | source)
XLA Modules:
  0.0 400.6 jit_solution(3879729815243239769)
XLA Ops:
  9.8 2.2 fusion.61
  12.9 2.5 fusion.106
  16.8 1.5 collective-permute-done
  18.6 1.8 collective-permute-start.1
  20.4 24.4 %collective-permute-done.1 = bf16[256,2048]{1,0:T(8,128)(2,1)} collective-permute-done((bf16[256,2048]{1,0:T(8,128)(2,1)S(1)}, bf16[256,2048]{1,0:T(8,128)(2,1)}, u32[]{:S(2)}, u32[]{:S(2)}) %collective-permute-start.1) | collective-permute-done | bytes 1048608 | tf_op jit(solution)/shard_map/ppermute | solution.py:19
  44.8 2.4 maximum_select_fusion.1
  47.2 3.4 collective-permute-start.2
  52.0 6.5 %copy.12 = bf16[1024,2048]{0,1:T(8,128)(2,1)} copy(bf16[1024,2048]{1,0:T(8,128)(2,1)} %param.13) | data formatting | bytes 8388608 | tf_op args[2]
  58.5 4.9 %pad_maximum_fusion = bf16[1152,8,256]{0,2,1:T(8,128)(2,1)} fusion(bf16[128,8,256]{0,2,1:T(8,128)(2,1)S(1)} %bitcast.93, bf16[1024,8,256]{0,2,1:T(8,128)(2,1)} %bitcast.73), kind=kLoop, calls=%fused_computation.26 | loop fusion | flops 9437184 | bytes 9437184 | tf_op jit(solution)/shard_map/concatenate | solution.py:133
  63.5 6.8 %copy.17 = bf16[1152,8,256]{2,0,1:T(8,128)(2,1)} copy(bf16[1152,8,256]{0,2,1:T(8,128)(2,1)} %pad_maximum_fusion) | data formatting | bytes 9437184
  70.5 6.4 %copy.14 = bf16[1024,2048]{0,1:T(8,128)(2,1)} copy(bf16[1024,2048]{1,0:T(8,128)(2,1)} %param.14) | data formatting | bytes 8388608 | tf_op args[3]
  77.7 4.9 %pad_maximum_fusion.1 = bf16[1152,8,256]{0,2,1:T(8,128)(2,1)} fusion(bf16[128,8,256]{0,2,1:T(8,128)(2,1)S(1)} %bitcast.92, bf16[1024,8,256]{0,2,1:T(8,128)(2,1)} %bitcast.71), kind=kLoop, calls=%fused_computation.27 | loop fusion | flops 9437184 | bytes 9437184 | tf_op jit(solution)/shard_map/concatenate | solution.py:134
  82.6 14.4 %collective-permute-done.2 = bf16[512,2048]{1,0:T(8,128)(2,1)} collective-permute-done((bf16[512,2048]{1,0:T(8,128)(2,1)S(1)}, bf16[512,2048]{1,0:T(8,128)(2,1)}, u32[]{:S(2)}, u32[]{:S(2)}) %collective-permute-start.2) | collective-permute-done | bytes 2097184 | tf_op jit(solution)/shard_map/ppermute | solution.py:19
  97.0 3.8 maximum_select_fusion
  100.8 3.4 copy.34
  104.2 86.5 %while.15 = (s32[]{:T(128)}, f32[2,512,2048]{2,1,0:T(8,128)}, f32[2,512,8]{1,2,0:T(8,128)S(1)}, f32[2,512,8]{1,2,0:T(8,128)S(1)}, s32[2]{0:T(128)S(1)}, /*index=...) while((s32[]{:T(128)}, f32[2,512,2048]{2,1,0:T(8,128)}, ...), condition=%wide.region_4.5_spmd.clone, body=%wide.region_1.4_spmd.clone.sunk | while | flops 4874957824 | bytes 128985080 | solution.py:147
  107.5 1.9 constant_dynamic-slice_fusion.6
  109.4 8.9 %fusion.128 = (f32[8,512]{1,0:T(8,128)S(1)}, f32[8,512,1152]{2,1,0:T(8,128)}) fusion(bf16[1152,8,256]{2,0,1:T(8,128)(2,1)S(1)} %copy-done.6, bf16[1,512,8,256]{3,2,1,0:T(8,128)(2,1)S(1)} %constant_dynamic-slice_fusion.6, pred[512,1152]{1,0:T(8,128)(4,1)S(1)} %pad_add_fusion.2), kind=kOutput, calls=%fused_computation.158.clone.1 | convolution fusion | flops 2430070784 | bytes 26296320 | tf_op jit(solution)/shard_map/while/body/eval_jaxpr/qhd,khd->hqk/dot_general | solution.py:40
  118.3 8.7 %fusion.130 = f32[8,512]{1,0:T(8,128)S(1)} fusion(f32[8,512,1152]{2,1,0:T(8,128)} %get-tuple-element.226, f32[8,512]{1,0:T(8,128)S(1)} %get-tuple-element.227, pred[512,1152]{1,0:T(8,128)(4,1)S(1)} %pad_add_fusion.2), kind=kLoop, calls=%fused_computation.5.clone.1 | loop fusion | flops 14151680 | bytes 19496960 | tf_op jit(solution)/shard_map/while/body/eval_jaxpr/reduce_sum | solution.py:46
  127.1 9.6 %fusion.129 = f32[8,512,256]{1,2,0:T(8,128)} fusion(bf16[1152,8,256]{0,2,1:T(8,128)(2,1)S(1)} %bitcast.83, f32[8,512,1152]{2,1,0:T(8,128)} %get-tuple-element.226, f32[8,512]{1,0:T(8,128)S(1)} %get-tuple-element.227, pred[512,1152]{1,0:T(8,128)(4,1)S(1)} %pad_add_fusion.2), kind=kOutput, calls=%fused_computation.7.clone.1 | convolution fusion | flops 2430074880 | bytes 28393472 | tf_op jit(solution)/shard_map/while/body/eval_jaxpr/hqk,khd->qhd/dot_general | solution.py:47
  136.6 5.4 %copy.51 = f32[1,512,2048]{2,1,0:T(8,128)} copy(f32[1,512,2048]{1,2,0:T(8,128)} %bitcast.69) | data formatting | bytes 8388608 | tf_op jit(solution)/shard_map/while/body/jit(dynamic_update_index_in_dim)/dynamic_update_slice | solution.py:147
  142.0 4.7 %constant_dynamic-update-slice_fusion.2 = f32[2,512,2048]{2,1,0:T(8,128)} fusion(f32[2,512,2048]{2,1,0:T(8,128)} %get-tuple-element.245, f32[1,512,2048]{2,1,0:T(8,128)} %copy.51, s32[]{:T(128)} %get-tuple-element.244), kind=kLoop, calls=%fused_computation.21.clone.1 | loop fusion | bytes 8389120 | tf_op jit(solution)/shard_map/while/body/jit(dynamic_update_index_in_dim)/dynamic_update_slice | solution.py:147
  150.1 1.9 constant_dynamic-slice_fusion.6
  152.0 8.9 %fusion.128 = (f32[8,512]{1,0:T(8,128)S(1)}, f32[8,512,1152]{2,1,0:T(8,128)}) fusion(bf16[1152,8,256]{2,0,1:T(8,128)(2,1)S(1)} %copy-done.6, bf16[1,512,8,256]{3,2,1,0:T(8,128)(2,1)S(1)} %constant_dynamic-slice_fusion.6, pred[512,1152]{1,0:T(8,128)(4,1)S(1)} %pad_add_fusion.2), kind=kOutput, calls=%fused_computation.158.clone.1 | convolution fusion | flops 2430070784 | bytes 26296320 | tf_op jit(solution)/shard_map/while/body/eval_jaxpr/qhd,khd->hqk/dot_general | solution.py:40
  160.9 8.9 %fusion.130 = f32[8,512]{1,0:T(8,128)S(1)} fusion(f32[8,512,1152]{2,1,0:T(8,128)} %get-tuple-element.226, f32[8,512]{1,0:T(8,128)S(1)} %get-tuple-element.227, pred[512,1152]{1,0:T(8,128)(4,1)S(1)} %pad_add_fusion.2), kind=kLoop, calls=%fused_computation.5.clone.1 | loop fusion | flops 14151680 | bytes 19496960 | tf_op jit(solution)/shard_map/while/body/eval_jaxpr/reduce_sum | solution.py:46
  169.9 10.6 %fusion.129 = f32[8,512,256]{1,2,0:T(8,128)} fusion(bf16[1152,8,256]{0,2,1:T(8,128)(2,1)S(1)} %bitcast.83, f32[8,512,1152]{2,1,0:T(8,128)} %get-tuple-element.226, f32[8,512]{1,0:T(8,128)S(1)} %get-tuple-element.227, pred[512,1152]{1,0:T(8,128)(4,1)S(1)} %pad_add_fusion.2), kind=kOutput, calls=%fused_computation.7.clone.1 | convolution fusion | flops 2430074880 | bytes 28393472 | tf_op jit(solution)/shard_map/while/body/eval_jaxpr/hqk,khd->qhd/dot_general | solution.py:47
  180.5 5.5 %copy.51 = f32[1,512,2048]{2,1,0:T(8,128)} copy(f32[1,512,2048]{1,2,0:T(8,128)} %bitcast.69) | data formatting | bytes 8388608 | tf_op jit(solution)/shard_map/while/body/jit(dynamic_update_index_in_dim)/dynamic_update_slice | solution.py:147
  186.0 4.8 %constant_dynamic-update-slice_fusion.2 = f32[2,512,2048]{2,1,0:T(8,128)} fusion(f32[2,512,2048]{2,1,0:T(8,128)} %get-tuple-element.245, f32[1,512,2048]{2,1,0:T(8,128)} %copy.51, s32[]{:T(128)} %get-tuple-element.244), kind=kLoop, calls=%fused_computation.21.clone.1 | loop fusion | bytes 8389120 | tf_op jit(solution)/shard_map/while/body/jit(dynamic_update_index_in_dim)/dynamic_update_slice | solution.py:147
  190.7 2.5 dynamic-slice_convert_fusion
  193.2 2.5 collective-permute-start.4
  196.7 2.0 collective-permute-start.9
  198.7 45.5 %collective-permute-done.3 = bf16[512,8]{0,1:T(8,128)(2,1)S(1)} collective-permute-done((bf16[512,8]{0,1:T(8,128)(2,1)S(1)}, bf16[512,8]{0,1:T(8,128)(2,1)S(1)}, u32[]{:S(2)}, u32[]{:S(2)}) %collective-permute-start.3) | collective-permute-done | bytes 8224 | tf_op jit(solution)/shard_map/ppermute | solution.py:19
  245.2 3.9 copy.35
  249.8 2.0 copy.36
  252.0 4.5 %multiply_add_fusion = f32[512,2048]{1,0:T(8,128)S(1)} fusion(f32[512,2048]{1,0:T(8,128)S(1)} %bitcast.77, bf16[512,2048]{1,0:T(8,128)(2,1)} %collective-permute-done.4, f32[512,2048]{1,0:T(8,128)S(1)} %bitcast.76, f32[1024,2048]{1,0:T(8,128)} %bitcast.85, s32[]{:T(128)S(6)} %select_n.90), kind=kLoop, calls=%fused_computation.45 | loop fusion | flops 4194304 | bytes 18874372 | tf_op jit(solution)/shard_map/add | solution.py:65
  256.5 2.0 copy-done.1
  259.6 1.6 collective-permute-start.6
  261.3 1.4 collective-permute-start.10
  262.8 34.0 %collective-permute-done.5 = bf16[256,8]{0,1:T(8,128)(2,1)S(1)} collective-permute-done((bf16[256,8]{0,1:T(8,128)(2,1)S(1)}, bf16[256,8]{0,1:T(8,128)(2,1)S(1)}, u32[]{:S(2)}, u32[]{:S(2)}) %collective-permute-start.5) | collective-permute-done | bytes 4128 | tf_op jit(solution)/shard_map/ppermute | solution.py:19
  303.4 1.9 collective-permute-start.8
  309.8 1.8 divide_convert_fusion
  312.5 4.0 all-to-all-start
  316.5 8.9 %all-to-all-done = bf16[128,4,512]{2,0,1:T(8,128)(2,1)S(1)} async-done(((bf16[128,4,512]{2,0,1:T(8,128)(2,1)}), bf16[128,4,512]{2,0,1:T(8,128)(2,1)S(1)}, u32[]{:S(2)}, u32[]{:S(2)}) %all-to-all-start) | async-done | bytes 524320 | tf_op jit(solution)/shard_map/all_to_all | solution.py:178
  325.4 4.2 %convolution_convert_fusion.1 = bf16[512,2048]{1,0:T(8,128)(2,1)} fusion(bf16[512,512]{1,0:T(8,128)(2,1)S(1)} %bitcast.95, bf16[512,2048]{1,0:T(8,128)(2,1)} %all-gather.5.cloned.1.call-done), kind=kOutput, calls=%fused_computation.50 | convolution fusion | flops 1074790400 | bytes 4718592 | tf_op jit(solution)/shard_map/dot_general | solution.py:179
  329.9 22.6 %convolution_convert_fusion = bf16[512,2048]{1,0:T(8,128)(2,1)} fusion(bf16[2048,2048]{1,0:T(8,128)(2,1)} %all-gather.11.cloned.1.call-done, bf16[512,2048]{1,0:T(8,128)(2,1)} %all-gather.7.cloned.1.call-done, bf16[2048,2048]{1,0:T(8,128)(2,1)} %all-gather.9.cloned.1.call-done), kind=kOutput, calls=%fused_computation.49 | convolution fusion | flops 8659140608 | bytes 20971520 | tf_op jit(solution)/shard_map/dot_general | solution.py:80
  352.6 6.9 %reduce-scatter.3.cloned.1.call-done = bf16[128,2048]{1,0:T(8,128)(2,1)} async-done(((bf16[512,2048]{1,0:T(8,128)(2,1)}), bf16[128,2048]{1,0:T(8,128)(2,1)}) %reduce-scatter.3.cloned.1.call-update) | async-done | bytes 524304 | tf_op jit(solution)/shard_map/reduce_scatter | solution.py:192
  359.5 31.8 %reduce-scatter.5.cloned.1.call-done = bf16[128,2048]{1,0:T(8,128)(2,1)} async-done(((bf16[512,2048]{1,0:T(8,128)(2,1)}), bf16[128,2048]{1,0:T(8,128)(2,1)}) %reduce-scatter.5.cloned.1.call-update) | async-done | bytes 524304 | tf_op jit(solution)/shard_map/reduce_scatter | solution.py:194
  391.3 2.2 fusion.62
  (119 shorter events, 31.0 us)
Async XLA Ops:
  6.5 309.9 %all-gather.5.cloned.1.call-start = ((), (), s32[]{:S(2)}) async-start(), calls=%async_computation.3 | async-start | bytes 2162688 | tf_op jit(solution)/shard_map/all_gather | solution.py:181
  7.3 322.6 %all-gather.7.cloned.1.call-start = ((), (), s32[]{:S(2)}) async-start(), calls=%async_computation.5 | async-start | bytes 2621440 | tf_op jit(solution)/shard_map/all_gather | solution.py:184
  12.1 317.8 %all-gather.11.cloned.1.call-start = ((), (), s32[]{:S(2)}) async-start(), calls=%async_computation.7 | async-start | bytes 8650752 | tf_op jit(solution)/shard_map/all_gather | solution.py:189
  12.8 317.1 %all-gather.9.cloned.1.call-start = ((), (), s32[]{:S(2)}) async-start(), calls=%async_computation.6 | async-start | bytes 8650752 | tf_op jit(solution)/shard_map/all_gather | solution.py:188
  15.4 3.0 collective-permute-start
  18.6 26.2 %collective-permute-start.1 = (bf16[256,2048]{1,0:T(8,128)(2,1)S(1)}, bf16[256,2048]{1,0:T(8,128)(2,1)}, u32[]{:S(2)}, u32[]{:S(2)}) collective-permute-start(bf16[256,2048]{1,0:T(8,128)(2,1)S(1)} %maximum_select_fusion.2), channel_id=1, source_target_pairs={{0,2},{1,3},{2,0},{3,1},{4,6},{5,7},{6,4},{7,5},{8,10},{9,11},{10,... | collective-permute-start | bytes 3145736 | tf_op jit(solution)/shard_map/ppermute | solution.py:19
  47.2 49.8 %collective-permute-start.2 = (bf16[512,2048]{1,0:T(8,128)(2,1)S(1)}, bf16[512,2048]{1,0:T(8,128)(2,1)}, u32[]{:S(2)}, u32[]{:S(2)}) collective-permute-start(bf16[512,2048]{1,0:T(8,128)(2,1)S(1)} %maximum_select_fusion.1), channel_id=1, source_target_pairs={{0,4},{1,5},{2,6},{3,7},{4,0},{5,1},{6,2},{7,3},{8,12},{9,13},{10,... | collective-permute-start | bytes 6291464 | tf_op jit(solution)/shard_map/ppermute | solution.py:19
  63.5 6.8 %copy-start.7 = (bf16[128,2048]{1,0:T(8,128)(2,1)S(1)}, bf16[128,2048]{1,0:T(8,128)(2,1)}, u32[]{:S(2)}) copy-start(bf16[128,2048]{1,0:T(8,128)(2,1)} %get-tuple-element.144) | copy-start | bytes 1572868
  70.5 6.4 %copy-start.8 = (s32[16,2]{0,1:T(2,128)S(1)}, s32[16,2]{0,1:T(2,128)}, u32[]{:S(2)}) copy-start(s32[16,2]{0,1:T(2,128)} %param.15) | copy-start | bytes 388
  104.2 5.2 %copy-start.6 = (bf16[1152,8,256]{2,0,1:T(8,128)(2,1)S(1)}, bf16[1152,8,256]{2,0,1:T(8,128)(2,1)}, u32[]{:S(2)}) copy-start(bf16[1152,8,256]{2,0,1:T(8,128)(2,1)} %get-tuple-element.264) | copy-start | bytes 14155780 | tf_op jit(solution)/shard_map/while
  107.5 19.5 %slice-start = ((s8[4718592]{0:T(1024)(128)(4,1)}), s8[4194304]{0:T(1024)(128)(4,1)S(1)}, s32[]{:S(2)}) async-start(s8[4718592]{0:T(1024)(128)(4,1)} %bitcast.82), calls=%async_computation.9 | async-start | bytes 8388608 | tf_op jit(solution)/shard_map/while
  109.4 17.6 %slice-start.1 = ((s8[4718592]{0:T(1024)(128)(4,1)}), s8[524288]{0:T(1024)(128)(4,1)S(1)}, s32[]{:S(2)}) async-start(s8[4718592]{0:T(1024)(128)(4,1)} %bitcast.82), calls=%async_computation.10 | async-start | bytes 1048576 | tf_op jit(solution)/shard_map/while
  146.7 5.3 %copy-start.6 = (bf16[1152,8,256]{2,0,1:T(8,128)(2,1)S(1)}, bf16[1152,8,256]{2,0,1:T(8,128)(2,1)}, u32[]{:S(2)}) copy-start(bf16[1152,8,256]{2,0,1:T(8,128)(2,1)} %get-tuple-element.264) | copy-start | bytes 14155780 | tf_op jit(solution)/shard_map/while
  150.1 19.8 %slice-start = ((s8[4718592]{0:T(1024)(128)(4,1)}), s8[4194304]{0:T(1024)(128)(4,1)S(1)}, s32[]{:S(2)}) async-start(s8[4718592]{0:T(1024)(128)(4,1)} %bitcast.82), calls=%async_computation.9 | async-start | bytes 8388608 | tf_op jit(solution)/shard_map/while
  152.0 17.8 %slice-start.1 = ((s8[4718592]{0:T(1024)(128)(4,1)}), s8[524288]{0:T(1024)(128)(4,1)S(1)}, s32[]{:S(2)}) async-start(s8[4718592]{0:T(1024)(128)(4,1)} %bitcast.82), calls=%async_computation.10 | async-start | bytes 1048576 | tf_op jit(solution)/shard_map/while
  193.2 58.6 %collective-permute-start.4 = (bf16[512,2048]{1,0:T(8,128)(2,1)S(1)}, bf16[512,2048]{1,0:T(8,128)(2,1)}, u32[]{:S(2)}, u32[]{:S(2)}) collective-permute-start(bf16[512,2048]{1,0:T(8,128)(2,1)S(1)} %dynamic-slice_convert_fusion), channel_id=1, source_target_pairs={{0,4},{1,5},{2,6},{3,7},{4,0},{5,1},{6,2},{7,3},{8,12},{9,13},{10,... | collective-permute-start | bytes 6291464 | tf_op jit(solution)/shard_map/ppermute | solution.py:19
  195.7 48.5 %collective-permute-start.3 = (bf16[512,8]{0,1:T(8,128)(2,1)S(1)}, bf16[512,8]{0,1:T(8,128)(2,1)S(1)}, u32[]{:S(2)}, u32[]{:S(2)}) collective-permute-start(bf16[512,8]{0,1:T(8,128)(2,1)S(1)} %dynamic-slice_convert_fusion.4), channel_id=1, source_target_pairs={{0,4},{1,5},{2,6},{3,7},{4,0},{5,1},{6,2},{7,3},{8,12},{9,13},{10,... | collective-permute-start | bytes 24584 | tf_op jit(solution)/shard_map/ppermute | solution.py:19
  196.7 47.7 %collective-permute-start.9 = (bf16[512,8]{0,1:T(8,128)(2,1)S(1)}, bf16[512,8]{0,1:T(8,128)(2,1)S(1)}, u32[]{:S(2)}, u32[]{:S(2)}) collective-permute-start(bf16[512,8]{0,1:T(8,128)(2,1)S(1)} %dynamic-slice_convert_fusion.3), channel_id=1, source_target_pairs={{0,4},{1,5},{2,6},{3,7},{4,0},{5,1},{6,2},{7,3},{8,12},{9,13},{10,... | collective-permute-start | bytes 24584 | tf_op jit(solution)/shard_map/ppermute | solution.py:19
  249.8 2.2 copy-start
  256.5 2.0 copy-start.1
  259.6 40.0 %collective-permute-start.6 = (bf16[256,2048]{1,0:T(8,128)(2,1)}, bf16[256,2048]{1,0:T(8,128)(2,1)S(1)}, u32[]{:S(2)}, u32[]{:S(2)}) collective-permute-start(bf16[256,2048]{1,0:T(8,128)(2,1)} %dynamic-slice_convert_fusion.1), channel_id=1, source_target_pairs={{0,2},{1,3},{2,0},{3,1},{4,6},{5,7},{6,4},{7,5},{8,10},{9,11},{10,... | collective-permute-start | bytes 3145736 | tf_op jit(solution)/shard_map/ppermute | solution.py:19
  261.3 35.5 %collective-permute-start.5 = (bf16[256,8]{0,1:T(8,128)(2,1)S(1)}, bf16[256,8]{0,1:T(8,128)(2,1)S(1)}, u32[]{:S(2)}, u32[]{:S(2)}) collective-permute-start(bf16[256,8]{0,1:T(8,128)(2,1)S(1)} %dynamic-slice_convert_fusion.6), channel_id=1, source_target_pairs={{0,2},{1,3},{2,0},{3,1},{4,6},{5,7},{6,4},{7,5},{8,10},{9,11},{10,... | collective-permute-start | bytes 12296 | tf_op jit(solution)/shard_map/ppermute | solution.py:19
  261.3 35.5 %collective-permute-start.10 = (bf16[256,8]{0,1:T(8,128)(2,1)S(1)}, bf16[256,8]{0,1:T(8,128)(2,1)S(1)}, u32[]{:S(2)}, u32[]{:S(2)}) collective-permute-start(bf16[256,8]{0,1:T(8,128)(2,1)S(1)} %dynamic-slice_convert_fusion.5), channel_id=1, source_target_pairs={{0,2},{1,3},{2,0},{3,1},{4,6},{5,7},{6,4},{7,5},{8,10},{9,11},{10,... | collective-permute-start | bytes 12296 | tf_op jit(solution)/shard_map/ppermute | solution.py:19
  298.3 2.2 copy-start.2
  301.2 1.4 copy-start.4
  303.4 6.4 %collective-permute-start.8 = (bf16[128,2048]{1,0:T(8,128)(2,1)}, bf16[128,2048]{1,0:T(8,128)(2,1)}, u32[]{:S(2)}, u32[]{:S(2)}) collective-permute-start(bf16[128,2048]{1,0:T(8,128)(2,1)} %dynamic-slice_convert_fusion.2), channel_id=1, source_target_pairs={{0,1},{1,0},{2,3},{3,2},{4,5},{5,4},{6,7},{7,6},{8,9},{9,8},{10,11... | collective-permute-start | bytes 1572872 | tf_op jit(solution)/shard_map/ppermute | solution.py:19
  305.3 1.4 collective-permute-start.7
  305.3 1.5 collective-permute-start.11
  307.2 2.7 copy-start.5
  312.5 12.9 %all-to-all-start = ((bf16[128,4,512]{2,0,1:T(8,128)(2,1)}), bf16[128,4,512]{2,0,1:T(8,128)(2,1)S(1)}, u32[]{:S(2)}, u32[]{:S(2)}) async-start(bf16[128,4,512]{2,0,1:T(8,128)(2,1)} %bitcast.56), calls=%async_computation | async-start | bytes 1048576 | tf_op jit(solution)/shard_map/all_to_all | solution.py:178
  316.5 43.0 %reduce-scatter.3.cloned.1.call-start = ((), (), s32[]{:S(2)}) async-start(), calls=%async_computation.4 | async-start | bytes 2621440 | tf_op jit(solution)/shard_map/reduce_scatter | solution.py:192
  329.6 61.7 %copy-start.3 = (bf16[128,2048]{1,0:T(8,128)(2,1)S(1)}, bf16[128,2048]{1,0:T(8,128)(2,1)}, u32[]{:S(2)}) copy-start(bf16[128,2048]{1,0:T(8,128)(2,1)} %param.11) | copy-start | bytes 1572868
  329.6 61.7 %reduce-scatter.5.cloned.1.call-start = ((), (), s32[]{:S(2)}) async-start(), calls=%async_computation.8 | async-start | bytes 2621440 | tf_op jit(solution)/shard_map/reduce_scatter | solution.py:194
Sparse Core Ops, SparseCore 0:
  9.6 49.3 all-gather.4
  60.7 73.1 all-gather.6
  136.2 53.5 all-gather.10
  191.9 97.3 all-gather.8
  329.7 29.7 reduce-scatter.2
  361.9 29.4 reduce-scatter.4
where the time goes:
time: 404 us; the launch traced here: 401 us
  waiting for transfers between devices  170 us (42%)
  local copies, waits for them, and re-layouts  76.1 us (19%)
  matrix products  64.8 us (16%)
  other arithmetic  53.3 us (13%)
  starting transfers between devices  21.9 us (5%)
  between operations  14.1 us (3%)
    ppermute x12, waiting for transfers between devices, partner_2(): return lax.ppermute(value, axis, pairs)  121 us
    unnamed x28, local copies, waits for them, and re-layouts  38.5 us
    reduce_scatter x1, waiting for transfers between devices, on_device(): lax.psum_scatter(units.astype(jnp.bfloat16), 'req', scatter_dimension=0,...  31.8 us
    dot_general x1, matrix products, unit_adder(): return jnp.dot(hidden, pieces[1], preferred_element_type=jnp.float32)  22.6 us
    dynamic_update_slice x6, local copies, waits for them, and re-layouts, on_device(): partial_sums = lax.map(one_block, (query_blocks, block_starts))  20.4 us
    dot_general x2, matrix products, attend_block(): jnp.einsum('hqk,khd->qhd', weights.astype(jnp.bfloat16), value_rows, pref...  20.2 us
    dot_general x2, matrix products, attend_block(): jnp.einsum('qhd,khd->hqk', query_block, key_rows, preferred_element_type=...  17.8 us
    reduce_sum x2, other arithmetic, attend_block(): denominator = jnp.sum(weights, axis=-1)  17.6 us
  transfers between devices with their start and end apart: 19, of which 12 were waited for; matrix products, arithmetic and copies ran while one was open for 47% of the time, Pallas kernels for 0%

commit v1 on v0

v1 whole, which is shorter than its diff:
```python
import math

import jax
import jax.numpy as jnp
from jax import lax
from jax.experimental import pallas as pl
from jax.experimental.pallas import tpu as pltpu
from jax.sharding import Mesh, PartitionSpec as P

HD = 256
NORM_EPS = 1e-05
NEG = -(2.0**100)
LOG2E = 1.4426950408889634
SCORE = LOG2E / math.sqrt(HD)
MIB = 1 << 20
F32 = jnp.float32
BF16 = jnp.bfloat16


def ring(step, count):
    return [(i, (i + step) % count) for i in range(count)]


def swap_cores(value):
    return lax.ppermute(value, "c", [(0, 1), (1, 0)])


def params(mib):
    return pltpu.CompilerParams(vmem_limit_bytes=mib * MIB)


def dot(a, b, dims):
    return lax.dot_general(a, b, (dims, ((), ())), preferred_element_type=F32)


def pick_new(place, projections):
    rows, width = projections.shape
    heads = width // (2 * HD)

    def body(place_ref, source, own, other):
        c = place_ref[0]
        for j in range(heads):
            other[:, j * HD : (j + 1) * HD] = source[:, pl.ds((2 * j + 1 - c) * HD, HD)]
        for j in range(heads // 3):
            own[:, j * HD : (j + 1) * HD] = source[:, pl.ds((2 * j + c) * HD, HD)]

    return pl.pallas_call(
        body,
        grid_spec=pltpu.PrefetchScalarGridSpec(
            num_scalar_prefetch=1,
            grid=(1,),
            in_specs=[pl.BlockSpec((rows, width), lambda i, s: (0, 0))],
            out_specs=[
                pl.BlockSpec((rows, width // 6), lambda i, s: (0, 0)),
                pl.BlockSpec((rows, width // 2), lambda i, s: (0, 0)),
            ],
        ),
        out_shape=[
            jax.ShapeDtypeStruct((rows, width // 6), BF16),
            jax.ShapeDtypeStruct((rows, width // 2), BF16),
        ],
        compiler_params=params(16),
        name="pick_new",
    )(place, projections)


def pick_cache(place, cache):
    rows, width = cache.shape
    heads = width // (2 * HD)

    def body(place_ref, source, other):
        other[...] = source[...]

    return pl.pallas_call(
        body,
        grid_spec=pltpu.PrefetchScalarGridSpec(
            num_scalar_prefetch=1,
            grid=(heads,),
            in_specs=[pl.BlockSpec((rows, HD), lambda j, s: (0, 2 * j + 1 - s[0]))],
            out_specs=pl.BlockSpec((rows, HD), lambda j, s: (0, j)),
        ),
        out_shape=jax.ShapeDtypeStruct((rows, width // 2), BF16),
        compiler_params=params(16),
        name="pick_cache",
    )(place, cache)


def norm_kernel(stream, gain, out):
    values = stream[...].astype(F32)
    width = values.shape[1]
    centred = values - jnp.sum(values, axis=-1, keepdims=True) * (1.0 / width)
    spread = jnp.sum(centred * centred, axis=-1, keepdims=True) * (1.0 / width)
    out[...] = (centred * lax.rsqrt(spread + NORM_EPS) * gain[...]).astype(BF16)


def layer_norm(stream, gain):
    return pl.pallas_call(
        norm_kernel,
        out_shape=jax.ShapeDtypeStruct(stream.shape, BF16),
        compiler_params=params(16),
        name="layer_norm",
    )(stream, gain.reshape(1, -1))


def attend_kernel(
    place, ranges, q_ref, k0, k1, v0, v1, nk0, nk1, nv0, nv1, out, stats
):
    j = pl.program_id(0)
    c, z, zq, request = place[0], place[1], place[2], place[3]
    first, end = ranges[request, 0], ranges[request, 1]
    rows = q_ref.shape[0]
    half = rows // 2
    cache_rows = k0.shape[0]
    query = q_ref[...]

    def cached(keys, member):
        position = member * cache_rows + lax.broadcasted_iota(jnp.int32, (1, cache_rows), 1)
        bias = jnp.where((position >= first) & (position < end), 0.0, NEG).astype(F32)
        return dot(query, keys[...], ((1,), (1,))) + bias

    def order(shape, axis):
        place_in = lax.broadcasted_iota(jnp.int32, shape, axis)
        return jnp.where(place_in < half, place_in + c * half, place_in - c * half)

    score_own = cached(k0, 2 * z + c)
    score_other = cached(k1, 2 * z + 1 - c)
    new_keys = jnp.concatenate([nk0[...], nk1[...]], 0)
    new_values = jnp.concatenate([nv0[...], nv1[...]], 0)
    visible = z * rows + order((1, rows), 1) <= zq * rows + order((rows, 1), 0)
    score_new = jnp.where(visible, dot(query, new_keys, ((1,), (1,))), NEG)
    top = jnp.maximum(
        jnp.maximum(
            jnp.max(score_own, axis=-1, keepdims=True),
            jnp.max(score_other, axis=-1, keepdims=True),
        ),
        jnp.max(score_new, axis=-1, keepdims=True),
    )
    shift = top.astype(BF16).astype(F32)

    def weigh(score, values):
        weight = jnp.exp2((score - shift) * SCORE)
        return (
            jnp.sum(weight, axis=-1, keepdims=True),
            dot(weight.astype(BF16), values, ((1,), (0,))),
        )

    parts = [
        weigh(score_own, v0[...]),
        weigh(score_other, v1[...]),
        weigh(score_new, new_values),
    ]
    total = parts[0][0] + parts[1][0] + parts[2][0]
    out[:, pl.ds(pl.multiple_of(j * HD, HD), HD)] = (
        parts[0][1] + parts[1][1] + parts[2][1]
    ).astype(BF16)
    high = total.astype(BF16).astype(F32)
    lane = lax.broadcasted_iota(jnp.int32, stats.shape, 1)
    kept = jnp.where(j == 0, 0.0, stats[...])
    kept = jnp.where(lane == 3 * j, shift, kept)
    kept = jnp.where(lane == 3 * j + 1, high, kept)
    kept = jnp.where(lane == 3 * j + 2, total - high, kept)
    stats[...] = kept
    base = out.shape[1] - stats.shape[1]
    out[:, base:] = kept.astype(BF16)


def attend(place, ranges, query, keys, values, projections, keys_in, values_in, new_in):
    rows, width = query.shape
    heads = width // HD
    cache_rows = keys.shape[0]
    new_rows = projections.shape[0]

    def columns(count, index):
        return pl.BlockSpec((count, HD), index)

    return pl.pallas_call(
        attend_kernel,
        grid_spec=pltpu.PrefetchScalarGridSpec(
            num_scalar_prefetch=2,
            grid=(heads,),
            in_specs=[
                columns(rows, lambda j, s, r: (0, j)),
                columns(cache_rows, lambda j, s, r: (0, 2 * j + s[0])),
                columns(cache_rows, lambda j, s, r: (0, j)),
                columns(cache_rows, lambda j, s, r: (0, 2 * j + s[0])),
                columns(cache_rows, lambda j, s, r: (0, j)),
                columns(new_rows, lambda j, s, r: (0, 2 * heads + 2 * j + s[0])),
                columns(new_rows, lambda j, s, r: (0, heads + j)),
                columns(new_rows, lambda j, s, r: (0, 4 * heads + 2 * j + s[0])),
                columns(new_rows, lambda j, s, r: (0, 2 * heads + j)),
            ],
            out_specs=pl.BlockSpec((rows, width + 128), lambda j, s, r: (0, 0)),
            scratch_shapes=[pltpu.VMEM((rows, 128), F32)],
        ),
        out_shape=jax.ShapeDtypeStruct((rows, width + 128), BF16),
        compiler_params=params(32),
        cost_estimate=pl.CostEstimate(
            flops=4 * rows * (2 * cache_rows + rows) * width,
            transcendentals=rows * (2 * cache_rows + rows) * heads,
            bytes_accessed=8 * cache_rows * width + 8 * rows * width,
        ),
        name="attend",
    )(
        place,
        ranges,
        query,
        keys,
        keys_in,
        values,
        values_in,
        projections,
        new_in,
        projections,
        new_in,
    )


def merge_kernel(place, a, b, c, d, out):
    y = place[4]
    count = out.shape[0]
    parts = (a, b, c, d)
    base = a.shape[1] - 128
    stats = [part[:, base:].astype(F32) for part in parts]
    for j in range(count):
        shifts = [s[:, 3 * j : 3 * j + 1] for s in stats]
        totals = [s[:, 3 * j + 1 : 3 * j + 2] + s[:, 3 * j + 2 : 3 * j + 3] for s in stats]
        top = jnp.maximum(
            jnp.maximum(shifts[0], shifts[1]), jnp.maximum(shifts[2], shifts[3])
        )
        factors = [jnp.exp2((s - top) * SCORE) for s in shifts]
        total = sum(f * t for f, t in zip(factors, totals))
        summed = sum(
            f * part[:, j * HD : (j + 1) * HD].astype(F32) for f, part in zip(factors, parts)
        )
        out[lax.rem(j - y + count, count)] = (summed / total).astype(BF16)


def merge(place, parts):
    rows, width = parts[0].shape
    count = (width - 128) // HD
    whole = pl.BlockSpec((rows, width), lambda i, s: (0, 0))
    return pl.pallas_call(
        merge_kernel,
        grid_spec=pltpu.PrefetchScalarGridSpec(
            num_scalar_prefetch=1,
            grid=(1,),
            in_specs=[whole] * 4,
            out_specs=pl.BlockSpec((count, rows, HD), lambda i, s: (0, 0, 0)),
        ),
        out_shape=jax.ShapeDtypeStruct((count, rows, HD), BF16),
        compiler_params=params(24),
        name="merge",
    )(place, *parts)


def units_kernel(own_in, other_in, attention, weights, out_rows, own, other, total):
    step = pl.program_id(0)
    unit_rows = (weights.shape[1] * 4) // 9
    count = weights.shape[0] * unit_rows
    width = own_in.shape[1]
    rows = own_in.shape[0]

    @pl.when(step == 0)
    def _():
        total[...] = dot(attention[...], out_rows[...], ((1,), (0,)))

    inputs = jnp.concatenate([own_in[...], other_in[...]], 0)
    up = weights[:, :unit_rows, :].reshape(count, width)
    down = weights[:, unit_rows : 2 * unit_rows, :].reshape(count, width)
    gates = dot(inputs, up, ((1,), (1,)))
    hidden = (0.5 * gates * (1.0 + lax.erf(gates * math.sqrt(0.5)))).astype(BF16)
    total[...] += dot(hidden, down, ((1,), (0,)))

    @pl.when(step == pl.num_programs(0) - 1)
    def _():
        own[...] = total[:rows, :]
        other[...] = total[rows:, :].astype(BF16)


def add_units(own_in, other_in, attention, weights, out_rows):
    rows, width = own_in.shape
    shards, shard_rows, _ = weights.shape
    chunk = 4
    return pl.pallas_call(
        units_kernel,
        grid=(shards // chunk,),
        in_specs=[
            pl.BlockSpec((rows, width), lambda i: (0, 0)),
            pl.BlockSpec((rows, width), lambda i: (0, 0)),
            pl.BlockSpec((2 * rows, HD), lambda i: (0, 0)),
            pl.BlockSpec((chunk, shard_rows, width), lambda i: (i, 0, 0)),
            pl.BlockSpec((HD, width), lambda i: (0, 0)),
        ],
        out_specs=[
            pl.BlockSpec((rows, width), lambda i: (0, 0)),
            pl.BlockSpec((rows, width), lambda i: (0, 0)),
        ],
        out_shape=[
            jax.ShapeDtypeStruct((rows, width), F32),
            jax.ShapeDtypeStruct((rows, width), BF16),
        ],
        scratch_shapes=[pltpu.VMEM((2 * rows, width), F32)],
        compiler_params=params(40),
        cost_estimate=pl.CostEstimate(
            flops=2 * 2 * rows * shards * shard_rows * width,
            transcendentals=0,
            bytes_accessed=2 * shards * shard_rows * width + 16 * rows * width,
        ),
        name="units",
    )(own_in, other_in, attention, weights, out_rows)


def on_device(
    stream,
    projections,
    key_cache,
    value_cache,
    cache_range,
    norm_gain,
    out_weight,
    up_weight,
    down_weight,
):
    width = stream.shape[1]
    half = width // 2
    y, x, z, c = (lax.axis_index(name) for name in "yxzc")
    ny, nz = lax.axis_size("y"), lax.axis_size("z")
    request = y * lax.axis_size("x") + x

    weights = lax.all_gather(
        jnp.concatenate([up_weight, down_weight, out_weight], 0), ("x", "z"), axis=0
    )

    def place_of(zq):
        return jnp.stack([c, z, zq, request, y]).astype(jnp.int32)

    place = place_of(z)
    own_query, new_out = pick_new(place, projections)
    new_in = swap_cores(new_out)
    query = jnp.concatenate([own_query, new_in[:, :half]], 0)
    queries = {k: lax.ppermute(query, "z", ring(k, nz)) for k in (2, 1, 3)}
    queries[0] = query
    keys_in = swap_cores(pick_cache(place, key_cache))
    values_in = swap_cores(pick_cache(place, value_cache))

    normed = layer_norm(stream, norm_gain)
    inputs = {k: lax.ppermute(normed, "y", ring(k, ny)) for k in (2, 1, 3)}
    inputs[0] = normed
    others = {k: swap_cores(inputs[k]) for k in (0, 1, 3, 2)}

    partials = {}
    for k in (0, 1, 3, 2):
        made = attend(
            place_of((z - k + nz) % nz),
            cache_range,
            queries[k],
            key_cache,
            value_cache,
            projections,
            keys_in,
            values_in,
            new_in,
        )
        partials[k] = made if k == 0 else lax.ppermute(made, "z", ring(-k, nz))
    heads = merge(place, [partials[k] for k in range(nz)])
    attention = {k: lax.ppermute(heads[k], "y", ring(k, ny)) for k in (2, 1, 3)}
    attention[0] = heads[0]

    shards = weights.shape[0]
    out_shards = weights[:, -out_weight.shape[0] :, :]
    mine = lax.dynamic_slice_in_dim(out_shards, c * (shards // 2), shards // 2, 0)
    theirs = swap_cores(
        lax.dynamic_slice_in_dim(out_shards, (1 - c) * (shards // 2), shards // 2, 0)
    )
    out_rows = jnp.where(
        c == 0, jnp.stack([mine, theirs], 1), jnp.stack([theirs, mine], 1)
    ).reshape(HD, width)

    summed = None
    returned = []
    for k in (2, 1, 3, 0):
        own, other = add_units(inputs[k], others[k], attention[k], weights, out_rows)
        both = own + swap_cores(other).astype(F32)
        if k == 0:
            summed = both
        else:
            returned.append(lax.ppermute(both.astype(BF16), "y", ring(-k, ny)))
    summed = summed + stream.astype(F32)
    for part in returned:
        summed = summed + part.astype(F32)
    return summed.astype(BF16)


def solution(mesh):
    names = ("y", "x", "z", "c")
    requests, others = mesh.devices.shape
    grid = Mesh(mesh.devices.reshape(requests, others // 8, 4, 2), names)
    rows = P(names, None)
    return jax.shard_map(
        on_device,
        mesh=grid,
        in_specs=(rows, rows, rows, rows, P(), P(), rows, rows, rows),
        out_specs=rows,
        check_vma=False,
    )
```

time: 404 us -> 230 us (0.57)
  waiting for transfers between devices: 170 us -> 88.1 us
  Pallas kernels: 0 us -> 79.7 us
  matrix products: 64.8 us -> 0 us
  local copies, waits for them, and re-layouts: 76.1 us -> 15.9 us
  other arithmetic: 53.3 us -> 4.94 us
  starting transfers between devices: 21.9 us -> 26.3 us
    pallas_call x0 -> x13, Pallas kernels: none -> 79.7 us  [the longest x4 41.5 us: attend(): pl.pallas_call(attend_kernel, grid_spec=pltpu.PrefetchScalarGridSpec(num_...]
    ppermute x12 -> x27, waiting for transfers between devices: 121 us -> 43.8 us  [the longest x3 21.2 us: on_device(): returned.append(lax.ppermute(both.astype(BF16), 'y', ring(-k, ny)))]
    dot_general x6 -> x0, matrix products: 64.8 us -> none  [the longest x1 22.6 us: unit_adder(): return jnp.dot(hidden, pieces[1], preferred_element_type=jnp.float32)]
    all_gather x4 -> x1, waiting for transfers between devices: 0.06 us -> 44.2 us  [on_device(): lax.all_gather(jnp.concatenate([up_weight, down_weight, out_weight], 0),...]
    reduce_scatter x2 -> x0, waiting for transfers between devices: 38.7 us -> none  [the longest x1 31.8 us: on_device(): lax.psum_scatter(units.astype(jnp.bfloat16), 'req', scatter_dimension=0,...]
    unnamed x28 -> x35, local copies, waits for them, and re-layouts: 38.5 us -> 13 us
    dynamic_update_slice x6 -> x0, local copies, waits for them, and re-layouts: 20.4 us -> none  [on_device(): partial_sums = lax.map(one_block, (query_blocks, block_starts))]
    reduce_sum x5 -> x0, other arithmetic: 20.2 us -> none  [the longest x2 17.6 us: attend_block(): denominator = jnp.sum(weights, axis=-1)]
  transfers between devices with their start and end apart: 19 -> 28, of which waited for: 12 -> 6; matrix products, arithmetic and copies ran while one was open for 47% -> 2% of each run, Pallas kernels for 0% -> 35%
where the time goes in v1:
time: 230 us; the launch traced here: 229 us
  waiting for transfers between devices  88.1 us (38%)
  Pallas kernels  79.7 us (35%)
  starting transfers between devices  26.3 us (11%)
  local copies, waits for them, and re-layouts  15.9 us (7%)
  between operations  13.6 us (6%)
  other arithmetic  4.94 us (2%)
    all_gather x1, waiting for transfers between devices, on_device(): lax.all_gather(jnp.concatenate([up_weight, down_weight, out_weight], 0),...  44.2 us
    pallas_call x4, Pallas kernels, attend(): pl.pallas_call(attend_kernel, grid_spec=pltpu.PrefetchScalarGridSpec(num_...  41.5 us
    pallas_call x4, Pallas kernels, add_units(): pl.pallas_call(units_kernel, grid=(shards // chunk,), in_specs=[pl.BlockS...  27.8 us
    ppermute x3, waiting for transfers between devices, on_device(): returned.append(lax.ppermute(both.astype(BF16), 'y', ring(-k, ny)))  21.2 us
    ppermute x3, waiting for transfers between devices, on_device(): queries = {k: lax.ppermute(query, 'z', ring(k, nz)) for k in (2, 1, 3)}  17.5 us
    unnamed x35, local copies, waits for them, and re-layouts  13 us
    ppermute x12, starting transfers between devices, swap_cores(): return lax.ppermute(value, 'c', [(0, 1), (1, 0)])  6 us
    ppermute x3, starting transfers between devices, on_device(): queries = {k: lax.ppermute(query, 'z', ring(k, nz)) for k in (2, 1, 3)}  5.82 us
  transfers between devices with their start and end apart: 28, of which 6 were waited for; matrix products, arithmetic and copies ran while one was open for 2% of the time, Pallas kernels for 35%

profile of v1, /device:TPU:1, one launch (start us, length us, event | category | flops | bytes accessed | tf_op | source)
XLA Modules:
  0.0 228.6 jit_solution(14913651795633410765)
XLA Ops:
  6.5 1.9 pad_maximum_fusion
  8.6 2.2 copy-done.1
  10.8 2.7 %pick_cache.2 = bf16[1024,1024]{1,0:T(8,128)(2,1)} custom-call(s32[5]{0:T(128)S(1)} %stack.74.place_ref.place, bf16[1024,2048]{1,0:T(8,128)(2,1)S(1)} %copy-done.1), custom_call_target="tpu_custom_call" | custom-call | tf_op jit(solution)/shard_map/pick_cache/pallas_call | solution.py:74
  13.5 1.4 collective-permute-start.2
  14.9 2.8 %pick_cache.3 = bf16[1024,1024]{1,0:T(8,128)(2,1)} custom-call(s32[5]{0:T(128)S(1)} %stack.74.place_ref.place, bf16[1024,2048]{1,0:T(8,128)(2,1)S(1)} %copy-done.4), custom_call_target="tpu_custom_call" | custom-call | tf_op jit(solution)/shard_map/pick_cache/pallas_call | solution.py:74
  17.7 0.7 pick_new.1
  18.4 0.6 collective-permute-start.1
  19.0 4.0 %collective-permute-done.1.nk1.nv1 = bf16[128,3072]{1,0:T(8,128)(2,1)S(1)} collective-permute-done((bf16[128,3072]{1,0:T(8,128)(2,1)S(1)}, bf16[128,3072]{1,0:T(8,128)(2,1)S(1)}, u32[]{:S(2)}, u32[]{:S(2)}) %collective-permute-start.1) | collective-permute-done | bytes 786464 | tf_op jit(solution)/shard_map/ppermute | solution.py:25
  23.1 1.8 collective-permute-start.4
  24.9 3.3 %collective-permute-start.6 = (bf16[256,1024]{1,0:T(8,128)(2,1)S(1)}, bf16[256,1024]{1,0:T(8,128)(2,1)}, u32[]{:S(2)}, u32[]{:S(2)}) collective-permute-start(bf16[256,1024]{1,0:T(8,128)(2,1)S(1)} %pad_maximum_fusion.1.q_ref), channel_id=1, source_target_pairs={{0,4},{2,6},{4,0},{6,2},{1,5},{3,7},{5,1},{7,3},{8,12},{10,14},{12... | collective-permute-start | bytes 1572872 | tf_op jit(solution)/shard_map/ppermute | solution.py:341
  28.2 0.7 collective-permute-start.8
  29.2 1.2 layer_norm.1.own_in
  30.4 17.5 %collective-permute-done.4.q_ref = bf16[256,1024]{1,0:T(8,128)(2,1)} collective-permute-done((bf16[256,1024]{1,0:T(8,128)(2,1)S(1)}, bf16[256,1024]{1,0:T(8,128)(2,1)}, u32[]{:S(2)}, u32[]{:S(2)}) %collective-permute-start.4) | collective-permute-done | bytes 524320 | tf_op jit(solution)/shard_map/ppermute | solution.py:341
  47.9 2.5 %collective-permute-start.22 = (bf16[128,2048]{1,0:T(8,128)(2,1)}, bf16[128,2048]{1,0:T(8,128)(2,1)}, u32[]{:S(2)}, u32[]{:S(2)}) collective-permute-start(bf16[128,2048]{1,0:T(8,128)(2,1)} %layer_norm.1.own_in), channel_id=1, source_target_pairs={{0,96},{32,0},{64,32},{96,64},{1,97},{33,1},{65,33},{97,65},{2,98}... | collective-permute-start | bytes 1572872 | tf_op jit(solution)/shard_map/ppermute | solution.py:347
  50.4 1.7 collective-permute-start.12
  52.1 2.2 copy-done.2
  54.3 2.2 copy-done.5
  56.5 10.6 %attend.5 = bf16[256,1152]{1,0:T(8,128)(2,1)} custom-call(s32[5]{0:T(128)S(1)} %stack.78.place, s32[16,2]{1,0:T(8,128)S(1)} %copy.10.ranges, bf16[256,1024]{1,0:T(8,128)(2,1)} %collective-permute-done.4.q_ref, bf16[1024,2048]{1,0:T(8,128)(2,1)S(1)} %copy-done.2, bf16[1024,1024]{1,0:T(8,128)(2,1)} %collective-permute-done.2.k1, ...), custom_call_target="tpu_custom_call" | custom-call | flops 2415919104 | bytes 10485760 | tf_op jit(solution)/shard_map/attend/pallas_call | solution.py:176
  67.1 0.8 collective-permute-start.5
  67.9 10.6 %attend.6 = bf16[256,1152]{1,0:T(8,128)(2,1)} custom-call(s32[5]{0:T(128)S(1)} %stack.80.place, s32[16,2]{1,0:T(8,128)S(1)} %copy.10.ranges, bf16[256,1024]{1,0:T(8,128)(2,1)} %collective-permute-done.6.q_ref, bf16[1024,2048]{1,0:T(8,128)(2,1)S(1)} %copy-done.2, bf16[1024,1024]{1,0:T(8,128)(2,1)} %collective-permute-done.2.k1, ...), custom_call_target="tpu_custom_call" | custom-call | flops 2415919104 | bytes 10485760 | tf_op jit(solution)/shard_map/attend/pallas_call | solution.py:176
  78.5 10.5 %attend.7 = bf16[256,1152]{1,0:T(8,128)(2,1)} custom-call(s32[5]{0:T(128)S(1)} %stack.82.place, s32[16,2]{1,0:T(8,128)S(1)} %copy.10.ranges, bf16[256,1024]{1,0:T(8,128)(2,1)} %collective-permute-done.8.q_ref, bf16[1024,2048]{1,0:T(8,128)(2,1)S(1)} %copy-done.2, bf16[1024,1024]{1,0:T(8,128)(2,1)} %collective-permute-done.2.k1, ...), custom_call_target="tpu_custom_call" | custom-call | flops 2415919104 | bytes 10485760 | tf_op jit(solution)/shard_map/attend/pallas_call | solution.py:176
  89.0 0.8 collective-permute-start.9
  89.8 44.2 %all-gather.3.cloned.1.call-done = bf16[2304,2048]{1,0:T(8,128)(2,1)} async-done(((bf16[144,2048]{1,0:T(8,128)(2,1)}), bf16[2304,2048]{1,0:T(8,128)(2,1)}) %all-gather.3.cloned.1.call-update) | async-done | bytes 9437200 | tf_op jit(solution)/shard_map/all_gather | solution.py:330
  134.1 1.3 slice.26
  135.4 1.0 dynamic-slice_bitcast_fusion
  136.4 0.7 collective-permute-start.10
  137.5 2.3 %copy-done.3 = bf16[1024,2048]{1,0:T(8,128)(2,1)S(1)} copy-done((bf16[1024,2048]{1,0:T(8,128)(2,1)S(1)}, bf16[1024,2048]{1,0:T(8,128)(2,1)}, u32[]{:S(2)}) %copy-start.3) | copy-done | bytes 4194328
  139.8 2.9 %copy-done.6 = bf16[1024,2048]{1,0:T(8,128)(2,1)S(1)} copy-done((bf16[1024,2048]{1,0:T(8,128)(2,1)S(1)}, bf16[1024,2048]{1,0:T(8,128)(2,1)}, u32[]{:S(2)}) %copy-start.6) | copy-done | bytes 4194328
  142.7 1.0 copy-done.8
  143.8 9.8 %attend.4.a = bf16[256,1152]{1,0:T(8,128)(2,1)S(1)} custom-call(s32[5]{0:T(128)S(1)} %stack.76.place, s32[16,2]{1,0:T(8,128)S(1)} %copy.10.ranges, bf16[256,1024]{1,0:T(8,128)(2,1)S(1)} %copy-done.8, bf16[1024,2048]{1,0:T(8,128)(2,1)S(1)} %copy-done.3, bf16[1024,1024]{1,0:T(8,128)(2,1)} %collective-permute-done.2.k1, bf16[1024,2048]{1,0:T(8,128)(2,1)S(1)} %copy-done.6, ...), custom_call_target="tpu_custom_call" | custom-call | flops 2415919104 | bytes 10485760 | tf_op jit(solution)/shard_map/attend/pallas_call | solution.py:176
  153.6 0.4 collective-permute-start
  154.5 3.1 %merge.1 = bf16[4,256,256]{2,1,0:T(8,128)(2,1)S(1)} custom-call(s32[5]{0:T(128)S(1)} %stack.74.place_ref.place, bf16[256,1152]{1,0:T(8,128)(2,1)S(1)} %attend.4.a, bf16[256,1152]{1,0:T(8,128)(2,1)} %collective-permute-done.5.b, bf16[256,1152]{1,0:T(8,128)(2,1)} %collective-permute-done.7.c, bf16[256,1152]{1,0:T(8,128)(2,1)} %collective-permute-done.9.d), custom_call_target="tpu_custom_call" | custom-call | tf_op jit(solution)/shard_map/merge/pallas_call | solution.py:242
  157.6 2.5 %collective-permute-start.24 = (bf16[256,256]{1,0:T(8,128)(2,1)S(1)}, bf16[256,256]{1,0:T(8,128)(2,1)S(1)}, u32[]{:S(2)}, u32[]{:S(2)}) collective-permute-start(bf16[256,256]{1,0:T(8,128)(2,1)S(1)} %get-tuple-element.28), channel_id=1, source_target_pairs={{0,96},{32,0},{64,32},{96,64},{1,97},{33,1},{65,33},{97,65},{2,98}... | collective-permute-start | bytes 393224 | tf_op jit(solution)/shard_map/ppermute | solution.py:366
  160.2 1.4 maximum_select_fusion
  161.8 1.1 collective-permute-done.24.attention
  162.9 2.5 %collective-permute-start.14 = (bf16[256,256]{1,0:T(8,128)(2,1)S(1)}, bf16[256,256]{1,0:T(8,128)(2,1)S(1)}, u32[]{:S(2)}, u32[]{:S(2)}) collective-permute-start(bf16[256,256]{1,0:T(8,128)(2,1)S(1)} %get-tuple-element.30), channel_id=1, source_target_pairs={{0,64},{32,96},{64,0},{96,32},{1,65},{33,97},{65,1},{97,33},{2,66}... | collective-permute-start | bytes 393224 | tf_op jit(solution)/shard_map/ppermute | solution.py:366
  165.4 7.0 %units.7 = (f32[128,2048]{1,0:T(8,128)S(1)}, bf16[128,2048]{1,0:T(8,128)(2,1)S(1)}) custom-call(bf16[128,2048]{1,0:T(8,128)(2,1)} %collective-permute-done.22.own_in, bf16[128,2048]{1,0:T(8,128)(2,1)S(1)} %collective-permute-done.23.other_in, bf16[256,256]{1,0:T(8,128)(2,1)S(1)} %collective-permute-done.24.attention, bf16[16,144,2048]{2,1,0:T(8,128)(2,1)S(1)} %bitcast.25, ...), custom_call_target="tpu_custom_call" | custom-call | flops 2415919104 | bytes 13631488 | tf_op jit(solution)/shard_map/units/pallas_call | solution.py:284
  172.4 1.3 collective-permute-start.25
  173.7 6.9 %units.6 = (f32[128,2048]{1,0:T(8,128)S(1)}, bf16[128,2048]{1,0:T(8,128)(2,1)S(1)}) custom-call(bf16[128,2048]{1,0:T(8,128)(2,1)} %collective-permute-done.17.own_in, bf16[128,2048]{1,0:T(8,128)(2,1)S(1)} %collective-permute-done.18.other_in, bf16[256,256]{1,0:T(8,128)(2,1)S(1)} %collective-permute-done.19.attention, bf16[16,144,2048]{2,1,0:T(8,128)(2,1)S(1)} %bitcast.26, ...), custom_call_target="tpu_custom_call" | custom-call | flops 2415919104 | bytes 13631488 | tf_op jit(solution)/shard_map/units/pallas_call | solution.py:284
  180.8 7.0 %units.5 = (f32[128,2048]{1,0:T(8,128)S(1)}, bf16[128,2048]{1,0:T(8,128)(2,1)S(1)}) custom-call(bf16[128,2048]{1,0:T(8,128)(2,1)} %collective-permute-done.12.own_in, bf16[128,2048]{1,0:T(8,128)(2,1)S(1)} %collective-permute-done.13.other_in, bf16[256,256]{1,0:T(8,128)(2,1)S(1)} %collective-permute-done.14.attention, bf16[16,144,2048]{2,1,0:T(8,128)(2,1)S(1)} %bitcast.27, ...), custom_call_target="tpu_custom_call" | custom-call | flops 2415919104 | bytes 13631488 | tf_op jit(solution)/shard_map/units/pallas_call | solution.py:284
  187.7 0.5 collective-permute-start.15
  188.3 6.9 %units.4 = (f32[128,2048]{1,0:T(8,128)S(1)}, bf16[128,2048]{1,0:T(8,128)(2,1)S(1)}) custom-call(bf16[128,2048]{1,0:T(8,128)(2,1)} %layer_norm.1.own_in, bf16[128,2048]{1,0:T(8,128)(2,1)S(1)} %collective-permute-done.other_in, bf16[256,256]{1,0:T(8,128)(2,1)S(1)} %get-tuple-element.27.attention, bf16[16,144,2048]{2,1,0:T(8,128)(2,1)S(1)} %bitcast.28, ...), custom_call_target="tpu_custom_call" | custom-call | flops 2415919104 | bytes 13631488 | tf_op jit(solution)/shard_map/units/pallas_call | solution.py:284
  195.5 1.6 collective-permute-start.26
  197.2 1.2 collective-permute-start.21
  198.5 0.7 collective-permute-start.16
  199.3 11.1 %collective-permute-done.26 = bf16[128,2048]{1,0:T(8,128)(2,1)S(1)} collective-permute-done((bf16[128,2048]{1,0:T(8,128)(2,1)S(1)}, bf16[128,2048]{1,0:T(8,128)(2,1)S(1)}, u32[]{:S(2)}, u32[]{:S(2)}) %collective-permute-start.26) | collective-permute-done | bytes 524320 | tf_op jit(solution)/shard_map/ppermute | solution.py:387
  210.4 10.0 %collective-permute-done.16 = bf16[128,2048]{1,0:T(8,128)(2,1)S(1)} collective-permute-done((bf16[128,2048]{1,0:T(8,128)(2,1)S(1)}, bf16[128,2048]{1,0:T(8,128)(2,1)S(1)}, u32[]{:S(2)}, u32[]{:S(2)}) %collective-permute-start.16) | collective-permute-done | bytes 524320 | tf_op jit(solution)/shard_map/ppermute | solution.py:387
  220.5 1.3 add_convert_fusion
  (75 shorter events, 2.3 us)
Async XLA Ops:
  6.5 127.5 %all-gather.3.cloned.1.call-start = ((), (), s32[]{:S(2)}) async-start(), calls=%async_computation | async-start | bytes 10027008 | tf_op jit(solution)/shard_map/all_gather | solution.py:330
  8.6 2.2 copy-start.1
  10.8 4.1 %copy-start.4 = (bf16[1024,2048]{1,0:T(8,128)(2,1)S(1)}, bf16[1024,2048]{1,0:T(8,128)(2,1)}, u32[]{:S(2)}) copy-start(bf16[1024,2048]{1,0:T(8,128)(2,1)} %v0.7) | copy-start | bytes 12582916
  13.5 4.2 %copy-start = (bf16[128,6144]{1,0:T(8,128)(2,1)S(1)}, bf16[128,6144]{1,0:T(8,128)(2,1)}, u32[]{:S(2)}) copy-start(bf16[128,6144]{1,0:T(8,128)(2,1)} %nv0.7) | copy-start | bytes 4718596
  13.5 36.9 %collective-permute-start.2 = (bf16[1024,1024]{1,0:T(8,128)(2,1)}, bf16[1024,1024]{1,0:T(8,128)(2,1)}, u32[]{:S(2)}, u32[]{:S(2)}) collective-permute-start(bf16[1024,1024]{1,0:T(8,128)(2,1)} %pick_cache.2), channel_id=1, source_target_pairs={{0,1},{1,0},{2,3},{3,2},{4,5},{5,4},{6,7},{7,6},{8,9},{9,8},{10,11... | collective-permute-start | bytes 6291464 | tf_op jit(solution)/shard_map/ppermute | solution.py:25
  17.7 11.2 %copy-start.13 = (s32[16,2]{0,1:T(2,128)S(1)}, s32[16,2]{0,1:T(2,128)}, u32[]{:S(2)}) copy-start(s32[16,2]{0,1:T(2,128)} %param.13) | copy-start | bytes 388
  17.7 11.5 %copy-start.9 = (bf16[128,2048]{1,0:T(8,128)(2,1)S(1)}, bf16[128,2048]{1,0:T(8,128)(2,1)}, u32[]{:S(2)}) copy-start(bf16[128,2048]{1,0:T(8,128)(2,1)} %stream.1) | copy-start | bytes 1572868
  17.7 11.5 %copy-start.11 = (f32[2048]{0:T(1024)S(1)}, f32[2048]{0:T(1024)}, u32[]{:S(2)}) copy-start(f32[2048]{0:T(1024)} %param.14) | copy-start | bytes 24580
  17.7 32.7 %collective-permute-start.3 = (bf16[1024,1024]{1,0:T(8,128)(2,1)}, bf16[1024,1024]{1,0:T(8,128)(2,1)}, u32[]{:S(2)}, u32[]{:S(2)}) collective-permute-start(bf16[1024,1024]{1,0:T(8,128)(2,1)} %pick_cache.3), channel_id=1, source_target_pairs={{0,1},{1,0},{2,3},{3,2},{4,5},{5,4},{6,7},{7,6},{8,9},{9,8},{10,11... | collective-permute-start | bytes 6291464 | tf_op jit(solution)/shard_map/ppermute | solution.py:25
  18.4 4.6 %collective-permute-start.1 = (bf16[128,3072]{1,0:T(8,128)(2,1)S(1)}, bf16[128,3072]{1,0:T(8,128)(2,1)S(1)}, u32[]{:S(2)}, u32[]{:S(2)}) collective-permute-start(bf16[128,3072]{1,0:T(8,128)(2,1)S(1)} %get-tuple-element.16), channel_id=1, source_target_pairs={{0,1},{1,0},{2,3},{3,2},{4,5},{5,4},{6,7},{7,6},{8,9},{9,8},{10,11... | collective-permute-start | bytes 2359304 | tf_op jit(solution)/shard_map/ppermute | solution.py:25
  23.1 44.0 %copy-start.7 = (bf16[256,1024]{1,0:T(8,128)(2,1)}, bf16[256,1024]{1,0:T(8,128)(2,1)S(1)}, u32[]{:S(2)}) copy-start(bf16[256,1024]{1,0:T(8,128)(2,1)S(1)} %pad_maximum_fusion.1.q_ref) | copy-start | bytes 1572868
  23.1 24.8 %collective-permute-start.4 = (bf16[256,1024]{1,0:T(8,128)(2,1)S(1)}, bf16[256,1024]{1,0:T(8,128)(2,1)}, u32[]{:S(2)}, u32[]{:S(2)}) collective-permute-start(bf16[256,1024]{1,0:T(8,128)(2,1)S(1)} %pad_maximum_fusion.1.q_ref), channel_id=1, source_target_pairs={{0,2},{2,4},{4,6},{6,0},{1,3},{3,5},{5,7},{7,1},{8,10},{10,12},{12... | collective-permute-start | bytes 1572872 | tf_op jit(solution)/shard_map/ppermute | solution.py:341
  24.9 42.2 %collective-permute-start.6 = (bf16[256,1024]{1,0:T(8,128)(2,1)S(1)}, bf16[256,1024]{1,0:T(8,128)(2,1)}, u32[]{:S(2)}, u32[]{:S(2)}) collective-permute-start(bf16[256,1024]{1,0:T(8,128)(2,1)S(1)} %pad_maximum_fusion.1.q_ref), channel_id=1, source_target_pairs={{0,4},{2,6},{4,0},{6,2},{1,5},{3,7},{5,1},{7,3},{8,12},{10,14},{12... | collective-permute-start | bytes 1572872 | tf_op jit(solution)/shard_map/ppermute | solution.py:341
  28.2 50.3 %collective-permute-start.8 = (bf16[256,1024]{1,0:T(8,128)(2,1)S(1)}, bf16[256,1024]{1,0:T(8,128)(2,1)}, u32[]{:S(2)}, u32[]{:S(2)}) collective-permute-start(bf16[256,1024]{1,0:T(8,128)(2,1)S(1)} %pad_maximum_fusion.1.q_ref), channel_id=1, source_target_pairs={{0,6},{2,0},{4,2},{6,4},{1,7},{3,1},{5,3},{7,5},{8,14},{10,8},{12,... | collective-permute-start | bytes 1572872 | tf_op jit(solution)/shard_map/ppermute | solution.py:341
  47.9 41.1 %collective-permute-start.22 = (bf16[128,2048]{1,0:T(8,128)(2,1)}, bf16[128,2048]{1,0:T(8,128)(2,1)}, u32[]{:S(2)}, u32[]{:S(2)}) collective-permute-start(bf16[128,2048]{1,0:T(8,128)(2,1)} %layer_norm.1.own_in), channel_id=1, source_target_pairs={{0,96},{32,0},{64,32},{96,64},{1,97},{33,1},{65,33},{97,65},{2,98}... | collective-permute-start | bytes 1572872 | tf_op jit(solution)/shard_map/ppermute | solution.py:347
  50.4 86.0 %collective-permute-start.17 = (bf16[128,2048]{1,0:T(8,128)(2,1)}, bf16[128,2048]{1,0:T(8,128)(2,1)}, u32[]{:S(2)}, u32[]{:S(2)}) collective-permute-start(bf16[128,2048]{1,0:T(8,128)(2,1)} %layer_norm.1.own_in), channel_id=1, source_target_pairs={{0,32},{32,64},{64,96},{96,0},{1,33},{33,65},{65,97},{97,1},{2,34}... | collective-permute-start | bytes 1572872 | tf_op jit(solution)/shard_map/ppermute | solution.py:347
  50.4 86.8 %collective-permute-start.12 = (bf16[128,2048]{1,0:T(8,128)(2,1)}, bf16[128,2048]{1,0:T(8,128)(2,1)}, u32[]{:S(2)}, u32[]{:S(2)}) collective-permute-start(bf16[128,2048]{1,0:T(8,128)(2,1)} %layer_norm.1.own_in), channel_id=1, source_target_pairs={{0,64},{32,96},{64,0},{96,32},{1,65},{33,97},{65,1},{97,33},{2,66}... | collective-permute-start | bytes 1572872 | tf_op jit(solution)/shard_map/ppermute | solution.py:347
  52.1 2.2 copy-start.2
  54.3 2.2 copy-start.5
  67.1 86.5 %collective-permute-start.5 = (bf16[256,1152]{1,0:T(8,128)(2,1)}, bf16[256,1152]{1,0:T(8,128)(2,1)}, u32[]{:S(2)}, u32[]{:S(2)}) collective-permute-start(bf16[256,1152]{1,0:T(8,128)(2,1)} %attend.5), channel_id=1, source_target_pairs={{0,6},{2,0},{4,2},{6,4},{1,7},{3,1},{5,3},{7,5},{8,14},{10,8},{12,... | collective-permute-start | bytes 1769480 | tf_op jit(solution)/shard_map/ppermute | solution.py:364
  78.4 75.6 %collective-permute-start.7 = (bf16[256,1152]{1,0:T(8,128)(2,1)}, bf16[256,1152]{1,0:T(8,128)(2,1)}, u32[]{:S(2)}, u32[]{:S(2)}) collective-permute-start(bf16[256,1152]{1,0:T(8,128)(2,1)} %attend.6), channel_id=1, source_target_pairs={{0,4},{2,6},{4,0},{6,2},{1,5},{3,7},{5,1},{7,3},{8,12},{10,14},{12... | collective-permute-start | bytes 1769480 | tf_op jit(solution)/shard_map/ppermute | solution.py:364
  89.0 65.2 %collective-permute-start.9 = (bf16[256,1152]{1,0:T(8,128)(2,1)}, bf16[256,1152]{1,0:T(8,128)(2,1)}, u32[]{:S(2)}, u32[]{:S(2)}) collective-permute-start(bf16[256,1152]{1,0:T(8,128)(2,1)} %attend.7), channel_id=1, source_target_pairs={{0,2},{2,4},{4,6},{6,0},{1,3},{3,5},{5,7},{7,1},{8,10},{10,12},{12... | collective-permute-start | bytes 1769480 | tf_op jit(solution)/shard_map/ppermute | solution.py:364
  135.4 30.0 %slice-start = ((s8[9437184]{0:T(1024)(128)(4,1)}), s8[1048576]{0:T(1024)(128)(4,1)S(1)}, s32[]{:S(2)}) async-start(s8[9437184]{0:T(1024)(128)(4,1)} %bitcast.23), calls=%async_computation.1 | async-start | bytes 2097152
  136.4 21.2 %collective-permute-start.10 = (bf16[8,16,2048]{2,1,0:T(8,128)(2,1)}, bf16[8,16,2048]{2,1,0:T(8,128)(2,1)}, u32[]{:S(2)}, u32[]{:S(2)}) collective-permute-start(bf16[8,16,2048]{2,1,0:T(8,128)(2,1)} %get-tuple-element.26), channel_id=1, source_target_pairs={{0,1},{1,0},{2,3},{3,2},{4,5},{5,4},{6,7},{7,6},{8,9},{9,8},{10,11... | collective-permute-start | bytes 1572872 | tf_op jit(solution)/shard_map/ppermute | solution.py:25
  137.2 28.2 %slice-start.1 = ((s8[9437184]{0:T(1024)(128)(4,1)}), s8[4194304]{0:T(1024)(128)(4,1)S(1)}, s32[]{:S(2)}) async-start(s8[9437184]{0:T(1024)(128)(4,1)} %bitcast.23), calls=%async_computation.2 | async-start | bytes 8388608
  137.2 28.2 %slice-start.2 = ((s8[9437184]{0:T(1024)(128)(4,1)}), s8[4194304]{0:T(1024)(128)(4,1)S(1)}, s32[]{:S(2)}) async-start(s8[9437184]{0:T(1024)(128)(4,1)} %bitcast.23), calls=%async_computation.3 | async-start | bytes 8388608
  137.2 24.5 %collective-permute-start.23 = (bf16[128,2048]{1,0:T(8,128)(2,1)}, bf16[128,2048]{1,0:T(8,128)(2,1)S(1)}, u32[]{:S(2)}, u32[]{:S(2)}) collective-permute-start(bf16[128,2048]{1,0:T(8,128)(2,1)} %collective-permute-done.22.own_in), channel_id=1, source_target_pairs={{0,1},{1,0},{2,3},{3,2},{4,5},{5,4},{6,7},{7,6},{8,9},{9,8},{10,11... | collective-permute-start | bytes 1572872 | tf_op jit(solution)/shard_map/ppermute | solution.py:25
  137.5 2.3 %copy-start.3 = (bf16[1024,2048]{1,0:T(8,128)(2,1)S(1)}, bf16[1024,2048]{1,0:T(8,128)(2,1)}, u32[]{:S(2)}) copy-start(bf16[1024,2048]{1,0:T(8,128)(2,1)} %k0.7) | copy-start | bytes 12582916
  139.8 2.9 %copy-start.6 = (bf16[1024,2048]{1,0:T(8,128)(2,1)S(1)}, bf16[1024,2048]{1,0:T(8,128)(2,1)}, u32[]{:S(2)}) copy-start(bf16[1024,2048]{1,0:T(8,128)(2,1)} %v0.7) | copy-start | bytes 12582916
  142.7 1.0 copy-start.8
  153.6 6.6 %copy-start.12 = (bf16[8,1,16,2048]{3,2,0,1:T(8,128)(2,1)S(1)}, bf16[8,1,16,2048]{3,2,0,1:T(8,128)(2,1)}, u32[]{:S(2)}) copy-start(bf16[8,1,16,2048]{3,2,0,1:T(8,128)(2,1)} %get-tuple-element.25) | copy-start | bytes 1572868
  153.6 34.7 %collective-permute-start = (bf16[128,2048]{1,0:T(8,128)(2,1)}, bf16[128,2048]{1,0:T(8,128)(2,1)S(1)}, u32[]{:S(2)}, u32[]{:S(2)}) collective-permute-start(bf16[128,2048]{1,0:T(8,128)(2,1)} %layer_norm.1.own_in), channel_id=1, source_target_pairs={{0,1},{1,0},{2,3},{3,2},{4,5},{5,4},{6,7},{7,6},{8,9},{9,8},{10,11... | collective-permute-start | bytes 1572872 | tf_op jit(solution)/shard_map/ppermute | solution.py:25
  154.0 18.3 %collective-permute-start.18 = (bf16[128,2048]{1,0:T(8,128)(2,1)}, bf16[128,2048]{1,0:T(8,128)(2,1)S(1)}, u32[]{:S(2)}, u32[]{:S(2)}) collective-permute-start(bf16[128,2048]{1,0:T(8,128)(2,1)} %collective-permute-done.17.own_in), channel_id=1, source_target_pairs={{0,1},{1,0},{2,3},{3,2},{4,5},{5,4},{6,7},{7,6},{8,9},{9,8},{10,11... | collective-permute-start | bytes 1572872 | tf_op jit(solution)/shard_map/ppermute | solution.py:25
  154.2 26.6 %collective-permute-start.13 = (bf16[128,2048]{1,0:T(8,128)(2,1)}, bf16[128,2048]{1,0:T(8,128)(2,1)S(1)}, u32[]{:S(2)}, u32[]{:S(2)}) collective-permute-start(bf16[128,2048]{1,0:T(8,128)(2,1)} %collective-permute-done.12.own_in), channel_id=1, source_target_pairs={{0,1},{1,0},{2,3},{3,2},{4,5},{5,4},{6,7},{7,6},{8,9},{9,8},{10,11... | collective-permute-start | bytes 1572872 | tf_op jit(solution)/shard_map/ppermute | solution.py:25
  157.6 5.3 %collective-permute-start.24 = (bf16[256,256]{1,0:T(8,128)(2,1)S(1)}, bf16[256,256]{1,0:T(8,128)(2,1)S(1)}, u32[]{:S(2)}, u32[]{:S(2)}) collective-permute-start(bf16[256,256]{1,0:T(8,128)(2,1)S(1)} %get-tuple-element.28), channel_id=1, source_target_pairs={{0,96},{32,0},{64,32},{96,64},{1,97},{33,1},{65,33},{97,65},{2,98}... | collective-permute-start | bytes 393224 | tf_op jit(solution)/shard_map/ppermute | solution.py:366
  161.7 12.0 %collective-permute-start.19 = (bf16[256,256]{1,0:T(8,128)(2,1)S(1)}, bf16[256,256]{1,0:T(8,128)(2,1)S(1)}, u32[]{:S(2)}, u32[]{:S(2)}) collective-permute-start(bf16[256,256]{1,0:T(8,128)(2,1)S(1)} %get-tuple-element.29), channel_id=1, source_target_pairs={{0,32},{32,64},{64,96},{96,0},{1,33},{33,65},{65,97},{97,1},{2,34}... | collective-permute-start | bytes 393224 | tf_op jit(solution)/shard_map/ppermute | solution.py:366
  162.9 17.9 %collective-permute-start.14 = (bf16[256,256]{1,0:T(8,128)(2,1)S(1)}, bf16[256,256]{1,0:T(8,128)(2,1)S(1)}, u32[]{:S(2)}, u32[]{:S(2)}) collective-permute-start(bf16[256,256]{1,0:T(8,128)(2,1)S(1)} %get-tuple-element.30), channel_id=1, source_target_pairs={{0,64},{32,96},{64,0},{96,32},{1,65},{33,97},{65,1},{97,33},{2,66}... | collective-permute-start | bytes 393224 | tf_op jit(solution)/shard_map/ppermute | solution.py:366
  172.4 23.0 %collective-permute-start.25 = (bf16[128,2048]{1,0:T(8,128)(2,1)S(1)}, bf16[128,2048]{1,0:T(8,128)(2,1)S(1)}, u32[]{:S(2)}, u32[]{:S(2)}) collective-permute-start(bf16[128,2048]{1,0:T(8,128)(2,1)S(1)} %get-tuple-element.24), channel_id=1, source_target_pairs={{0,1},{1,0},{2,3},{3,2},{4,5},{5,4},{6,7},{7,6},{8,9},{9,8},{10,11... | collective-permute-start | bytes 1572872 | tf_op jit(solution)/shard_map/ppermute | solution.py:25
  180.7 16.4 %collective-permute-start.20 = (bf16[128,2048]{1,0:T(8,128)(2,1)S(1)}, bf16[128,2048]{1,0:T(8,128)(2,1)S(1)}, u32[]{:S(2)}, u32[]{:S(2)}) collective-permute-start(bf16[128,2048]{1,0:T(8,128)(2,1)S(1)} %get-tuple-element.22), channel_id=1, source_target_pairs={{0,1},{1,0},{2,3},{3,2},{4,5},{5,4},{6,7},{7,6},{8,9},{9,8},{10,11... | collective-permute-start | bytes 1572872 | tf_op jit(solution)/shard_map/ppermute | solution.py:25
  187.7 10.7 %collective-permute-start.15 = (bf16[128,2048]{1,0:T(8,128)(2,1)S(1)}, bf16[128,2048]{1,0:T(8,128)(2,1)S(1)}, u32[]{:S(2)}, u32[]{:S(2)}) collective-permute-start(bf16[128,2048]{1,0:T(8,128)(2,1)S(1)} %get-tuple-element.20), channel_id=1, source_target_pairs={{0,1},{1,0},{2,3},{3,2},{4,5},{5,4},{6,7},{7,6},{8,9},{9,8},{10,11... | collective-permute-start | bytes 1572872 | tf_op jit(solution)/shard_map/ppermute | solution.py:25
  195.2 4.0 %collective-permute-start.11 = (bf16[128,2048]{1,0:T(8,128)(2,1)S(1)}, bf16[128,2048]{1,0:T(8,128)(2,1)S(1)}, u32[]{:S(2)}, u32[]{:S(2)}) collective-permute-start(bf16[128,2048]{1,0:T(8,128)(2,1)S(1)} %get-tuple-element.18), channel_id=1, source_target_pairs={{0,1},{1,0},{2,3},{3,2},{4,5},{5,4},{6,7},{7,6},{8,9},{9,8},{10,11... | collective-permute-start | bytes 1572872 | tf_op jit(solution)/shard_map/ppermute | solution.py:25
  195.5 14.9 %collective-permute-start.26 = (bf16[128,2048]{1,0:T(8,128)(2,1)S(1)}, bf16[128,2048]{1,0:T(8,128)(2,1)S(1)}, u32[]{:S(2)}, u32[]{:S(2)}) collective-permute-start(bf16[128,2048]{1,0:T(8,128)(2,1)S(1)} %add_convert_fusion.1), channel_id=1, source_target_pairs={{0,32},{32,64},{64,96},{96,0},{1,33},{33,65},{65,97},{97,1},{2,34}... | collective-permute-start | bytes 1572872 | tf_op jit(solution)/shard_map/ppermute | solution.py:387
  197.1 23.4 %copy-start.10 = (bf16[128,2048]{1,0:T(8,128)(2,1)S(1)}, bf16[128,2048]{1,0:T(8,128)(2,1)}, u32[]{:S(2)}) copy-start(bf16[128,2048]{1,0:T(8,128)(2,1)} %stream.1) | copy-start | bytes 1572868
  197.2 13.2 %collective-permute-start.21 = (bf16[128,2048]{1,0:T(8,128)(2,1)S(1)}, bf16[128,2048]{1,0:T(8,128)(2,1)S(1)}, u32[]{:S(2)}, u32[]{:S(2)}) collective-permute-start(bf16[128,2048]{1,0:T(8,128)(2,1)S(1)} %add_convert_fusion.2), channel_id=1, source_target_pairs={{0,96},{32,0},{64,32},{96,64},{1,97},{33,1},{65,33},{97,65},{2,98}... | collective-permute-start | bytes 1572872 | tf_op jit(solution)/shard_map/ppermute | solution.py:387
  198.5 21.9 %collective-permute-start.16 = (bf16[128,2048]{1,0:T(8,128)(2,1)S(1)}, bf16[128,2048]{1,0:T(8,128)(2,1)S(1)}, u32[]{:S(2)}, u32[]{:S(2)}) collective-permute-start(bf16[128,2048]{1,0:T(8,128)(2,1)S(1)} %add_convert_fusion.3), channel_id=1, source_target_pairs={{0,64},{32,96},{64,0},{96,32},{1,65},{33,97},{65,1},{97,33},{2,66}... | collective-permute-start | bytes 1572872 | tf_op jit(solution)/shard_map/ppermute | solution.py:387
Sparse Core Ops, SparseCore 0:
  9.5 124.4 all-gather.2

commit v2 on v1

--- a/solution.py
+++ b/solution.py
@@ -216,7 +216,7 @@
 
 
 def merge_kernel(place, a, b, c, d, out):
-    y = place[4]
+    z = place[1]
     count = out.shape[0]
     parts = (a, b, c, d)
     base = a.shape[1] - 128
@@ -232,7 +232,7 @@
         summed = sum(
             f * part[:, j * HD : (j + 1) * HD].astype(F32) for f, part in zip(factors, parts)
         )
-        out[lax.rem(j - y + count, count)] = (summed / total).astype(BF16)
+        out[lax.rem(j - z + count, count)] = (summed / total).astype(BF16)
 
 
 def merge(place, parts):
@@ -253,61 +253,95 @@
     )(place, *parts)
 
 
-def units_kernel(own_in, other_in, attention, weights, out_rows, own, other, total):
-    step = pl.program_id(0)
-    unit_rows = (weights.shape[1] * 4) // 9
-    count = weights.shape[0] * unit_rows
-    width = own_in.shape[1]
-    rows = own_in.shape[0]
-
-    @pl.when(step == 0)
-    def _():
-        total[...] = dot(attention[...], out_rows[...], ((1,), (0,)))
-
-    inputs = jnp.concatenate([own_in[...], other_in[...]], 0)
-    up = weights[:, :unit_rows, :].reshape(count, width)
-    down = weights[:, unit_rows : 2 * unit_rows, :].reshape(count, width)
-    gates = dot(inputs, up, ((1,), (1,)))
-    hidden = (0.5 * gates * (1.0 + lax.erf(gates * math.sqrt(0.5)))).astype(BF16)
-    total[...] += dot(hidden, down, ((1,), (0,)))
-
-    @pl.when(step == pl.num_programs(0) - 1)
-    def _():
-        own[...] = total[:rows, :]
-        other[...] = total[rows:, :].astype(BF16)
-
-
-def add_units(own_in, other_in, attention, weights, out_rows):
+def hidden_kernel(own_in, other_in, up_ref, own, other):
+    shards, rows, width = up_ref.shape
+    up = up_ref[...].reshape(shards * rows, width)
+    for inputs, out in ((own_in, own), (other_in, other)):
+        gates = dot(inputs[...], up, ((1,), (1,)))
+        out[...] = (0.5 * gates * (1.0 + lax.erf(gates * math.sqrt(0.5)))).astype(BF16)
+
+
+def hidden_units(own_in, other_in, weights, unit_rows):
     rows, width = own_in.shape
-    shards, shard_rows, _ = weights.shape
+    shards = weights.shape[0]
     chunk = 4
-    return pl.pallas_call(
-        units_kernel,
+    count = chunk * unit_rows
+    whole = pl.BlockSpec((rows, width), lambda i: (0, 0))
+    part = pl.BlockSpec((rows, count), lambda i: (0, i))
+    return pl.pallas_call(
+        hidden_kernel,
         grid=(shards // chunk,),
         in_specs=[
-            pl.BlockSpec((rows, width), lambda i: (0, 0)),
-            pl.BlockSpec((rows, width), lambda i: (0, 0)),
-            pl.BlockSpec((2 * rows, HD), lambda i: (0, 0)),
-            pl.BlockSpec((chunk, shard_rows, width), lambda i: (i, 0, 0)),
-            pl.BlockSpec((HD, width), lambda i: (0, 0)),
+            whole,
+            whole,
+            pl.BlockSpec((chunk, unit_rows, width), lambda i: (i, 0, 0)),
         ],
-        out_specs=[
-            pl.BlockSpec((rows, width), lambda i: (0, 0)),
-            pl.BlockSpec((rows, width), lambda i: (0, 0)),
-        ],
-        out_shape=[
-            jax.ShapeDtypeStruct((rows, width), F32),
-            jax.ShapeDtypeStruct((rows, width), BF16),
-        ],
-        scratch_shapes=[pltpu.VMEM((2 * rows, width), F32)],
+        out_specs=[part, part],
+        out_shape=[jax.ShapeDtypeStruct((rows, shards * unit_rows), BF16)] * 2,
         compiler_params=params(40),
         cost_estimate=pl.CostEstimate(
-            flops=2 * 2 * rows * shards * shard_rows * width,
+            flops=4 * rows * shards * unit_rows * width,
             transcendentals=0,
-            bytes_accessed=2 * shards * shard_rows * width + 16 * rows * width,
-        ),
-        name="units",
-    )(own_in, other_in, attention, weights, out_rows)
+            bytes_accessed=2 * shards * unit_rows * width + 4 * rows * width,
+        ),
+        name="hidden_units",
+    )(own_in, other_in, weights)
+
+
+def down_kernel(hidden, a0, a1, a2, a3, down_ref, out_ref, *outs):
+    shards, rows, columns = down_ref.shape
+    down = down_ref[...].reshape(shards * rows, columns)
+    out_rows = out_ref[...].reshape(shards * out_ref.shape[1], columns)
+    heads = jnp.concatenate([a0[...], a1[...], a2[...], a3[...]], 0)
+    made = dot(hidden[...], down, ((1,), (0,))) + dot(heads, out_rows, ((1,), (0,)))
+    count = made.shape[0] // len(outs)
+    for i, out in enumerate(outs):
+        out[...] = made[i * count : (i + 1) * count].astype(out.dtype)
+
+
+def down_units(hidden, heads, side, weights, unit_rows, dtype):
+    rows, units = hidden.shape
+    shards, shard_rows, width = weights.shape
+    out_rows = shard_rows - 2 * unit_rows
+    count = rows // len(heads)
+    columns = 512
+    return pl.pallas_call(
+        down_kernel,
+        grid=(width // columns,),
+        in_specs=[pl.BlockSpec((rows, units), lambda i: (0, 0))]
+        + [pl.BlockSpec((count, HD), lambda i: (side, 0))] * len(heads)
+        + [
+            pl.BlockSpec((shards, unit_rows, columns), lambda i: (0, 1, i)),
+            pl.BlockSpec(
+                (shards, out_rows, columns), lambda i: (0, 2 * unit_rows // out_rows, i)
+            ),
+        ],
+        out_specs=[pl.BlockSpec((count, columns), lambda i: (0, i))] * len(heads),
+        out_shape=[jax.ShapeDtypeStruct((count, width), dtype)] * len(heads),
+        compiler_params=params(40),
+        cost_estimate=pl.CostEstimate(
+            flops=2 * rows * (units + HD) * width,
+            transcendentals=0,
+            bytes_accessed=2 * (units + HD) * width + 2 * rows * units + 4 * rows * width,
+        ),
+        name="down_units",
+    )(hidden, *heads, weights, weights)
+
+
+def head_owners(ny, nx, nz):
+    pairs = []
+    for y in range(ny):
+        for x in range(nx):
+            for z in range(nz):
+                for c in range(2):
+                    place = (x % 2) * 8 + z * 2 + c
+                    target = ((place // nx * nx + place % nx) * nz + y) * 2 + x // 2
+                    pairs.append((((y * nx + x) * nz + z) * 2 + c, target))
+    return pairs
+
+
+def after(value, *others):
+    return lax.optimization_barrier((value, *others))[0]
 
 
 def on_device(
@@ -324,15 +358,17 @@
     width = stream.shape[1]
     half = width // 2
     y, x, z, c = (lax.axis_index(name) for name in "yxzc")
-    ny, nz = lax.axis_size("y"), lax.axis_size("z")
-    request = y * lax.axis_size("x") + x
-
+    ny, nx, nz = (lax.axis_size(name) for name in "yxz")
+    request = y * nx + x
+    unit_rows = up_weight.shape[0]
+
+    head_rows = lax.ppermute(out_weight, ("y", "x", "z", "c"), head_owners(ny, nx, nz))
     weights = lax.all_gather(
-        jnp.concatenate([up_weight, down_weight, out_weight], 0), ("x", "z"), axis=0
+        jnp.concatenate([up_weight, down_weight, head_rows], 0), ("y", "x"), axis=0
     )
 
     def place_of(zq):
-        return jnp.stack([c, z, zq, request, y]).astype(jnp.int32)
+        return jnp.stack([c, z, zq, request]).astype(jnp.int32)
 
     place = place_of(z)
     own_query, new_out = pick_new(place, projections)
@@ -340,18 +376,15 @@
     query = jnp.concatenate([own_query, new_in[:, :half]], 0)
     queries = {k: lax.ppermute(query, "z", ring(k, nz)) for k in (2, 1, 3)}
     queries[0] = query
-    keys_in = swap_cores(pick_cache(place, key_cache))
-    values_in = swap_cores(pick_cache(place, value_cache))
-
-    normed = layer_norm(stream, norm_gain)
-    inputs = {k: lax.ppermute(normed, "y", ring(k, ny)) for k in (2, 1, 3)}
-    inputs[0] = normed
-    others = {k: swap_cores(inputs[k]) for k in (0, 1, 3, 2)}
-
-    partials = {}
+    place_cache = after(place, query)
+    keys_in = swap_cores(pick_cache(place_cache, key_cache))
+    values_in = swap_cores(pick_cache(place_cache, value_cache))
+
+    made, partials = keys_in, {}
+    normed = None
     for k in (0, 1, 3, 2):
         made = attend(
-            place_of((z - k + nz) % nz),
+            after(place_of((z - k + nz) % nz), made),
             cache_range,
             queries[k],
             key_cache,
@@ -362,32 +395,23 @@
             new_in,
         )
         partials[k] = made if k == 0 else lax.ppermute(made, "z", ring(-k, nz))
+        if k == 0:
+            normed = layer_norm(stream, after(norm_gain, made))
+    inputs = [normed] + [lax.ppermute(normed, "z", ring(k, nz)) for k in range(1, nz)]
+    own_in = jnp.concatenate(inputs, 0)
+    other_in = swap_cores(own_in)
     heads = merge(place, [partials[k] for k in range(nz)])
-    attention = {k: lax.ppermute(heads[k], "y", ring(k, ny)) for k in (2, 1, 3)}
-    attention[0] = heads[0]
-
-    shards = weights.shape[0]
-    out_shards = weights[:, -out_weight.shape[0] :, :]
-    mine = lax.dynamic_slice_in_dim(out_shards, c * (shards // 2), shards // 2, 0)
-    theirs = swap_cores(
-        lax.dynamic_slice_in_dim(out_shards, (1 - c) * (shards // 2), shards // 2, 0)
-    )
-    out_rows = jnp.where(
-        c == 0, jnp.stack([mine, theirs], 1), jnp.stack([theirs, mine], 1)
-    ).reshape(HD, width)
-
-    summed = None
-    returned = []
-    for k in (2, 1, 3, 0):
-        own, other = add_units(inputs[k], others[k], attention[k], weights, out_rows)
-        both = own + swap_cores(other).astype(F32)
-        if k == 0:
-            summed = both
-        else:
-            returned.append(lax.ppermute(both.astype(BF16), "y", ring(-k, ny)))
-    summed = summed + stream.astype(F32)
-    for part in returned:
-        summed = summed + part.astype(F32)
+    attention = [heads[0]] + [lax.ppermute(heads[k], "z", ring(k, nz)) for k in range(1, nz)]
+
+    weights = after(weights, heads, other_in)
+    own_hidden, other_hidden = hidden_units(own_in, other_in, weights, unit_rows)
+    given = down_units(other_hidden, attention, 1, weights, unit_rows, BF16)
+    taken = [swap_cores(part) for part in given]
+    kept = down_units(own_hidden, attention, 0, after(weights, *given), unit_rows, F32)
+    summed = stream.astype(F32) + kept[0] + taken[0].astype(F32)
+    for k in (2, 1, 3):
+        both = (kept[k] + taken[k].astype(F32)).astype(BF16)
+        summed = summed + lax.ppermute(both, "z", ring(-k, nz)).astype(F32)
     return summed.astype(BF16)
 
 

time: 230 us -> 220 us (0.957)
  Pallas kernels: 79.7 us -> 64.9 us
  starting transfers between devices: 26.3 us -> 34.4 us
  local copies, waits for them, and re-layouts: 15.9 us -> 10.6 us
  waiting for transfers between devices: 88.1 us -> 91 us
    all_gather x1, waiting for transfers between devices: 44.2 us -> 0.01 us  [on_device(): lax.all_gather(jnp.concatenate([up_weight, down_weight, head_rows], 0), (...]
    ppermute x9 -> x10, waiting for transfers between devices: 22.3 us -> 48.5 us  [the longest x3 23.2 us: on_device(): summed = summed + lax.ppermute(both, 'z', ring(-k, nz)).astype(F32)]
    ppermute x3, waiting for transfers between devices: 0.01 us -> 25.3 us  [on_device(): partials[k] = made if k == 0 else lax.ppermute(made, 'z', ring(-k, nz))]
    pallas_call x4 -> x3, Pallas kernels: 27.8 us -> 17.5 us  [the longest x2 10.1 us: down_units(): pl.pallas_call(down_kernel, grid=(width // columns,), in_specs=[pl.BlockS...]
    ppermute x9 -> x10, starting transfers between devices: 12.8 us -> 22.3 us  [the longest x3 10.9 us: on_device(): lax.ppermute(normed, 'z', ring(k, nz))]
    ppermute x3, waiting for transfers between devices: 17.5 us -> 10.8 us  [on_device(): queries = {k: lax.ppermute(query, 'z', ring(k, nz)) for k in (2, 1, 3)}]
    unnamed x35 -> x29, local copies, waits for them, and re-layouts: 13 us -> 9.86 us
    ppermute x3, starting transfers between devices: 1.69 us -> 4.19 us  [on_device(): partials[k] = made if k == 0 else lax.ppermute(made, 'z', ring(-k, nz))]
  transfers between devices with their start and end apart: 28 -> 25, of which waited for: 6 -> 12; matrix products, arithmetic and copies ran while one was open for 2% -> 1% of each run, Pallas kernels for 35% -> 28%
where the time goes in v2:
time: 220 us; the launch traced here: 218 us
  waiting for transfers between devices  91 us (41%)
  Pallas kernels  64.9 us (30%)
  starting transfers between devices  34.4 us (16%)
  between operations  13.7 us (6%)
  local copies, waits for them, and re-layouts  10.6 us (5%)
  other arithmetic  3.81 us (2%)
    pallas_call x4, Pallas kernels, attend(): pl.pallas_call(attend_kernel, grid_spec=pltpu.PrefetchScalarGridSpec(num_...  39.2 us
    ppermute x3, waiting for transfers between devices, on_device(): partials[k] = made if k == 0 else lax.ppermute(made, 'z', ring(-k, nz))  25.3 us
    ppermute x3, waiting for transfers between devices, on_device(): summed = summed + lax.ppermute(both, 'z', ring(-k, nz)).astype(F32)  23.2 us
    ppermute x3, waiting for transfers between devices, on_device(): lax.ppermute(normed, 'z', ring(k, nz))  21.6 us
    ppermute x3, starting transfers between devices, on_device(): lax.ppermute(normed, 'z', ring(k, nz))  10.9 us
    ppermute x3, waiting for transfers between devices, on_device(): queries = {k: lax.ppermute(query, 'z', ring(k, nz)) for k in (2, 1, 3)}  10.8 us
    pallas_call x2, Pallas kernels, down_units(): pl.pallas_call(down_kernel, grid=(width // columns,), in_specs=[pl.BlockS...  10.1 us
    unnamed x29, local copies, waits for them, and re-layouts  9.86 us
  transfers between devices with their start and end apart: 25, of which 12 were waited for; matrix products, arithmetic and copies ran while one was open for 1% of the time, Pallas kernels for 28%

profile of v2, /device:TPU:1, one launch (start us, length us, event | category | flops | bytes accessed | tf_op | source)
XLA Modules:
  0.0 218.5 jit_solution(4890735560463181671)
XLA Ops:
  6.5 4.6 %collective-permute-start.7 = (bf16[16,2048]{1,0:T(8,128)(2,1)}, bf16[16,2048]{1,0:T(8,128)(2,1)S(1)}, u32[]{:S(2)}, u32[]{:S(2)}) collective-permute-start(bf16[16,2048]{1,0:T(8,128)(2,1)} %param.15), channel_id=1, source_target_pairs={{0,0},{1,8},{2,16},{3,24},{4,32},{5,40},{6,48},{7,56},{8,64},{9,72... | collective-permute-start | bytes 196616 | tf_op jit(solution)/shard_map/ppermute | solution.py:365
  11.2 3.7 %collective-permute-done.7 = bf16[16,2048]{1,0:T(8,128)(2,1)S(1)} collective-permute-done((bf16[16,2048]{1,0:T(8,128)(2,1)}, bf16[16,2048]{1,0:T(8,128)(2,1)S(1)}, u32[]{:S(2)}, u32[]{:S(2)}) %collective-permute-start.7) | collective-permute-done | bytes 65568 | tf_op jit(solution)/shard_map/ppermute | solution.py:365
  14.9 1.9 pad_maximum_fusion.1
  17.0 0.7 pick_new.1
  17.8 2.3 %collective-permute-done.nk1.nv1 = bf16[128,3072]{1,0:T(8,128)(2,1)S(1)} collective-permute-done((bf16[128,3072]{1,0:T(8,128)(2,1)S(1)}, bf16[128,3072]{1,0:T(8,128)(2,1)S(1)}, u32[]{:S(2)}, u32[]{:S(2)}) %collective-permute-start) | collective-permute-done | bytes 786464 | tf_op jit(solution)/shard_map/ppermute | solution.py:25
  20.1 2.2 copy-done.2
  22.3 2.7 %pick_cache.2 = bf16[1024,1024]{1,0:T(8,128)(2,1)} custom-call(s32[4]{0:T(128)S(1)} %get-tuple-element.27.place_ref.place, bf16[1024,2048]{1,0:T(8,128)(2,1)S(1)} %copy-done.2), custom_call_target="tpu_custom_call" | custom-call | tf_op jit(solution)/shard_map/pick_cache/pallas_call | solution.py:74
  25.2 2.8 %pick_cache.3 = bf16[1024,1024]{1,0:T(8,128)(2,1)} custom-call(s32[4]{0:T(128)S(1)} %get-tuple-element.27.place_ref.place, bf16[1024,2048]{1,0:T(8,128)(2,1)S(1)} %copy-done.4), custom_call_target="tpu_custom_call" | custom-call | tf_op jit(solution)/shard_map/pick_cache/pallas_call | solution.py:74
  28.4 1.1 collective-permute-done.1.k1
  29.5 3.0 %collective-permute-done.2.v1 = bf16[1024,1024]{1,0:T(8,128)(2,1)} collective-permute-done((bf16[1024,1024]{1,0:T(8,128)(2,1)}, bf16[1024,1024]{1,0:T(8,128)(2,1)}, u32[]{:S(2)}, u32[]{:S(2)}) %collective-permute-start.2) | collective-permute-done | bytes 2097184 | tf_op jit(solution)/shard_map/ppermute | solution.py:25
  32.5 2.4 %copy-done.3 = bf16[1024,2048]{1,0:T(8,128)(2,1)S(1)} copy-done((bf16[1024,2048]{1,0:T(8,128)(2,1)S(1)}, bf16[1024,2048]{1,0:T(8,128)(2,1)}, u32[]{:S(2)}) %copy-start.3) | copy-done | bytes 4194328
  34.9 2.2 %copy-done.5 = bf16[1024,2048]{1,0:T(8,128)(2,1)S(1)} copy-done((bf16[1024,2048]{1,0:T(8,128)(2,1)S(1)}, bf16[1024,2048]{1,0:T(8,128)(2,1)}, u32[]{:S(2)}) %copy-start.5) | copy-done | bytes 4194328
  37.1 9.8 %attend.4.a = bf16[256,1152]{1,0:T(8,128)(2,1)S(1)} custom-call(s32[4]{0:T(128)S(1)} %get-tuple-element.28.place, s32[16,2]{1,0:T(8,128)S(1)} %copy.10.ranges, bf16[256,1024]{1,0:T(8,128)(2,1)S(1)} %pad_maximum_fusion.2.q_ref, bf16[1024,2048]{1,0:T(8,128)(2,1)S(1)} %copy-done.3, bf16[1024,1024]{1,0:T(8,128)(2,1)} %collective-permute-done.1.k1, ...), custom_call_target="tpu_custom_call" | custom-call | flops 2415919104 | bytes 10485760 | tf_op jit(solution)/shard_map/attend/pallas_call | solution.py:176
  47.4 3.3 %collective-permute-start.3 = (bf16[128,2048]{1,0:T(8,128)(2,1)S(1)}, bf16[128,2048]{1,0:T(8,128)(2,1)S(1)}, u32[]{:S(2)}, u32[]{:S(2)}) collective-permute-start(bf16[128,2048]{1,0:T(8,128)(2,1)S(1)} %layer_norm.1), channel_id=1, source_target_pairs={{0,2},{2,4},{4,6},{6,0},{1,3},{3,5},{5,7},{7,1},{8,10},{10,12},{12... | collective-permute-start | bytes 1572872 | tf_op jit(solution)/shard_map/ppermute | solution.py:400
  50.6 6.4 %collective-permute-start.4 = (bf16[128,2048]{1,0:T(8,128)(2,1)S(1)}, bf16[128,2048]{1,0:T(8,128)(2,1)S(1)}, u32[]{:S(2)}, u32[]{:S(2)}) collective-permute-start(bf16[128,2048]{1,0:T(8,128)(2,1)S(1)} %layer_norm.1), channel_id=1, source_target_pairs={{0,4},{2,6},{4,0},{6,2},{1,5},{3,7},{5,1},{7,3},{8,12},{10,14},{12... | collective-permute-start | bytes 1572872 | tf_op jit(solution)/shard_map/ppermute | solution.py:400
  57.0 1.3 collective-permute-start.5
  58.3 9.6 %collective-permute-done.3 = bf16[128,2048]{1,0:T(8,128)(2,1)S(1)} collective-permute-done((bf16[128,2048]{1,0:T(8,128)(2,1)S(1)}, bf16[128,2048]{1,0:T(8,128)(2,1)S(1)}, u32[]{:S(2)}, u32[]{:S(2)}) %collective-permute-start.3) | collective-permute-done | bytes 524320 | tf_op jit(solution)/shard_map/ppermute | solution.py:400
  67.9 12.0 %collective-permute-done.4 = bf16[128,2048]{1,0:T(8,128)(2,1)S(1)} collective-permute-done((bf16[128,2048]{1,0:T(8,128)(2,1)S(1)}, bf16[128,2048]{1,0:T(8,128)(2,1)S(1)}, u32[]{:S(2)}, u32[]{:S(2)}) %collective-permute-start.4) | collective-permute-done | bytes 524320 | tf_op jit(solution)/shard_map/ppermute | solution.py:400
  80.1 1.2 collective-permute-start.6
  81.3 1.0 collective-permute-start.8
  82.3 1.7 collective-permute-start.10
  84.0 1.3 collective-permute-start.11
  85.3 10.8 %collective-permute-done.8.q_ref = bf16[256,1024]{1,0:T(8,128)(2,1)S(1)} collective-permute-done((bf16[256,1024]{1,0:T(8,128)(2,1)S(1)}, bf16[256,1024]{1,0:T(8,128)(2,1)S(1)}, u32[]{:S(2)}, u32[]{:S(2)}) %collective-permute-start.8) | collective-permute-done | bytes 524320 | tf_op jit(solution)/shard_map/ppermute | solution.py:377
  96.1 9.8 %attend.5 = bf16[256,1152]{1,0:T(8,128)(2,1)S(1)} custom-call(s32[4]{0:T(128)S(1)} %get-tuple-element.30.place, s32[16,2]{1,0:T(8,128)S(1)} %copy.10.ranges, bf16[256,1024]{1,0:T(8,128)(2,1)S(1)} %collective-permute-done.8.q_ref, bf16[1024,2048]{1,0:T(8,128)(2,1)S(1)} %copy-done.3, bf16[1024,1024]{1,0:T(8,128)(2,1)} %collective-permute-done.1.k1, ...), custom_call_target="tpu_custom_call" | custom-call | flops 2415919104 | bytes 10485760 | tf_op jit(solution)/shard_map/attend/pallas_call | solution.py:176
  105.9 9.8 %attend.6 = bf16[256,1152]{1,0:T(8,128)(2,1)S(1)} custom-call(s32[4]{0:T(128)S(1)} %get-tuple-element.31.place, s32[16,2]{1,0:T(8,128)S(1)} %copy.10.ranges, bf16[256,1024]{1,0:T(8,128)(2,1)S(1)} %collective-permute-done.10.q_ref, bf16[1024,2048]{1,0:T(8,128)(2,1)S(1)} %copy-done.3, bf16[1024,1024]{1,0:T(8,128)(2,1)} %collective-permute-done.1.k1, ...), custom_call_target="tpu_custom_call" | custom-call | flops 2415919104 | bytes 10485760 | tf_op jit(solution)/shard_map/attend/pallas_call | solution.py:176
  115.8 9.8 %attend.7 = bf16[256,1152]{1,0:T(8,128)(2,1)S(1)} custom-call(s32[4]{0:T(128)S(1)} %get-tuple-element.32.place, s32[16,2]{1,0:T(8,128)S(1)} %copy.10.ranges, bf16[256,1024]{1,0:T(8,128)(2,1)S(1)} %collective-permute-done.11.q_ref, bf16[1024,2048]{1,0:T(8,128)(2,1)S(1)} %copy-done.3, bf16[1024,1024]{1,0:T(8,128)(2,1)} %collective-permute-done.1.k1, ...), custom_call_target="tpu_custom_call" | custom-call | flops 2415919104 | bytes 10485760 | tf_op jit(solution)/shard_map/attend/pallas_call | solution.py:176
  125.6 1.5 collective-permute-start.12
  127.1 2.7 %collective-permute-start.9 = (bf16[256,1152]{1,0:T(8,128)(2,1)S(1)}, bf16[256,1152]{1,0:T(8,128)(2,1)S(1)}, u32[]{:S(2)}, u32[]{:S(2)}) collective-permute-start(bf16[256,1152]{1,0:T(8,128)(2,1)S(1)} %attend.5), channel_id=1, source_target_pairs={{0,6},{2,0},{4,2},{6,4},{1,7},{3,1},{5,3},{7,5},{8,14},{10,8},{12,... | collective-permute-start | bytes 1769480 | tf_op jit(solution)/shard_map/ppermute | solution.py:397
  129.8 10.8 %collective-permute-done.12.c = bf16[256,1152]{1,0:T(8,128)(2,1)S(1)} collective-permute-done((bf16[256,1152]{1,0:T(8,128)(2,1)S(1)}, bf16[256,1152]{1,0:T(8,128)(2,1)S(1)}, u32[]{:S(2)}, u32[]{:S(2)}) %collective-permute-start.12) | collective-permute-done | bytes 589856 | tf_op jit(solution)/shard_map/ppermute | solution.py:397
  140.6 14.5 %collective-permute-done.13.d = bf16[256,1152]{1,0:T(8,128)(2,1)S(1)} collective-permute-done((bf16[256,1152]{1,0:T(8,128)(2,1)S(1)}, bf16[256,1152]{1,0:T(8,128)(2,1)S(1)}, u32[]{:S(2)}, u32[]{:S(2)}) %collective-permute-start.13) | collective-permute-done | bytes 589856 | tf_op jit(solution)/shard_map/ppermute | solution.py:397
  155.1 1.7 merge.1
  156.8 0.7 slice_bitcast_fusion
  157.5 1.7 collective-permute-start.15
  159.2 1.8 collective-permute-start.16
  161.0 1.4 copy-done.11
  162.4 1.6 copy-done.12
  164.0 7.4 %hidden_units.1 = (bf16[512,1024]{1,0:T(8,128)(2,1)S(1)}, bf16[512,1024]{1,0:T(8,128)(2,1)S(1)}) custom-call(bf16[512,2048]{1,0:T(8,128)(2,1)S(1)} %copy-done.7, bf16[512,2048]{1,0:T(8,128)(2,1)S(1)} %copy-done.12, bf16[16,144,2048]{2,1,0:T(8,128)(2,1)} %bitcast.17), custom_call_target="tpu_custom_call" | custom-call | flops 4294967296 | bytes 8388608 | tf_op jit(solution)/shard_map/hidden_units/pallas_call | solution.py:271
  171.4 4.7 %down_units.2 = (bf16[128,2048]{1,0:T(8,128)(2,1)S(1)}, bf16[128,2048]{1,0:T(8,128)(2,1)S(1)}, bf16[128,2048]{1,0:T(8,128)(2,1)S(1)}, bf16[128,2048]{1,0:T(8,128)(2,1)S(1)}) custom-call(bf16[512,1024]{1,0:T(8,128)(2,1)S(1)} %get-tuple-element.35.hidden, bf16[256,256]{1,0:T(8,128)(2,1)S(1)} %get-tuple-element.50.a0, ...), custom_call_target="tpu_custom_call" | custom-call | flops 2684354560 | bytes 10485760 | tf_op jit(solution)/shard_map/down_units/pallas_call | solution.py:308
  176.1 1.4 collective-permute-start.18
  177.6 0.4 collective-permute-start.22
  178.1 5.4 %down_units.3 = (f32[128,2048]{1,0:T(8,128)S(1)}, f32[128,2048]{1,0:T(8,128)S(1)}, f32[128,2048]{1,0:T(8,128)S(1)}, f32[128,2048]{1,0:T(8,128)S(1)}) custom-call(bf16[512,1024]{1,0:T(8,128)(2,1)S(1)} %get-tuple-element.34.hidden, bf16[256,256]{1,0:T(8,128)(2,1)S(1)} %get-tuple-element.50.a0, bf16[256,256]{1,0:T(8,128)(2,1)S(1)} %collective-permute-done.14.a1, ...), custom_call_target="tpu_custom_call" | custom-call | flops 2684354560 | bytes 10485760 | tf_op jit(solution)/shard_map/down_units/pallas_call | solution.py:308
  183.7 1.6 collective-permute-start.19
  185.4 0.6 collective-permute-start.21
  186.2 1.0 collective-permute-start.23
  187.1 11.3 %collective-permute-done.19 = bf16[128,2048]{1,0:T(8,128)(2,1)S(1)} collective-permute-done((bf16[128,2048]{1,0:T(8,128)(2,1)S(1)}, bf16[128,2048]{1,0:T(8,128)(2,1)S(1)}, u32[]{:S(2)}, u32[]{:S(2)}) %collective-permute-start.19) | collective-permute-done | bytes 524320 | tf_op jit(solution)/shard_map/ppermute | solution.py:414
  198.4 8.6 %collective-permute-done.21 = bf16[128,2048]{1,0:T(8,128)(2,1)S(1)} collective-permute-done((bf16[128,2048]{1,0:T(8,128)(2,1)S(1)}, bf16[128,2048]{1,0:T(8,128)(2,1)S(1)}, u32[]{:S(2)}, u32[]{:S(2)}) %collective-permute-start.21) | collective-permute-done | bytes 524320 | tf_op jit(solution)/shard_map/ppermute | solution.py:414
  207.0 3.4 %collective-permute-done.23 = bf16[128,2048]{1,0:T(8,128)(2,1)S(1)} collective-permute-done((bf16[128,2048]{1,0:T(8,128)(2,1)S(1)}, bf16[128,2048]{1,0:T(8,128)(2,1)S(1)}, u32[]{:S(2)}, u32[]{:S(2)}) %collective-permute-start.23) | collective-permute-done | bytes 524320 | tf_op jit(solution)/shard_map/ppermute | solution.py:414
  210.4 1.3 add_convert_fusion
  (55 shorter events, 2.0 us)
Async XLA Ops:
  6.5 10.5 %copy-start.1 = (bf16[128,6144]{1,0:T(8,128)(2,1)S(1)}, bf16[128,6144]{1,0:T(8,128)(2,1)}, u32[]{:S(2)}) copy-start(bf16[128,6144]{1,0:T(8,128)(2,1)} %nv0.7) | copy-start | bytes 4718596
  6.5 155.8 %all-gather.3.cloned.1.call-start = ((), (), s32[]{:S(2)}) async-start(), calls=%async_computation | async-start | bytes 10027008 | tf_op jit(solution)/shard_map/all_gather | solution.py:366
  6.5 8.3 %collective-permute-start.7 = (bf16[16,2048]{1,0:T(8,128)(2,1)}, bf16[16,2048]{1,0:T(8,128)(2,1)S(1)}, u32[]{:S(2)}, u32[]{:S(2)}) collective-permute-start(bf16[16,2048]{1,0:T(8,128)(2,1)} %param.15), channel_id=1, source_target_pairs={{0,0},{1,8},{2,16},{3,24},{4,32},{5,40},{6,48},{7,56},{8,64},{9,72... | collective-permute-start | bytes 196616 | tf_op jit(solution)/shard_map/ppermute | solution.py:365
  17.7 2.4 %collective-permute-start = (bf16[128,3072]{1,0:T(8,128)(2,1)S(1)}, bf16[128,3072]{1,0:T(8,128)(2,1)S(1)}, u32[]{:S(2)}, u32[]{:S(2)}) collective-permute-start(bf16[128,3072]{1,0:T(8,128)(2,1)S(1)} %get-tuple-element.26), channel_id=1, source_target_pairs={{0,1},{1,0},{2,3},{3,2},{4,5},{5,4},{6,7},{7,6},{8,9},{9,8},{10,11... | collective-permute-start | bytes 2359304 | tf_op jit(solution)/shard_map/ppermute | solution.py:25
  20.1 2.2 %copy-start.2 = (bf16[1024,2048]{1,0:T(8,128)(2,1)S(1)}, bf16[1024,2048]{1,0:T(8,128)(2,1)}, u32[]{:S(2)}) copy-start(bf16[1024,2048]{1,0:T(8,128)(2,1)} %k0.7) | copy-start | bytes 12582916
  22.3 2.8 %copy-start.4 = (bf16[1024,2048]{1,0:T(8,128)(2,1)S(1)}, bf16[1024,2048]{1,0:T(8,128)(2,1)}, u32[]{:S(2)}) copy-start(bf16[1024,2048]{1,0:T(8,128)(2,1)} %v0.7) | copy-start | bytes 12582916
  25.0 3.3 %copy-start.13 = (s32[16,2]{0,1:T(2,128)S(1)}, s32[16,2]{0,1:T(2,128)}, u32[]{:S(2)}) copy-start(s32[16,2]{0,1:T(2,128)} %param.13) | copy-start | bytes 388
  25.0 4.5 %collective-permute-start.1 = (bf16[1024,1024]{1,0:T(8,128)(2,1)}, bf16[1024,1024]{1,0:T(8,128)(2,1)}, u32[]{:S(2)}, u32[]{:S(2)}) collective-permute-start(bf16[1024,1024]{1,0:T(8,128)(2,1)} %pick_cache.2), channel_id=1, source_target_pairs={{0,1},{1,0},{2,3},{3,2},{4,5},{5,4},{6,7},{7,6},{8,9},{9,8},{10,11... | collective-permute-start | bytes 6291464 | tf_op jit(solution)/shard_map/ppermute | solution.py:25
  27.9 4.6 %collective-permute-start.2 = (bf16[1024,1024]{1,0:T(8,128)(2,1)}, bf16[1024,1024]{1,0:T(8,128)(2,1)}, u32[]{:S(2)}, u32[]{:S(2)}) collective-permute-start(bf16[1024,1024]{1,0:T(8,128)(2,1)} %pick_cache.3), channel_id=1, source_target_pairs={{0,1},{1,0},{2,3},{3,2},{4,5},{5,4},{6,7},{7,6},{8,9},{9,8},{10,11... | collective-permute-start | bytes 6291464 | tf_op jit(solution)/shard_map/ppermute | solution.py:25
  32.5 2.4 %copy-start.3 = (bf16[1024,2048]{1,0:T(8,128)(2,1)S(1)}, bf16[1024,2048]{1,0:T(8,128)(2,1)}, u32[]{:S(2)}) copy-start(bf16[1024,2048]{1,0:T(8,128)(2,1)} %k0.7) | copy-start | bytes 12582916
  34.9 2.2 %copy-start.5 = (bf16[1024,2048]{1,0:T(8,128)(2,1)S(1)}, bf16[1024,2048]{1,0:T(8,128)(2,1)}, u32[]{:S(2)}) copy-start(bf16[1024,2048]{1,0:T(8,128)(2,1)} %v0.7) | copy-start | bytes 12582916
  37.1 9.8 %copy-start.8 = (bf16[128,2048]{1,0:T(8,128)(2,1)S(1)}, bf16[128,2048]{1,0:T(8,128)(2,1)}, u32[]{:S(2)}) copy-start(bf16[128,2048]{1,0:T(8,128)(2,1)} %stream.1) | copy-start | bytes 1572868
  37.1 9.8 %copy-start.10 = (f32[2048]{0:T(1024)S(1)}, f32[2048]{0:T(1024)}, u32[]{:S(2)}) copy-start(f32[2048]{0:T(1024)} %param.14) | copy-start | bytes 24580
  47.4 20.6 %collective-permute-start.3 = (bf16[128,2048]{1,0:T(8,128)(2,1)S(1)}, bf16[128,2048]{1,0:T(8,128)(2,1)S(1)}, u32[]{:S(2)}, u32[]{:S(2)}) collective-permute-start(bf16[128,2048]{1,0:T(8,128)(2,1)S(1)} %layer_norm.1), channel_id=1, source_target_pairs={{0,2},{2,4},{4,6},{6,0},{1,3},{3,5},{5,7},{7,1},{8,10},{10,12},{12... | collective-permute-start | bytes 1572872 | tf_op jit(solution)/shard_map/ppermute | solution.py:400
  50.6 29.3 %collective-permute-start.4 = (bf16[128,2048]{1,0:T(8,128)(2,1)S(1)}, bf16[128,2048]{1,0:T(8,128)(2,1)S(1)}, u32[]{:S(2)}, u32[]{:S(2)}) collective-permute-start(bf16[128,2048]{1,0:T(8,128)(2,1)S(1)} %layer_norm.1), channel_id=1, source_target_pairs={{0,4},{2,6},{4,0},{6,2},{1,5},{3,7},{5,1},{7,3},{8,12},{10,14},{12... | collective-permute-start | bytes 1572872 | tf_op jit(solution)/shard_map/ppermute | solution.py:400
  57.0 23.0 %collective-permute-start.5 = (bf16[128,2048]{1,0:T(8,128)(2,1)S(1)}, bf16[128,2048]{1,0:T(8,128)(2,1)S(1)}, u32[]{:S(2)}, u32[]{:S(2)}) collective-permute-start(bf16[128,2048]{1,0:T(8,128)(2,1)S(1)} %layer_norm.1), channel_id=1, source_target_pairs={{0,6},{2,0},{4,2},{6,4},{1,7},{3,1},{5,3},{7,5},{8,14},{10,8},{12,... | collective-permute-start | bytes 1572872 | tf_op jit(solution)/shard_map/ppermute | solution.py:400
  80.1 25.9 %copy-start.6 = (bf16[512,2048]{1,0:T(8,128)(2,1)}, bf16[512,2048]{1,0:T(8,128)(2,1)S(1)}, u32[]{:S(2)}) copy-start(bf16[512,2048]{1,0:T(8,128)(2,1)S(1)} %pad_maximum_fusion.own_in) | copy-start | bytes 6291460
  80.1 80.9 %collective-permute-start.6 = (bf16[512,2048]{1,0:T(8,128)(2,1)S(1)}, bf16[512,2048]{1,0:T(8,128)(2,1)S(1)}, u32[]{:S(2)}, u32[]{:S(2)}) collective-permute-start(bf16[512,2048]{1,0:T(8,128)(2,1)S(1)} %pad_maximum_fusion.own_in), channel_id=1, source_target_pairs={{0,1},{1,0},{2,3},{3,2},{4,5},{5,4},{6,7},{7,6},{8,9},{9,8},{10,11... | collective-permute-start | bytes 6291464 | tf_op jit(solution)/shard_map/ppermute | solution.py:25
  81.3 14.8 %collective-permute-start.8 = (bf16[256,1024]{1,0:T(8,128)(2,1)S(1)}, bf16[256,1024]{1,0:T(8,128)(2,1)S(1)}, u32[]{:S(2)}, u32[]{:S(2)}) collective-permute-start(bf16[256,1024]{1,0:T(8,128)(2,1)S(1)} %pad_maximum_fusion.2.q_ref), channel_id=1, source_target_pairs={{0,2},{2,4},{4,6},{6,0},{1,3},{3,5},{5,7},{7,1},{8,10},{10,12},{12... | collective-permute-start | bytes 1572872 | tf_op jit(solution)/shard_map/ppermute | solution.py:377
  82.3 23.7 %collective-permute-start.10 = (bf16[256,1024]{1,0:T(8,128)(2,1)S(1)}, bf16[256,1024]{1,0:T(8,128)(2,1)S(1)}, u32[]{:S(2)}, u32[]{:S(2)}) collective-permute-start(bf16[256,1024]{1,0:T(8,128)(2,1)S(1)} %pad_maximum_fusion.2.q_ref), channel_id=1, source_target_pairs={{0,6},{2,0},{4,2},{6,4},{1,7},{3,1},{5,3},{7,5},{8,14},{10,8},{12,... | collective-permute-start | bytes 1572872 | tf_op jit(solution)/shard_map/ppermute | solution.py:377
  84.0 31.8 %collective-permute-start.11 = (bf16[256,1024]{1,0:T(8,128)(2,1)S(1)}, bf16[256,1024]{1,0:T(8,128)(2,1)S(1)}, u32[]{:S(2)}, u32[]{:S(2)}) collective-permute-start(bf16[256,1024]{1,0:T(8,128)(2,1)S(1)} %pad_maximum_fusion.2.q_ref), channel_id=1, source_target_pairs={{0,4},{2,6},{4,0},{6,2},{1,5},{3,7},{5,1},{7,3},{8,12},{10,14},{12... | collective-permute-start | bytes 1572872 | tf_op jit(solution)/shard_map/ppermute | solution.py:377
  125.6 36.8 %copy-start.7 = (bf16[512,2048]{1,0:T(8,128)(2,1)S(1)}, bf16[512,2048]{1,0:T(8,128)(2,1)}, u32[]{:S(2)}) copy-start(bf16[512,2048]{1,0:T(8,128)(2,1)} %copy-done.6) | copy-start | bytes 6291460
  125.6 15.0 %collective-permute-start.12 = (bf16[256,1152]{1,0:T(8,128)(2,1)S(1)}, bf16[256,1152]{1,0:T(8,128)(2,1)S(1)}, u32[]{:S(2)}, u32[]{:S(2)}) collective-permute-start(bf16[256,1152]{1,0:T(8,128)(2,1)S(1)} %attend.7), channel_id=1, source_target_pairs={{0,4},{2,6},{4,0},{6,2},{1,5},{3,7},{5,1},{7,3},{8,12},{10,14},{12... | collective-permute-start | bytes 1769480 | tf_op jit(solution)/shard_map/ppermute | solution.py:397
  127.1 28.0 %collective-permute-start.13 = (bf16[256,1152]{1,0:T(8,128)(2,1)S(1)}, bf16[256,1152]{1,0:T(8,128)(2,1)S(1)}, u32[]{:S(2)}, u32[]{:S(2)}) collective-permute-start(bf16[256,1152]{1,0:T(8,128)(2,1)S(1)} %attend.6), channel_id=1, source_target_pairs={{0,2},{2,4},{4,6},{6,0},{1,3},{3,5},{5,7},{7,1},{8,10},{10,12},{12... | collective-permute-start | bytes 1769480 | tf_op jit(solution)/shard_map/ppermute | solution.py:397
  127.1 28.0 %collective-permute-start.9 = (bf16[256,1152]{1,0:T(8,128)(2,1)S(1)}, bf16[256,1152]{1,0:T(8,128)(2,1)S(1)}, u32[]{:S(2)}, u32[]{:S(2)}) collective-permute-start(bf16[256,1152]{1,0:T(8,128)(2,1)S(1)} %attend.5), channel_id=1, source_target_pairs={{0,6},{2,0},{4,2},{6,4},{1,7},{3,1},{5,3},{7,5},{8,14},{10,8},{12,... | collective-permute-start | bytes 1769480 | tf_op jit(solution)/shard_map/ppermute | solution.py:397
  157.5 13.9 %collective-permute-start.14 = (bf16[256,256]{1,0:T(8,128)(2,1)}, bf16[256,256]{1,0:T(8,128)(2,1)S(1)}, u32[]{:S(2)}, u32[]{:S(2)}) collective-permute-start(bf16[256,256]{1,0:T(8,128)(2,1)} %get-tuple-element.49), channel_id=1, source_target_pairs={{0,2},{2,4},{4,6},{6,0},{1,3},{3,5},{5,7},{7,1},{8,10},{10,12},{12... | collective-permute-start | bytes 393224 | tf_op jit(solution)/shard_map/ppermute | solution.py:404
  157.5 13.9 %collective-permute-start.15 = (bf16[256,256]{1,0:T(8,128)(2,1)}, bf16[256,256]{1,0:T(8,128)(2,1)S(1)}, u32[]{:S(2)}, u32[]{:S(2)}) collective-permute-start(bf16[256,256]{1,0:T(8,128)(2,1)} %get-tuple-element.48), channel_id=1, source_target_pairs={{0,4},{2,6},{4,0},{6,2},{1,5},{3,7},{5,1},{7,3},{8,12},{10,14},{12... | collective-permute-start | bytes 393224 | tf_op jit(solution)/shard_map/ppermute | solution.py:404
  159.2 12.1 %collective-permute-start.16 = (bf16[256,256]{1,0:T(8,128)(2,1)}, bf16[256,256]{1,0:T(8,128)(2,1)}, u32[]{:S(2)}, u32[]{:S(2)}) collective-permute-start(bf16[256,256]{1,0:T(8,128)(2,1)} %get-tuple-element.47), channel_id=1, source_target_pairs={{0,6},{2,0},{4,2},{6,4},{1,7},{3,1},{5,3},{7,5},{8,14},{10,8},{12,... | collective-permute-start | bytes 393224 | tf_op jit(solution)/shard_map/ppermute | solution.py:404
  161.0 1.4 copy-start.11
  162.4 1.6 copy-start.12
  164.0 7.4 %copy-start = (bf16[2304,2048]{1,0:T(8,128)(2,1)S(1)}, bf16[2304,2048]{1,0:T(8,128)(2,1)}, u32[]{:S(2)}) copy-start(bf16[2304,2048]{1,0:T(8,128)(2,1)} %all-gather.3.cloned.1.call-done) | copy-start | bytes 28311556
  176.1 7.5 %collective-permute-start.18 = (bf16[128,2048]{1,0:T(8,128)(2,1)S(1)}, bf16[128,2048]{1,0:T(8,128)(2,1)S(1)}, u32[]{:S(2)}, u32[]{:S(2)}) collective-permute-start(bf16[128,2048]{1,0:T(8,128)(2,1)S(1)} %get-tuple-element.38), channel_id=1, source_target_pairs={{0,1},{1,0},{2,3},{3,2},{4,5},{5,4},{6,7},{7,6},{8,9},{9,8},{10,11... | collective-permute-start | bytes 1572872 | tf_op jit(solution)/shard_map/ppermute | solution.py:25
  177.5 7.8 %collective-permute-start.20 = (bf16[128,2048]{1,0:T(8,128)(2,1)S(1)}, bf16[128,2048]{1,0:T(8,128)(2,1)S(1)}, u32[]{:S(2)}, u32[]{:S(2)}) collective-permute-start(bf16[128,2048]{1,0:T(8,128)(2,1)S(1)} %get-tuple-element.37), channel_id=1, source_target_pairs={{0,1},{1,0},{2,3},{3,2},{4,5},{5,4},{6,7},{7,6},{8,9},{9,8},{10,11... | collective-permute-start | bytes 1572872 | tf_op jit(solution)/shard_map/ppermute | solution.py:25
  177.6 8.4 %collective-permute-start.22 = (bf16[128,2048]{1,0:T(8,128)(2,1)S(1)}, bf16[128,2048]{1,0:T(8,128)(2,1)S(1)}, u32[]{:S(2)}, u32[]{:S(2)}) collective-permute-start(bf16[128,2048]{1,0:T(8,128)(2,1)S(1)} %get-tuple-element.39), channel_id=1, source_target_pairs={{0,1},{1,0},{2,3},{3,2},{4,5},{5,4},{6,7},{7,6},{8,9},{9,8},{10,11... | collective-permute-start | bytes 1572872 | tf_op jit(solution)/shard_map/ppermute | solution.py:25
  178.0 9.1 %collective-permute-start.17 = (bf16[128,2048]{1,0:T(8,128)(2,1)S(1)}, bf16[128,2048]{1,0:T(8,128)(2,1)S(1)}, u32[]{:S(2)}, u32[]{:S(2)}) collective-permute-start(bf16[128,2048]{1,0:T(8,128)(2,1)S(1)} %get-tuple-element.36), channel_id=1, source_target_pairs={{0,1},{1,0},{2,3},{3,2},{4,5},{5,4},{6,7},{7,6},{8,9},{9,8},{10,11... | collective-permute-start | bytes 1572872 | tf_op jit(solution)/shard_map/ppermute | solution.py:25
  183.7 14.7 %collective-permute-start.19 = (bf16[128,2048]{1,0:T(8,128)(2,1)S(1)}, bf16[128,2048]{1,0:T(8,128)(2,1)S(1)}, u32[]{:S(2)}, u32[]{:S(2)}) collective-permute-start(bf16[128,2048]{1,0:T(8,128)(2,1)S(1)} %add_convert_fusion.3), channel_id=1, source_target_pairs={{0,4},{2,6},{4,0},{6,2},{1,5},{3,7},{5,1},{7,3},{8,12},{10,14},{12... | collective-permute-start | bytes 1572872 | tf_op jit(solution)/shard_map/ppermute | solution.py:414
  185.3 25.0 %copy-start.9 = (bf16[128,2048]{1,0:T(8,128)(2,1)S(1)}, bf16[128,2048]{1,0:T(8,128)(2,1)}, u32[]{:S(2)}) copy-start(bf16[128,2048]{1,0:T(8,128)(2,1)} %stream.1) | copy-start | bytes 1572868
  185.4 21.5 %collective-permute-start.21 = (bf16[128,2048]{1,0:T(8,128)(2,1)S(1)}, bf16[128,2048]{1,0:T(8,128)(2,1)S(1)}, u32[]{:S(2)}, u32[]{:S(2)}) collective-permute-start(bf16[128,2048]{1,0:T(8,128)(2,1)S(1)} %add_convert_fusion.2), channel_id=1, source_target_pairs={{0,6},{2,0},{4,2},{6,4},{1,7},{3,1},{5,3},{7,5},{8,14},{10,8},{12,... | collective-permute-start | bytes 1572872 | tf_op jit(solution)/shard_map/ppermute | solution.py:414
  186.2 24.2 %collective-permute-start.23 = (bf16[128,2048]{1,0:T(8,128)(2,1)S(1)}, bf16[128,2048]{1,0:T(8,128)(2,1)S(1)}, u32[]{:S(2)}, u32[]{:S(2)}) collective-permute-start(bf16[128,2048]{1,0:T(8,128)(2,1)S(1)} %add_convert_fusion.1), channel_id=1, source_target_pairs={{0,2},{2,4},{4,6},{6,0},{1,3},{3,5},{5,7},{7,1},{8,10},{10,12},{12... | collective-permute-start | bytes 1572872 | tf_op jit(solution)/shard_map/ppermute | solution.py:414
Sparse Core Ops, SparseCore 0:
  16.9 80.9 all-gather.2

commit v3 on v2

--- a/solution.py
+++ b/solution.py
@@ -1,3 +1,4 @@
+import functools
 import math
 
 import jax
@@ -64,25 +65,42 @@
     )(place, projections)
 
 
-def pick_cache(place, cache):
-    rows, width = cache.shape
+def pick_cache(place, keys, values):
+    rows, width = keys.shape
     heads = width // (2 * HD)
 
-    def body(place_ref, source, other):
-        other[...] = source[...]
-
+    def body(place_ref, key_ref, value_ref, other, arrived):
+        c = place_ref[0]
+        copies = []
+        for i, source in enumerate((key_ref, value_ref)):
+            for j in range(heads):
+                start = pl.multiple_of((2 * j + 1 - c) * HD, HD)
+                copies.append(
+                    pltpu.make_async_copy(
+                        source.at[:, pl.ds(start, HD)],
+                        other.at[i, :, pl.ds(j * HD, HD)],
+                        arrived.at[i * heads + j],
+                    )
+                )
+        for copy in copies:
+            copy.start()
+        for copy in copies:
+            copy.wait()
+
+    whole = pl.BlockSpec(memory_space=pl.ANY)
     return pl.pallas_call(
         body,
         grid_spec=pltpu.PrefetchScalarGridSpec(
             num_scalar_prefetch=1,
-            grid=(heads,),
-            in_specs=[pl.BlockSpec((rows, HD), lambda j, s: (0, 2 * j + 1 - s[0]))],
-            out_specs=pl.BlockSpec((rows, HD), lambda j, s: (0, j)),
-        ),
-        out_shape=jax.ShapeDtypeStruct((rows, width // 2), BF16),
+            grid=(1,),
+            in_specs=[whole, whole],
+            out_specs=whole,
+            scratch_shapes=[pltpu.SemaphoreType.DMA((2 * heads,))],
+        ),
+        out_shape=jax.ShapeDtypeStruct((2, rows, width // 2), BF16),
         compiler_params=params(16),
         name="pick_cache",
-    )(place, cache)
+    )(place, keys, values)
 
 
 def norm_kernel(stream, gain, out):
@@ -102,70 +120,74 @@
     )(stream, gain.reshape(1, -1))
 
 
-def attend_kernel(
-    place, ranges, q_ref, k0, k1, v0, v1, nk0, nk1, nv0, nv1, out, stats
-):
+def attend_kernel(steps, place, ranges, *refs):
+    blocks = len(steps)
+    queries, refs = refs[:blocks], refs[blocks:]
+    k0, k1, v0, v1, nk0, nk1, nv0, nv1 = refs[:8]
+    outs, stats = refs[8 : 8 + blocks], refs[8 + blocks]
     j = pl.program_id(0)
-    c, z, zq, request = place[0], place[1], place[2], place[3]
+    c, z, request = place[0], place[1], place[2]
     first, end = ranges[request, 0], ranges[request, 1]
-    rows = q_ref.shape[0]
+    rows = queries[0].shape[0]
     half = rows // 2
     cache_rows = k0.shape[0]
-    query = q_ref[...]
-
-    def cached(keys, member):
+    lane = lax.broadcasted_iota(jnp.int32, stats.shape[1:], 1)
+
+    def bias(member):
         position = member * cache_rows + lax.broadcasted_iota(jnp.int32, (1, cache_rows), 1)
-        bias = jnp.where((position >= first) & (position < end), 0.0, NEG).astype(F32)
-        return dot(query, keys[...], ((1,), (1,))) + bias
+        return jnp.where((position >= first) & (position < end), 0.0, NEG).astype(F32)
 
     def order(shape, axis):
         place_in = lax.broadcasted_iota(jnp.int32, shape, axis)
         return jnp.where(place_in < half, place_in + c * half, place_in - c * half)
 
-    score_own = cached(k0, 2 * z + c)
-    score_other = cached(k1, 2 * z + 1 - c)
+    bias_own, bias_other = bias(2 * z + c), bias(2 * z + 1 - c)
     new_keys = jnp.concatenate([nk0[...], nk1[...]], 0)
     new_values = jnp.concatenate([nv0[...], nv1[...]], 0)
-    visible = z * rows + order((1, rows), 1) <= zq * rows + order((rows, 1), 0)
-    score_new = jnp.where(visible, dot(query, new_keys, ((1,), (1,))), NEG)
-    top = jnp.maximum(
-        jnp.maximum(
-            jnp.max(score_own, axis=-1, keepdims=True),
-            jnp.max(score_other, axis=-1, keepdims=True),
-        ),
-        jnp.max(score_new, axis=-1, keepdims=True),
-    )
-    shift = top.astype(BF16).astype(F32)
-
-    def weigh(score, values):
-        weight = jnp.exp2((score - shift) * SCORE)
-        return (
-            jnp.sum(weight, axis=-1, keepdims=True),
-            dot(weight.astype(BF16), values, ((1,), (0,))),
+    for i, (step, out) in enumerate(zip(steps, outs)):
+        zq = lax.rem(z - step + 4, 4)
+        query = queries[i][...]
+        score_own = dot(query, k0[...], ((1,), (1,))) + bias_own
+        score_other = dot(query, k1[...], ((1,), (1,))) + bias_other
+        visible = z * rows + order((1, rows), 1) <= zq * rows + order((rows, 1), 0)
+        score_new = jnp.where(visible, dot(query, new_keys, ((1,), (1,))), NEG)
+        top = jnp.maximum(
+            jnp.maximum(
+                jnp.max(score_own, axis=-1, keepdims=True),
+                jnp.max(score_other, axis=-1, keepdims=True),
+            ),
+            jnp.max(score_new, axis=-1, keepdims=True),
         )
-
-    parts = [
-        weigh(score_own, v0[...]),
-        weigh(score_other, v1[...]),
-        weigh(score_new, new_values),
-    ]
-    total = parts[0][0] + parts[1][0] + parts[2][0]
-    out[:, pl.ds(pl.multiple_of(j * HD, HD), HD)] = (
-        parts[0][1] + parts[1][1] + parts[2][1]
-    ).astype(BF16)
-    high = total.astype(BF16).astype(F32)
-    lane = lax.broadcasted_iota(jnp.int32, stats.shape, 1)
-    kept = jnp.where(j == 0, 0.0, stats[...])
-    kept = jnp.where(lane == 3 * j, shift, kept)
-    kept = jnp.where(lane == 3 * j + 1, high, kept)
-    kept = jnp.where(lane == 3 * j + 2, total - high, kept)
-    stats[...] = kept
-    base = out.shape[1] - stats.shape[1]
-    out[:, base:] = kept.astype(BF16)
-
-
-def attend(place, ranges, query, keys, values, projections, keys_in, values_in, new_in):
-    rows, width = query.shape
+        shift = top.astype(BF16).astype(F32)
+
+        def weigh(score, values):
+            weight = jnp.exp2((score - shift) * SCORE)
+            return (
+                jnp.sum(weight, axis=-1, keepdims=True),
+                dot(weight.astype(BF16), values, ((1,), (0,))),
+            )
+
+        parts = [
+            weigh(score_own, v0[...]),
+            weigh(score_other, v1[...]),
+            weigh(score_new, new_values),
+        ]
+        total = parts[0][0] + parts[1][0] + parts[2][0]
+        out[:, pl.ds(pl.multiple_of(j * HD, HD), HD)] = (
+            parts[0][1] + parts[1][1] + parts[2][1]
+        ).astype(BF16)
+        high = total.astype(BF16).astype(F32)
+        kept = jnp.where(j == 0, 0.0, stats[i])
+        kept = jnp.where(lane == 3 * j, shift, kept)
+        kept = jnp.where(lane == 3 * j + 1, high, kept)
+        kept = jnp.where(lane == 3 * j + 2, total - high, kept)
+        stats[i] = kept
+        out[:, out.shape[1] - 128 :] = kept.astype(BF16)
+
+
+def attend(steps, place, ranges, queries, keys, values, projections, cache_in, new_in):
+    rows, width = queries[0].shape
+    blocks = len(steps)
     heads = width // HD
     cache_rows = keys.shape[0]
     new_rows = projections.shape[0]
@@ -173,41 +195,44 @@
     def columns(count, index):
         return pl.BlockSpec((count, HD), index)
 
-    return pl.pallas_call(
-        attend_kernel,
+    def received(i):
+        return pl.BlockSpec((None, cache_rows, HD), lambda j, s, r: (i, 0, j))
+
+    return pl.pallas_call(
+        functools.partial(attend_kernel, steps),
         grid_spec=pltpu.PrefetchScalarGridSpec(
             num_scalar_prefetch=2,
             grid=(heads,),
-            in_specs=[
-                columns(rows, lambda j, s, r: (0, j)),
+            in_specs=[columns(rows, lambda j, s, r: (0, j))] * blocks
+            + [
                 columns(cache_rows, lambda j, s, r: (0, 2 * j + s[0])),
-                columns(cache_rows, lambda j, s, r: (0, j)),
+                received(0),
                 columns(cache_rows, lambda j, s, r: (0, 2 * j + s[0])),
-                columns(cache_rows, lambda j, s, r: (0, j)),
+                received(1),
                 columns(new_rows, lambda j, s, r: (0, 2 * heads + 2 * j + s[0])),
                 columns(new_rows, lambda j, s, r: (0, heads + j)),
                 columns(new_rows, lambda j, s, r: (0, 4 * heads + 2 * j + s[0])),
                 columns(new_rows, lambda j, s, r: (0, 2 * heads + j)),
             ],
-            out_specs=pl.BlockSpec((rows, width + 128), lambda j, s, r: (0, 0)),
-            scratch_shapes=[pltpu.VMEM((rows, 128), F32)],
-        ),
-        out_shape=jax.ShapeDtypeStruct((rows, width + 128), BF16),
-        compiler_params=params(32),
+            out_specs=[pl.BlockSpec((rows, width + 128), lambda j, s, r: (0, 0))] * blocks,
+            scratch_shapes=[pltpu.VMEM((blocks, rows, 128), F32)],
+        ),
+        out_shape=[jax.ShapeDtypeStruct((rows, width + 128), BF16)] * blocks,
+        compiler_params=params(40),
         cost_estimate=pl.CostEstimate(
-            flops=4 * rows * (2 * cache_rows + rows) * width,
-            transcendentals=rows * (2 * cache_rows + rows) * heads,
-            bytes_accessed=8 * cache_rows * width + 8 * rows * width,
+            flops=4 * blocks * rows * (2 * cache_rows + rows) * width,
+            transcendentals=blocks * rows * (2 * cache_rows + rows) * heads,
+            bytes_accessed=8 * cache_rows * width + 8 * blocks * rows * width,
         ),
         name="attend",
     )(
         place,
         ranges,
-        query,
+        *queries,
         keys,
-        keys_in,
+        cache_in,
         values,
-        values_in,
+        cache_in,
         projections,
         new_in,
         projections,
@@ -367,40 +392,27 @@
         jnp.concatenate([up_weight, down_weight, head_rows], 0), ("y", "x"), axis=0
     )
 
-    def place_of(zq):
-        return jnp.stack([c, z, zq, request]).astype(jnp.int32)
-
-    place = place_of(z)
+    place = jnp.stack([c, z, request]).astype(jnp.int32)
     own_query, new_out = pick_new(place, projections)
     new_in = swap_cores(new_out)
     query = jnp.concatenate([own_query, new_in[:, :half]], 0)
-    queries = {k: lax.ppermute(query, "z", ring(k, nz)) for k in (2, 1, 3)}
-    queries[0] = query
-    place_cache = after(place, query)
-    keys_in = swap_cores(pick_cache(place_cache, key_cache))
-    values_in = swap_cores(pick_cache(place_cache, value_cache))
-
-    made, partials = keys_in, {}
-    normed = None
-    for k in (0, 1, 3, 2):
-        made = attend(
-            after(place_of((z - k + nz) % nz), made),
-            cache_range,
-            queries[k],
-            key_cache,
-            value_cache,
-            projections,
-            keys_in,
-            values_in,
-            new_in,
-        )
-        partials[k] = made if k == 0 else lax.ppermute(made, "z", ring(-k, nz))
-        if k == 0:
-            normed = layer_norm(stream, after(norm_gain, made))
+    queries = [lax.ppermute(query, "z", ring(k, nz)) for k in (2, 1, 3)]
+    cache_in = swap_cores(pick_cache(after(place, query), key_cache, value_cache))
+    context = (key_cache, value_cache, projections, cache_in, new_in)
+    (partial,) = attend((0,), place, cache_range, [query], *context)
+
+    norm_gain, place_late = after((norm_gain, place), partial, *queries)
+    normed = layer_norm(stream, norm_gain)
+    place_late = after(place_late, normed)
+    sent = attend((2, 1, 3), place_late, cache_range, queries, *context)
     inputs = [normed] + [lax.ppermute(normed, "z", ring(k, nz)) for k in range(1, nz)]
+    sent, inputs = lax.optimization_barrier((sent, inputs))
+    partials = [partial] + [
+        lax.ppermute(made, "z", ring(-k, nz)) for k, made in zip((2, 1, 3), sent)
+    ]
     own_in = jnp.concatenate(inputs, 0)
     other_in = swap_cores(own_in)
-    heads = merge(place, [partials[k] for k in range(nz)])
+    heads = merge(place, partials)
     attention = [heads[0]] + [lax.ppermute(heads[k], "z", ring(k, nz)) for k in range(1, nz)]
 
     weights = after(weights, heads, other_in)

time: 220 us -> 181 us (0.82)
  waiting for transfers between devices: 91 us -> 70.6 us
  Pallas kernels: 64.9 us -> 48 us
    ppermute x3, waiting for transfers between devices: 21.6 us -> 6.83 us  [on_device(): lax.ppermute(normed, 'z', ring(k, nz))]
    pallas_call x4 -> x2, Pallas kernels: 39.2 us -> 25.8 us  [attend(): pl.pallas_call(functools.partial(attend_kernel, steps), grid_spec=pltpu.P...]
    ppermute x3, starting transfers between devices: 10.9 us -> 3.76 us  [on_device(): lax.ppermute(normed, 'z', ring(k, nz))]
    ppermute x6, starting transfers between devices: 8.23 us -> 14.2 us  [the longest x3 11.6 us: on_device(): queries = [lax.ppermute(query, 'z', ring(k, nz)) for k in (2, 1, 3)]]
    ppermute x8 -> x7, waiting for transfers between devices: 6.42 us -> 2.29 us  [swap_cores(): return lax.ppermute(value, 'c', [(0, 1), (1, 0)])]
    pallas_call x2 -> x1, Pallas kernels: 5.47 us -> 2.67 us  [pick_cache(): pl.pallas_call(body, grid_spec=pltpu.PrefetchScalarGridSpec(num_scalar_pr...]
    unnamed x29 -> x28, local copies, waits for them, and re-layouts: 9.86 us -> 11.4 us
  transfers between devices with their start and end apart: 25 -> 24, of which waited for: 12 -> 10; matrix products, arithmetic and copies ran while one was open for 1% -> 0% of each run, Pallas kernels for 28% -> 24%
where the time goes in v3:
time: 181 us
  waiting for transfers between devices  70.6 us (39%)
  Pallas kernels  48 us (27%)
  starting transfers between devices  33.6 us (19%)
  between operations  13.7 us (8%)
  local copies, waits for them, and re-layouts  11.5 us (6%)
  other arithmetic  3.57 us (2%)
    ppermute x3, waiting for transfers between devices, on_device(): lax.ppermute(made, 'z', ring(-k, nz))  26.8 us
    pallas_call x2, Pallas kernels, attend(): pl.pallas_call(functools.partial(attend_kernel, steps), grid_spec=pltpu.P...  25.8 us
    ppermute x3, waiting for transfers between devices, on_device(): summed = summed + lax.ppermute(both, 'z', ring(-k, nz)).astype(F32)  22.1 us
    ppermute x3, starting transfers between devices, on_device(): queries = [lax.ppermute(query, 'z', ring(k, nz)) for k in (2, 1, 3)]  11.6 us
    unnamed x28, local copies, waits for them, and re-layouts  11.4 us
    pallas_call x2, Pallas kernels, down_units(): pl.pallas_call(down_kernel, grid=(width // columns,), in_specs=[pl.BlockS...  9.39 us
    ppermute x3, waiting for transfers between devices, on_device(): queries = [lax.ppermute(query, 'z', ring(k, nz)) for k in (2, 1, 3)]  8.8 us
    pallas_call x1, Pallas kernels, hidden_units(): pl.pallas_call(hidden_kernel, grid=(shards // chunk,), in_specs=[whole, w...  7.37 us
  transfers between devices with their start and end apart: 24, of which 10 were waited for; matrix products, arithmetic and copies ran while one was open for 0% of the time, Pallas kernels for 24%

profile of v3, /device:TPU:1, one launch (start us, length us, event | category | flops | bytes accessed | tf_op | source)
XLA Modules:
  0.0 180.8 jit_solution(9407628416472835869)
XLA Ops:
  6.5 4.6 %collective-permute-start.9 = (bf16[16,2048]{1,0:T(8,128)(2,1)}, bf16[16,2048]{1,0:T(8,128)(2,1)S(1)}, u32[]{:S(2)}, u32[]{:S(2)}) collective-permute-start(bf16[16,2048]{1,0:T(8,128)(2,1)} %param.15), channel_id=1, source_target_pairs={{0,0},{1,8},{2,16},{3,24},{4,32},{5,40},{6,48},{7,56},{8,64},{9,72... | collective-permute-start | bytes 196616 | tf_op jit(solution)/shard_map/ppermute | solution.py:390
  11.2 3.7 %collective-permute-done.9 = bf16[16,2048]{1,0:T(8,128)(2,1)S(1)} collective-permute-done((bf16[16,2048]{1,0:T(8,128)(2,1)}, bf16[16,2048]{1,0:T(8,128)(2,1)S(1)}, u32[]{:S(2)}, u32[]{:S(2)}) %collective-permute-start.9) | collective-permute-done | bytes 65568 | tf_op jit(solution)/shard_map/ppermute | solution.py:390
  14.9 1.9 %pad_maximum_fusion = bf16[144,2048]{1,0:T(8,128)(2,1)} fusion(bf16[16,2048]{1,0:T(8,128)(2,1)S(1)} %collective-permute-done.9, bf16[64,2048]{1,0:T(8,128)(2,1)} %param.17, bf16[64,2048]{1,0:T(8,128)(2,1)} %param.16), kind=kLoop, calls=%fused_computation.4 | loop fusion | flops 1769472 | bytes 1179648 | tf_op jit(solution)/shard_map/concatenate | solution.py:392
  16.9 0.7 pick_new.1
  17.7 2.3 %collective-permute-done.refs_6_.refs_8_.refs_10_ = bf16[128,3072]{1,0:T(8,128)(2,1)S(1)} collective-permute-done((bf16[128,3072]{1,0:T(8,128)(2,1)S(1)}, bf16[128,3072]{1,0:T(8,128)(2,1)S(1)}, u32[]{:S(2)}, u32[]{:S(2)}) %collective-permute-start) | collective-permute-done | bytes 786464 | tf_op jit(solution)/shard_map/ppermute | solution.py:26
  20.0 2.2 %copy-done.1 = bf16[1024,2048]{1,0:T(8,128)(2,1)S(1)} copy-done((bf16[1024,2048]{1,0:T(8,128)(2,1)S(1)}, bf16[1024,2048]{1,0:T(8,128)(2,1)}, u32[]{:S(2)}) %copy-start.1) | copy-done | bytes 4194328
  22.2 2.2 %copy-done.3 = bf16[1024,2048]{1,0:T(8,128)(2,1)S(1)} copy-done((bf16[1024,2048]{1,0:T(8,128)(2,1)S(1)}, bf16[1024,2048]{1,0:T(8,128)(2,1)}, u32[]{:S(2)}) %copy-start.3) | copy-done | bytes 4194328
  24.4 2.7 %pick_cache.1 = bf16[2,1024,1024]{2,1,0:T(8,128)(2,1)} custom-call(s32[3]{0:T(128)S(1)} %pad_add_fusion.place_ref.place, bf16[1024,2048]{1,0:T(8,128)(2,1)S(1)} %copy-done.1, bf16[1024,2048]{1,0:T(8,128)(2,1)S(1)} %copy-done.3), custom_call_target="tpu_custom_call" | custom-call | tf_op jit(solution)/shard_map/pick_cache/pallas_call | solution.py:91
  27.1 0.2 collective-permute-start.1
  27.3 8.9 %collective-permute-start.2 = (bf16[256,1024]{1,0:T(8,128)(2,1)S(1)}, bf16[256,1024]{1,0:T(8,128)(2,1)}, u32[]{:S(2)}, u32[]{:S(2)}) collective-permute-start(bf16[256,1024]{1,0:T(8,128)(2,1)S(1)} %pad_maximum_fusion.1.refs_0_), channel_id=1, source_target_pairs={{0,4},{2,6},{4,0},{6,2},{1,5},{3,7},{5,1},{7,3},{8,12},{10,14},{12... | collective-permute-start | bytes 1572872 | tf_op jit(solution)/shard_map/ppermute | solution.py:399
  36.2 0.1 collective-permute-start.3
  36.3 2.6 %collective-permute-start.4 = (bf16[256,1024]{1,0:T(8,128)(2,1)S(1)}, bf16[256,1024]{1,0:T(8,128)(2,1)}, u32[]{:S(2)}, u32[]{:S(2)}) collective-permute-start(bf16[256,1024]{1,0:T(8,128)(2,1)S(1)} %pad_maximum_fusion.1.refs_0_), channel_id=1, source_target_pairs={{0,6},{2,0},{4,2},{6,4},{1,7},{3,1},{5,3},{7,5},{8,14},{10,8},{12,... | collective-permute-start | bytes 1572872 | tf_op jit(solution)/shard_map/ppermute | solution.py:399
  38.9 2.3 %copy-done.2 = bf16[1024,2048]{1,0:T(8,128)(2,1)S(1)} copy-done((bf16[1024,2048]{1,0:T(8,128)(2,1)S(1)}, bf16[1024,2048]{1,0:T(8,128)(2,1)}, u32[]{:S(2)}) %copy-start.2) | copy-done | bytes 4194328
  41.2 9.9 %attend.2.a = bf16[256,1152]{1,0:T(8,128)(2,1)S(1)} custom-call(s32[3]{0:T(128)S(1)} %pad_add_fusion.place_ref.place, s32[16,2]{1,0:T(8,128)S(1)} %copy.10.ranges, bf16[256,1024]{1,0:T(8,128)(2,1)S(1)} %pad_maximum_fusion.1.refs_0_, bf16[1024,2048]{1,0:T(8,128)(2,1)S(1)} %copy-done.2, bf16[2,1024,1024]{2,1,0:T(8,128)(2,1)} %collective-permute-done.1.refs_2_.refs_4_.refs_6_, ...), custom_call_target="tpu_custom_call" | custom-call | flops 2415919104 | bytes 10485760 | tf_op jit(solution)/shard_map/attend/pallas_call | solution.py:201
  51.1 8.8 %collective-permute-done.3.refs_1_ = bf16[256,1024]{1,0:T(8,128)(2,1)} collective-permute-done((bf16[256,1024]{1,0:T(8,128)(2,1)S(1)}, bf16[256,1024]{1,0:T(8,128)(2,1)}, u32[]{:S(2)}, u32[]{:S(2)}) %collective-permute-start.3) | collective-permute-done | bytes 524320 | tf_op jit(solution)/shard_map/ppermute | solution.py:399
  59.9 0.4 layer_norm.1
  60.3 0.9 collective-permute-start.5
  61.2 2.9 %collective-permute-start.6 = (bf16[128,2048]{1,0:T(8,128)(2,1)S(1)}, bf16[128,2048]{1,0:T(8,128)(2,1)S(1)}, u32[]{:S(2)}, u32[]{:S(2)}) collective-permute-start(bf16[128,2048]{1,0:T(8,128)(2,1)S(1)} %layer_norm.1), channel_id=1, source_target_pairs={{0,4},{2,6},{4,0},{6,2},{1,5},{3,7},{5,1},{7,3},{8,12},{10,14},{12... | collective-permute-start | bytes 1572872 | tf_op jit(solution)/shard_map/ppermute | solution.py:408
  64.0 15.9 %attend.3 = (bf16[256,1152]{1,0:T(8,128)(2,1)S(1)}, bf16[256,1152]{1,0:T(8,128)(2,1)S(1)}, bf16[256,1152]{1,0:T(8,128)(2,1)S(1)}) custom-call(s32[3]{0:T(128)S(1)} %pad_add_fusion.place_ref.place, s32[16,2]{1,0:T(8,128)S(1)} %copy.10.ranges, bf16[256,1024]{1,0:T(8,128)(2,1)} %collective-permute-done.2.refs_0_, ...), custom_call_target="tpu_custom_call" | custom-call | flops 7247757312 | bytes 14680064 | tf_op jit(solution)/shard_map/attend/pallas_call | solution.py:201
  80.0 6.8 %collective-permute-done.6 = bf16[128,2048]{1,0:T(8,128)(2,1)S(1)} collective-permute-done((bf16[128,2048]{1,0:T(8,128)(2,1)S(1)}, bf16[128,2048]{1,0:T(8,128)(2,1)S(1)}, u32[]{:S(2)}, u32[]{:S(2)}) %collective-permute-start.6) | collective-permute-done | bytes 524320 | tf_op jit(solution)/shard_map/ppermute | solution.py:408
  87.0 1.4 collective-permute-start.8
  88.4 0.8 collective-permute-start.10
  89.3 1.7 collective-permute-start.11
  91.0 13.9 %collective-permute-done.10.b = bf16[256,1152]{1,0:T(8,128)(2,1)S(1)} collective-permute-done((bf16[256,1152]{1,0:T(8,128)(2,1)S(1)}, bf16[256,1152]{1,0:T(8,128)(2,1)S(1)}, u32[]{:S(2)}, u32[]{:S(2)}) %collective-permute-start.10) | collective-permute-done | bytes 589856 | tf_op jit(solution)/shard_map/ppermute | solution.py:411
  104.8 12.1 %collective-permute-done.11.c = bf16[256,1152]{1,0:T(8,128)(2,1)S(1)} collective-permute-done((bf16[256,1152]{1,0:T(8,128)(2,1)S(1)}, bf16[256,1152]{1,0:T(8,128)(2,1)S(1)}, u32[]{:S(2)}, u32[]{:S(2)}) %collective-permute-start.11) | collective-permute-done | bytes 589856 | tf_op jit(solution)/shard_map/ppermute | solution.py:411
  117.0 0.9 collective-permute-done.12.d
  117.8 1.7 merge.1
  119.6 0.2 collective-permute-start.13
  119.8 3.0 %collective-permute-start.14 = (bf16[256,256]{1,0:T(8,128)(2,1)S(1)}, bf16[256,256]{1,0:T(8,128)(2,1)S(1)}, u32[]{:S(2)}, u32[]{:S(2)}) collective-permute-start(bf16[256,256]{1,0:T(8,128)(2,1)S(1)} %get-tuple-element.62), channel_id=1, source_target_pairs={{0,4},{2,6},{4,0},{6,2},{1,5},{3,7},{5,1},{7,3},{8,12},{10,14},{12... | collective-permute-start | bytes 393224 | tf_op jit(solution)/shard_map/ppermute | solution.py:416
  122.8 1.3 copy-done.9
  124.1 1.6 copy-done.7
  125.7 1.6 copy-done.10
  127.3 7.4 %hidden_units.1 = (bf16[512,1024]{1,0:T(8,128)(2,1)S(1)}, bf16[512,1024]{1,0:T(8,128)(2,1)S(1)}) custom-call(bf16[512,2048]{1,0:T(8,128)(2,1)S(1)} %copy-done.7, bf16[512,2048]{1,0:T(8,128)(2,1)S(1)} %copy-done.10, bf16[16,144,2048]{2,1,0:T(8,128)(2,1)} %bitcast.13), custom_call_target="tpu_custom_call" | custom-call | flops 4294967296 | bytes 8388608 | tf_op jit(solution)/shard_map/hidden_units/pallas_call | solution.py:296
  134.7 4.0 %down_units.2 = (bf16[128,2048]{1,0:T(8,128)(2,1)S(1)}, bf16[128,2048]{1,0:T(8,128)(2,1)S(1)}, bf16[128,2048]{1,0:T(8,128)(2,1)S(1)}, bf16[128,2048]{1,0:T(8,128)(2,1)S(1)}) custom-call(bf16[512,1024]{1,0:T(8,128)(2,1)S(1)} %get-tuple-element.51.hidden, bf16[256,256]{1,0:T(8,128)(2,1)S(1)} %get-tuple-element.64.a0, ...), custom_call_target="tpu_custom_call" | custom-call | flops 2684354560 | bytes 10485760 | tf_op jit(solution)/shard_map/down_units/pallas_call | solution.py:333
  138.7 1.2 collective-permute-start.17
  139.9 0.1 collective-permute-start.19
  140.0 0.4 collective-permute-start.21
  140.4 0.1 collective-permute-start.16
  140.5 5.4 %down_units.3 = (f32[128,2048]{1,0:T(8,128)S(1)}, f32[128,2048]{1,0:T(8,128)S(1)}, f32[128,2048]{1,0:T(8,128)S(1)}, f32[128,2048]{1,0:T(8,128)S(1)}) custom-call(bf16[512,1024]{1,0:T(8,128)(2,1)S(1)} %get-tuple-element.50.hidden, bf16[256,256]{1,0:T(8,128)(2,1)S(1)} %get-tuple-element.64.a0, bf16[256,256]{1,0:T(8,128)(2,1)S(1)} %collective-permute-done.13.a1, ...), custom_call_target="tpu_custom_call" | custom-call | flops 2684354560 | bytes 10485760 | tf_op jit(solution)/shard_map/down_units/pallas_call | solution.py:333
  145.9 0.1 add_convert_fusion.3
  146.1 2.2 %collective-permute-start.18 = (bf16[128,2048]{1,0:T(8,128)(2,1)S(1)}, bf16[128,2048]{1,0:T(8,128)(2,1)S(1)}, u32[]{:S(2)}, u32[]{:S(2)}) collective-permute-start(bf16[128,2048]{1,0:T(8,128)(2,1)S(1)} %add_convert_fusion.3), channel_id=1, source_target_pairs={{0,4},{2,6},{4,0},{6,2},{1,5},{3,7},{5,1},{7,3},{8,12},{10,14},{12... | collective-permute-start | bytes 1572872 | tf_op jit(solution)/shard_map/ppermute | solution.py:426
  148.3 0.1 add_convert_fusion.2
  148.4 2.0 %collective-permute-start.20 = (bf16[128,2048]{1,0:T(8,128)(2,1)S(1)}, bf16[128,2048]{1,0:T(8,128)(2,1)S(1)}, u32[]{:S(2)}, u32[]{:S(2)}) collective-permute-start(bf16[128,2048]{1,0:T(8,128)(2,1)S(1)} %add_convert_fusion.2), channel_id=1, source_target_pairs={{0,6},{2,0},{4,2},{6,4},{1,7},{3,1},{5,3},{7,5},{8,14},{10,8},{12,... | collective-permute-start | bytes 1572872 | tf_op jit(solution)/shard_map/ppermute | solution.py:426
  150.4 0.1 add_convert_fusion.1
  150.6 10.2 %collective-permute-done.18 = bf16[128,2048]{1,0:T(8,128)(2,1)S(1)} collective-permute-done((bf16[128,2048]{1,0:T(8,128)(2,1)S(1)}, bf16[128,2048]{1,0:T(8,128)(2,1)S(1)}, u32[]{:S(2)}, u32[]{:S(2)}) %collective-permute-start.18) | collective-permute-done | bytes 524320 | tf_op jit(solution)/shard_map/ppermute | solution.py:426
  160.8 10.3 %collective-permute-done.20 = bf16[128,2048]{1,0:T(8,128)(2,1)S(1)} collective-permute-done((bf16[128,2048]{1,0:T(8,128)(2,1)S(1)}, bf16[128,2048]{1,0:T(8,128)(2,1)S(1)}, u32[]{:S(2)}, u32[]{:S(2)}) %collective-permute-start.20) | collective-permute-done | bytes 524320 | tf_op jit(solution)/shard_map/ppermute | solution.py:426
  171.0 1.7 collective-permute-done.22
  172.7 1.2 add_convert_fusion
  (48 shorter events, 0.7 us)
Async XLA Ops:
  6.5 10.3 %copy-start.4 = (bf16[128,6144]{1,0:T(8,128)(2,1)S(1)}, bf16[128,6144]{1,0:T(8,128)(2,1)}, u32[]{:S(2)}) copy-start(bf16[128,6144]{1,0:T(8,128)(2,1)} %refs_9_.1) | copy-start | bytes 4718596
  6.5 117.6 %all-gather.3.cloned.1.call-start = ((), (), s32[]{:S(2)}) async-start(), calls=%async_computation | async-start | bytes 10027008 | tf_op jit(solution)/shard_map/all_gather | solution.py:391
  6.5 8.3 %collective-permute-start.9 = (bf16[16,2048]{1,0:T(8,128)(2,1)}, bf16[16,2048]{1,0:T(8,128)(2,1)S(1)}, u32[]{:S(2)}, u32[]{:S(2)}) collective-permute-start(bf16[16,2048]{1,0:T(8,128)(2,1)} %param.15), channel_id=1, source_target_pairs={{0,0},{1,8},{2,16},{3,24},{4,32},{5,40},{6,48},{7,56},{8,64},{9,72... | collective-permute-start | bytes 196616 | tf_op jit(solution)/shard_map/ppermute | solution.py:390
  17.6 2.4 %collective-permute-start = (bf16[128,3072]{1,0:T(8,128)(2,1)S(1)}, bf16[128,3072]{1,0:T(8,128)(2,1)S(1)}, u32[]{:S(2)}, u32[]{:S(2)}) collective-permute-start(bf16[128,3072]{1,0:T(8,128)(2,1)S(1)} %get-tuple-element.34), channel_id=1, source_target_pairs={{0,1},{1,0},{2,3},{3,2},{4,5},{5,4},{6,7},{7,6},{8,9},{9,8},{10,11... | collective-permute-start | bytes 2359304 | tf_op jit(solution)/shard_map/ppermute | solution.py:26
  20.0 2.2 %copy-start.1 = (bf16[1024,2048]{1,0:T(8,128)(2,1)S(1)}, bf16[1024,2048]{1,0:T(8,128)(2,1)}, u32[]{:S(2)}) copy-start(bf16[1024,2048]{1,0:T(8,128)(2,1)} %refs_3_.3) | copy-start | bytes 12582916
  22.2 2.2 %copy-start.3 = (bf16[1024,2048]{1,0:T(8,128)(2,1)S(1)}, bf16[1024,2048]{1,0:T(8,128)(2,1)}, u32[]{:S(2)}) copy-start(bf16[1024,2048]{1,0:T(8,128)(2,1)} %refs_5_.3) | copy-start | bytes 12582916
  24.4 14.5 %copy-start.11 = (s32[16,2]{0,1:T(2,128)S(1)}, s32[16,2]{0,1:T(2,128)}, u32[]{:S(2)}) copy-start(s32[16,2]{0,1:T(2,128)} %param.13) | copy-start | bytes 388
  27.1 11.9 %collective-permute-start.1 = (bf16[2,1024,1024]{2,1,0:T(8,128)(2,1)}, bf16[2,1024,1024]{2,1,0:T(8,128)(2,1)}, u32[]{:S(2)}, u32[]{:S(2)}) collective-permute-start(bf16[2,1024,1024]{2,1,0:T(8,128)(2,1)} %pick_cache.1), channel_id=1, source_target_pairs={{0,1},{1,0},{2,3},{3,2},{4,5},{5,4},{6,7},{7,6},{8,9},{9,8},{10,11... | collective-permute-start | bytes 12582920 | tf_op jit(solution)/shard_map/ppermute | solution.py:26
  27.3 23.8 %collective-permute-start.2 = (bf16[256,1024]{1,0:T(8,128)(2,1)S(1)}, bf16[256,1024]{1,0:T(8,128)(2,1)}, u32[]{:S(2)}, u32[]{:S(2)}) collective-permute-start(bf16[256,1024]{1,0:T(8,128)(2,1)S(1)} %pad_maximum_fusion.1.refs_0_), channel_id=1, source_target_pairs={{0,4},{2,6},{4,0},{6,2},{1,5},{3,7},{5,1},{7,3},{8,12},{10,14},{12... | collective-permute-start | bytes 1572872 | tf_op jit(solution)/shard_map/ppermute | solution.py:399
  36.2 23.7 %collective-permute-start.3 = (bf16[256,1024]{1,0:T(8,128)(2,1)S(1)}, bf16[256,1024]{1,0:T(8,128)(2,1)}, u32[]{:S(2)}, u32[]{:S(2)}) collective-permute-start(bf16[256,1024]{1,0:T(8,128)(2,1)S(1)} %pad_maximum_fusion.1.refs_0_), channel_id=1, source_target_pairs={{0,2},{2,4},{4,6},{6,0},{1,3},{3,5},{5,7},{7,1},{8,10},{10,12},{12... | collective-permute-start | bytes 1572872 | tf_op jit(solution)/shard_map/ppermute | solution.py:399
  36.3 23.6 %collective-permute-start.4 = (bf16[256,1024]{1,0:T(8,128)(2,1)S(1)}, bf16[256,1024]{1,0:T(8,128)(2,1)}, u32[]{:S(2)}, u32[]{:S(2)}) collective-permute-start(bf16[256,1024]{1,0:T(8,128)(2,1)S(1)} %pad_maximum_fusion.1.refs_0_), channel_id=1, source_target_pairs={{0,6},{2,0},{4,2},{6,4},{1,7},{3,1},{5,3},{7,5},{8,14},{10,8},{12,... | collective-permute-start | bytes 1572872 | tf_op jit(solution)/shard_map/ppermute | solution.py:399
  38.9 2.3 %copy-start.2 = (bf16[1024,2048]{1,0:T(8,128)(2,1)S(1)}, bf16[1024,2048]{1,0:T(8,128)(2,1)}, u32[]{:S(2)}) copy-start(bf16[1024,2048]{1,0:T(8,128)(2,1)} %refs_3_.3) | copy-start | bytes 12582916
  41.2 18.7 %copy-start.5 = (bf16[128,2048]{1,0:T(8,128)(2,1)S(1)}, bf16[128,2048]{1,0:T(8,128)(2,1)}, u32[]{:S(2)}) copy-start(bf16[128,2048]{1,0:T(8,128)(2,1)} %stream.1) | copy-start | bytes 1572868
  41.2 18.7 %copy-start.8 = (f32[2048]{0:T(1024)S(1)}, f32[2048]{0:T(1024)}, u32[]{:S(2)}) copy-start(f32[2048]{0:T(1024)} %param.14) | copy-start | bytes 24580
  60.3 19.7 %collective-permute-start.5 = (bf16[128,2048]{1,0:T(8,128)(2,1)S(1)}, bf16[128,2048]{1,0:T(8,128)(2,1)S(1)}, u32[]{:S(2)}, u32[]{:S(2)}) collective-permute-start(bf16[128,2048]{1,0:T(8,128)(2,1)S(1)} %layer_norm.1), channel_id=1, source_target_pairs={{0,2},{2,4},{4,6},{6,0},{1,3},{3,5},{5,7},{7,1},{8,10},{10,12},{12... | collective-permute-start | bytes 1572872 | tf_op jit(solution)/shard_map/ppermute | solution.py:408
  61.2 25.7 %collective-permute-start.6 = (bf16[128,2048]{1,0:T(8,128)(2,1)S(1)}, bf16[128,2048]{1,0:T(8,128)(2,1)S(1)}, u32[]{:S(2)}, u32[]{:S(2)}) collective-permute-start(bf16[128,2048]{1,0:T(8,128)(2,1)S(1)} %layer_norm.1), channel_id=1, source_target_pairs={{0,4},{2,6},{4,0},{6,2},{1,5},{3,7},{5,1},{7,3},{8,12},{10,14},{12... | collective-permute-start | bytes 1572872 | tf_op jit(solution)/shard_map/ppermute | solution.py:408
  64.0 22.8 %collective-permute-start.7 = (bf16[128,2048]{1,0:T(8,128)(2,1)S(1)}, bf16[128,2048]{1,0:T(8,128)(2,1)S(1)}, u32[]{:S(2)}, u32[]{:S(2)}) collective-permute-start(bf16[128,2048]{1,0:T(8,128)(2,1)S(1)} %layer_norm.1), channel_id=1, source_target_pairs={{0,6},{2,0},{4,2},{6,4},{1,7},{3,1},{5,3},{7,5},{8,14},{10,8},{12,... | collective-permute-start | bytes 1572872 | tf_op jit(solution)/shard_map/ppermute | solution.py:408
  87.0 35.8 %copy-start.6 = (bf16[512,2048]{1,0:T(8,128)(2,1)}, bf16[512,2048]{1,0:T(8,128)(2,1)S(1)}, u32[]{:S(2)}) copy-start(bf16[512,2048]{1,0:T(8,128)(2,1)S(1)} %constant_dynamic-update-slice_fusion.own_in) | copy-start | bytes 6291460
  87.0 35.8 %collective-permute-start.8 = (bf16[512,2048]{1,0:T(8,128)(2,1)S(1)}, bf16[512,2048]{1,0:T(8,128)(2,1)S(1)}, u32[]{:S(2)}, u32[]{:S(2)}) collective-permute-start(bf16[512,2048]{1,0:T(8,128)(2,1)S(1)} %constant_dynamic-update-slice_fusion.own_in), channel_id=1, source_target_pairs={{0,1},{1,0},{2,3},{3,2},{4,5},{5,4},{6,7},{7,6},{8,9},{9,8},{10,11... | collective-permute-start | bytes 6291464 | tf_op jit(solution)/shard_map/ppermute | solution.py:26
  88.4 16.4 %collective-permute-start.10 = (bf16[256,1152]{1,0:T(8,128)(2,1)S(1)}, bf16[256,1152]{1,0:T(8,128)(2,1)S(1)}, u32[]{:S(2)}, u32[]{:S(2)}) collective-permute-start(bf16[256,1152]{1,0:T(8,128)(2,1)S(1)} %get-tuple-element.46), channel_id=1, source_target_pairs={{0,4},{2,6},{4,0},{6,2},{1,5},{3,7},{5,1},{7,3},{8,12},{10,14},{12... | collective-permute-start | bytes 1769480 | tf_op jit(solution)/shard_map/ppermute | solution.py:411
  89.3 27.7 %collective-permute-start.11 = (bf16[256,1152]{1,0:T(8,128)(2,1)S(1)}, bf16[256,1152]{1,0:T(8,128)(2,1)S(1)}, u32[]{:S(2)}, u32[]{:S(2)}) collective-permute-start(bf16[256,1152]{1,0:T(8,128)(2,1)S(1)} %get-tuple-element.47), channel_id=1, source_target_pairs={{0,6},{2,0},{4,2},{6,4},{1,7},{3,1},{5,3},{7,5},{8,14},{10,8},{12,... | collective-permute-start | bytes 1769480 | tf_op jit(solution)/shard_map/ppermute | solution.py:411
  91.0 26.8 %collective-permute-start.12 = (bf16[256,1152]{1,0:T(8,128)(2,1)S(1)}, bf16[256,1152]{1,0:T(8,128)(2,1)S(1)}, u32[]{:S(2)}, u32[]{:S(2)}) collective-permute-start(bf16[256,1152]{1,0:T(8,128)(2,1)S(1)} %get-tuple-element.48), channel_id=1, source_target_pairs={{0,2},{2,4},{4,6},{6,0},{1,3},{3,5},{5,7},{7,1},{8,10},{10,12},{12... | collective-permute-start | bytes 1769480 | tf_op jit(solution)/shard_map/ppermute | solution.py:411
  119.6 15.1 %collective-permute-start.13 = (bf16[256,256]{1,0:T(8,128)(2,1)S(1)}, bf16[256,256]{1,0:T(8,128)(2,1)S(1)}, u32[]{:S(2)}, u32[]{:S(2)}) collective-permute-start(bf16[256,256]{1,0:T(8,128)(2,1)S(1)} %get-tuple-element.63), channel_id=1, source_target_pairs={{0,2},{2,4},{4,6},{6,0},{1,3},{3,5},{5,7},{7,1},{8,10},{10,12},{12... | collective-permute-start | bytes 393224 | tf_op jit(solution)/shard_map/ppermute | solution.py:416
  119.8 14.9 %collective-permute-start.14 = (bf16[256,256]{1,0:T(8,128)(2,1)S(1)}, bf16[256,256]{1,0:T(8,128)(2,1)S(1)}, u32[]{:S(2)}, u32[]{:S(2)}) collective-permute-start(bf16[256,256]{1,0:T(8,128)(2,1)S(1)} %get-tuple-element.62), channel_id=1, source_target_pairs={{0,4},{2,6},{4,0},{6,2},{1,5},{3,7},{5,1},{7,3},{8,12},{10,14},{12... | collective-permute-start | bytes 393224 | tf_op jit(solution)/shard_map/ppermute | solution.py:416
  122.8 11.9 %collective-permute-start.15 = (bf16[256,256]{1,0:T(8,128)(2,1)S(1)}, bf16[256,256]{1,0:T(8,128)(2,1)S(1)}, u32[]{:S(2)}, u32[]{:S(2)}) collective-permute-start(bf16[256,256]{1,0:T(8,128)(2,1)S(1)} %get-tuple-element.61), channel_id=1, source_target_pairs={{0,6},{2,0},{4,2},{6,4},{1,7},{3,1},{5,3},{7,5},{8,14},{10,8},{12,... | collective-permute-start | bytes 393224 | tf_op jit(solution)/shard_map/ppermute | solution.py:416
  122.8 1.4 copy-start.9
  124.1 1.6 copy-start.7
  125.7 1.6 copy-start.10
  127.3 7.4 %copy-start = (bf16[2304,2048]{1,0:T(8,128)(2,1)S(1)}, bf16[2304,2048]{1,0:T(8,128)(2,1)}, u32[]{:S(2)}) copy-start(bf16[2304,2048]{1,0:T(8,128)(2,1)} %all-gather.3.cloned.1.call-done) | copy-start | bytes 28311556
  138.7 7.2 %collective-permute-start.17 = (bf16[128,2048]{1,0:T(8,128)(2,1)S(1)}, bf16[128,2048]{1,0:T(8,128)(2,1)S(1)}, u32[]{:S(2)}, u32[]{:S(2)}) collective-permute-start(bf16[128,2048]{1,0:T(8,128)(2,1)S(1)} %get-tuple-element.54), channel_id=1, source_target_pairs={{0,1},{1,0},{2,3},{3,2},{4,5},{5,4},{6,7},{7,6},{8,9},{9,8},{10,11... | collective-permute-start | bytes 1572872 | tf_op jit(solution)/shard_map/ppermute | solution.py:26
  139.9 8.4 %collective-permute-start.19 = (bf16[128,2048]{1,0:T(8,128)(2,1)S(1)}, bf16[128,2048]{1,0:T(8,128)(2,1)S(1)}, u32[]{:S(2)}, u32[]{:S(2)}) collective-permute-start(bf16[128,2048]{1,0:T(8,128)(2,1)S(1)} %get-tuple-element.53), channel_id=1, source_target_pairs={{0,1},{1,0},{2,3},{3,2},{4,5},{5,4},{6,7},{7,6},{8,9},{9,8},{10,11... | collective-permute-start | bytes 1572872 | tf_op jit(solution)/shard_map/ppermute | solution.py:26
  140.0 10.4 %collective-permute-start.21 = (bf16[128,2048]{1,0:T(8,128)(2,1)S(1)}, bf16[128,2048]{1,0:T(8,128)(2,1)S(1)}, u32[]{:S(2)}, u32[]{:S(2)}) collective-permute-start(bf16[128,2048]{1,0:T(8,128)(2,1)S(1)} %get-tuple-element.55), channel_id=1, source_target_pairs={{0,1},{1,0},{2,3},{3,2},{4,5},{5,4},{6,7},{7,6},{8,9},{9,8},{10,11... | collective-permute-start | bytes 1572872 | tf_op jit(solution)/shard_map/ppermute | solution.py:26
  140.4 10.2 %collective-permute-start.16 = (bf16[128,2048]{1,0:T(8,128)(2,1)S(1)}, bf16[128,2048]{1,0:T(8,128)(2,1)S(1)}, u32[]{:S(2)}, u32[]{:S(2)}) collective-permute-start(bf16[128,2048]{1,0:T(8,128)(2,1)S(1)} %get-tuple-element.52), channel_id=1, source_target_pairs={{0,1},{1,0},{2,3},{3,2},{4,5},{5,4},{6,7},{7,6},{8,9},{9,8},{10,11... | collective-permute-start | bytes 1572872 | tf_op jit(solution)/shard_map/ppermute | solution.py:26
  146.1 14.7 %collective-permute-start.18 = (bf16[128,2048]{1,0:T(8,128)(2,1)S(1)}, bf16[128,2048]{1,0:T(8,128)(2,1)S(1)}, u32[]{:S(2)}, u32[]{:S(2)}) collective-permute-start(bf16[128,2048]{1,0:T(8,128)(2,1)S(1)} %add_convert_fusion.3), channel_id=1, source_target_pairs={{0,4},{2,6},{4,0},{6,2},{1,5},{3,7},{5,1},{7,3},{8,12},{10,14},{12... | collective-permute-start | bytes 1572872 | tf_op jit(solution)/shard_map/ppermute | solution.py:426
  148.4 22.6 %collective-permute-start.20 = (bf16[128,2048]{1,0:T(8,128)(2,1)S(1)}, bf16[128,2048]{1,0:T(8,128)(2,1)S(1)}, u32[]{:S(2)}, u32[]{:S(2)}) collective-permute-start(bf16[128,2048]{1,0:T(8,128)(2,1)S(1)} %add_convert_fusion.2), channel_id=1, source_target_pairs={{0,6},{2,0},{4,2},{6,4},{1,7},{3,1},{5,3},{7,5},{8,14},{10,8},{12,... | collective-permute-start | bytes 1572872 | tf_op jit(solution)/shard_map/ppermute | solution.py:426
  150.5 22.2 %collective-permute-start.22 = (bf16[128,2048]{1,0:T(8,128)(2,1)S(1)}, bf16[128,2048]{1,0:T(8,128)(2,1)S(1)}, u32[]{:S(2)}, u32[]{:S(2)}) collective-permute-start(bf16[128,2048]{1,0:T(8,128)(2,1)S(1)} %add_convert_fusion.1), channel_id=1, source_target_pairs={{0,2},{2,4},{4,6},{6,0},{1,3},{3,5},{5,7},{7,1},{8,10},{10,12},{12... | collective-permute-start | bytes 1572872 | tf_op jit(solution)/shard_map/ppermute | solution.py:426
Sparse Core Ops, SparseCore 0:
  16.9 80.9 all-gather.2

commit v4 on v3

--- a/solution.py
+++ b/solution.py
@@ -69,23 +69,31 @@
     rows, width = keys.shape
     heads = width // (2 * HD)
 
-    def body(place_ref, key_ref, value_ref, other, arrived):
+    def body(place_ref, key_ref, value_ref, other, held, arrived, left):
         c = place_ref[0]
         copies = []
         for i, source in enumerate((key_ref, value_ref)):
             for j in range(heads):
                 start = pl.multiple_of((2 * j + 1 - c) * HD, HD)
+                columns = pl.ds(j * HD, HD)
+                slot = held.at[i, :, columns]
                 copies.append(
-                    pltpu.make_async_copy(
-                        source.at[:, pl.ds(start, HD)],
-                        other.at[i, :, pl.ds(j * HD, HD)],
-                        arrived.at[i * heads + j],
+                    (
+                        pltpu.make_async_copy(
+                            source.at[:, pl.ds(start, HD)], slot, arrived.at[i * heads + j]
+                        ),
+                        pltpu.make_async_copy(
+                            slot, other.at[i, :, columns], left.at[i * heads + j]
+                        ),
                     )
                 )
-        for copy in copies:
-            copy.start()
-        for copy in copies:
-            copy.wait()
+        for come, _ in copies:
+            come.start()
+        for come, leave in copies:
+            come.wait()
+            leave.start()
+        for _, leave in copies:
+            leave.wait()
 
     whole = pl.BlockSpec(memory_space=pl.ANY)
     return pl.pallas_call(
@@ -94,8 +102,12 @@
             num_scalar_prefetch=1,
             grid=(1,),
             in_specs=[whole, whole],
-            out_specs=whole,
-            scratch_shapes=[pltpu.SemaphoreType.DMA((2 * heads,))],
+            out_specs=pl.BlockSpec(memory_space=pltpu.HBM),
+            scratch_shapes=[
+                pltpu.VMEM((2, rows, width // 2), BF16),
+                pltpu.SemaphoreType.DMA((2 * heads,)),
+                pltpu.SemaphoreType.DMA((2 * heads,)),
+            ],
         ),
         out_shape=jax.ShapeDtypeStruct((2, rows, width // 2), BF16),
         compiler_params=params(16),
@@ -273,7 +285,7 @@
             out_specs=pl.BlockSpec((count, rows, HD), lambda i, s: (0, 0, 0)),
         ),
         out_shape=jax.ShapeDtypeStruct((count, rows, HD), BF16),
-        compiler_params=params(24),
+        compiler_params=params(12),
         name="merge",
     )(place, *parts)
 
@@ -303,7 +315,7 @@
         ],
         out_specs=[part, part],
         out_shape=[jax.ShapeDtypeStruct((rows, shards * unit_rows), BF16)] * 2,
-        compiler_params=params(40),
+        compiler_params=params(20),
         cost_estimate=pl.CostEstimate(
             flops=4 * rows * shards * unit_rows * width,
             transcendentals=0,
@@ -313,44 +325,75 @@
     )(own_in, other_in, weights)
 
 
-def down_kernel(hidden, a0, a1, a2, a3, down_ref, out_ref, *outs):
+def down_kernel(own_hidden, other_hidden, down_ref, own, other):
     shards, rows, columns = down_ref.shape
     down = down_ref[...].reshape(shards * rows, columns)
-    out_rows = out_ref[...].reshape(shards * out_ref.shape[1], columns)
+    other[...] = dot(other_hidden[...], down, ((1,), (0,)))
+    own[...] = dot(own_hidden[...], down, ((1,), (0,)))
+
+
+def down_units(own_hidden, other_hidden, weights, unit_rows):
+    rows, units = own_hidden.shape
+    shards, _, width = weights.shape
+    columns = 512
+    whole = pl.BlockSpec((rows, units), lambda i: (0, 0))
+    part = pl.BlockSpec((rows, columns), lambda i: (0, i))
+    return pl.pallas_call(
+        down_kernel,
+        grid=(width // columns,),
+        in_specs=[
+            whole,
+            whole,
+            pl.BlockSpec((shards, unit_rows, columns), lambda i: (0, 1, i)),
+        ],
+        out_specs=[part, part],
+        out_shape=[jax.ShapeDtypeStruct((rows, width), F32)] * 2,
+        compiler_params=params(20),
+        cost_estimate=pl.CostEstimate(
+            flops=4 * rows * units * width,
+            transcendentals=0,
+            bytes_accessed=2 * units * width + 4 * rows * units + 8 * rows * width,
+        ),
+        name="down_units",
+    )(own_hidden, other_hidden, weights)
+
+
+def finish_kernel(partial, a0, a1, a2, a3, out_ref, *outs):
+    shards, rows, columns = out_ref.shape
     heads = jnp.concatenate([a0[...], a1[...], a2[...], a3[...]], 0)
-    made = dot(hidden[...], down, ((1,), (0,))) + dot(heads, out_rows, ((1,), (0,)))
+    out_rows = out_ref[...].reshape(shards * rows, columns)
+    made = partial[...] + dot(heads, out_rows, ((1,), (0,)))
     count = made.shape[0] // len(outs)
     for i, out in enumerate(outs):
         out[...] = made[i * count : (i + 1) * count].astype(out.dtype)
 
 
-def down_units(hidden, heads, side, weights, unit_rows, dtype):
-    rows, units = hidden.shape
-    shards, shard_rows, width = weights.shape
+def finish(partial, heads, side, weights, unit_rows, dtype):
+    rows, width = partial.shape
+    shards, shard_rows, _ = weights.shape
     out_rows = shard_rows - 2 * unit_rows
     count = rows // len(heads)
     columns = 512
     return pl.pallas_call(
-        down_kernel,
+        finish_kernel,
         grid=(width // columns,),
-        in_specs=[pl.BlockSpec((rows, units), lambda i: (0, 0))]
+        in_specs=[pl.BlockSpec((rows, columns), lambda i: (0, i))]
         + [pl.BlockSpec((count, HD), lambda i: (side, 0))] * len(heads)
         + [
-            pl.BlockSpec((shards, unit_rows, columns), lambda i: (0, 1, i)),
             pl.BlockSpec(
                 (shards, out_rows, columns), lambda i: (0, 2 * unit_rows // out_rows, i)
             ),
         ],
         out_specs=[pl.BlockSpec((count, columns), lambda i: (0, i))] * len(heads),
         out_shape=[jax.ShapeDtypeStruct((count, width), dtype)] * len(heads),
-        compiler_params=params(40),
+        compiler_params=params(16),
         cost_estimate=pl.CostEstimate(
-            flops=2 * rows * (units + HD) * width,
+            flops=2 * rows * HD * width,
             transcendentals=0,
-            bytes_accessed=2 * (units + HD) * width + 2 * rows * units + 4 * rows * width,
-        ),
-        name="down_units",
-    )(hidden, *heads, weights, weights)
+            bytes_accessed=2 * HD * width + 8 * rows * width,
+        ),
+        name="finish",
+    )(partial, *heads, weights)
 
 
 def head_owners(ny, nx, nz):
@@ -363,6 +406,10 @@
                     target = ((place // nx * nx + place % nx) * nz + y) * 2 + x // 2
                     pairs.append((((y * nx + x) * nz + z) * 2 + c, target))
     return pairs
+
+
+def in_hbm(*arrays):
+    return tuple(pltpu.with_memory_space_constraint(array, pltpu.HBM) for array in arrays)
 
 
 def after(value, *others):
@@ -387,18 +434,20 @@
     request = y * nx + x
     unit_rows = up_weight.shape[0]
 
+    place = jnp.stack([c, z, request]).astype(jnp.int32)
     head_rows = lax.ppermute(out_weight, ("y", "x", "z", "c"), head_owners(ny, nx, nz))
+    cached = in_hbm(key_cache, value_cache)
+    own_query, new_out = pick_new(place, projections)
+    new_in = swap_cores(new_out)
+    (cache_out,) = in_hbm(pick_cache(after(place, new_out), *cached))
+    head_rows = after(head_rows, cache_out)
     weights = lax.all_gather(
         jnp.concatenate([up_weight, down_weight, head_rows], 0), ("y", "x"), axis=0
     )
-
-    place = jnp.stack([c, z, request]).astype(jnp.int32)
-    own_query, new_out = pick_new(place, projections)
-    new_in = swap_cores(new_out)
     query = jnp.concatenate([own_query, new_in[:, :half]], 0)
     queries = [lax.ppermute(query, "z", ring(k, nz)) for k in (2, 1, 3)]
-    cache_in = swap_cores(pick_cache(after(place, query), key_cache, value_cache))
-    context = (key_cache, value_cache, projections, cache_in, new_in)
+    cache_in = swap_cores(after(cache_out, query))
+    context = (*cached, *in_hbm(projections), cache_in, new_in)
     (partial,) = attend((0,), place, cache_range, [query], *context)
 
     norm_gain, place_late = after((norm_gain, place), partial, *queries)
@@ -410,16 +459,18 @@
     partials = [partial] + [
         lax.ppermute(made, "z", ring(-k, nz)) for k, made in zip((2, 1, 3), sent)
     ]
-    own_in = jnp.concatenate(inputs, 0)
-    other_in = swap_cores(own_in)
-    heads = merge(place, partials)
+    (own_in,) = in_hbm(jnp.concatenate(inputs, 0))
+    (other_in,) = in_hbm(swap_cores(own_in))
+    own_hidden, other_hidden = hidden_units(own_in, other_in, weights, unit_rows)
+    heads = merge(after(place, own_hidden), partials)
     attention = [heads[0]] + [lax.ppermute(heads[k], "z", ring(k, nz)) for k in range(1, nz)]
 
-    weights = after(weights, heads, other_in)
-    own_hidden, other_hidden = hidden_units(own_in, other_in, weights, unit_rows)
-    given = down_units(other_hidden, attention, 1, weights, unit_rows, BF16)
+    other_hidden, own_hidden = after((other_hidden, own_hidden), heads)
+    own_part, other_part = down_units(own_hidden, other_hidden, weights, unit_rows)
+    attention = after(tuple(attention), other_part, own_part)
+    given = finish(other_part, attention, 1, weights, unit_rows, BF16)
     taken = [swap_cores(part) for part in given]
-    kept = down_units(own_hidden, attention, 0, after(weights, *given), unit_rows, F32)
+    kept = finish(after(own_part, *given), attention, 0, weights, unit_rows, F32)
     summed = stream.astype(F32) + kept[0] + taken[0].astype(F32)
     for k in (2, 1, 3):
         both = (kept[k] + taken[k].astype(F32)).astype(BF16)

time: 181 us -> 164 us (0.906)
  waiting for transfers between devices: 70.6 us -> 56.4 us
  local copies, waits for them, and re-layouts: 11.5 us -> 7.38 us
  Pallas kernels: 48 us -> 51.4 us
    ppermute x3, waiting for transfers between devices: 26.8 us -> 0.77 us  [on_device(): lax.ppermute(made, 'z', ring(-k, nz))]
    all_gather x1, waiting for transfers between devices: 0.01 us -> 13.2 us  [on_device(): lax.all_gather(jnp.concatenate([up_weight, down_weight, head_rows], 0), (...]
    unnamed x28, local copies, waits for them, and re-layouts: 11.4 us -> 7.29 us
    ppermute x1, waiting for transfers between devices: 3.68 us -> 0.01 us  [on_device(): lax.ppermute(out_weight, ('y', 'x', 'z', 'c'), head_owners(ny, nx, nz))]
    ppermute x3, starting transfers between devices: 11.6 us -> 8.09 us  [on_device(): queries = [lax.ppermute(query, 'z', ring(k, nz)) for k in (2, 1, 3)]]
    ppermute x3, waiting for transfers between devices: 8.8 us -> 10.9 us  [on_device(): queries = [lax.ppermute(query, 'z', ring(k, nz)) for k in (2, 1, 3)]]
    pallas_call x2 -> x3, Pallas kernels: 9.39 us -> 9.46 us  [the longest x1 5.87 us: down_units(): pl.pallas_call(down_kernel, grid=(width // columns,), in_specs=[whole, wh...]
  transfers between devices with their start and end apart: 24 -> 24, of which waited for: 10 -> 10; matrix products, arithmetic and copies ran while one was open for 0% -> 0% of each run, Pallas kernels for 24% -> 29%
where the time goes in v4:
time: 164 us; the launch traced here: 163 us
  waiting for transfers between devices  56.4 us (34%)
  Pallas kernels  51.4 us (31%)
  starting transfers between devices  31.9 us (19%)
  between operations  13.7 us (8%)
  local copies, waits for them, and re-layouts  7.38 us (4%)
  other arithmetic  2.55 us (2%)
    pallas_call x2, Pallas kernels, attend(): pl.pallas_call(functools.partial(attend_kernel, steps), grid_spec=pltpu.P...  26.8 us
    ppermute x3, waiting for transfers between devices, on_device(): summed = summed + lax.ppermute(both, 'z', ring(-k, nz)).astype(F32)  22.9 us
    all_gather x1, waiting for transfers between devices, on_device(): lax.all_gather(jnp.concatenate([up_weight, down_weight, head_rows], 0), (...  13.2 us
    ppermute x3, waiting for transfers between devices, on_device(): queries = [lax.ppermute(query, 'z', ring(k, nz)) for k in (2, 1, 3)]  10.9 us
    pallas_call x1, Pallas kernels, hidden_units(): pl.pallas_call(hidden_kernel, grid=(shards // chunk,), in_specs=[whole, w...  8.12 us
    ppermute x3, starting transfers between devices, on_device(): queries = [lax.ppermute(query, 'z', ring(k, nz)) for k in (2, 1, 3)]  8.09 us
    unnamed x28, local copies, waits for them, and re-layouts  7.29 us
    ppermute x3, waiting for transfers between devices, on_device(): lax.ppermute(normed, 'z', ring(k, nz))  5.94 us
  transfers between devices with their start and end apart: 24, of which 10 were waited for; matrix products, arithmetic and copies ran while one was open for 0% of the time, Pallas kernels for 29%

profile of v4, /device:TPU:1, one launch (start us, length us, event | category | flops | bytes accessed | tf_op | source)
XLA Modules:
  0.0 163.3 jit_solution(17053856387394072272)
XLA Ops:
  6.5 4.5 %collective-permute-start.9 = (bf16[16,2048]{1,0:T(8,128)(2,1)}, bf16[16,2048]{1,0:T(8,128)(2,1)S(1)}, u32[]{:S(2)}, u32[]{:S(2)}) collective-permute-start(bf16[16,2048]{1,0:T(8,128)(2,1)} %param.15), channel_id=1, source_target_pairs={{0,0},{1,8},{2,16},{3,24},{4,32},{5,40},{6,48},{7,56},{8,64},{9,72... | collective-permute-start | bytes 196616 | tf_op jit(solution)/shard_map/ppermute | solution.py:438
  11.1 1.4 copy-done.1
  12.5 0.7 pick_new.1
  13.3 3.0 %pick_cache.1 = bf16[2,1024,1024]{2,1,0:T(8,128)(2,1)S(1)} custom-call(s32[3]{0:T(128)S(1)} %pad_add_fusion.place_ref.place, bf16[1024,2048]{1,0:T(8,128)(2,1)} %refs_3_.3, bf16[1024,2048]{1,0:T(8,128)(2,1)} %refs_5_.3), custom_call_target="tpu_custom_call" | custom-call | tf_op jit(solution)/shard_map/pick_cache/pallas_call | solution.py:99
  16.2 2.0 %copy-done.2 = bf16[2,1024,1024]{2,1,0:T(8,128)(2,1)} copy-done((bf16[2,1024,1024]{2,1,0:T(8,128)(2,1)}, bf16[2,1024,1024]{2,1,0:T(8,128)(2,1)S(1)}, u32[]{:S(2)}) %copy-start.2) | copy-done | bytes 4194328
  18.2 0.9 pad_maximum_fusion
  19.1 0.1 collective-permute-start
  19.2 2.3 %collective-permute-done.refs_6_.refs_8_.refs_10_ = bf16[128,3072]{1,0:T(8,128)(2,1)S(1)} collective-permute-done((bf16[128,3072]{1,0:T(8,128)(2,1)S(1)}, bf16[128,3072]{1,0:T(8,128)(2,1)S(1)}, u32[]{:S(2)}, u32[]{:S(2)}) %collective-permute-start) | collective-permute-done | bytes 786464 | tf_op jit(solution)/shard_map/ppermute | solution.py:26
  21.5 0.2 collective-permute-start.1
  21.8 5.4 %collective-permute-start.2 = (bf16[256,1024]{1,0:T(8,128)(2,1)S(1)}, bf16[256,1024]{1,0:T(8,128)(2,1)S(1)}, u32[]{:S(2)}, u32[]{:S(2)}) collective-permute-start(bf16[256,1024]{1,0:T(8,128)(2,1)S(1)} %pad_maximum_fusion.1.refs_0_), channel_id=1, source_target_pairs={{0,4},{2,6},{4,0},{6,2},{1,5},{3,7},{5,1},{7,3},{8,12},{10,14},{12... | collective-permute-start | bytes 1572872 | tf_op jit(solution)/shard_map/ppermute | solution.py:448
  27.2 0.4 collective-permute-start.3
  27.5 2.3 %collective-permute-start.4 = (bf16[256,1024]{1,0:T(8,128)(2,1)S(1)}, bf16[256,1024]{1,0:T(8,128)(2,1)}, u32[]{:S(2)}, u32[]{:S(2)}) collective-permute-start(bf16[256,1024]{1,0:T(8,128)(2,1)S(1)} %pad_maximum_fusion.1.refs_0_), channel_id=1, source_target_pairs={{0,6},{2,0},{4,2},{6,4},{1,7},{3,1},{5,3},{7,5},{8,14},{10,8},{12,... | collective-permute-start | bytes 1572872 | tf_op jit(solution)/shard_map/ppermute | solution.py:448
  30.0 10.0 %attend.2.a = bf16[256,1152]{1,0:T(8,128)(2,1)S(1)} custom-call(s32[3]{0:T(128)S(1)} %pad_add_fusion.place_ref.place, s32[16,2]{1,0:T(8,128)S(1)} %copy.10.ranges, bf16[256,1024]{1,0:T(8,128)(2,1)S(1)} %pad_maximum_fusion.1.refs_0_, bf16[1024,2048]{1,0:T(8,128)(2,1)} %refs_3_.3, bf16[2,1024,1024]{2,1,0:T(8,128)(2,1)} %collective-permute-done.1.refs_2_.refs_4_.refs_6_, ...), custom_call_target="tpu_custom_call" | custom-call | flops 2415919104 | bytes 10485760 | tf_op jit(solution)/shard_map/attend/pallas_call | solution.py:213
  40.0 10.8 %collective-permute-done.3.refs_1_ = bf16[256,1024]{1,0:T(8,128)(2,1)S(1)} collective-permute-done((bf16[256,1024]{1,0:T(8,128)(2,1)S(1)}, bf16[256,1024]{1,0:T(8,128)(2,1)S(1)}, u32[]{:S(2)}, u32[]{:S(2)}) %collective-permute-start.3) | collective-permute-done | bytes 524320 | tf_op jit(solution)/shard_map/ppermute | solution.py:448
  50.8 0.4 layer_norm.1
  51.2 0.8 collective-permute-start.5
  52.1 3.2 %collective-permute-start.6 = (bf16[128,2048]{1,0:T(8,128)(2,1)S(1)}, bf16[128,2048]{1,0:T(8,128)(2,1)S(1)}, u32[]{:S(2)}, u32[]{:S(2)}) collective-permute-start(bf16[128,2048]{1,0:T(8,128)(2,1)S(1)} %layer_norm.1), channel_id=1, source_target_pairs={{0,4},{2,6},{4,0},{6,2},{1,5},{3,7},{5,1},{7,3},{8,12},{10,14},{12... | collective-permute-start | bytes 1572872 | tf_op jit(solution)/shard_map/ppermute | solution.py:457
  55.3 16.8 %attend.3 = (bf16[256,1152]{1,0:T(8,128)(2,1)}, bf16[256,1152]{1,0:T(8,128)(2,1)}, bf16[256,1152]{1,0:T(8,128)(2,1)}) custom-call(s32[3]{0:T(128)S(1)} %pad_add_fusion.place_ref.place, s32[16,2]{1,0:T(8,128)S(1)} %copy.10.ranges, bf16[256,1024]{1,0:T(8,128)(2,1)S(1)} %collective-permute-done.2.refs_0_, bf16[256,1024]{1,0:T(8,128)(2,1)S(1)} %collective-permute-done.3.refs_1_, ...), custom_call_target="tpu_custom_call" | custom-call | flops 7247757312 | bytes 14680064 | tf_op jit(solution)/shard_map/attend/pallas_call | solution.py:213
  72.1 5.9 %collective-permute-done.6 = bf16[128,2048]{1,0:T(8,128)(2,1)S(1)} collective-permute-done((bf16[128,2048]{1,0:T(8,128)(2,1)S(1)}, bf16[128,2048]{1,0:T(8,128)(2,1)S(1)}, u32[]{:S(2)}, u32[]{:S(2)}) %collective-permute-start.6) | collective-permute-done | bytes 524320 | tf_op jit(solution)/shard_map/ppermute | solution.py:457
  78.3 1.4 collective-permute-start.8
  79.7 1.0 collective-permute-start.10
  80.6 2.6 %collective-permute-start.11 = (bf16[256,1152]{1,0:T(8,128)(2,1)}, bf16[256,1152]{1,0:T(8,128)(2,1)S(1)}, u32[]{:S(2)}, u32[]{:S(2)}) collective-permute-start(bf16[256,1152]{1,0:T(8,128)(2,1)} %get-tuple-element.62), channel_id=1, source_target_pairs={{0,6},{2,0},{4,2},{6,4},{1,7},{3,1},{5,3},{7,5},{8,14},{10,8},{12,... | collective-permute-start | bytes 1769480 | tf_op jit(solution)/shard_map/ppermute | solution.py:460
  83.2 0.4 collective-permute-done.8.other_in
  83.6 13.2 %all-gather.3.cloned.1.call-done = bf16[2304,2048]{1,0:T(8,128)(2,1)} async-done(((bf16[144,2048]{1,0:T(8,128)(2,1)}), bf16[2304,2048]{1,0:T(8,128)(2,1)}) %all-gather.3.cloned.1.call-update) | async-done | bytes 9437200 | tf_op jit(solution)/shard_map/all_gather | solution.py:444
  96.8 3.7 %copy-done = bf16[2304,2048]{1,0:T(8,128)(2,1)S(1)} copy-done((bf16[2304,2048]{1,0:T(8,128)(2,1)S(1)}, bf16[2304,2048]{1,0:T(8,128)(2,1)}, u32[]{:S(2)}) %copy-start) | copy-done | bytes 9437208
  100.5 8.1 %hidden_units.1 = (bf16[512,1024]{1,0:T(8,128)(2,1)S(1)}, bf16[512,1024]{1,0:T(8,128)(2,1)S(1)}) custom-call(bf16[512,2048]{1,0:T(8,128)(2,1)} %copy-done.7, bf16[512,2048]{1,0:T(8,128)(2,1)} %collective-permute-done.8.other_in, bf16[16,144,2048]{2,1,0:T(8,128)(2,1)S(1)} %bitcast.13), custom_call_target="tpu_custom_call" | custom-call | flops 4294967296 | bytes 8388608 | tf_op jit(solution)/shard_map/hidden_units/pallas_call | solution.py:308
  108.6 0.4 collective-permute-done.11.c
  109.0 0.4 collective-permute-done.12.d
  109.4 3.0 %merge.1 = bf16[4,256,256]{2,1,0:T(8,128)(2,1)S(1)} custom-call(s32[3]{0:T(128)S(1)} %pad_add_fusion.place_ref.place, bf16[256,1152]{1,0:T(8,128)(2,1)S(1)} %attend.2.a, bf16[256,1152]{1,0:T(8,128)(2,1)S(1)} %collective-permute-done.10.b, bf16[256,1152]{1,0:T(8,128)(2,1)S(1)} %collective-permute-done.11.c, bf16[256,1152]{1,0:T(8,128)(2,1)} %collective-permute-done.12.d), custom_call_target="tpu_custom_call" | custom-call | tf_op jit(solution)/shard_map/merge/pallas_call | solution.py:279
  112.4 1.1 collective-permute-start.13
  113.5 2.8 %collective-permute-start.14 = (bf16[256,256]{1,0:T(8,128)(2,1)S(1)}, bf16[256,256]{1,0:T(8,128)(2,1)S(1)}, u32[]{:S(2)}, u32[]{:S(2)}) collective-permute-start(bf16[256,256]{1,0:T(8,128)(2,1)S(1)} %get-tuple-element.82), channel_id=1, source_target_pairs={{0,4},{2,6},{4,0},{6,2},{1,5},{3,7},{5,1},{7,3},{8,12},{10,14},{12... | collective-permute-start | bytes 393224 | tf_op jit(solution)/shard_map/ppermute | solution.py:466
  116.3 0.4 collective-permute-start.15
  116.7 5.9 %down_units.1 = (f32[512,2048]{1,0:T(8,128)S(1)}, f32[512,2048]{1,0:T(8,128)S(1)}) custom-call(bf16[512,1024]{1,0:T(8,128)(2,1)S(1)} %get-tuple-element.64.own_hidden, bf16[512,1024]{1,0:T(8,128)(2,1)S(1)} %get-tuple-element.65.other_hidden, bf16[16,144,2048]{2,1,0:T(8,128)(2,1)S(1)} %bitcast.14), custom_call_target="tpu_custom_call" | custom-call | flops 4294967296 | bytes 14680064 | tf_op jit(solution)/shard_map/down_units/pallas_call | solution.py:341
  122.6 1.7 %finish.2 = (bf16[128,2048]{1,0:T(8,128)(2,1)S(1)}, bf16[128,2048]{1,0:T(8,128)(2,1)S(1)}, bf16[128,2048]{1,0:T(8,128)(2,1)S(1)}, bf16[128,2048]{1,0:T(8,128)(2,1)S(1)}) custom-call(f32[512,2048]{1,0:T(8,128)S(1)} %get-tuple-element.67.partial, bf16[256,256]{1,0:T(8,128)(2,1)S(1)} %get-tuple-element.68.a0, bf16[256,256]{1,0:T(8,128)(2,1)S(1)} %collective-permute-done.13.a1, ...), custom_call_target="tpu_custom_call" | custom-call | flops 536870912 | bytes 9437184 | tf_op jit(solution)/shard_map/finish/pallas_call | solution.py:377
  124.4 1.6 collective-permute-start.17
  126.0 0.1 collective-permute-start.19
  126.1 0.4 collective-permute-start.21
  126.5 0.1 collective-permute-start.16
  126.6 1.9 %finish.3 = (f32[128,2048]{1,0:T(8,128)S(1)}, f32[128,2048]{1,0:T(8,128)S(1)}, f32[128,2048]{1,0:T(8,128)S(1)}, f32[128,2048]{1,0:T(8,128)S(1)}) custom-call(f32[512,2048]{1,0:T(8,128)S(1)} %get-tuple-element.76.partial, bf16[256,256]{1,0:T(8,128)(2,1)S(1)} %get-tuple-element.68.a0, bf16[256,256]{1,0:T(8,128)(2,1)S(1)} %collective-permute-done.13.a1, ...), custom_call_target="tpu_custom_call" | custom-call | flops 536870912 | bytes 9437184 | tf_op jit(solution)/shard_map/finish/pallas_call | solution.py:377
  128.4 0.1 add_convert_fusion.3
  128.6 1.1 collective-permute-start.18
  129.7 0.1 add_convert_fusion.2
  129.8 2.3 %collective-permute-start.20 = (bf16[128,2048]{1,0:T(8,128)(2,1)S(1)}, bf16[128,2048]{1,0:T(8,128)(2,1)S(1)}, u32[]{:S(2)}, u32[]{:S(2)}) collective-permute-start(bf16[128,2048]{1,0:T(8,128)(2,1)S(1)} %add_convert_fusion.2), channel_id=1, source_target_pairs={{0,6},{2,0},{4,2},{6,4},{1,7},{3,1},{5,3},{7,5},{8,14},{10,8},{12,... | collective-permute-start | bytes 1572872 | tf_op jit(solution)/shard_map/ppermute | solution.py:477
  132.1 0.1 add_convert_fusion.1
  132.3 10.9 %collective-permute-done.18 = bf16[128,2048]{1,0:T(8,128)(2,1)S(1)} collective-permute-done((bf16[128,2048]{1,0:T(8,128)(2,1)S(1)}, bf16[128,2048]{1,0:T(8,128)(2,1)S(1)}, u32[]{:S(2)}, u32[]{:S(2)}) %collective-permute-start.18) | collective-permute-done | bytes 524320 | tf_op jit(solution)/shard_map/ppermute | solution.py:477
  143.2 10.1 %collective-permute-done.20 = bf16[128,2048]{1,0:T(8,128)(2,1)S(1)} collective-permute-done((bf16[128,2048]{1,0:T(8,128)(2,1)S(1)}, bf16[128,2048]{1,0:T(8,128)(2,1)S(1)}, u32[]{:S(2)}, u32[]{:S(2)}) %collective-permute-start.20) | collective-permute-done | bytes 524320 | tf_op jit(solution)/shard_map/ppermute | solution.py:477
  153.4 1.9 %collective-permute-done.22 = bf16[128,2048]{1,0:T(8,128)(2,1)S(1)} collective-permute-done((bf16[128,2048]{1,0:T(8,128)(2,1)S(1)}, bf16[128,2048]{1,0:T(8,128)(2,1)S(1)}, u32[]{:S(2)}, u32[]{:S(2)}) %collective-permute-start.22) | collective-permute-done | bytes 524320 | tf_op jit(solution)/shard_map/ppermute | solution.py:477
  155.2 1.2 add_convert_fusion
  (50 shorter events, 0.6 us)
Async XLA Ops:
  6.5 90.3 %all-gather.3.cloned.1.call-start = ((), (), s32[]{:S(2)}) async-start(), calls=%async_computation | async-start | bytes 10027008 | tf_op jit(solution)/shard_map/all_gather | solution.py:444
  6.5 11.7 %collective-permute-start.9 = (bf16[16,2048]{1,0:T(8,128)(2,1)}, bf16[16,2048]{1,0:T(8,128)(2,1)S(1)}, u32[]{:S(2)}, u32[]{:S(2)}) collective-permute-start(bf16[16,2048]{1,0:T(8,128)(2,1)} %param.15), channel_id=1, source_target_pairs={{0,0},{1,8},{2,16},{3,24},{4,32},{5,40},{6,48},{7,56},{8,64},{9,72... | collective-permute-start | bytes 196616 | tf_op jit(solution)/shard_map/ppermute | solution.py:438
  11.1 1.4 copy-start.1
  13.2 5.0 %copy-start.5 = (bf16[64,2048]{1,0:T(8,128)(2,1)S(1)}, bf16[64,2048]{1,0:T(8,128)(2,1)}, u32[]{:S(2)}) copy-start(bf16[64,2048]{1,0:T(8,128)(2,1)} %param.17) | copy-start | bytes 786436
  13.2 5.0 %copy-start.6 = (bf16[64,2048]{1,0:T(8,128)(2,1)S(1)}, bf16[64,2048]{1,0:T(8,128)(2,1)}, u32[]{:S(2)}) copy-start(bf16[64,2048]{1,0:T(8,128)(2,1)} %param.16) | copy-start | bytes 786436
  16.2 2.0 %copy-start.2 = (bf16[2,1024,1024]{2,1,0:T(8,128)(2,1)}, bf16[2,1024,1024]{2,1,0:T(8,128)(2,1)S(1)}, u32[]{:S(2)}) copy-start(bf16[2,1024,1024]{2,1,0:T(8,128)(2,1)S(1)} %pick_cache.1) | copy-start | bytes 12582916
  18.2 11.7 %copy-start.8 = (s32[16,2]{0,1:T(2,128)S(1)}, s32[16,2]{0,1:T(2,128)}, u32[]{:S(2)}) copy-start(s32[16,2]{0,1:T(2,128)} %param.13) | copy-start | bytes 388
  19.1 2.4 %collective-permute-start = (bf16[128,3072]{1,0:T(8,128)(2,1)S(1)}, bf16[128,3072]{1,0:T(8,128)(2,1)S(1)}, u32[]{:S(2)}, u32[]{:S(2)}) collective-permute-start(bf16[128,3072]{1,0:T(8,128)(2,1)S(1)} %get-tuple-element.44), channel_id=1, source_target_pairs={{0,1},{1,0},{2,3},{3,2},{4,5},{5,4},{6,7},{7,6},{8,9},{9,8},{10,11... | collective-permute-start | bytes 2359304 | tf_op jit(solution)/shard_map/ppermute | solution.py:26
  21.5 8.4 %collective-permute-start.1 = (bf16[2,1024,1024]{2,1,0:T(8,128)(2,1)}, bf16[2,1024,1024]{2,1,0:T(8,128)(2,1)}, u32[]{:S(2)}, u32[]{:S(2)}) collective-permute-start(bf16[2,1024,1024]{2,1,0:T(8,128)(2,1)} %copy-done.2), channel_id=1, source_target_pairs={{0,1},{1,0},{2,3},{3,2},{4,5},{5,4},{6,7},{7,6},{8,9},{9,8},{10,11... | collective-permute-start | bytes 12582920 | tf_op jit(solution)/shard_map/ppermute | solution.py:26
  21.8 18.2 %collective-permute-start.2 = (bf16[256,1024]{1,0:T(8,128)(2,1)S(1)}, bf16[256,1024]{1,0:T(8,128)(2,1)S(1)}, u32[]{:S(2)}, u32[]{:S(2)}) collective-permute-start(bf16[256,1024]{1,0:T(8,128)(2,1)S(1)} %pad_maximum_fusion.1.refs_0_), channel_id=1, source_target_pairs={{0,4},{2,6},{4,0},{6,2},{1,5},{3,7},{5,1},{7,3},{8,12},{10,14},{12... | collective-permute-start | bytes 1572872 | tf_op jit(solution)/shard_map/ppermute | solution.py:448
  27.2 23.6 %collective-permute-start.3 = (bf16[256,1024]{1,0:T(8,128)(2,1)S(1)}, bf16[256,1024]{1,0:T(8,128)(2,1)S(1)}, u32[]{:S(2)}, u32[]{:S(2)}) collective-permute-start(bf16[256,1024]{1,0:T(8,128)(2,1)S(1)} %pad_maximum_fusion.1.refs_0_), channel_id=1, source_target_pairs={{0,2},{2,4},{4,6},{6,0},{1,3},{3,5},{5,7},{7,1},{8,10},{10,12},{12... | collective-permute-start | bytes 1572872 | tf_op jit(solution)/shard_map/ppermute | solution.py:448
  27.5 23.3 %collective-permute-start.4 = (bf16[256,1024]{1,0:T(8,128)(2,1)S(1)}, bf16[256,1024]{1,0:T(8,128)(2,1)}, u32[]{:S(2)}, u32[]{:S(2)}) collective-permute-start(bf16[256,1024]{1,0:T(8,128)(2,1)S(1)} %pad_maximum_fusion.1.refs_0_), channel_id=1, source_target_pairs={{0,6},{2,0},{4,2},{6,4},{1,7},{3,1},{5,3},{7,5},{8,14},{10,8},{12,... | collective-permute-start | bytes 1572872 | tf_op jit(solution)/shard_map/ppermute | solution.py:448
  29.9 20.9 %copy-start.3 = (bf16[128,2048]{1,0:T(8,128)(2,1)S(1)}, bf16[128,2048]{1,0:T(8,128)(2,1)}, u32[]{:S(2)}) copy-start(bf16[128,2048]{1,0:T(8,128)(2,1)} %stream.1) | copy-start | bytes 1572868
  29.9 20.9 %copy-start.4 = (f32[2048]{0:T(1024)S(1)}, f32[2048]{0:T(1024)}, u32[]{:S(2)}) copy-start(f32[2048]{0:T(1024)} %param.14) | copy-start | bytes 24580
  51.2 20.9 %collective-permute-start.5 = (bf16[128,2048]{1,0:T(8,128)(2,1)S(1)}, bf16[128,2048]{1,0:T(8,128)(2,1)S(1)}, u32[]{:S(2)}, u32[]{:S(2)}) collective-permute-start(bf16[128,2048]{1,0:T(8,128)(2,1)S(1)} %layer_norm.1), channel_id=1, source_target_pairs={{0,2},{2,4},{4,6},{6,0},{1,3},{3,5},{5,7},{7,1},{8,10},{10,12},{12... | collective-permute-start | bytes 1572872 | tf_op jit(solution)/shard_map/ppermute | solution.py:457
  52.1 26.0 %collective-permute-start.6 = (bf16[128,2048]{1,0:T(8,128)(2,1)S(1)}, bf16[128,2048]{1,0:T(8,128)(2,1)S(1)}, u32[]{:S(2)}, u32[]{:S(2)}) collective-permute-start(bf16[128,2048]{1,0:T(8,128)(2,1)S(1)} %layer_norm.1), channel_id=1, source_target_pairs={{0,4},{2,6},{4,0},{6,2},{1,5},{3,7},{5,1},{7,3},{8,12},{10,14},{12... | collective-permute-start | bytes 1572872 | tf_op jit(solution)/shard_map/ppermute | solution.py:457
  55.3 22.8 %collective-permute-start.7 = (bf16[128,2048]{1,0:T(8,128)(2,1)S(1)}, bf16[128,2048]{1,0:T(8,128)(2,1)S(1)}, u32[]{:S(2)}, u32[]{:S(2)}) collective-permute-start(bf16[128,2048]{1,0:T(8,128)(2,1)S(1)} %layer_norm.1), channel_id=1, source_target_pairs={{0,6},{2,0},{4,2},{6,4},{1,7},{3,1},{5,3},{7,5},{8,14},{10,8},{12,... | collective-permute-start | bytes 1572872 | tf_op jit(solution)/shard_map/ppermute | solution.py:457
  78.2 1.4 copy-start.7
  78.3 5.3 %collective-permute-start.8 = (bf16[512,2048]{1,0:T(8,128)(2,1)S(1)}, bf16[512,2048]{1,0:T(8,128)(2,1)}, u32[]{:S(2)}, u32[]{:S(2)}) collective-permute-start(bf16[512,2048]{1,0:T(8,128)(2,1)S(1)} %constant_dynamic-update-slice_fusion.own_in), channel_id=1, source_target_pairs={{0,1},{1,0},{2,3},{3,2},{4,5},{5,4},{6,7},{7,6},{8,9},{9,8},{10,11... | collective-permute-start | bytes 6291464 | tf_op jit(solution)/shard_map/ppermute | solution.py:26
  79.7 28.9 %collective-permute-start.10 = (bf16[256,1152]{1,0:T(8,128)(2,1)}, bf16[256,1152]{1,0:T(8,128)(2,1)S(1)}, u32[]{:S(2)}, u32[]{:S(2)}) collective-permute-start(bf16[256,1152]{1,0:T(8,128)(2,1)} %get-tuple-element.61), channel_id=1, source_target_pairs={{0,4},{2,6},{4,0},{6,2},{1,5},{3,7},{5,1},{7,3},{8,12},{10,14},{12... | collective-permute-start | bytes 1769480 | tf_op jit(solution)/shard_map/ppermute | solution.py:460
  80.6 28.4 %collective-permute-start.11 = (bf16[256,1152]{1,0:T(8,128)(2,1)}, bf16[256,1152]{1,0:T(8,128)(2,1)S(1)}, u32[]{:S(2)}, u32[]{:S(2)}) collective-permute-start(bf16[256,1152]{1,0:T(8,128)(2,1)} %get-tuple-element.62), channel_id=1, source_target_pairs={{0,6},{2,0},{4,2},{6,4},{1,7},{3,1},{5,3},{7,5},{8,14},{10,8},{12,... | collective-permute-start | bytes 1769480 | tf_op jit(solution)/shard_map/ppermute | solution.py:460
  83.2 26.2 %collective-permute-start.12 = (bf16[256,1152]{1,0:T(8,128)(2,1)}, bf16[256,1152]{1,0:T(8,128)(2,1)}, u32[]{:S(2)}, u32[]{:S(2)}) collective-permute-start(bf16[256,1152]{1,0:T(8,128)(2,1)} %get-tuple-element.63), channel_id=1, source_target_pairs={{0,2},{2,4},{4,6},{6,0},{1,3},{3,5},{5,7},{7,1},{8,10},{10,12},{12... | collective-permute-start | bytes 1769480 | tf_op jit(solution)/shard_map/ppermute | solution.py:460
  96.8 3.7 %copy-start = (bf16[2304,2048]{1,0:T(8,128)(2,1)S(1)}, bf16[2304,2048]{1,0:T(8,128)(2,1)}, u32[]{:S(2)}) copy-start(bf16[2304,2048]{1,0:T(8,128)(2,1)} %all-gather.3.cloned.1.call-done) | copy-start | bytes 28311556
  109.4 13.2 %slice-start = ((s8[9437184]{0:T(1024)(128)(4,1)}), s8[4194304]{0:T(1024)(128)(4,1)S(1)}, s32[]{:S(2)}) async-start(s8[9437184]{0:T(1024)(128)(4,1)} %bitcast.15), calls=%async_computation.1 | async-start | bytes 8388608
  112.4 10.1 %collective-permute-start.13 = (bf16[256,256]{1,0:T(8,128)(2,1)S(1)}, bf16[256,256]{1,0:T(8,128)(2,1)S(1)}, u32[]{:S(2)}, u32[]{:S(2)}) collective-permute-start(bf16[256,256]{1,0:T(8,128)(2,1)S(1)} %get-tuple-element.83), channel_id=1, source_target_pairs={{0,2},{2,4},{4,6},{6,0},{1,3},{3,5},{5,7},{7,1},{8,10},{10,12},{12... | collective-permute-start | bytes 393224 | tf_op jit(solution)/shard_map/ppermute | solution.py:466
  113.5 9.1 %collective-permute-start.14 = (bf16[256,256]{1,0:T(8,128)(2,1)S(1)}, bf16[256,256]{1,0:T(8,128)(2,1)S(1)}, u32[]{:S(2)}, u32[]{:S(2)}) collective-permute-start(bf16[256,256]{1,0:T(8,128)(2,1)S(1)} %get-tuple-element.82), channel_id=1, source_target_pairs={{0,4},{2,6},{4,0},{6,2},{1,5},{3,7},{5,1},{7,3},{8,12},{10,14},{12... | collective-permute-start | bytes 393224 | tf_op jit(solution)/shard_map/ppermute | solution.py:466
  116.3 6.3 %slice-start.1 = ((s8[9437184]{0:T(1024)(128)(4,1)}), s8[4194304]{0:T(1024)(128)(4,1)S(1)}, s32[]{:S(2)}) async-start(s8[9437184]{0:T(1024)(128)(4,1)} %bitcast.15), calls=%async_computation.2 | async-start | bytes 8388608
  116.3 6.3 %slice-start.2 = ((s8[9437184]{0:T(1024)(128)(4,1)}), s8[1048576]{0:T(1024)(128)(4,1)S(1)}, s32[]{:S(2)}) async-start(s8[9437184]{0:T(1024)(128)(4,1)} %bitcast.15), calls=%async_computation.3 | async-start | bytes 2097152
  116.3 6.3 %collective-permute-start.15 = (bf16[256,256]{1,0:T(8,128)(2,1)S(1)}, bf16[256,256]{1,0:T(8,128)(2,1)S(1)}, u32[]{:S(2)}, u32[]{:S(2)}) collective-permute-start(bf16[256,256]{1,0:T(8,128)(2,1)S(1)} %get-tuple-element.81), channel_id=1, source_target_pairs={{0,6},{2,0},{4,2},{6,4},{1,7},{3,1},{5,3},{7,5},{8,14},{10,8},{12,... | collective-permute-start | bytes 393224 | tf_op jit(solution)/shard_map/ppermute | solution.py:466
  124.4 4.1 %collective-permute-start.17 = (bf16[128,2048]{1,0:T(8,128)(2,1)S(1)}, bf16[128,2048]{1,0:T(8,128)(2,1)S(1)}, u32[]{:S(2)}, u32[]{:S(2)}) collective-permute-start(bf16[128,2048]{1,0:T(8,128)(2,1)S(1)} %get-tuple-element.74), channel_id=1, source_target_pairs={{0,1},{1,0},{2,3},{3,2},{4,5},{5,4},{6,7},{7,6},{8,9},{9,8},{10,11... | collective-permute-start | bytes 1572872 | tf_op jit(solution)/shard_map/ppermute | solution.py:26
  126.0 3.7 %collective-permute-start.19 = (bf16[128,2048]{1,0:T(8,128)(2,1)S(1)}, bf16[128,2048]{1,0:T(8,128)(2,1)S(1)}, u32[]{:S(2)}, u32[]{:S(2)}) collective-permute-start(bf16[128,2048]{1,0:T(8,128)(2,1)S(1)} %get-tuple-element.73), channel_id=1, source_target_pairs={{0,1},{1,0},{2,3},{3,2},{4,5},{5,4},{6,7},{7,6},{8,9},{9,8},{10,11... | collective-permute-start | bytes 1572872 | tf_op jit(solution)/shard_map/ppermute | solution.py:26
  126.1 6.0 %collective-permute-start.21 = (bf16[128,2048]{1,0:T(8,128)(2,1)S(1)}, bf16[128,2048]{1,0:T(8,128)(2,1)S(1)}, u32[]{:S(2)}, u32[]{:S(2)}) collective-permute-start(bf16[128,2048]{1,0:T(8,128)(2,1)S(1)} %get-tuple-element.75), channel_id=1, source_target_pairs={{0,1},{1,0},{2,3},{3,2},{4,5},{5,4},{6,7},{7,6},{8,9},{9,8},{10,11... | collective-permute-start | bytes 1572872 | tf_op jit(solution)/shard_map/ppermute | solution.py:26
  126.5 5.8 %collective-permute-start.16 = (bf16[128,2048]{1,0:T(8,128)(2,1)S(1)}, bf16[128,2048]{1,0:T(8,128)(2,1)S(1)}, u32[]{:S(2)}, u32[]{:S(2)}) collective-permute-start(bf16[128,2048]{1,0:T(8,128)(2,1)S(1)} %get-tuple-element.72), channel_id=1, source_target_pairs={{0,1},{1,0},{2,3},{3,2},{4,5},{5,4},{6,7},{7,6},{8,9},{9,8},{10,11... | collective-permute-start | bytes 1572872 | tf_op jit(solution)/shard_map/ppermute | solution.py:26
  128.6 14.7 %collective-permute-start.18 = (bf16[128,2048]{1,0:T(8,128)(2,1)S(1)}, bf16[128,2048]{1,0:T(8,128)(2,1)S(1)}, u32[]{:S(2)}, u32[]{:S(2)}) collective-permute-start(bf16[128,2048]{1,0:T(8,128)(2,1)S(1)} %add_convert_fusion.3), channel_id=1, source_target_pairs={{0,4},{2,6},{4,0},{6,2},{1,5},{3,7},{5,1},{7,3},{8,12},{10,14},{12... | collective-permute-start | bytes 1572872 | tf_op jit(solution)/shard_map/ppermute | solution.py:477
  129.8 23.6 %collective-permute-start.20 = (bf16[128,2048]{1,0:T(8,128)(2,1)S(1)}, bf16[128,2048]{1,0:T(8,128)(2,1)S(1)}, u32[]{:S(2)}, u32[]{:S(2)}) collective-permute-start(bf16[128,2048]{1,0:T(8,128)(2,1)S(1)} %add_convert_fusion.2), channel_id=1, source_target_pairs={{0,6},{2,0},{4,2},{6,4},{1,7},{3,1},{5,3},{7,5},{8,14},{10,8},{12,... | collective-permute-start | bytes 1572872 | tf_op jit(solution)/shard_map/ppermute | solution.py:477
  132.2 23.0 %collective-permute-start.22 = (bf16[128,2048]{1,0:T(8,128)(2,1)S(1)}, bf16[128,2048]{1,0:T(8,128)(2,1)S(1)}, u32[]{:S(2)}, u32[]{:S(2)}) collective-permute-start(bf16[128,2048]{1,0:T(8,128)(2,1)S(1)} %add_convert_fusion.1), channel_id=1, source_target_pairs={{0,2},{2,4},{4,6},{6,0},{1,3},{3,5},{5,7},{7,1},{8,10},{10,12},{12... | collective-permute-start | bytes 1572872 | tf_op jit(solution)/shard_map/ppermute | solution.py:477
Sparse Core Ops, SparseCore 0:
  19.2 77.5 all-gather.2

commit v5 on v4

--- a/solution.py
+++ b/solution.py
@@ -439,8 +439,8 @@
     cached = in_hbm(key_cache, value_cache)
     own_query, new_out = pick_new(place, projections)
     new_in = swap_cores(new_out)
-    (cache_out,) = in_hbm(pick_cache(after(place, new_out), *cached))
-    head_rows = after(head_rows, cache_out)
+    cache_out = pick_cache(after(place, new_out), *cached)
+    head_rows = after(head_rows, cache_out, new_in)
     weights = lax.all_gather(
         jnp.concatenate([up_weight, down_weight, head_rows], 0), ("y", "x"), axis=0
     )
@@ -455,12 +455,13 @@
     place_late = after(place_late, normed)
     sent = attend((2, 1, 3), place_late, cache_range, queries, *context)
     inputs = [normed] + [lax.ppermute(normed, "z", ring(k, nz)) for k in range(1, nz)]
-    sent, inputs = lax.optimization_barrier((sent, inputs))
+    inputs = after(inputs, *sent)
     partials = [partial] + [
         lax.ppermute(made, "z", ring(-k, nz)) for k, made in zip((2, 1, 3), sent)
     ]
     (own_in,) = in_hbm(jnp.concatenate(inputs, 0))
     (other_in,) = in_hbm(swap_cores(own_in))
+    (weights,) = in_hbm(weights)
     own_hidden, other_hidden = hidden_units(own_in, other_in, weights, unit_rows)
     heads = merge(after(place, own_hidden), partials)
     attention = [heads[0]] + [lax.ppermute(heads[k], "z", ring(k, nz)) for k in range(1, nz)]

time: 164 us -> 167 us (1.018)
  local copies, waits for them, and re-layouts: 7.38 us -> 3.67 us
  Pallas kernels: 51.4 us -> 54.7 us
  starting transfers between devices: 31.9 us -> 34.3 us
    unnamed x28 -> x20, local copies, waits for them, and re-layouts: 7.29 us -> 3.58 us
    pallas_call x2, Pallas kernels: 3.58 us -> 6.47 us  [finish(): pl.pallas_call(finish_kernel, grid=(width // columns,), in_specs=[pl.Bloc...]
    ppermute x3, starting transfers between devices: 8.09 us -> 10.9 us  [on_device(): queries = [lax.ppermute(query, 'z', ring(k, nz)) for k in (2, 1, 3)]]
    all_gather x1, waiting for transfers between devices: 13.2 us -> 15.6 us  [on_device(): lax.all_gather(jnp.concatenate([up_weight, down_weight, head_rows], 0), (...]
    ppermute x7, waiting for transfers between devices: 2.68 us -> 0.58 us  [swap_cores(): return lax.ppermute(value, 'c', [(0, 1), (1, 0)])]
  transfers between devices with their start and end apart: 24 -> 24, of which waited for: 10 -> 9; matrix products, arithmetic and copies ran while one was open for 0% -> 0% of each run, Pallas kernels for 29% -> 29%
where the time goes in v5:
time: 167 us; the launch traced here: 166 us
  waiting for transfers between devices  57.4 us (34%)
  Pallas kernels  54.7 us (33%)
  starting transfers between devices  34.3 us (21%)
  between operations  13.7 us (8%)
  local copies, waits for them, and re-layouts  3.67 us (2%)
  other arithmetic  2.54 us (2%)
    pallas_call x2, Pallas kernels, attend(): pl.pallas_call(functools.partial(attend_kernel, steps), grid_spec=pltpu.P...  26.5 us
    ppermute x3, waiting for transfers between devices, on_device(): summed = summed + lax.ppermute(both, 'z', ring(-k, nz)).astype(F32)  22.1 us
    all_gather x1, waiting for transfers between devices, on_device(): lax.all_gather(jnp.concatenate([up_weight, down_weight, head_rows], 0), (...  15.6 us
    ppermute x3, waiting for transfers between devices, on_device(): queries = [lax.ppermute(query, 'z', ring(k, nz)) for k in (2, 1, 3)]  11 us
    ppermute x3, starting transfers between devices, on_device(): queries = [lax.ppermute(query, 'z', ring(k, nz)) for k in (2, 1, 3)]  10.9 us
    pallas_call x1, Pallas kernels, hidden_units(): pl.pallas_call(hidden_kernel, grid=(shards // chunk,), in_specs=[whole, w...  8.23 us
    pallas_call x1, Pallas kernels, down_units(): pl.pallas_call(down_kernel, grid=(width // columns,), in_specs=[whole, wh...  6.79 us
    pallas_call x2, Pallas kernels, finish(): pl.pallas_call(finish_kernel, grid=(width // columns,), in_specs=[pl.Bloc...  6.47 us
  transfers between devices with their start and end apart: 24, of which 9 were waited for; matrix products, arithmetic and copies ran while one was open for 0% of the time, Pallas kernels for 29%

profile of v5, /device:TPU:1, one launch (start us, length us, event | category | flops | bytes accessed | tf_op | source)
XLA Modules:
  0.0 166.3 jit_solution(5382898098744949218)
XLA Ops:
  6.5 0.1 pad_add_fusion.place_ref.place
  6.6 1.4 copy-done
  8.0 0.7 pick_new.1
  8.7 1.5 collective-permute-start
  10.2 3.2 %collective-permute-start.9 = (bf16[16,2048]{1,0:T(8,128)(2,1)}, bf16[16,2048]{1,0:T(8,128)(2,1)S(1)}, u32[]{:S(2)}, u32[]{:S(2)}) collective-permute-start(bf16[16,2048]{1,0:T(8,128)(2,1)} %param.15), channel_id=1, source_target_pairs={{0,0},{1,8},{2,16},{3,24},{4,32},{5,40},{6,48},{7,56},{8,64},{9,72... | collective-permute-start | bytes 196616 | tf_op jit(solution)/shard_map/ppermute | solution.py:438
  13.5 3.0 %pick_cache.1 = bf16[2,1024,1024]{2,1,0:T(8,128)(2,1)S(1)} custom-call(s32[3]{0:T(128)S(1)} %pad_add_fusion.place_ref.place, bf16[1024,2048]{1,0:T(8,128)(2,1)} %refs_3_.3, bf16[1024,2048]{1,0:T(8,128)(2,1)} %refs_5_.3), custom_call_target="tpu_custom_call" | custom-call | tf_op jit(solution)/shard_map/pick_cache/pallas_call | solution.py:99
  16.5 1.9 %copy-done.1 = bf16[2,1024,1024]{2,1,0:T(8,128)(2,1)} copy-done((bf16[2,1024,1024]{2,1,0:T(8,128)(2,1)}, bf16[2,1024,1024]{2,1,0:T(8,128)(2,1)S(1)}, u32[]{:S(2)}) %copy-start.1) | copy-done | bytes 4194328
  18.4 0.9 pad_maximum_fusion
  19.4 0.1 collective-permute-start.1
  19.5 8.2 %collective-permute-start.2 = (bf16[256,1024]{1,0:T(8,128)(2,1)S(1)}, bf16[256,1024]{1,0:T(8,128)(2,1)S(1)}, u32[]{:S(2)}, u32[]{:S(2)}) collective-permute-start(bf16[256,1024]{1,0:T(8,128)(2,1)S(1)} %pad_maximum_fusion.1.refs_0_), channel_id=1, source_target_pairs={{0,4},{2,6},{4,0},{6,2},{1,5},{3,7},{5,1},{7,3},{8,12},{10,14},{12... | collective-permute-start | bytes 1572872 | tf_op jit(solution)/shard_map/ppermute | solution.py:448
  27.7 0.1 collective-permute-start.3
  27.9 2.6 %collective-permute-start.4 = (bf16[256,1024]{1,0:T(8,128)(2,1)S(1)}, bf16[256,1024]{1,0:T(8,128)(2,1)}, u32[]{:S(2)}, u32[]{:S(2)}) collective-permute-start(bf16[256,1024]{1,0:T(8,128)(2,1)S(1)} %pad_maximum_fusion.1.refs_0_), channel_id=1, source_target_pairs={{0,6},{2,0},{4,2},{6,4},{1,7},{3,1},{5,3},{7,5},{8,14},{10,8},{12,... | collective-permute-start | bytes 1572872 | tf_op jit(solution)/shard_map/ppermute | solution.py:448
  30.4 0.1 copy.10.ranges
  30.5 9.8 %attend.2.a = bf16[256,1152]{1,0:T(8,128)(2,1)S(1)} custom-call(s32[3]{0:T(128)S(1)} %pad_add_fusion.place_ref.place, s32[16,2]{1,0:T(8,128)S(1)} %copy.10.ranges, bf16[256,1024]{1,0:T(8,128)(2,1)S(1)} %pad_maximum_fusion.1.refs_0_, bf16[1024,2048]{1,0:T(8,128)(2,1)} %refs_3_.3, bf16[2,1024,1024]{2,1,0:T(8,128)(2,1)} %collective-permute-done.1.refs_2_.refs_4_.refs_6_, ...), custom_call_target="tpu_custom_call" | custom-call | flops 2415919104 | bytes 10485760 | tf_op jit(solution)/shard_map/attend/pallas_call | solution.py:213
  40.3 11.0 %collective-permute-done.3.refs_1_ = bf16[256,1024]{1,0:T(8,128)(2,1)S(1)} collective-permute-done((bf16[256,1024]{1,0:T(8,128)(2,1)S(1)}, bf16[256,1024]{1,0:T(8,128)(2,1)S(1)}, u32[]{:S(2)}, u32[]{:S(2)}) %collective-permute-start.3) | collective-permute-done | bytes 524320 | tf_op jit(solution)/shard_map/ppermute | solution.py:448
  51.4 0.4 layer_norm.1
  51.7 0.8 collective-permute-start.5
  52.6 3.0 %collective-permute-start.6 = (bf16[128,2048]{1,0:T(8,128)(2,1)S(1)}, bf16[128,2048]{1,0:T(8,128)(2,1)S(1)}, u32[]{:S(2)}, u32[]{:S(2)}) collective-permute-start(bf16[128,2048]{1,0:T(8,128)(2,1)S(1)} %layer_norm.1), channel_id=1, source_target_pairs={{0,4},{2,6},{4,0},{6,2},{1,5},{3,7},{5,1},{7,3},{8,12},{10,14},{12... | collective-permute-start | bytes 1572872 | tf_op jit(solution)/shard_map/ppermute | solution.py:457
  55.6 16.7 %attend.3 = (bf16[256,1152]{1,0:T(8,128)(2,1)}, bf16[256,1152]{1,0:T(8,128)(2,1)}, bf16[256,1152]{1,0:T(8,128)(2,1)}) custom-call(s32[3]{0:T(128)S(1)} %pad_add_fusion.place_ref.place, s32[16,2]{1,0:T(8,128)S(1)} %copy.10.ranges, bf16[256,1024]{1,0:T(8,128)(2,1)S(1)} %collective-permute-done.2.refs_0_, bf16[256,1024]{1,0:T(8,128)(2,1)S(1)} %collective-permute-done.3.refs_1_, ...), custom_call_target="tpu_custom_call" | custom-call | flops 7247757312 | bytes 14680064 | tf_op jit(solution)/shard_map/attend/pallas_call | solution.py:213
  72.3 6.1 %collective-permute-done.6 = bf16[128,2048]{1,0:T(8,128)(2,1)S(1)} collective-permute-done((bf16[128,2048]{1,0:T(8,128)(2,1)S(1)}, bf16[128,2048]{1,0:T(8,128)(2,1)S(1)}, u32[]{:S(2)}, u32[]{:S(2)}) %collective-permute-start.6) | collective-permute-done | bytes 524320 | tf_op jit(solution)/shard_map/ppermute | solution.py:457
  78.6 1.4 collective-permute-start.8
  80.0 0.8 collective-permute-start.10
  80.7 2.6 %collective-permute-start.11 = (bf16[256,1152]{1,0:T(8,128)(2,1)}, bf16[256,1152]{1,0:T(8,128)(2,1)S(1)}, u32[]{:S(2)}, u32[]{:S(2)}) collective-permute-start(bf16[256,1152]{1,0:T(8,128)(2,1)} %get-tuple-element.48), channel_id=1, source_target_pairs={{0,6},{2,0},{4,2},{6,4},{1,7},{3,1},{5,3},{7,5},{8,14},{10,8},{12,... | collective-permute-start | bytes 1769480 | tf_op jit(solution)/shard_map/ppermute | solution.py:460
  83.3 0.6 collective-permute-done.8.other_in
  83.9 15.6 %all-gather.3.cloned.1.call-done = bf16[2304,2048]{1,0:T(8,128)(2,1)} async-done(((bf16[144,2048]{1,0:T(8,128)(2,1)}), bf16[2304,2048]{1,0:T(8,128)(2,1)}) %all-gather.3.cloned.1.call-update) | async-done | bytes 9437200 | tf_op jit(solution)/shard_map/all_gather | solution.py:444
  99.5 8.2 %hidden_units.1 = (bf16[512,1024]{1,0:T(8,128)(2,1)S(1)}, bf16[512,1024]{1,0:T(8,128)(2,1)S(1)}) custom-call(bf16[512,2048]{1,0:T(8,128)(2,1)} %copy-done.6, bf16[512,2048]{1,0:T(8,128)(2,1)} %collective-permute-done.8.other_in, bf16[16,144,2048]{2,1,0:T(8,128)(2,1)} %bitcast.14), custom_call_target="tpu_custom_call" | custom-call | flops 4294967296 | bytes 8388608 | tf_op jit(solution)/shard_map/hidden_units/pallas_call | solution.py:308
  107.7 1.6 collective-permute-done.11.c
  109.3 0.4 collective-permute-done.12.d
  109.7 2.7 %merge.1 = bf16[4,256,256]{2,1,0:T(8,128)(2,1)S(1)} custom-call(s32[3]{0:T(128)S(1)} %pad_add_fusion.place_ref.place, bf16[256,1152]{1,0:T(8,128)(2,1)S(1)} %attend.2.a, bf16[256,1152]{1,0:T(8,128)(2,1)S(1)} %collective-permute-done.10.b, bf16[256,1152]{1,0:T(8,128)(2,1)S(1)} %collective-permute-done.11.c, bf16[256,1152]{1,0:T(8,128)(2,1)} %collective-permute-done.12.d), custom_call_target="tpu_custom_call" | custom-call | tf_op jit(solution)/shard_map/merge/pallas_call | solution.py:279
  112.5 0.9 collective-permute-start.13
  113.4 2.9 %collective-permute-start.14 = (bf16[256,256]{1,0:T(8,128)(2,1)S(1)}, bf16[256,256]{1,0:T(8,128)(2,1)S(1)}, u32[]{:S(2)}, u32[]{:S(2)}) collective-permute-start(bf16[256,256]{1,0:T(8,128)(2,1)S(1)} %get-tuple-element.76), channel_id=1, source_target_pairs={{0,4},{2,6},{4,0},{6,2},{1,5},{3,7},{5,1},{7,3},{8,12},{10,14},{12... | collective-permute-start | bytes 393224 | tf_op jit(solution)/shard_map/ppermute | solution.py:467
  116.3 6.8 %down_units.1 = (f32[512,2048]{1,0:T(8,128)S(1)}, f32[512,2048]{1,0:T(8,128)S(1)}) custom-call(bf16[512,1024]{1,0:T(8,128)(2,1)S(1)} %get-tuple-element.58.own_hidden, bf16[512,1024]{1,0:T(8,128)(2,1)S(1)} %get-tuple-element.59.other_hidden, bf16[16,144,2048]{2,1,0:T(8,128)(2,1)} %bitcast.15), custom_call_target="tpu_custom_call" | custom-call | flops 4294967296 | bytes 14680064 | tf_op jit(solution)/shard_map/down_units/pallas_call | solution.py:341
  123.2 3.2 %finish.2 = (bf16[128,2048]{1,0:T(8,128)(2,1)S(1)}, bf16[128,2048]{1,0:T(8,128)(2,1)S(1)}, bf16[128,2048]{1,0:T(8,128)(2,1)S(1)}, bf16[128,2048]{1,0:T(8,128)(2,1)S(1)}) custom-call(f32[512,2048]{1,0:T(8,128)S(1)} %get-tuple-element.61.partial, bf16[256,256]{1,0:T(8,128)(2,1)S(1)} %get-tuple-element.62.a0, bf16[256,256]{1,0:T(8,128)(2,1)S(1)} %collective-permute-done.13.a1, ...), custom_call_target="tpu_custom_call" | custom-call | flops 536870912 | bytes 9437184 | tf_op jit(solution)/shard_map/finish/pallas_call | solution.py:377
  126.4 1.2 collective-permute-start.17
  127.5 0.1 collective-permute-start.19
  127.6 0.4 collective-permute-start.21
  128.1 0.1 collective-permute-start.16
  128.2 3.3 %finish.3 = (f32[128,2048]{1,0:T(8,128)S(1)}, f32[128,2048]{1,0:T(8,128)S(1)}, f32[128,2048]{1,0:T(8,128)S(1)}, f32[128,2048]{1,0:T(8,128)S(1)}) custom-call(f32[512,2048]{1,0:T(8,128)S(1)} %get-tuple-element.70.partial, bf16[256,256]{1,0:T(8,128)(2,1)S(1)} %get-tuple-element.62.a0, bf16[256,256]{1,0:T(8,128)(2,1)S(1)} %collective-permute-done.13.a1, ...), custom_call_target="tpu_custom_call" | custom-call | flops 536870912 | bytes 9437184 | tf_op jit(solution)/shard_map/finish/pallas_call | solution.py:377
  131.4 0.1 add_convert_fusion.3
  131.6 1.8 %collective-permute-start.18 = (bf16[128,2048]{1,0:T(8,128)(2,1)S(1)}, bf16[128,2048]{1,0:T(8,128)(2,1)S(1)}, u32[]{:S(2)}, u32[]{:S(2)}) collective-permute-start(bf16[128,2048]{1,0:T(8,128)(2,1)S(1)} %add_convert_fusion.3), channel_id=1, source_target_pairs={{0,4},{2,6},{4,0},{6,2},{1,5},{3,7},{5,1},{7,3},{8,12},{10,14},{12... | collective-permute-start | bytes 1572872 | tf_op jit(solution)/shard_map/ppermute | solution.py:478
  133.4 0.1 add_convert_fusion.2
  133.5 2.4 %collective-permute-start.20 = (bf16[128,2048]{1,0:T(8,128)(2,1)S(1)}, bf16[128,2048]{1,0:T(8,128)(2,1)S(1)}, u32[]{:S(2)}, u32[]{:S(2)}) collective-permute-start(bf16[128,2048]{1,0:T(8,128)(2,1)S(1)} %add_convert_fusion.2), channel_id=1, source_target_pairs={{0,6},{2,0},{4,2},{6,4},{1,7},{3,1},{5,3},{7,5},{8,14},{10,8},{12,... | collective-permute-start | bytes 1572872 | tf_op jit(solution)/shard_map/ppermute | solution.py:478
  135.9 0.1 add_convert_fusion.1
  136.0 0.1 collective-permute-start.22
  136.1 10.1 %collective-permute-done.18 = bf16[128,2048]{1,0:T(8,128)(2,1)S(1)} collective-permute-done((bf16[128,2048]{1,0:T(8,128)(2,1)S(1)}, bf16[128,2048]{1,0:T(8,128)(2,1)S(1)}, u32[]{:S(2)}, u32[]{:S(2)}) %collective-permute-start.18) | collective-permute-done | bytes 524320 | tf_op jit(solution)/shard_map/ppermute | solution.py:478
  146.3 10.0 %collective-permute-done.20 = bf16[128,2048]{1,0:T(8,128)(2,1)S(1)} collective-permute-done((bf16[128,2048]{1,0:T(8,128)(2,1)S(1)}, bf16[128,2048]{1,0:T(8,128)(2,1)S(1)}, u32[]{:S(2)}, u32[]{:S(2)}) %collective-permute-start.20) | collective-permute-done | bytes 524320 | tf_op jit(solution)/shard_map/ppermute | solution.py:478
  156.3 2.0 %collective-permute-done.22 = bf16[128,2048]{1,0:T(8,128)(2,1)S(1)} collective-permute-done((bf16[128,2048]{1,0:T(8,128)(2,1)S(1)}, bf16[128,2048]{1,0:T(8,128)(2,1)S(1)}, u32[]{:S(2)}, u32[]{:S(2)}) %collective-permute-start.22) | collective-permute-done | bytes 524320 | tf_op jit(solution)/shard_map/ppermute | solution.py:478
  158.2 1.2 add_convert_fusion
  (41 shorter events, 0.3 us)
Async XLA Ops:
  6.5 92.9 %all-gather.3.cloned.1.call-start = ((), (), s32[]{:S(2)}) async-start(), calls=%async_computation | async-start | bytes 10027008 | tf_op jit(solution)/shard_map/all_gather | solution.py:444
  6.6 1.4 copy-start
  8.7 9.7 %copy-start.4 = (bf16[64,2048]{1,0:T(8,128)(2,1)S(1)}, bf16[64,2048]{1,0:T(8,128)(2,1)}, u32[]{:S(2)}) copy-start(bf16[64,2048]{1,0:T(8,128)(2,1)} %param.17) | copy-start | bytes 786436
  8.7 9.7 %copy-start.5 = (bf16[64,2048]{1,0:T(8,128)(2,1)S(1)}, bf16[64,2048]{1,0:T(8,128)(2,1)}, u32[]{:S(2)}) copy-start(bf16[64,2048]{1,0:T(8,128)(2,1)} %param.16) | copy-start | bytes 786436
  8.7 9.7 %collective-permute-start = (bf16[128,3072]{1,0:T(8,128)(2,1)S(1)}, bf16[128,3072]{1,0:T(8,128)(2,1)S(1)}, u32[]{:S(2)}, u32[]{:S(2)}) collective-permute-start(bf16[128,3072]{1,0:T(8,128)(2,1)S(1)} %get-tuple-element.41), channel_id=1, source_target_pairs={{0,1},{1,0},{2,3},{3,2},{4,5},{5,4},{6,7},{7,6},{8,9},{9,8},{10,11... | collective-permute-start | bytes 2359304 | tf_op jit(solution)/shard_map/ppermute | solution.py:26
  10.2 8.2 %collective-permute-start.9 = (bf16[16,2048]{1,0:T(8,128)(2,1)}, bf16[16,2048]{1,0:T(8,128)(2,1)S(1)}, u32[]{:S(2)}, u32[]{:S(2)}) collective-permute-start(bf16[16,2048]{1,0:T(8,128)(2,1)} %param.15), channel_id=1, source_target_pairs={{0,0},{1,8},{2,16},{3,24},{4,32},{5,40},{6,48},{7,56},{8,64},{9,72... | collective-permute-start | bytes 196616 | tf_op jit(solution)/shard_map/ppermute | solution.py:438
  16.5 1.9 %copy-start.1 = (bf16[2,1024,1024]{2,1,0:T(8,128)(2,1)}, bf16[2,1024,1024]{2,1,0:T(8,128)(2,1)S(1)}, u32[]{:S(2)}) copy-start(bf16[2,1024,1024]{2,1,0:T(8,128)(2,1)S(1)} %pick_cache.1) | copy-start | bytes 12582916
  18.4 12.0 %copy-start.7 = (s32[16,2]{0,1:T(2,128)S(1)}, s32[16,2]{0,1:T(2,128)}, u32[]{:S(2)}) copy-start(s32[16,2]{0,1:T(2,128)} %param.13) | copy-start | bytes 388
  19.4 11.1 %collective-permute-start.1 = (bf16[2,1024,1024]{2,1,0:T(8,128)(2,1)}, bf16[2,1024,1024]{2,1,0:T(8,128)(2,1)}, u32[]{:S(2)}, u32[]{:S(2)}) collective-permute-start(bf16[2,1024,1024]{2,1,0:T(8,128)(2,1)} %copy-done.1), channel_id=1, source_target_pairs={{0,1},{1,0},{2,3},{3,2},{4,5},{5,4},{6,7},{7,6},{8,9},{9,8},{10,11... | collective-permute-start | bytes 12582920 | tf_op jit(solution)/shard_map/ppermute | solution.py:26
  19.5 20.8 %collective-permute-start.2 = (bf16[256,1024]{1,0:T(8,128)(2,1)S(1)}, bf16[256,1024]{1,0:T(8,128)(2,1)S(1)}, u32[]{:S(2)}, u32[]{:S(2)}) collective-permute-start(bf16[256,1024]{1,0:T(8,128)(2,1)S(1)} %pad_maximum_fusion.1.refs_0_), channel_id=1, source_target_pairs={{0,4},{2,6},{4,0},{6,2},{1,5},{3,7},{5,1},{7,3},{8,12},{10,14},{12... | collective-permute-start | bytes 1572872 | tf_op jit(solution)/shard_map/ppermute | solution.py:448
  27.7 23.6 %collective-permute-start.3 = (bf16[256,1024]{1,0:T(8,128)(2,1)S(1)}, bf16[256,1024]{1,0:T(8,128)(2,1)S(1)}, u32[]{:S(2)}, u32[]{:S(2)}) collective-permute-start(bf16[256,1024]{1,0:T(8,128)(2,1)S(1)} %pad_maximum_fusion.1.refs_0_), channel_id=1, source_target_pairs={{0,2},{2,4},{4,6},{6,0},{1,3},{3,5},{5,7},{7,1},{8,10},{10,12},{12... | collective-permute-start | bytes 1572872 | tf_op jit(solution)/shard_map/ppermute | solution.py:448
  27.9 23.5 %collective-permute-start.4 = (bf16[256,1024]{1,0:T(8,128)(2,1)S(1)}, bf16[256,1024]{1,0:T(8,128)(2,1)}, u32[]{:S(2)}, u32[]{:S(2)}) collective-permute-start(bf16[256,1024]{1,0:T(8,128)(2,1)S(1)} %pad_maximum_fusion.1.refs_0_), channel_id=1, source_target_pairs={{0,6},{2,0},{4,2},{6,4},{1,7},{3,1},{5,3},{7,5},{8,14},{10,8},{12,... | collective-permute-start | bytes 1572872 | tf_op jit(solution)/shard_map/ppermute | solution.py:448
  30.5 20.9 %copy-start.2 = (bf16[128,2048]{1,0:T(8,128)(2,1)S(1)}, bf16[128,2048]{1,0:T(8,128)(2,1)}, u32[]{:S(2)}) copy-start(bf16[128,2048]{1,0:T(8,128)(2,1)} %stream.1) | copy-start | bytes 1572868
  30.5 20.9 %copy-start.3 = (f32[2048]{0:T(1024)S(1)}, f32[2048]{0:T(1024)}, u32[]{:S(2)}) copy-start(f32[2048]{0:T(1024)} %param.14) | copy-start | bytes 24580
  51.7 20.5 %collective-permute-start.5 = (bf16[128,2048]{1,0:T(8,128)(2,1)S(1)}, bf16[128,2048]{1,0:T(8,128)(2,1)S(1)}, u32[]{:S(2)}, u32[]{:S(2)}) collective-permute-start(bf16[128,2048]{1,0:T(8,128)(2,1)S(1)} %layer_norm.1), channel_id=1, source_target_pairs={{0,2},{2,4},{4,6},{6,0},{1,3},{3,5},{5,7},{7,1},{8,10},{10,12},{12... | collective-permute-start | bytes 1572872 | tf_op jit(solution)/shard_map/ppermute | solution.py:457
  52.6 25.8 %collective-permute-start.6 = (bf16[128,2048]{1,0:T(8,128)(2,1)S(1)}, bf16[128,2048]{1,0:T(8,128)(2,1)S(1)}, u32[]{:S(2)}, u32[]{:S(2)}) collective-permute-start(bf16[128,2048]{1,0:T(8,128)(2,1)S(1)} %layer_norm.1), channel_id=1, source_target_pairs={{0,4},{2,6},{4,0},{6,2},{1,5},{3,7},{5,1},{7,3},{8,12},{10,14},{12... | collective-permute-start | bytes 1572872 | tf_op jit(solution)/shard_map/ppermute | solution.py:457
  55.6 22.8 %collective-permute-start.7 = (bf16[128,2048]{1,0:T(8,128)(2,1)S(1)}, bf16[128,2048]{1,0:T(8,128)(2,1)S(1)}, u32[]{:S(2)}, u32[]{:S(2)}) collective-permute-start(bf16[128,2048]{1,0:T(8,128)(2,1)S(1)} %layer_norm.1), channel_id=1, source_target_pairs={{0,6},{2,0},{4,2},{6,4},{1,7},{3,1},{5,3},{7,5},{8,14},{10,8},{12,... | collective-permute-start | bytes 1572872 | tf_op jit(solution)/shard_map/ppermute | solution.py:457
  78.6 1.4 copy-start.6
  78.6 5.3 %collective-permute-start.8 = (bf16[512,2048]{1,0:T(8,128)(2,1)S(1)}, bf16[512,2048]{1,0:T(8,128)(2,1)}, u32[]{:S(2)}, u32[]{:S(2)}) collective-permute-start(bf16[512,2048]{1,0:T(8,128)(2,1)S(1)} %constant_dynamic-update-slice_fusion.own_in), channel_id=1, source_target_pairs={{0,1},{1,0},{2,3},{3,2},{4,5},{5,4},{6,7},{7,6},{8,9},{9,8},{10,11... | collective-permute-start | bytes 6291464 | tf_op jit(solution)/shard_map/ppermute | solution.py:26
  80.0 27.7 %collective-permute-start.10 = (bf16[256,1152]{1,0:T(8,128)(2,1)}, bf16[256,1152]{1,0:T(8,128)(2,1)S(1)}, u32[]{:S(2)}, u32[]{:S(2)}) collective-permute-start(bf16[256,1152]{1,0:T(8,128)(2,1)} %get-tuple-element.47), channel_id=1, source_target_pairs={{0,4},{2,6},{4,0},{6,2},{1,5},{3,7},{5,1},{7,3},{8,12},{10,14},{12... | collective-permute-start | bytes 1769480 | tf_op jit(solution)/shard_map/ppermute | solution.py:460
  80.7 28.6 %collective-permute-start.11 = (bf16[256,1152]{1,0:T(8,128)(2,1)}, bf16[256,1152]{1,0:T(8,128)(2,1)S(1)}, u32[]{:S(2)}, u32[]{:S(2)}) collective-permute-start(bf16[256,1152]{1,0:T(8,128)(2,1)} %get-tuple-element.48), channel_id=1, source_target_pairs={{0,6},{2,0},{4,2},{6,4},{1,7},{3,1},{5,3},{7,5},{8,14},{10,8},{12,... | collective-permute-start | bytes 1769480 | tf_op jit(solution)/shard_map/ppermute | solution.py:460
  83.3 26.4 %collective-permute-start.12 = (bf16[256,1152]{1,0:T(8,128)(2,1)}, bf16[256,1152]{1,0:T(8,128)(2,1)}, u32[]{:S(2)}, u32[]{:S(2)}) collective-permute-start(bf16[256,1152]{1,0:T(8,128)(2,1)} %get-tuple-element.49), channel_id=1, source_target_pairs={{0,2},{2,4},{4,6},{6,0},{1,3},{3,5},{5,7},{7,1},{8,10},{10,12},{12... | collective-permute-start | bytes 1769480 | tf_op jit(solution)/shard_map/ppermute | solution.py:460
  112.5 10.7 %collective-permute-start.13 = (bf16[256,256]{1,0:T(8,128)(2,1)S(1)}, bf16[256,256]{1,0:T(8,128)(2,1)S(1)}, u32[]{:S(2)}, u32[]{:S(2)}) collective-permute-start(bf16[256,256]{1,0:T(8,128)(2,1)S(1)} %get-tuple-element.77), channel_id=1, source_target_pairs={{0,2},{2,4},{4,6},{6,0},{1,3},{3,5},{5,7},{7,1},{8,10},{10,12},{12... | collective-permute-start | bytes 393224 | tf_op jit(solution)/shard_map/ppermute | solution.py:467
  113.4 9.8 %collective-permute-start.14 = (bf16[256,256]{1,0:T(8,128)(2,1)S(1)}, bf16[256,256]{1,0:T(8,128)(2,1)S(1)}, u32[]{:S(2)}, u32[]{:S(2)}) collective-permute-start(bf16[256,256]{1,0:T(8,128)(2,1)S(1)} %get-tuple-element.76), channel_id=1, source_target_pairs={{0,4},{2,6},{4,0},{6,2},{1,5},{3,7},{5,1},{7,3},{8,12},{10,14},{12... | collective-permute-start | bytes 393224 | tf_op jit(solution)/shard_map/ppermute | solution.py:467
  116.3 6.8 %collective-permute-start.15 = (bf16[256,256]{1,0:T(8,128)(2,1)S(1)}, bf16[256,256]{1,0:T(8,128)(2,1)S(1)}, u32[]{:S(2)}, u32[]{:S(2)}) collective-permute-start(bf16[256,256]{1,0:T(8,128)(2,1)S(1)} %get-tuple-element.75), channel_id=1, source_target_pairs={{0,6},{2,0},{4,2},{6,4},{1,7},{3,1},{5,3},{7,5},{8,14},{10,8},{12,... | collective-permute-start | bytes 393224 | tf_op jit(solution)/shard_map/ppermute | solution.py:467
  126.4 5.1 %collective-permute-start.17 = (bf16[128,2048]{1,0:T(8,128)(2,1)S(1)}, bf16[128,2048]{1,0:T(8,128)(2,1)S(1)}, u32[]{:S(2)}, u32[]{:S(2)}) collective-permute-start(bf16[128,2048]{1,0:T(8,128)(2,1)S(1)} %get-tuple-element.68), channel_id=1, source_target_pairs={{0,1},{1,0},{2,3},{3,2},{4,5},{5,4},{6,7},{7,6},{8,9},{9,8},{10,11... | collective-permute-start | bytes 1572872 | tf_op jit(solution)/shard_map/ppermute | solution.py:26
  127.5 5.8 %collective-permute-start.19 = (bf16[128,2048]{1,0:T(8,128)(2,1)S(1)}, bf16[128,2048]{1,0:T(8,128)(2,1)S(1)}, u32[]{:S(2)}, u32[]{:S(2)}) collective-permute-start(bf16[128,2048]{1,0:T(8,128)(2,1)S(1)} %get-tuple-element.67), channel_id=1, source_target_pairs={{0,1},{1,0},{2,3},{3,2},{4,5},{5,4},{6,7},{7,6},{8,9},{9,8},{10,11... | collective-permute-start | bytes 1572872 | tf_op jit(solution)/shard_map/ppermute | solution.py:26
  127.6 8.3 %collective-permute-start.21 = (bf16[128,2048]{1,0:T(8,128)(2,1)S(1)}, bf16[128,2048]{1,0:T(8,128)(2,1)S(1)}, u32[]{:S(2)}, u32[]{:S(2)}) collective-permute-start(bf16[128,2048]{1,0:T(8,128)(2,1)S(1)} %get-tuple-element.69), channel_id=1, source_target_pairs={{0,1},{1,0},{2,3},{3,2},{4,5},{5,4},{6,7},{7,6},{8,9},{9,8},{10,11... | collective-permute-start | bytes 1572872 | tf_op jit(solution)/shard_map/ppermute | solution.py:26
  128.1 8.0 %collective-permute-start.16 = (bf16[128,2048]{1,0:T(8,128)(2,1)S(1)}, bf16[128,2048]{1,0:T(8,128)(2,1)S(1)}, u32[]{:S(2)}, u32[]{:S(2)}) collective-permute-start(bf16[128,2048]{1,0:T(8,128)(2,1)S(1)} %get-tuple-element.66), channel_id=1, source_target_pairs={{0,1},{1,0},{2,3},{3,2},{4,5},{5,4},{6,7},{7,6},{8,9},{9,8},{10,11... | collective-permute-start | bytes 1572872 | tf_op jit(solution)/shard_map/ppermute | solution.py:26
  131.6 14.7 %collective-permute-start.18 = (bf16[128,2048]{1,0:T(8,128)(2,1)S(1)}, bf16[128,2048]{1,0:T(8,128)(2,1)S(1)}, u32[]{:S(2)}, u32[]{:S(2)}) collective-permute-start(bf16[128,2048]{1,0:T(8,128)(2,1)S(1)} %add_convert_fusion.3), channel_id=1, source_target_pairs={{0,4},{2,6},{4,0},{6,2},{1,5},{3,7},{5,1},{7,3},{8,12},{10,14},{12... | collective-permute-start | bytes 1572872 | tf_op jit(solution)/shard_map/ppermute | solution.py:478
  133.5 22.8 %collective-permute-start.20 = (bf16[128,2048]{1,0:T(8,128)(2,1)S(1)}, bf16[128,2048]{1,0:T(8,128)(2,1)S(1)}, u32[]{:S(2)}, u32[]{:S(2)}) collective-permute-start(bf16[128,2048]{1,0:T(8,128)(2,1)S(1)} %add_convert_fusion.2), channel_id=1, source_target_pairs={{0,6},{2,0},{4,2},{6,4},{1,7},{3,1},{5,3},{7,5},{8,14},{10,8},{12,... | collective-permute-start | bytes 1572872 | tf_op jit(solution)/shard_map/ppermute | solution.py:478
  136.0 22.2 %collective-permute-start.22 = (bf16[128,2048]{1,0:T(8,128)(2,1)S(1)}, bf16[128,2048]{1,0:T(8,128)(2,1)S(1)}, u32[]{:S(2)}, u32[]{:S(2)}) collective-permute-start(bf16[128,2048]{1,0:T(8,128)(2,1)S(1)} %add_convert_fusion.1), channel_id=1, source_target_pairs={{0,2},{2,4},{4,6},{6,0},{1,3},{3,5},{5,7},{7,1},{8,10},{10,12},{12... | collective-permute-start | bytes 1572872 | tf_op jit(solution)/shard_map/ppermute | solution.py:478
Sparse Core Ops, SparseCore 0:
  19.5 79.9 all-gather.2

commit v6 on v4

--- a/solution.py
+++ b/solution.py
@@ -109,7 +109,7 @@
                 pltpu.SemaphoreType.DMA((2 * heads,)),
             ],
         ),
-        out_shape=jax.ShapeDtypeStruct((2, rows, width // 2), BF16),
+        out_shape=pltpu.HBM((2, rows, width // 2), BF16),
         compiler_params=params(16),
         name="pick_cache",
     )(place, keys, values)
@@ -439,21 +439,19 @@
     cached = in_hbm(key_cache, value_cache)
     own_query, new_out = pick_new(place, projections)
     new_in = swap_cores(new_out)
-    (cache_out,) = in_hbm(pick_cache(after(place, new_out), *cached))
+    cache_out = pick_cache(after(place, new_out), *cached)
     head_rows = after(head_rows, cache_out)
     weights = lax.all_gather(
         jnp.concatenate([up_weight, down_weight, head_rows], 0), ("y", "x"), axis=0
     )
-    query = jnp.concatenate([own_query, new_in[:, :half]], 0)
+    (query,) = in_hbm(jnp.concatenate([own_query, new_in[:, :half]], 0))
     queries = [lax.ppermute(query, "z", ring(k, nz)) for k in (2, 1, 3)]
     cache_in = swap_cores(after(cache_out, query))
     context = (*cached, *in_hbm(projections), cache_in, new_in)
-    (partial,) = attend((0,), place, cache_range, [query], *context)
-
-    norm_gain, place_late = after((norm_gain, place), partial, *queries)
+    norm_gain, place_late = after((norm_gain, place), *queries, cache_in)
     normed = layer_norm(stream, norm_gain)
     place_late = after(place_late, normed)
-    sent = attend((2, 1, 3), place_late, cache_range, queries, *context)
+    partial, *sent = attend((0, 2, 1, 3), place_late, cache_range, [query, *queries], *context)
     inputs = [normed] + [lax.ppermute(normed, "z", ring(k, nz)) for k in range(1, nz)]
     sent, inputs = lax.optimization_barrier((sent, inputs))
     partials = [partial] + [
@@ -461,7 +459,7 @@
     ]
     (own_in,) = in_hbm(jnp.concatenate(inputs, 0))
     (other_in,) = in_hbm(swap_cores(own_in))
-    own_hidden, other_hidden = hidden_units(own_in, other_in, weights, unit_rows)
+    own_hidden, other_hidden = hidden_units(own_in, other_in, *in_hbm(weights), unit_rows)
     heads = merge(after(place, own_hidden), partials)
     attention = [heads[0]] + [lax.ppermute(heads[k], "z", ring(k, nz)) for k in range(1, nz)]
 

time: 164 us -> 161 us (0.982)
  waiting for transfers between devices: 56.4 us -> 66.9 us
  Pallas kernels: 51.4 us -> 45 us
  local copies, waits for them, and re-layouts: 7.38 us -> 1.78 us
    ppermute x3, waiting for transfers between devices: 10.9 us -> 20.9 us  [on_device(): queries = [lax.ppermute(query, 'z', ring(k, nz)) for k in (2, 1, 3)]]
    pallas_call x2 -> x1, Pallas kernels: 26.8 us -> 19.7 us  [attend(): pl.pallas_call(functools.partial(attend_kernel, steps), grid_spec=pltpu.P...]
    unnamed x28 -> x32, local copies, waits for them, and re-layouts: 7.29 us -> 1.68 us
    ppermute x3, waiting for transfers between devices: 5.94 us -> 3.02 us  [on_device(): lax.ppermute(normed, 'z', ring(k, nz))]
    ppermute x3, waiting for transfers between devices: 0.77 us -> 3.58 us  [on_device(): lax.ppermute(made, 'z', ring(-k, nz))]
  transfers between devices with their start and end apart: 24 -> 24, of which waited for: 10 -> 11; matrix products, arithmetic and copies ran while one was open for 0% -> 0% of each run, Pallas kernels for 29% -> 26%
where the time goes in v6:
time: 161 us
  waiting for transfers between devices  66.9 us (42%)
  Pallas kernels  45 us (28%)
  starting transfers between devices  30.4 us (19%)
  between operations  13.8 us (9%)
  other arithmetic  2.6 us (2%)
  local copies, waits for them, and re-layouts  1.78 us (1%)
    ppermute x3, waiting for transfers between devices, on_device(): summed = summed + lax.ppermute(both, 'z', ring(-k, nz)).astype(F32)  22.4 us
    ppermute x3, waiting for transfers between devices, on_device(): queries = [lax.ppermute(query, 'z', ring(k, nz)) for k in (2, 1, 3)]  20.9 us
    pallas_call x1, Pallas kernels, attend(): pl.pallas_call(functools.partial(attend_kernel, steps), grid_spec=pltpu.P...  19.7 us
    all_gather x1, waiting for transfers between devices, on_device(): lax.all_gather(jnp.concatenate([up_weight, down_weight, head_rows], 0), (...  13.4 us
    pallas_call x1, Pallas kernels, hidden_units(): pl.pallas_call(hidden_kernel, grid=(shards // chunk,), in_specs=[whole, w...  8.68 us
    ppermute x3, starting transfers between devices, on_device(): queries = [lax.ppermute(query, 'z', ring(k, nz)) for k in (2, 1, 3)]  8.6 us
    pallas_call x1, Pallas kernels, down_units(): pl.pallas_call(down_kernel, grid=(width // columns,), in_specs=[whole, wh...  5.88 us
    ppermute x1, starting transfers between devices, on_device(): lax.ppermute(out_weight, ('y', 'x', 'z', 'c'), head_owners(ny, nx, nz))  4.5 us
  transfers between devices with their start and end apart: 24, of which 11 were waited for; matrix products, arithmetic and copies ran while one was open for 0% of the time, Pallas kernels for 26%

profile of v6, /device:TPU:1, one launch (start us, length us, event | category | flops | bytes accessed | tf_op | source)
XLA Modules:
  0.0 160.5 jit_solution(17832988102563137880)
XLA Ops:
  6.5 4.5 %collective-permute-start.9 = (bf16[16,2048]{1,0:T(8,128)(2,1)}, bf16[16,2048]{1,0:T(8,128)(2,1)S(1)}, u32[]{:S(2)}, u32[]{:S(2)}) collective-permute-start(bf16[16,2048]{1,0:T(8,128)(2,1)} %param.15), channel_id=1, source_target_pairs={{0,0},{1,8},{2,16},{3,24},{4,32},{5,40},{6,48},{7,56},{8,64},{9,72... | collective-permute-start | bytes 196616 | tf_op jit(solution)/shard_map/ppermute | solution.py:438
  11.1 0.1 pad_add_fusion.place_ref.place
  11.1 1.4 copy-done.1
  12.5 0.7 pick_new.1
  13.3 4.4 %pick_cache.1 = bf16[2,1024,1024]{2,1,0:T(8,128)(2,1)} custom-call(s32[3]{0:T(128)S(1)} %pad_add_fusion.place_ref.place, bf16[1024,2048]{1,0:T(8,128)(2,1)} %refs_4_.1, bf16[1024,2048]{1,0:T(8,128)(2,1)} %refs_6_.1), custom_call_target="tpu_custom_call" | custom-call | tf_op jit(solution)/shard_map/pick_cache/pallas_call | solution.py:99
  17.7 0.9 pad_maximum_fusion
  18.6 0.1 collective-permute-start
  18.7 2.3 %collective-permute-done.refs_9_.refs_11_ = bf16[128,3072]{1,0:T(8,128)(2,1)S(1)} collective-permute-done((bf16[128,3072]{1,0:T(8,128)(2,1)S(1)}, bf16[128,3072]{1,0:T(8,128)(2,1)S(1)}, u32[]{:S(2)}, u32[]{:S(2)}) %collective-permute-start) | collective-permute-done | bytes 786464 | tf_op jit(solution)/shard_map/ppermute | solution.py:26
  21.1 0.2 collective-permute-start.4
  21.3 5.9 %collective-permute-start.1 = (bf16[256,1024]{1,0:T(8,128)(2,1)S(1)}, bf16[256,1024]{1,0:T(8,128)(2,1)S(1)}, u32[]{:S(2)}, u32[]{:S(2)}) collective-permute-start(bf16[256,1024]{1,0:T(8,128)(2,1)S(1)} %pad_maximum_fusion.1.refs_0_), channel_id=1, source_target_pairs={{0,4},{2,6},{4,0},{6,2},{1,5},{3,7},{5,1},{7,3},{8,12},{10,14},{12... | collective-permute-start | bytes 1572872 | tf_op jit(solution)/shard_map/ppermute | solution.py:448
  27.2 0.1 collective-permute-start.2
  27.3 2.6 %collective-permute-start.3 = (bf16[256,1024]{1,0:T(8,128)(2,1)S(1)}, bf16[256,1024]{1,0:T(8,128)(2,1)S(1)}, u32[]{:S(2)}, u32[]{:S(2)}) collective-permute-start(bf16[256,1024]{1,0:T(8,128)(2,1)S(1)} %pad_maximum_fusion.1.refs_0_), channel_id=1, source_target_pairs={{0,6},{2,0},{4,2},{6,4},{1,7},{3,1},{5,3},{7,5},{8,14},{10,8},{12,... | collective-permute-start | bytes 1572872 | tf_op jit(solution)/shard_map/ppermute | solution.py:448
  29.9 0.1 copy.10.ranges
  30.0 9.3 %collective-permute-done.1.refs_1_ = bf16[256,1024]{1,0:T(8,128)(2,1)S(1)} collective-permute-done((bf16[256,1024]{1,0:T(8,128)(2,1)S(1)}, bf16[256,1024]{1,0:T(8,128)(2,1)S(1)}, u32[]{:S(2)}, u32[]{:S(2)}) %collective-permute-start.1) | collective-permute-done | bytes 524320 | tf_op jit(solution)/shard_map/ppermute | solution.py:448
  39.2 11.6 %collective-permute-done.2.refs_2_ = bf16[256,1024]{1,0:T(8,128)(2,1)S(1)} collective-permute-done((bf16[256,1024]{1,0:T(8,128)(2,1)S(1)}, bf16[256,1024]{1,0:T(8,128)(2,1)S(1)}, u32[]{:S(2)}, u32[]{:S(2)}) %collective-permute-start.2) | collective-permute-done | bytes 524320 | tf_op jit(solution)/shard_map/ppermute | solution.py:448
  50.9 0.4 layer_norm.1
  51.2 0.9 collective-permute-start.5
  52.1 2.9 %collective-permute-start.6 = (bf16[128,2048]{1,0:T(8,128)(2,1)S(1)}, bf16[128,2048]{1,0:T(8,128)(2,1)S(1)}, u32[]{:S(2)}, u32[]{:S(2)}) collective-permute-start(bf16[128,2048]{1,0:T(8,128)(2,1)S(1)} %layer_norm.1), channel_id=1, source_target_pairs={{0,4},{2,6},{4,0},{6,2},{1,5},{3,7},{5,1},{7,3},{8,12},{10,14},{12... | collective-permute-start | bytes 1572872 | tf_op jit(solution)/shard_map/ppermute | solution.py:455
  55.0 19.7 %attend.1 = (bf16[256,1152]{1,0:T(8,128)(2,1)S(1)}, bf16[256,1152]{1,0:T(8,128)(2,1)}, bf16[256,1152]{1,0:T(8,128)(2,1)}, bf16[256,1152]{1,0:T(8,128)(2,1)S(1)}) custom-call(s32[3]{0:T(128)S(1)} %pad_add_fusion.place_ref.place, s32[16,2]{1,0:T(8,128)S(1)} %copy.10.ranges, bf16[256,1024]{1,0:T(8,128)(2,1)} %copy-done.3, bf16[256,1024]{1,0:T(8,128)(2,1)} %copy-done.8, ...), custom_call_target="tpu_custom_call" | custom-call | flops 9663676416 | bytes 16777216 | tf_op jit(solution)/shard_map/attend/pallas_call | solution.py:213
  74.7 3.0 %collective-permute-done.6 = bf16[128,2048]{1,0:T(8,128)(2,1)S(1)} collective-permute-done((bf16[128,2048]{1,0:T(8,128)(2,1)S(1)}, bf16[128,2048]{1,0:T(8,128)(2,1)S(1)}, u32[]{:S(2)}, u32[]{:S(2)}) %collective-permute-start.6) | collective-permute-done | bytes 524320 | tf_op jit(solution)/shard_map/ppermute | solution.py:455
  78.0 1.4 collective-permute-start.8
  79.4 0.8 collective-permute-start.10
  80.2 1.7 %collective-permute-start.11 = (bf16[256,1152]{1,0:T(8,128)(2,1)}, bf16[256,1152]{1,0:T(8,128)(2,1)S(1)}, u32[]{:S(2)}, u32[]{:S(2)}) collective-permute-start(bf16[256,1152]{1,0:T(8,128)(2,1)} %get-tuple-element.64), channel_id=1, source_target_pairs={{0,6},{2,0},{4,2},{6,4},{1,7},{3,1},{5,3},{7,5},{8,14},{10,8},{12,... | collective-permute-start | bytes 1769480 | tf_op jit(solution)/shard_map/ppermute | solution.py:458
  82.0 1.3 collective-permute-done.8.other_in
  83.3 13.4 %all-gather.3.cloned.1.call-done = bf16[2304,2048]{1,0:T(8,128)(2,1)} async-done(((bf16[144,2048]{1,0:T(8,128)(2,1)}), bf16[2304,2048]{1,0:T(8,128)(2,1)}) %all-gather.3.cloned.1.call-update) | async-done | bytes 9437200 | tf_op jit(solution)/shard_map/all_gather | solution.py:444
  96.7 8.7 %hidden_units.1 = (bf16[512,1024]{1,0:T(8,128)(2,1)S(1)}, bf16[512,1024]{1,0:T(8,128)(2,1)S(1)}) custom-call(bf16[512,2048]{1,0:T(8,128)(2,1)} %copy-done.6, bf16[512,2048]{1,0:T(8,128)(2,1)} %collective-permute-done.8.other_in, bf16[16,144,2048]{2,1,0:T(8,128)(2,1)} %bitcast.13), custom_call_target="tpu_custom_call" | custom-call | flops 4294967296 | bytes 8388608 | tf_op jit(solution)/shard_map/hidden_units/pallas_call | solution.py:308
  105.4 2.7 %collective-permute-done.11.c = bf16[256,1152]{1,0:T(8,128)(2,1)S(1)} collective-permute-done((bf16[256,1152]{1,0:T(8,128)(2,1)}, bf16[256,1152]{1,0:T(8,128)(2,1)S(1)}, u32[]{:S(2)}, u32[]{:S(2)}) %collective-permute-start.11) | collective-permute-done | bytes 589856 | tf_op jit(solution)/shard_map/ppermute | solution.py:458
  108.2 0.9 collective-permute-done.12.d
  109.0 1.7 %merge.1 = bf16[4,256,256]{2,1,0:T(8,128)(2,1)S(1)} custom-call(s32[3]{0:T(128)S(1)} %pad_add_fusion.place_ref.place, bf16[256,1152]{1,0:T(8,128)(2,1)S(1)} %get-tuple-element.62.a, bf16[256,1152]{1,0:T(8,128)(2,1)S(1)} %collective-permute-done.10.b, bf16[256,1152]{1,0:T(8,128)(2,1)S(1)} %collective-permute-done.11.c, ...), custom_call_target="tpu_custom_call" | custom-call | tf_op jit(solution)/shard_map/merge/pallas_call | solution.py:279
  110.7 0.3 collective-permute-start.13
  111.0 3.0 %collective-permute-start.14 = (bf16[256,256]{1,0:T(8,128)(2,1)S(1)}, bf16[256,256]{1,0:T(8,128)(2,1)S(1)}, u32[]{:S(2)}, u32[]{:S(2)}) collective-permute-start(bf16[256,256]{1,0:T(8,128)(2,1)S(1)} %get-tuple-element.84), channel_id=1, source_target_pairs={{0,4},{2,6},{4,0},{6,2},{1,5},{3,7},{5,1},{7,3},{8,12},{10,14},{12... | collective-permute-start | bytes 393224 | tf_op jit(solution)/shard_map/ppermute | solution.py:464
  114.0 5.9 %down_units.1 = (f32[512,2048]{1,0:T(8,128)S(1)}, f32[512,2048]{1,0:T(8,128)S(1)}) custom-call(bf16[512,1024]{1,0:T(8,128)(2,1)S(1)} %get-tuple-element.66.own_hidden, bf16[512,1024]{1,0:T(8,128)(2,1)S(1)} %get-tuple-element.67.other_hidden, bf16[16,144,2048]{2,1,0:T(8,128)(2,1)S(1)} %bitcast.16), custom_call_target="tpu_custom_call" | custom-call | flops 4294967296 | bytes 14680064 | tf_op jit(solution)/shard_map/down_units/pallas_call | solution.py:341
  119.9 1.7 %finish.2 = (bf16[128,2048]{1,0:T(8,128)(2,1)S(1)}, bf16[128,2048]{1,0:T(8,128)(2,1)S(1)}, bf16[128,2048]{1,0:T(8,128)(2,1)S(1)}, bf16[128,2048]{1,0:T(8,128)(2,1)S(1)}) custom-call(f32[512,2048]{1,0:T(8,128)S(1)} %get-tuple-element.69.partial, bf16[256,256]{1,0:T(8,128)(2,1)S(1)} %get-tuple-element.70.a0, bf16[256,256]{1,0:T(8,128)(2,1)S(1)} %collective-permute-done.13.a1, ...), custom_call_target="tpu_custom_call" | custom-call | flops 536870912 | bytes 9437184 | tf_op jit(solution)/shard_map/finish/pallas_call | solution.py:377
  121.7 1.5 collective-permute-start.17
  123.1 0.1 collective-permute-start.19
  123.2 0.4 collective-permute-start.21
  123.6 0.1 collective-permute-start.16
  123.7 1.8 %finish.3 = (f32[128,2048]{1,0:T(8,128)S(1)}, f32[128,2048]{1,0:T(8,128)S(1)}, f32[128,2048]{1,0:T(8,128)S(1)}, f32[128,2048]{1,0:T(8,128)S(1)}) custom-call(f32[512,2048]{1,0:T(8,128)S(1)} %get-tuple-element.78.partial, bf16[256,256]{1,0:T(8,128)(2,1)S(1)} %get-tuple-element.70.a0, bf16[256,256]{1,0:T(8,128)(2,1)S(1)} %collective-permute-done.13.a1, ...), custom_call_target="tpu_custom_call" | custom-call | flops 536870912 | bytes 9437184 | tf_op jit(solution)/shard_map/finish/pallas_call | solution.py:377
  125.6 0.1 add_convert_fusion.3
  125.7 1.9 %collective-permute-start.18 = (bf16[128,2048]{1,0:T(8,128)(2,1)S(1)}, bf16[128,2048]{1,0:T(8,128)(2,1)S(1)}, u32[]{:S(2)}, u32[]{:S(2)}) collective-permute-start(bf16[128,2048]{1,0:T(8,128)(2,1)S(1)} %add_convert_fusion.3), channel_id=1, source_target_pairs={{0,4},{2,6},{4,0},{6,2},{1,5},{3,7},{5,1},{7,3},{8,12},{10,14},{12... | collective-permute-start | bytes 1572872 | tf_op jit(solution)/shard_map/ppermute | solution.py:475
  127.6 0.1 add_convert_fusion.2
  127.7 2.0 %collective-permute-start.20 = (bf16[128,2048]{1,0:T(8,128)(2,1)S(1)}, bf16[128,2048]{1,0:T(8,128)(2,1)S(1)}, u32[]{:S(2)}, u32[]{:S(2)}) collective-permute-start(bf16[128,2048]{1,0:T(8,128)(2,1)S(1)} %add_convert_fusion.2), channel_id=1, source_target_pairs={{0,6},{2,0},{4,2},{6,4},{1,7},{3,1},{5,3},{7,5},{8,14},{10,8},{12,... | collective-permute-start | bytes 1572872 | tf_op jit(solution)/shard_map/ppermute | solution.py:475
  129.8 0.1 add_convert_fusion.1
  129.9 0.1 collective-permute-start.22
  130.0 10.4 %collective-permute-done.18 = bf16[128,2048]{1,0:T(8,128)(2,1)S(1)} collective-permute-done((bf16[128,2048]{1,0:T(8,128)(2,1)S(1)}, bf16[128,2048]{1,0:T(8,128)(2,1)S(1)}, u32[]{:S(2)}, u32[]{:S(2)}) %collective-permute-start.18) | collective-permute-done | bytes 524320 | tf_op jit(solution)/shard_map/ppermute | solution.py:475
  140.4 11.2 %collective-permute-done.20 = bf16[128,2048]{1,0:T(8,128)(2,1)S(1)} collective-permute-done((bf16[128,2048]{1,0:T(8,128)(2,1)S(1)}, bf16[128,2048]{1,0:T(8,128)(2,1)S(1)}, u32[]{:S(2)}, u32[]{:S(2)}) %collective-permute-start.20) | collective-permute-done | bytes 524320 | tf_op jit(solution)/shard_map/ppermute | solution.py:475
  151.6 0.7 collective-permute-done.22
  152.4 1.3 add_convert_fusion
  (53 shorter events, 0.4 us)
Async XLA Ops:
  6.5 90.2 %all-gather.3.cloned.1.call-start = ((), (), s32[]{:S(2)}) async-start(), calls=%async_computation | async-start | bytes 10027008 | tf_op jit(solution)/shard_map/all_gather | solution.py:444
  6.5 11.1 %collective-permute-start.9 = (bf16[16,2048]{1,0:T(8,128)(2,1)}, bf16[16,2048]{1,0:T(8,128)(2,1)S(1)}, u32[]{:S(2)}, u32[]{:S(2)}) collective-permute-start(bf16[16,2048]{1,0:T(8,128)(2,1)} %param.15), channel_id=1, source_target_pairs={{0,0},{1,8},{2,16},{3,24},{4,32},{5,40},{6,48},{7,56},{8,64},{9,72... | collective-permute-start | bytes 196616 | tf_op jit(solution)/shard_map/ppermute | solution.py:438
  11.1 1.4 copy-start.1
  13.2 4.5 %copy-start.4 = (bf16[64,2048]{1,0:T(8,128)(2,1)S(1)}, bf16[64,2048]{1,0:T(8,128)(2,1)}, u32[]{:S(2)}) copy-start(bf16[64,2048]{1,0:T(8,128)(2,1)} %param.17) | copy-start | bytes 786436
  13.2 4.5 %copy-start.5 = (bf16[64,2048]{1,0:T(8,128)(2,1)S(1)}, bf16[64,2048]{1,0:T(8,128)(2,1)}, u32[]{:S(2)}) copy-start(bf16[64,2048]{1,0:T(8,128)(2,1)} %param.16) | copy-start | bytes 786436
  17.6 12.2 %copy-start.7 = (s32[16,2]{0,1:T(2,128)S(1)}, s32[16,2]{0,1:T(2,128)}, u32[]{:S(2)}) copy-start(s32[16,2]{0,1:T(2,128)} %param.13) | copy-start | bytes 388
  17.7 33.2 %copy-start = (bf16[128,2048]{1,0:T(8,128)(2,1)S(1)}, bf16[128,2048]{1,0:T(8,128)(2,1)}, u32[]{:S(2)}) copy-start(bf16[128,2048]{1,0:T(8,128)(2,1)} %stream.1) | copy-start | bytes 1572868
  17.7 33.2 %copy-start.2 = (f32[2048]{0:T(1024)S(1)}, f32[2048]{0:T(1024)}, u32[]{:S(2)}) copy-start(f32[2048]{0:T(1024)} %param.14) | copy-start | bytes 24580
  18.6 2.4 %collective-permute-start = (bf16[128,3072]{1,0:T(8,128)(2,1)S(1)}, bf16[128,3072]{1,0:T(8,128)(2,1)S(1)}, u32[]{:S(2)}, u32[]{:S(2)}) collective-permute-start(bf16[128,3072]{1,0:T(8,128)(2,1)S(1)} %get-tuple-element.45), channel_id=1, source_target_pairs={{0,1},{1,0},{2,3},{3,2},{4,5},{5,4},{6,7},{7,6},{8,9},{9,8},{10,11... | collective-permute-start | bytes 2359304 | tf_op jit(solution)/shard_map/ppermute | solution.py:26
  21.1 33.9 %copy-start.3 = (bf16[256,1024]{1,0:T(8,128)(2,1)}, bf16[256,1024]{1,0:T(8,128)(2,1)S(1)}, u32[]{:S(2)}) copy-start(bf16[256,1024]{1,0:T(8,128)(2,1)S(1)} %pad_maximum_fusion.1.refs_0_) | copy-start | bytes 1572868
  21.1 29.8 %collective-permute-start.4 = (bf16[2,1024,1024]{2,1,0:T(8,128)(2,1)}, bf16[2,1024,1024]{2,1,0:T(8,128)(2,1)}, u32[]{:S(2)}, u32[]{:S(2)}) collective-permute-start(bf16[2,1024,1024]{2,1,0:T(8,128)(2,1)} %pick_cache.1), channel_id=1, source_target_pairs={{0,1},{1,0},{2,3},{3,2},{4,5},{5,4},{6,7},{7,6},{8,9},{9,8},{10,11... | collective-permute-start | bytes 12582920 | tf_op jit(solution)/shard_map/ppermute | solution.py:26
  21.3 18.0 %collective-permute-start.1 = (bf16[256,1024]{1,0:T(8,128)(2,1)S(1)}, bf16[256,1024]{1,0:T(8,128)(2,1)S(1)}, u32[]{:S(2)}, u32[]{:S(2)}) collective-permute-start(bf16[256,1024]{1,0:T(8,128)(2,1)S(1)} %pad_maximum_fusion.1.refs_0_), channel_id=1, source_target_pairs={{0,4},{2,6},{4,0},{6,2},{1,5},{3,7},{5,1},{7,3},{8,12},{10,14},{12... | collective-permute-start | bytes 1572872 | tf_op jit(solution)/shard_map/ppermute | solution.py:448
  27.2 23.6 %collective-permute-start.2 = (bf16[256,1024]{1,0:T(8,128)(2,1)S(1)}, bf16[256,1024]{1,0:T(8,128)(2,1)S(1)}, u32[]{:S(2)}, u32[]{:S(2)}) collective-permute-start(bf16[256,1024]{1,0:T(8,128)(2,1)S(1)} %pad_maximum_fusion.1.refs_0_), channel_id=1, source_target_pairs={{0,2},{2,4},{4,6},{6,0},{1,3},{3,5},{5,7},{7,1},{8,10},{10,12},{12... | collective-permute-start | bytes 1572872 | tf_op jit(solution)/shard_map/ppermute | solution.py:448
  27.3 23.5 %collective-permute-start.3 = (bf16[256,1024]{1,0:T(8,128)(2,1)S(1)}, bf16[256,1024]{1,0:T(8,128)(2,1)S(1)}, u32[]{:S(2)}, u32[]{:S(2)}) collective-permute-start(bf16[256,1024]{1,0:T(8,128)(2,1)S(1)} %pad_maximum_fusion.1.refs_0_), channel_id=1, source_target_pairs={{0,6},{2,0},{4,2},{6,4},{1,7},{3,1},{5,3},{7,5},{8,14},{10,8},{12,... | collective-permute-start | bytes 1572872 | tf_op jit(solution)/shard_map/ppermute | solution.py:448
  39.2 15.8 %copy-start.8 = (bf16[256,1024]{1,0:T(8,128)(2,1)}, bf16[256,1024]{1,0:T(8,128)(2,1)S(1)}, u32[]{:S(2)}) copy-start(bf16[256,1024]{1,0:T(8,128)(2,1)S(1)} %collective-permute-done.1.refs_1_) | copy-start | bytes 1572868
  50.8 4.2 %copy-start.9 = (bf16[256,1024]{1,0:T(8,128)(2,1)}, bf16[256,1024]{1,0:T(8,128)(2,1)S(1)}, u32[]{:S(2)}) copy-start(bf16[256,1024]{1,0:T(8,128)(2,1)S(1)} %collective-permute-done.2.refs_2_) | copy-start | bytes 1572868
  50.8 4.2 %copy-start.10 = (bf16[256,1024]{1,0:T(8,128)(2,1)}, bf16[256,1024]{1,0:T(8,128)(2,1)S(1)}, u32[]{:S(2)}) copy-start(bf16[256,1024]{1,0:T(8,128)(2,1)S(1)} %collective-permute-done.3.refs_3_) | copy-start | bytes 1572868
  51.2 23.5 %collective-permute-start.5 = (bf16[128,2048]{1,0:T(8,128)(2,1)S(1)}, bf16[128,2048]{1,0:T(8,128)(2,1)S(1)}, u32[]{:S(2)}, u32[]{:S(2)}) collective-permute-start(bf16[128,2048]{1,0:T(8,128)(2,1)S(1)} %layer_norm.1), channel_id=1, source_target_pairs={{0,2},{2,4},{4,6},{6,0},{1,3},{3,5},{5,7},{7,1},{8,10},{10,12},{12... | collective-permute-start | bytes 1572872 | tf_op jit(solution)/shard_map/ppermute | solution.py:455
  52.1 25.6 %collective-permute-start.6 = (bf16[128,2048]{1,0:T(8,128)(2,1)S(1)}, bf16[128,2048]{1,0:T(8,128)(2,1)S(1)}, u32[]{:S(2)}, u32[]{:S(2)}) collective-permute-start(bf16[128,2048]{1,0:T(8,128)(2,1)S(1)} %layer_norm.1), channel_id=1, source_target_pairs={{0,4},{2,6},{4,0},{6,2},{1,5},{3,7},{5,1},{7,3},{8,12},{10,14},{12... | collective-permute-start | bytes 1572872 | tf_op jit(solution)/shard_map/ppermute | solution.py:455
  55.0 22.8 %collective-permute-start.7 = (bf16[128,2048]{1,0:T(8,128)(2,1)S(1)}, bf16[128,2048]{1,0:T(8,128)(2,1)S(1)}, u32[]{:S(2)}, u32[]{:S(2)}) collective-permute-start(bf16[128,2048]{1,0:T(8,128)(2,1)S(1)} %layer_norm.1), channel_id=1, source_target_pairs={{0,6},{2,0},{4,2},{6,4},{1,7},{3,1},{5,3},{7,5},{8,14},{10,8},{12,... | collective-permute-start | bytes 1572872 | tf_op jit(solution)/shard_map/ppermute | solution.py:455
  78.0 4.0 %copy-start.6 = (bf16[512,2048]{1,0:T(8,128)(2,1)}, bf16[512,2048]{1,0:T(8,128)(2,1)S(1)}, u32[]{:S(2)}) copy-start(bf16[512,2048]{1,0:T(8,128)(2,1)S(1)} %constant_dynamic-update-slice_fusion.own_in) | copy-start | bytes 6291460
  78.0 5.3 %collective-permute-start.8 = (bf16[512,2048]{1,0:T(8,128)(2,1)S(1)}, bf16[512,2048]{1,0:T(8,128)(2,1)}, u32[]{:S(2)}, u32[]{:S(2)}) collective-permute-start(bf16[512,2048]{1,0:T(8,128)(2,1)S(1)} %constant_dynamic-update-slice_fusion.own_in), channel_id=1, source_target_pairs={{0,1},{1,0},{2,3},{3,2},{4,5},{5,4},{6,7},{7,6},{8,9},{9,8},{10,11... | collective-permute-start | bytes 6291464 | tf_op jit(solution)/shard_map/ppermute | solution.py:26
  79.4 26.0 %collective-permute-start.10 = (bf16[256,1152]{1,0:T(8,128)(2,1)}, bf16[256,1152]{1,0:T(8,128)(2,1)S(1)}, u32[]{:S(2)}, u32[]{:S(2)}) collective-permute-start(bf16[256,1152]{1,0:T(8,128)(2,1)} %get-tuple-element.63), channel_id=1, source_target_pairs={{0,4},{2,6},{4,0},{6,2},{1,5},{3,7},{5,1},{7,3},{8,12},{10,14},{12... | collective-permute-start | bytes 1769480 | tf_op jit(solution)/shard_map/ppermute | solution.py:458
  80.2 27.9 %collective-permute-start.11 = (bf16[256,1152]{1,0:T(8,128)(2,1)}, bf16[256,1152]{1,0:T(8,128)(2,1)S(1)}, u32[]{:S(2)}, u32[]{:S(2)}) collective-permute-start(bf16[256,1152]{1,0:T(8,128)(2,1)} %get-tuple-element.64), channel_id=1, source_target_pairs={{0,6},{2,0},{4,2},{6,4},{1,7},{3,1},{5,3},{7,5},{8,14},{10,8},{12,... | collective-permute-start | bytes 1769480 | tf_op jit(solution)/shard_map/ppermute | solution.py:458
  82.0 27.0 %collective-permute-start.12 = (bf16[256,1152]{1,0:T(8,128)(2,1)S(1)}, bf16[256,1152]{1,0:T(8,128)(2,1)S(1)}, u32[]{:S(2)}, u32[]{:S(2)}) collective-permute-start(bf16[256,1152]{1,0:T(8,128)(2,1)S(1)} %get-tuple-element.65), channel_id=1, source_target_pairs={{0,2},{2,4},{4,6},{6,0},{1,3},{3,5},{5,7},{7,1},{8,10},{10,12},{12... | collective-permute-start | bytes 1769480 | tf_op jit(solution)/shard_map/ppermute | solution.py:458
  96.7 17.2 %slice-start = ((s8[9437184]{0:T(1024)(128)(4,1)}), s8[4194304]{0:T(1024)(128)(4,1)S(1)}, s32[]{:S(2)}) async-start(s8[9437184]{0:T(1024)(128)(4,1)} %bitcast.14), calls=%async_computation.1 | async-start | bytes 8388608
  96.7 17.2 %slice-start.1 = ((s8[9437184]{0:T(1024)(128)(4,1)}), s8[4194304]{0:T(1024)(128)(4,1)S(1)}, s32[]{:S(2)}) async-start(s8[9437184]{0:T(1024)(128)(4,1)} %bitcast.14), calls=%async_computation.2 | async-start | bytes 8388608
  96.7 17.2 %slice-start.2 = ((s8[9437184]{0:T(1024)(128)(4,1)}), s8[1048576]{0:T(1024)(128)(4,1)S(1)}, s32[]{:S(2)}) async-start(s8[9437184]{0:T(1024)(128)(4,1)} %bitcast.14), calls=%async_computation.3 | async-start | bytes 2097152
  110.7 9.1 %collective-permute-start.13 = (bf16[256,256]{1,0:T(8,128)(2,1)S(1)}, bf16[256,256]{1,0:T(8,128)(2,1)S(1)}, u32[]{:S(2)}, u32[]{:S(2)}) collective-permute-start(bf16[256,256]{1,0:T(8,128)(2,1)S(1)} %get-tuple-element.85), channel_id=1, source_target_pairs={{0,2},{2,4},{4,6},{6,0},{1,3},{3,5},{5,7},{7,1},{8,10},{10,12},{12... | collective-permute-start | bytes 393224 | tf_op jit(solution)/shard_map/ppermute | solution.py:464
  111.0 8.9 %collective-permute-start.14 = (bf16[256,256]{1,0:T(8,128)(2,1)S(1)}, bf16[256,256]{1,0:T(8,128)(2,1)S(1)}, u32[]{:S(2)}, u32[]{:S(2)}) collective-permute-start(bf16[256,256]{1,0:T(8,128)(2,1)S(1)} %get-tuple-element.84), channel_id=1, source_target_pairs={{0,4},{2,6},{4,0},{6,2},{1,5},{3,7},{5,1},{7,3},{8,12},{10,14},{12... | collective-permute-start | bytes 393224 | tf_op jit(solution)/shard_map/ppermute | solution.py:464
  114.0 5.9 %collective-permute-start.15 = (bf16[256,256]{1,0:T(8,128)(2,1)S(1)}, bf16[256,256]{1,0:T(8,128)(2,1)S(1)}, u32[]{:S(2)}, u32[]{:S(2)}) collective-permute-start(bf16[256,256]{1,0:T(8,128)(2,1)S(1)} %get-tuple-element.83), channel_id=1, source_target_pairs={{0,6},{2,0},{4,2},{6,4},{1,7},{3,1},{5,3},{7,5},{8,14},{10,8},{12,... | collective-permute-start | bytes 393224 | tf_op jit(solution)/shard_map/ppermute | solution.py:464
  121.7 3.9 %collective-permute-start.17 = (bf16[128,2048]{1,0:T(8,128)(2,1)S(1)}, bf16[128,2048]{1,0:T(8,128)(2,1)S(1)}, u32[]{:S(2)}, u32[]{:S(2)}) collective-permute-start(bf16[128,2048]{1,0:T(8,128)(2,1)S(1)} %get-tuple-element.76), channel_id=1, source_target_pairs={{0,1},{1,0},{2,3},{3,2},{4,5},{5,4},{6,7},{7,6},{8,9},{9,8},{10,11... | collective-permute-start | bytes 1572872 | tf_op jit(solution)/shard_map/ppermute | solution.py:26
  123.1 4.5 %collective-permute-start.19 = (bf16[128,2048]{1,0:T(8,128)(2,1)S(1)}, bf16[128,2048]{1,0:T(8,128)(2,1)S(1)}, u32[]{:S(2)}, u32[]{:S(2)}) collective-permute-start(bf16[128,2048]{1,0:T(8,128)(2,1)S(1)} %get-tuple-element.75), channel_id=1, source_target_pairs={{0,1},{1,0},{2,3},{3,2},{4,5},{5,4},{6,7},{7,6},{8,9},{9,8},{10,11... | collective-permute-start | bytes 1572872 | tf_op jit(solution)/shard_map/ppermute | solution.py:26
  123.2 6.5 %collective-permute-start.21 = (bf16[128,2048]{1,0:T(8,128)(2,1)S(1)}, bf16[128,2048]{1,0:T(8,128)(2,1)S(1)}, u32[]{:S(2)}, u32[]{:S(2)}) collective-permute-start(bf16[128,2048]{1,0:T(8,128)(2,1)S(1)} %get-tuple-element.77), channel_id=1, source_target_pairs={{0,1},{1,0},{2,3},{3,2},{4,5},{5,4},{6,7},{7,6},{8,9},{9,8},{10,11... | collective-permute-start | bytes 1572872 | tf_op jit(solution)/shard_map/ppermute | solution.py:26
  123.6 6.3 %collective-permute-start.16 = (bf16[128,2048]{1,0:T(8,128)(2,1)S(1)}, bf16[128,2048]{1,0:T(8,128)(2,1)S(1)}, u32[]{:S(2)}, u32[]{:S(2)}) collective-permute-start(bf16[128,2048]{1,0:T(8,128)(2,1)S(1)} %get-tuple-element.74), channel_id=1, source_target_pairs={{0,1},{1,0},{2,3},{3,2},{4,5},{5,4},{6,7},{7,6},{8,9},{9,8},{10,11... | collective-permute-start | bytes 1572872 | tf_op jit(solution)/shard_map/ppermute | solution.py:26
  125.7 14.7 %collective-permute-start.18 = (bf16[128,2048]{1,0:T(8,128)(2,1)S(1)}, bf16[128,2048]{1,0:T(8,128)(2,1)S(1)}, u32[]{:S(2)}, u32[]{:S(2)}) collective-permute-start(bf16[128,2048]{1,0:T(8,128)(2,1)S(1)} %add_convert_fusion.3), channel_id=1, source_target_pairs={{0,4},{2,6},{4,0},{6,2},{1,5},{3,7},{5,1},{7,3},{8,12},{10,14},{12... | collective-permute-start | bytes 1572872 | tf_op jit(solution)/shard_map/ppermute | solution.py:475
  127.7 23.9 %collective-permute-start.20 = (bf16[128,2048]{1,0:T(8,128)(2,1)S(1)}, bf16[128,2048]{1,0:T(8,128)(2,1)S(1)}, u32[]{:S(2)}, u32[]{:S(2)}) collective-permute-start(bf16[128,2048]{1,0:T(8,128)(2,1)S(1)} %add_convert_fusion.2), channel_id=1, source_target_pairs={{0,6},{2,0},{4,2},{6,4},{1,7},{3,1},{5,3},{7,5},{8,14},{10,8},{12,... | collective-permute-start | bytes 1572872 | tf_op jit(solution)/shard_map/ppermute | solution.py:475
  129.9 22.5 %collective-permute-start.22 = (bf16[128,2048]{1,0:T(8,128)(2,1)S(1)}, bf16[128,2048]{1,0:T(8,128)(2,1)S(1)}, u32[]{:S(2)}, u32[]{:S(2)}) collective-permute-start(bf16[128,2048]{1,0:T(8,128)(2,1)S(1)} %add_convert_fusion.1), channel_id=1, source_target_pairs={{0,2},{2,4},{4,6},{6,0},{1,3},{3,5},{5,7},{7,1},{8,10},{10,12},{12... | collective-permute-start | bytes 1572872 | tf_op jit(solution)/shard_map/ppermute | solution.py:475
Sparse Core Ops, SparseCore 0:
  18.7 77.9 all-gather.2

commit v7 on v6

--- a/solution.py
+++ b/solution.py
@@ -87,11 +87,14 @@
                         ),
                     )
                 )
-        for come, _ in copies:
+        ahead = 3
+        for come, _ in copies[:ahead]:
             come.start()
-        for come, leave in copies:
+        for i, (come, leave) in enumerate(copies):
             come.wait()
             leave.start()
+            if i + ahead < len(copies):
+                copies[i + ahead][0].start()
         for _, leave in copies:
             leave.wait()
 
@@ -452,7 +455,8 @@
     normed = layer_norm(stream, norm_gain)
     place_late = after(place_late, normed)
     partial, *sent = attend((0, 2, 1, 3), place_late, cache_range, [query, *queries], *context)
-    inputs = [normed] + [lax.ppermute(normed, "z", ring(k, nz)) for k in range(1, nz)]
+    inputs = {k: lax.ppermute(normed, "z", ring(k, nz)) for k in (2, 1, 3)}
+    inputs = [normed] + [inputs[k] for k in range(1, nz)]
     sent, inputs = lax.optimization_barrier((sent, inputs))
     partials = [partial] + [
         lax.ppermute(made, "z", ring(-k, nz)) for k, made in zip((2, 1, 3), sent)
@@ -461,7 +465,8 @@
     (other_in,) = in_hbm(swap_cores(own_in))
     own_hidden, other_hidden = hidden_units(own_in, other_in, *in_hbm(weights), unit_rows)
     heads = merge(after(place, own_hidden), partials)
-    attention = [heads[0]] + [lax.ppermute(heads[k], "z", ring(k, nz)) for k in range(1, nz)]
+    attention = {k: lax.ppermute(heads[k], "z", ring(k, nz)) for k in (2, 1, 3)}
+    attention = [heads[0]] + [attention[k] for k in range(1, nz)]
 
     other_hidden, own_hidden = after((other_hidden, own_hidden), heads)
     own_part, other_part = down_units(own_hidden, other_hidden, weights, unit_rows)

time: 161 us -> 163 us (1.012)
  transfers between devices with their start and end apart: 24 -> 24, of which waited for: 11 -> 12; matrix products, arithmetic and copies ran while one was open for 0% -> 0% of each run, Pallas kernels for 26% -> 26%
where the time goes in v7:
time: 163 us; the launch traced here: 162 us
  waiting for transfers between devices  67.6 us (41%)
  Pallas kernels  46.3 us (28%)
  starting transfers between devices  30 us (18%)
  between operations  13.7 us (8%)
  other arithmetic  2.6 us (2%)
  local copies, waits for them, and re-layouts  1.78 us (1%)
    ppermute x3, waiting for transfers between devices, on_device(): summed = summed + lax.ppermute(both, 'z', ring(-k, nz)).astype(F32)  22.8 us
    ppermute x3, waiting for transfers between devices, on_device(): queries = [lax.ppermute(query, 'z', ring(k, nz)) for k in (2, 1, 3)]  21.8 us
    pallas_call x1, Pallas kernels, attend(): pl.pallas_call(functools.partial(attend_kernel, steps), grid_spec=pltpu.P...  19.5 us
    all_gather x1, waiting for transfers between devices, on_device(): lax.all_gather(jnp.concatenate([up_weight, down_weight, head_rows], 0), (...  13.3 us
    pallas_call x1, Pallas kernels, hidden_units(): pl.pallas_call(hidden_kernel, grid=(shards // chunk,), in_specs=[whole, w...  8.68 us
    ppermute x3, starting transfers between devices, on_device(): queries = [lax.ppermute(query, 'z', ring(k, nz)) for k in (2, 1, 3)]  7.12 us
    pallas_call x1, Pallas kernels, down_units(): pl.pallas_call(down_kernel, grid=(width // columns,), in_specs=[whole, wh...  5.88 us
    pallas_call x1, Pallas kernels, pick_cache(): pl.pallas_call(body, grid_spec=pltpu.PrefetchScalarGridSpec(num_scalar_pr...  5.86 us
  transfers between devices with their start and end apart: 24, of which 12 were waited for; matrix products, arithmetic and copies ran while one was open for 0% of the time, Pallas kernels for 26%

profile of v7, /device:TPU:1, one launch (start us, length us, event | category | flops | bytes accessed | tf_op | source)
XLA Modules:
  0.0 162.0 jit_solution(7830028734597913231)
XLA Ops:
  6.5 4.5 %collective-permute-start.9 = (bf16[16,2048]{1,0:T(8,128)(2,1)}, bf16[16,2048]{1,0:T(8,128)(2,1)S(1)}, u32[]{:S(2)}, u32[]{:S(2)}) collective-permute-start(bf16[16,2048]{1,0:T(8,128)(2,1)} %param.15), channel_id=1, source_target_pairs={{0,0},{1,8},{2,16},{3,24},{4,32},{5,40},{6,48},{7,56},{8,64},{9,72... | collective-permute-start | bytes 196616 | tf_op jit(solution)/shard_map/ppermute | solution.py:441
  11.1 1.4 copy-done.1
  12.5 0.7 pick_new.1
  13.3 5.9 %pick_cache.1 = bf16[2,1024,1024]{2,1,0:T(8,128)(2,1)} custom-call(s32[3]{0:T(128)S(1)} %pad_add_fusion.place_ref.place, bf16[1024,2048]{1,0:T(8,128)(2,1)} %refs_4_.1, bf16[1024,2048]{1,0:T(8,128)(2,1)} %refs_6_.1), custom_call_target="tpu_custom_call" | custom-call | tf_op jit(solution)/shard_map/pick_cache/pallas_call | solution.py:102
  19.2 0.9 pad_maximum_fusion
  20.1 0.1 collective-permute-start
  20.2 2.3 %collective-permute-done.refs_9_.refs_11_ = bf16[128,3072]{1,0:T(8,128)(2,1)S(1)} collective-permute-done((bf16[128,3072]{1,0:T(8,128)(2,1)S(1)}, bf16[128,3072]{1,0:T(8,128)(2,1)S(1)}, u32[]{:S(2)}, u32[]{:S(2)}) %collective-permute-start) | collective-permute-done | bytes 786464 | tf_op jit(solution)/shard_map/ppermute | solution.py:26
  22.5 0.2 collective-permute-start.4
  22.8 4.4 %collective-permute-start.1 = (bf16[256,1024]{1,0:T(8,128)(2,1)S(1)}, bf16[256,1024]{1,0:T(8,128)(2,1)S(1)}, u32[]{:S(2)}, u32[]{:S(2)}) collective-permute-start(bf16[256,1024]{1,0:T(8,128)(2,1)S(1)} %pad_maximum_fusion.1.refs_0_), channel_id=1, source_target_pairs={{0,4},{2,6},{4,0},{6,2},{1,5},{3,7},{5,1},{7,3},{8,12},{10,14},{12... | collective-permute-start | bytes 1572872 | tf_op jit(solution)/shard_map/ppermute | solution.py:451
  27.2 1.3 collective-permute-start.2
  28.5 1.4 collective-permute-start.3
  30.0 9.3 %collective-permute-done.1.refs_1_ = bf16[256,1024]{1,0:T(8,128)(2,1)S(1)} collective-permute-done((bf16[256,1024]{1,0:T(8,128)(2,1)S(1)}, bf16[256,1024]{1,0:T(8,128)(2,1)S(1)}, u32[]{:S(2)}, u32[]{:S(2)}) %collective-permute-start.1) | collective-permute-done | bytes 524320 | tf_op jit(solution)/shard_map/ppermute | solution.py:451
  39.2 11.6 %collective-permute-done.2.refs_2_ = bf16[256,1024]{1,0:T(8,128)(2,1)S(1)} collective-permute-done((bf16[256,1024]{1,0:T(8,128)(2,1)S(1)}, bf16[256,1024]{1,0:T(8,128)(2,1)S(1)}, u32[]{:S(2)}, u32[]{:S(2)}) %collective-permute-start.2) | collective-permute-done | bytes 524320 | tf_op jit(solution)/shard_map/ppermute | solution.py:451
  50.8 0.9 collective-permute-done.3.refs_3_
  51.8 0.4 layer_norm.1
  52.1 0.7 collective-permute-start.5
  52.8 3.4 %collective-permute-start.6 = (bf16[128,2048]{1,0:T(8,128)(2,1)S(1)}, bf16[128,2048]{1,0:T(8,128)(2,1)S(1)}, u32[]{:S(2)}, u32[]{:S(2)}) collective-permute-start(bf16[128,2048]{1,0:T(8,128)(2,1)S(1)} %layer_norm.1), channel_id=1, source_target_pairs={{0,4},{2,6},{4,0},{6,2},{1,5},{3,7},{5,1},{7,3},{8,12},{10,14},{12... | collective-permute-start | bytes 1572872 | tf_op jit(solution)/shard_map/ppermute | solution.py:458
  56.2 0.2 collective-permute-start.7
  56.4 19.5 %attend.1 = (bf16[256,1152]{1,0:T(8,128)(2,1)S(1)}, bf16[256,1152]{1,0:T(8,128)(2,1)}, bf16[256,1152]{1,0:T(8,128)(2,1)}, bf16[256,1152]{1,0:T(8,128)(2,1)S(1)}) custom-call(s32[3]{0:T(128)S(1)} %pad_add_fusion.place_ref.place, s32[16,2]{1,0:T(8,128)S(1)} %copy.10.ranges, bf16[256,1024]{1,0:T(8,128)(2,1)} %copy-done.3, bf16[256,1024]{1,0:T(8,128)(2,1)} %copy-done.8, ...), custom_call_target="tpu_custom_call" | custom-call | flops 9663676416 | bytes 16777216 | tf_op jit(solution)/shard_map/attend/pallas_call | solution.py:216
  76.0 3.0 %collective-permute-done.6 = bf16[128,2048]{1,0:T(8,128)(2,1)S(1)} collective-permute-done((bf16[128,2048]{1,0:T(8,128)(2,1)S(1)}, bf16[128,2048]{1,0:T(8,128)(2,1)S(1)}, u32[]{:S(2)}, u32[]{:S(2)}) %collective-permute-start.6) | collective-permute-done | bytes 524320 | tf_op jit(solution)/shard_map/ppermute | solution.py:458
  79.2 1.4 collective-permute-start.8
  80.6 1.4 collective-permute-start.10
  82.0 1.7 %collective-permute-start.11 = (bf16[256,1152]{1,0:T(8,128)(2,1)}, bf16[256,1152]{1,0:T(8,128)(2,1)S(1)}, u32[]{:S(2)}, u32[]{:S(2)}) collective-permute-start(bf16[256,1152]{1,0:T(8,128)(2,1)} %get-tuple-element.64), channel_id=1, source_target_pairs={{0,6},{2,0},{4,2},{6,4},{1,7},{3,1},{5,3},{7,5},{8,14},{10,8},{12,... | collective-permute-start | bytes 1769480 | tf_op jit(solution)/shard_map/ppermute | solution.py:462
  83.8 0.8 collective-permute-done.8.other_in
  84.5 13.3 %all-gather.3.cloned.1.call-done = bf16[2304,2048]{1,0:T(8,128)(2,1)} async-done(((bf16[144,2048]{1,0:T(8,128)(2,1)}), bf16[2304,2048]{1,0:T(8,128)(2,1)}) %all-gather.3.cloned.1.call-update) | async-done | bytes 9437200 | tf_op jit(solution)/shard_map/all_gather | solution.py:447
  97.8 8.7 %hidden_units.1 = (bf16[512,1024]{1,0:T(8,128)(2,1)S(1)}, bf16[512,1024]{1,0:T(8,128)(2,1)S(1)}) custom-call(bf16[512,2048]{1,0:T(8,128)(2,1)} %copy-done.6, bf16[512,2048]{1,0:T(8,128)(2,1)} %collective-permute-done.8.other_in, bf16[16,144,2048]{2,1,0:T(8,128)(2,1)} %bitcast.13), custom_call_target="tpu_custom_call" | custom-call | flops 4294967296 | bytes 8388608 | tf_op jit(solution)/shard_map/hidden_units/pallas_call | solution.py:311
  106.5 2.8 %collective-permute-done.11.c = bf16[256,1152]{1,0:T(8,128)(2,1)S(1)} collective-permute-done((bf16[256,1152]{1,0:T(8,128)(2,1)}, bf16[256,1152]{1,0:T(8,128)(2,1)S(1)}, u32[]{:S(2)}, u32[]{:S(2)}) %collective-permute-start.11) | collective-permute-done | bytes 589856 | tf_op jit(solution)/shard_map/ppermute | solution.py:462
  109.3 0.9 collective-permute-done.12.d
  110.2 1.7 %merge.1 = bf16[4,256,256]{2,1,0:T(8,128)(2,1)S(1)} custom-call(s32[3]{0:T(128)S(1)} %pad_add_fusion.place_ref.place, bf16[256,1152]{1,0:T(8,128)(2,1)S(1)} %get-tuple-element.62.a, bf16[256,1152]{1,0:T(8,128)(2,1)S(1)} %collective-permute-done.10.b, bf16[256,1152]{1,0:T(8,128)(2,1)S(1)} %collective-permute-done.11.c, ...), custom_call_target="tpu_custom_call" | custom-call | tf_op jit(solution)/shard_map/merge/pallas_call | solution.py:282
  112.0 0.8 collective-permute-start.13
  112.8 2.3 %collective-permute-start.14 = (bf16[256,256]{1,0:T(8,128)(2,1)S(1)}, bf16[256,256]{1,0:T(8,128)(2,1)S(1)}, u32[]{:S(2)}, u32[]{:S(2)}) collective-permute-start(bf16[256,256]{1,0:T(8,128)(2,1)S(1)} %get-tuple-element.84), channel_id=1, source_target_pairs={{0,4},{2,6},{4,0},{6,2},{1,5},{3,7},{5,1},{7,3},{8,12},{10,14},{12... | collective-permute-start | bytes 393224 | tf_op jit(solution)/shard_map/ppermute | solution.py:468
  115.1 0.4 collective-permute-start.15
  115.5 5.9 %down_units.1 = (f32[512,2048]{1,0:T(8,128)S(1)}, f32[512,2048]{1,0:T(8,128)S(1)}) custom-call(bf16[512,1024]{1,0:T(8,128)(2,1)S(1)} %get-tuple-element.66.own_hidden, bf16[512,1024]{1,0:T(8,128)(2,1)S(1)} %get-tuple-element.67.other_hidden, bf16[16,144,2048]{2,1,0:T(8,128)(2,1)S(1)} %bitcast.16), custom_call_target="tpu_custom_call" | custom-call | flops 4294967296 | bytes 14680064 | tf_op jit(solution)/shard_map/down_units/pallas_call | solution.py:344
  121.4 1.7 %finish.2 = (bf16[128,2048]{1,0:T(8,128)(2,1)S(1)}, bf16[128,2048]{1,0:T(8,128)(2,1)S(1)}, bf16[128,2048]{1,0:T(8,128)(2,1)S(1)}, bf16[128,2048]{1,0:T(8,128)(2,1)S(1)}) custom-call(f32[512,2048]{1,0:T(8,128)S(1)} %get-tuple-element.69.partial, bf16[256,256]{1,0:T(8,128)(2,1)S(1)} %get-tuple-element.70.a0, bf16[256,256]{1,0:T(8,128)(2,1)S(1)} %collective-permute-done.13.a1, ...), custom_call_target="tpu_custom_call" | custom-call | flops 536870912 | bytes 9437184 | tf_op jit(solution)/shard_map/finish/pallas_call | solution.py:380
  123.2 1.4 collective-permute-start.17
  124.6 0.1 collective-permute-start.19
  124.7 0.4 collective-permute-start.21
  125.1 0.1 collective-permute-start.16
  125.2 1.9 %finish.3 = (f32[128,2048]{1,0:T(8,128)S(1)}, f32[128,2048]{1,0:T(8,128)S(1)}, f32[128,2048]{1,0:T(8,128)S(1)}, f32[128,2048]{1,0:T(8,128)S(1)}) custom-call(f32[512,2048]{1,0:T(8,128)S(1)} %get-tuple-element.78.partial, bf16[256,256]{1,0:T(8,128)(2,1)S(1)} %get-tuple-element.70.a0, bf16[256,256]{1,0:T(8,128)(2,1)S(1)} %collective-permute-done.13.a1, ...), custom_call_target="tpu_custom_call" | custom-call | flops 536870912 | bytes 9437184 | tf_op jit(solution)/shard_map/finish/pallas_call | solution.py:380
  127.1 0.1 add_convert_fusion.3
  127.2 1.6 collective-permute-start.18
  128.8 0.1 add_convert_fusion.2
  128.9 2.0 %collective-permute-start.20 = (bf16[128,2048]{1,0:T(8,128)(2,1)S(1)}, bf16[128,2048]{1,0:T(8,128)(2,1)S(1)}, u32[]{:S(2)}, u32[]{:S(2)}) collective-permute-start(bf16[128,2048]{1,0:T(8,128)(2,1)S(1)} %add_convert_fusion.2), channel_id=1, source_target_pairs={{0,6},{2,0},{4,2},{6,4},{1,7},{3,1},{5,3},{7,5},{8,14},{10,8},{12,... | collective-permute-start | bytes 1572872 | tf_op jit(solution)/shard_map/ppermute | solution.py:480
  130.9 0.1 add_convert_fusion.1
  131.1 10.8 %collective-permute-done.18 = bf16[128,2048]{1,0:T(8,128)(2,1)S(1)} collective-permute-done((bf16[128,2048]{1,0:T(8,128)(2,1)S(1)}, bf16[128,2048]{1,0:T(8,128)(2,1)S(1)}, u32[]{:S(2)}, u32[]{:S(2)}) %collective-permute-start.18) | collective-permute-done | bytes 524320 | tf_op jit(solution)/shard_map/ppermute | solution.py:480
  141.9 11.0 %collective-permute-done.20 = bf16[128,2048]{1,0:T(8,128)(2,1)S(1)} collective-permute-done((bf16[128,2048]{1,0:T(8,128)(2,1)S(1)}, bf16[128,2048]{1,0:T(8,128)(2,1)S(1)}, u32[]{:S(2)}, u32[]{:S(2)}) %collective-permute-start.20) | collective-permute-done | bytes 524320 | tf_op jit(solution)/shard_map/ppermute | solution.py:480
  152.8 1.0 collective-permute-done.22
  153.9 1.3 add_convert_fusion
  (53 shorter events, 0.6 us)
Async XLA Ops:
  6.5 91.2 %all-gather.3.cloned.1.call-start = ((), (), s32[]{:S(2)}) async-start(), calls=%async_computation | async-start | bytes 10027008 | tf_op jit(solution)/shard_map/all_gather | solution.py:447
  6.5 12.6 %collective-permute-start.9 = (bf16[16,2048]{1,0:T(8,128)(2,1)}, bf16[16,2048]{1,0:T(8,128)(2,1)S(1)}, u32[]{:S(2)}, u32[]{:S(2)}) collective-permute-start(bf16[16,2048]{1,0:T(8,128)(2,1)} %param.15), channel_id=1, source_target_pairs={{0,0},{1,8},{2,16},{3,24},{4,32},{5,40},{6,48},{7,56},{8,64},{9,72... | collective-permute-start | bytes 196616 | tf_op jit(solution)/shard_map/ppermute | solution.py:441
  11.1 1.4 copy-start.1
  13.2 5.9 %copy-start.4 = (bf16[64,2048]{1,0:T(8,128)(2,1)S(1)}, bf16[64,2048]{1,0:T(8,128)(2,1)}, u32[]{:S(2)}) copy-start(bf16[64,2048]{1,0:T(8,128)(2,1)} %param.17) | copy-start | bytes 786436
  13.2 5.9 %copy-start.5 = (bf16[64,2048]{1,0:T(8,128)(2,1)S(1)}, bf16[64,2048]{1,0:T(8,128)(2,1)}, u32[]{:S(2)}) copy-start(bf16[64,2048]{1,0:T(8,128)(2,1)} %param.16) | copy-start | bytes 786436
  19.1 10.8 %copy-start.7 = (s32[16,2]{0,1:T(2,128)S(1)}, s32[16,2]{0,1:T(2,128)}, u32[]{:S(2)}) copy-start(s32[16,2]{0,1:T(2,128)} %param.13) | copy-start | bytes 388
  19.1 32.6 %copy-start = (bf16[128,2048]{1,0:T(8,128)(2,1)S(1)}, bf16[128,2048]{1,0:T(8,128)(2,1)}, u32[]{:S(2)}) copy-start(bf16[128,2048]{1,0:T(8,128)(2,1)} %stream.1) | copy-start | bytes 1572868
  19.1 32.6 %copy-start.2 = (f32[2048]{0:T(1024)S(1)}, f32[2048]{0:T(1024)}, u32[]{:S(2)}) copy-start(f32[2048]{0:T(1024)} %param.14) | copy-start | bytes 24580
  20.1 2.4 %collective-permute-start = (bf16[128,3072]{1,0:T(8,128)(2,1)S(1)}, bf16[128,3072]{1,0:T(8,128)(2,1)S(1)}, u32[]{:S(2)}, u32[]{:S(2)}) collective-permute-start(bf16[128,3072]{1,0:T(8,128)(2,1)S(1)} %get-tuple-element.45), channel_id=1, source_target_pairs={{0,1},{1,0},{2,3},{3,2},{4,5},{5,4},{6,7},{7,6},{8,9},{9,8},{10,11... | collective-permute-start | bytes 2359304 | tf_op jit(solution)/shard_map/ppermute | solution.py:26
  22.5 33.9 %copy-start.3 = (bf16[256,1024]{1,0:T(8,128)(2,1)}, bf16[256,1024]{1,0:T(8,128)(2,1)S(1)}, u32[]{:S(2)}) copy-start(bf16[256,1024]{1,0:T(8,128)(2,1)S(1)} %pad_maximum_fusion.1.refs_0_) | copy-start | bytes 1572868
  22.5 29.2 %collective-permute-start.4 = (bf16[2,1024,1024]{2,1,0:T(8,128)(2,1)}, bf16[2,1024,1024]{2,1,0:T(8,128)(2,1)}, u32[]{:S(2)}, u32[]{:S(2)}) collective-permute-start(bf16[2,1024,1024]{2,1,0:T(8,128)(2,1)} %pick_cache.1), channel_id=1, source_target_pairs={{0,1},{1,0},{2,3},{3,2},{4,5},{5,4},{6,7},{7,6},{8,9},{9,8},{10,11... | collective-permute-start | bytes 12582920 | tf_op jit(solution)/shard_map/ppermute | solution.py:26
  22.8 16.5 %collective-permute-start.1 = (bf16[256,1024]{1,0:T(8,128)(2,1)S(1)}, bf16[256,1024]{1,0:T(8,128)(2,1)S(1)}, u32[]{:S(2)}, u32[]{:S(2)}) collective-permute-start(bf16[256,1024]{1,0:T(8,128)(2,1)S(1)} %pad_maximum_fusion.1.refs_0_), channel_id=1, source_target_pairs={{0,4},{2,6},{4,0},{6,2},{1,5},{3,7},{5,1},{7,3},{8,12},{10,14},{12... | collective-permute-start | bytes 1572872 | tf_op jit(solution)/shard_map/ppermute | solution.py:451
  27.2 23.6 %collective-permute-start.2 = (bf16[256,1024]{1,0:T(8,128)(2,1)S(1)}, bf16[256,1024]{1,0:T(8,128)(2,1)S(1)}, u32[]{:S(2)}, u32[]{:S(2)}) collective-permute-start(bf16[256,1024]{1,0:T(8,128)(2,1)S(1)} %pad_maximum_fusion.1.refs_0_), channel_id=1, source_target_pairs={{0,2},{2,4},{4,6},{6,0},{1,3},{3,5},{5,7},{7,1},{8,10},{10,12},{12... | collective-permute-start | bytes 1572872 | tf_op jit(solution)/shard_map/ppermute | solution.py:451
  28.5 23.2 %collective-permute-start.3 = (bf16[256,1024]{1,0:T(8,128)(2,1)S(1)}, bf16[256,1024]{1,0:T(8,128)(2,1)S(1)}, u32[]{:S(2)}, u32[]{:S(2)}) collective-permute-start(bf16[256,1024]{1,0:T(8,128)(2,1)S(1)} %pad_maximum_fusion.1.refs_0_), channel_id=1, source_target_pairs={{0,6},{2,0},{4,2},{6,4},{1,7},{3,1},{5,3},{7,5},{8,14},{10,8},{12,... | collective-permute-start | bytes 1572872 | tf_op jit(solution)/shard_map/ppermute | solution.py:451
  39.2 17.2 %copy-start.8 = (bf16[256,1024]{1,0:T(8,128)(2,1)}, bf16[256,1024]{1,0:T(8,128)(2,1)S(1)}, u32[]{:S(2)}) copy-start(bf16[256,1024]{1,0:T(8,128)(2,1)S(1)} %collective-permute-done.1.refs_1_) | copy-start | bytes 1572868
  50.8 5.4 %copy-start.9 = (bf16[256,1024]{1,0:T(8,128)(2,1)}, bf16[256,1024]{1,0:T(8,128)(2,1)S(1)}, u32[]{:S(2)}) copy-start(bf16[256,1024]{1,0:T(8,128)(2,1)S(1)} %collective-permute-done.2.refs_2_) | copy-start | bytes 1572868
  51.7 4.5 %copy-start.10 = (bf16[256,1024]{1,0:T(8,128)(2,1)}, bf16[256,1024]{1,0:T(8,128)(2,1)S(1)}, u32[]{:S(2)}) copy-start(bf16[256,1024]{1,0:T(8,128)(2,1)S(1)} %collective-permute-done.3.refs_3_) | copy-start | bytes 1572868
  52.1 23.8 %collective-permute-start.5 = (bf16[128,2048]{1,0:T(8,128)(2,1)S(1)}, bf16[128,2048]{1,0:T(8,128)(2,1)S(1)}, u32[]{:S(2)}, u32[]{:S(2)}) collective-permute-start(bf16[128,2048]{1,0:T(8,128)(2,1)S(1)} %layer_norm.1), channel_id=1, source_target_pairs={{0,2},{2,4},{4,6},{6,0},{1,3},{3,5},{5,7},{7,1},{8,10},{10,12},{12... | collective-permute-start | bytes 1572872 | tf_op jit(solution)/shard_map/ppermute | solution.py:458
  52.8 26.2 %collective-permute-start.6 = (bf16[128,2048]{1,0:T(8,128)(2,1)S(1)}, bf16[128,2048]{1,0:T(8,128)(2,1)S(1)}, u32[]{:S(2)}, u32[]{:S(2)}) collective-permute-start(bf16[128,2048]{1,0:T(8,128)(2,1)S(1)} %layer_norm.1), channel_id=1, source_target_pairs={{0,4},{2,6},{4,0},{6,2},{1,5},{3,7},{5,1},{7,3},{8,12},{10,14},{12... | collective-permute-start | bytes 1572872 | tf_op jit(solution)/shard_map/ppermute | solution.py:458
  56.2 22.8 %collective-permute-start.7 = (bf16[128,2048]{1,0:T(8,128)(2,1)S(1)}, bf16[128,2048]{1,0:T(8,128)(2,1)S(1)}, u32[]{:S(2)}, u32[]{:S(2)}) collective-permute-start(bf16[128,2048]{1,0:T(8,128)(2,1)S(1)} %layer_norm.1), channel_id=1, source_target_pairs={{0,6},{2,0},{4,2},{6,4},{1,7},{3,1},{5,3},{7,5},{8,14},{10,8},{12,... | collective-permute-start | bytes 1572872 | tf_op jit(solution)/shard_map/ppermute | solution.py:458
  79.2 4.6 %copy-start.6 = (bf16[512,2048]{1,0:T(8,128)(2,1)}, bf16[512,2048]{1,0:T(8,128)(2,1)S(1)}, u32[]{:S(2)}) copy-start(bf16[512,2048]{1,0:T(8,128)(2,1)S(1)} %constant_dynamic-update-slice_fusion.own_in) | copy-start | bytes 6291460
  79.2 5.3 %collective-permute-start.8 = (bf16[512,2048]{1,0:T(8,128)(2,1)S(1)}, bf16[512,2048]{1,0:T(8,128)(2,1)}, u32[]{:S(2)}, u32[]{:S(2)}) collective-permute-start(bf16[512,2048]{1,0:T(8,128)(2,1)S(1)} %constant_dynamic-update-slice_fusion.own_in), channel_id=1, source_target_pairs={{0,1},{1,0},{2,3},{3,2},{4,5},{5,4},{6,7},{7,6},{8,9},{9,8},{10,11... | collective-permute-start | bytes 6291464 | tf_op jit(solution)/shard_map/ppermute | solution.py:26
  80.6 25.9 %collective-permute-start.10 = (bf16[256,1152]{1,0:T(8,128)(2,1)}, bf16[256,1152]{1,0:T(8,128)(2,1)S(1)}, u32[]{:S(2)}, u32[]{:S(2)}) collective-permute-start(bf16[256,1152]{1,0:T(8,128)(2,1)} %get-tuple-element.63), channel_id=1, source_target_pairs={{0,4},{2,6},{4,0},{6,2},{1,5},{3,7},{5,1},{7,3},{8,12},{10,14},{12... | collective-permute-start | bytes 1769480 | tf_op jit(solution)/shard_map/ppermute | solution.py:462
  82.0 27.2 %collective-permute-start.11 = (bf16[256,1152]{1,0:T(8,128)(2,1)}, bf16[256,1152]{1,0:T(8,128)(2,1)S(1)}, u32[]{:S(2)}, u32[]{:S(2)}) collective-permute-start(bf16[256,1152]{1,0:T(8,128)(2,1)} %get-tuple-element.64), channel_id=1, source_target_pairs={{0,6},{2,0},{4,2},{6,4},{1,7},{3,1},{5,3},{7,5},{8,14},{10,8},{12,... | collective-permute-start | bytes 1769480 | tf_op jit(solution)/shard_map/ppermute | solution.py:462
  83.8 26.5 %collective-permute-start.12 = (bf16[256,1152]{1,0:T(8,128)(2,1)S(1)}, bf16[256,1152]{1,0:T(8,128)(2,1)S(1)}, u32[]{:S(2)}, u32[]{:S(2)}) collective-permute-start(bf16[256,1152]{1,0:T(8,128)(2,1)S(1)} %get-tuple-element.65), channel_id=1, source_target_pairs={{0,2},{2,4},{4,6},{6,0},{1,3},{3,5},{5,7},{7,1},{8,10},{10,12},{12... | collective-permute-start | bytes 1769480 | tf_op jit(solution)/shard_map/ppermute | solution.py:462
  97.8 17.7 %slice-start = ((s8[9437184]{0:T(1024)(128)(4,1)}), s8[4194304]{0:T(1024)(128)(4,1)S(1)}, s32[]{:S(2)}) async-start(s8[9437184]{0:T(1024)(128)(4,1)} %bitcast.14), calls=%async_computation.1 | async-start | bytes 8388608
  97.8 17.7 %slice-start.1 = ((s8[9437184]{0:T(1024)(128)(4,1)}), s8[4194304]{0:T(1024)(128)(4,1)S(1)}, s32[]{:S(2)}) async-start(s8[9437184]{0:T(1024)(128)(4,1)} %bitcast.14), calls=%async_computation.2 | async-start | bytes 8388608
  97.8 17.7 %slice-start.2 = ((s8[9437184]{0:T(1024)(128)(4,1)}), s8[1048576]{0:T(1024)(128)(4,1)S(1)}, s32[]{:S(2)}) async-start(s8[9437184]{0:T(1024)(128)(4,1)} %bitcast.14), calls=%async_computation.3 | async-start | bytes 2097152
  112.0 9.5 %collective-permute-start.13 = (bf16[256,256]{1,0:T(8,128)(2,1)S(1)}, bf16[256,256]{1,0:T(8,128)(2,1)S(1)}, u32[]{:S(2)}, u32[]{:S(2)}) collective-permute-start(bf16[256,256]{1,0:T(8,128)(2,1)S(1)} %get-tuple-element.85), channel_id=1, source_target_pairs={{0,2},{2,4},{4,6},{6,0},{1,3},{3,5},{5,7},{7,1},{8,10},{10,12},{12... | collective-permute-start | bytes 393224 | tf_op jit(solution)/shard_map/ppermute | solution.py:468
  112.8 8.6 %collective-permute-start.14 = (bf16[256,256]{1,0:T(8,128)(2,1)S(1)}, bf16[256,256]{1,0:T(8,128)(2,1)S(1)}, u32[]{:S(2)}, u32[]{:S(2)}) collective-permute-start(bf16[256,256]{1,0:T(8,128)(2,1)S(1)} %get-tuple-element.84), channel_id=1, source_target_pairs={{0,4},{2,6},{4,0},{6,2},{1,5},{3,7},{5,1},{7,3},{8,12},{10,14},{12... | collective-permute-start | bytes 393224 | tf_op jit(solution)/shard_map/ppermute | solution.py:468
  115.1 6.4 %collective-permute-start.15 = (bf16[256,256]{1,0:T(8,128)(2,1)S(1)}, bf16[256,256]{1,0:T(8,128)(2,1)S(1)}, u32[]{:S(2)}, u32[]{:S(2)}) collective-permute-start(bf16[256,256]{1,0:T(8,128)(2,1)S(1)} %get-tuple-element.83), channel_id=1, source_target_pairs={{0,6},{2,0},{4,2},{6,4},{1,7},{3,1},{5,3},{7,5},{8,14},{10,8},{12,... | collective-permute-start | bytes 393224 | tf_op jit(solution)/shard_map/ppermute | solution.py:468
  123.2 3.9 %collective-permute-start.17 = (bf16[128,2048]{1,0:T(8,128)(2,1)S(1)}, bf16[128,2048]{1,0:T(8,128)(2,1)S(1)}, u32[]{:S(2)}, u32[]{:S(2)}) collective-permute-start(bf16[128,2048]{1,0:T(8,128)(2,1)S(1)} %get-tuple-element.76), channel_id=1, source_target_pairs={{0,1},{1,0},{2,3},{3,2},{4,5},{5,4},{6,7},{7,6},{8,9},{9,8},{10,11... | collective-permute-start | bytes 1572872 | tf_op jit(solution)/shard_map/ppermute | solution.py:26
  124.6 4.2 %collective-permute-start.19 = (bf16[128,2048]{1,0:T(8,128)(2,1)S(1)}, bf16[128,2048]{1,0:T(8,128)(2,1)S(1)}, u32[]{:S(2)}, u32[]{:S(2)}) collective-permute-start(bf16[128,2048]{1,0:T(8,128)(2,1)S(1)} %get-tuple-element.75), channel_id=1, source_target_pairs={{0,1},{1,0},{2,3},{3,2},{4,5},{5,4},{6,7},{7,6},{8,9},{9,8},{10,11... | collective-permute-start | bytes 1572872 | tf_op jit(solution)/shard_map/ppermute | solution.py:26
  124.7 6.2 %collective-permute-start.21 = (bf16[128,2048]{1,0:T(8,128)(2,1)S(1)}, bf16[128,2048]{1,0:T(8,128)(2,1)S(1)}, u32[]{:S(2)}, u32[]{:S(2)}) collective-permute-start(bf16[128,2048]{1,0:T(8,128)(2,1)S(1)} %get-tuple-element.77), channel_id=1, source_target_pairs={{0,1},{1,0},{2,3},{3,2},{4,5},{5,4},{6,7},{7,6},{8,9},{9,8},{10,11... | collective-permute-start | bytes 1572872 | tf_op jit(solution)/shard_map/ppermute | solution.py:26
  125.1 6.0 %collective-permute-start.16 = (bf16[128,2048]{1,0:T(8,128)(2,1)S(1)}, bf16[128,2048]{1,0:T(8,128)(2,1)S(1)}, u32[]{:S(2)}, u32[]{:S(2)}) collective-permute-start(bf16[128,2048]{1,0:T(8,128)(2,1)S(1)} %get-tuple-element.74), channel_id=1, source_target_pairs={{0,1},{1,0},{2,3},{3,2},{4,5},{5,4},{6,7},{7,6},{8,9},{9,8},{10,11... | collective-permute-start | bytes 1572872 | tf_op jit(solution)/shard_map/ppermute | solution.py:26
  127.2 14.7 %collective-permute-start.18 = (bf16[128,2048]{1,0:T(8,128)(2,1)S(1)}, bf16[128,2048]{1,0:T(8,128)(2,1)S(1)}, u32[]{:S(2)}, u32[]{:S(2)}) collective-permute-start(bf16[128,2048]{1,0:T(8,128)(2,1)S(1)} %add_convert_fusion.3), channel_id=1, source_target_pairs={{0,4},{2,6},{4,0},{6,2},{1,5},{3,7},{5,1},{7,3},{8,12},{10,14},{12... | collective-permute-start | bytes 1572872 | tf_op jit(solution)/shard_map/ppermute | solution.py:480
  128.9 23.9 %collective-permute-start.20 = (bf16[128,2048]{1,0:T(8,128)(2,1)S(1)}, bf16[128,2048]{1,0:T(8,128)(2,1)S(1)}, u32[]{:S(2)}, u32[]{:S(2)}) collective-permute-start(bf16[128,2048]{1,0:T(8,128)(2,1)S(1)} %add_convert_fusion.2), channel_id=1, source_target_pairs={{0,6},{2,0},{4,2},{6,4},{1,7},{3,1},{5,3},{7,5},{8,14},{10,8},{12,... | collective-permute-start | bytes 1572872 | tf_op jit(solution)/shard_map/ppermute | solution.py:480
  131.0 22.9 %collective-permute-start.22 = (bf16[128,2048]{1,0:T(8,128)(2,1)S(1)}, bf16[128,2048]{1,0:T(8,128)(2,1)S(1)}, u32[]{:S(2)}, u32[]{:S(2)}) collective-permute-start(bf16[128,2048]{1,0:T(8,128)(2,1)S(1)} %add_convert_fusion.1), channel_id=1, source_target_pairs={{0,2},{2,4},{4,6},{6,0},{1,3},{3,5},{5,7},{7,1},{8,10},{10,12},{12... | collective-permute-start | bytes 1572872 | tf_op jit(solution)/shard_map/ppermute | solution.py:480
Sparse Core Ops, SparseCore 0:
  20.2 77.5 all-gather.2

commit v8 on v6

--- a/solution.py
+++ b/solution.py
@@ -444,7 +444,7 @@
     weights = lax.all_gather(
         jnp.concatenate([up_weight, down_weight, head_rows], 0), ("y", "x"), axis=0
     )
-    (query,) = in_hbm(jnp.concatenate([own_query, new_in[:, :half]], 0))
+    query = jnp.concatenate([own_query, new_in[:, :half]], 0)
     queries = [lax.ppermute(query, "z", ring(k, nz)) for k in (2, 1, 3)]
     cache_in = swap_cores(after(cache_out, query))
     context = (*cached, *in_hbm(projections), cache_in, new_in)

time: 161 us -> 161 us (level)
  no operation moved by 1% of the time
where the time goes in v8:
time: 161 us
  waiting for transfers between devices  66.3 us (41%)
  Pallas kernels  44.6 us (28%)
  starting transfers between devices  30.4 us (19%)
  between operations  13.7 us (9%)
  local copies, waits for them, and re-layouts  2.96 us (2%)
  other arithmetic  2.59 us (2%)
    ppermute x3, waiting for transfers between devices, on_device(): summed = summed + lax.ppermute(both, 'z', ring(-k, nz)).astype(F32)  22.4 us
    ppermute x3, waiting for transfers between devices, on_device(): queries = [lax.ppermute(query, 'z', ring(k, nz)) for k in (2, 1, 3)]  21 us
    pallas_call x1, Pallas kernels, attend(): pl.pallas_call(functools.partial(attend_kernel, steps), grid_spec=pltpu.P...  19.3 us
    all_gather x1, waiting for transfers between devices, on_device(): lax.all_gather(jnp.concatenate([up_weight, down_weight, head_rows], 0), (...  13.3 us
    pallas_call x1, Pallas kernels, hidden_units(): pl.pallas_call(hidden_kernel, grid=(shards // chunk,), in_specs=[whole, w...  8.68 us
    ppermute x3, starting transfers between devices, on_device(): queries = [lax.ppermute(query, 'z', ring(k, nz)) for k in (2, 1, 3)]  8.59 us
    pallas_call x1, Pallas kernels, down_units(): pl.pallas_call(down_kernel, grid=(width // columns,), in_specs=[whole, wh...  5.88 us
    ppermute x1, starting transfers between devices, on_device(): lax.ppermute(out_weight, ('y', 'x', 'z', 'c'), head_owners(ny, nx, nz))  4.5 us
  transfers between devices with their start and end apart: 24, of which 11 were waited for; matrix products, arithmetic and copies ran while one was open for 0% of the time, Pallas kernels for 26%

profile of v8, /device:TPU:1, one launch (start us, length us, event | category | flops | bytes accessed | tf_op | source)
XLA Modules:
  0.0 160.6 jit_solution(10997564607803831609)
XLA Ops:
  6.5 4.5 %collective-permute-start.9 = (bf16[16,2048]{1,0:T(8,128)(2,1)}, bf16[16,2048]{1,0:T(8,128)(2,1)S(1)}, u32[]{:S(2)}, u32[]{:S(2)}) collective-permute-start(bf16[16,2048]{1,0:T(8,128)(2,1)} %param.15), channel_id=1, source_target_pairs={{0,0},{1,8},{2,16},{3,24},{4,32},{5,40},{6,48},{7,56},{8,64},{9,72... | collective-permute-start | bytes 196616 | tf_op jit(solution)/shard_map/ppermute | solution.py:438
  11.1 0.1 pad_add_fusion.place_ref.place
  11.1 1.4 copy-done.1
  12.5 0.7 pick_new.1
  13.3 4.4 %pick_cache.1 = bf16[2,1024,1024]{2,1,0:T(8,128)(2,1)} custom-call(s32[3]{0:T(128)S(1)} %pad_add_fusion.place_ref.place, bf16[1024,2048]{1,0:T(8,128)(2,1)} %refs_4_.1, bf16[1024,2048]{1,0:T(8,128)(2,1)} %refs_6_.1), custom_call_target="tpu_custom_call" | custom-call | tf_op jit(solution)/shard_map/pick_cache/pallas_call | solution.py:99
  17.7 0.9 pad_maximum_fusion
  18.6 0.1 collective-permute-start
  18.7 2.3 %collective-permute-done.refs_9_.refs_11_ = bf16[128,3072]{1,0:T(8,128)(2,1)S(1)} collective-permute-done((bf16[128,3072]{1,0:T(8,128)(2,1)S(1)}, bf16[128,3072]{1,0:T(8,128)(2,1)S(1)}, u32[]{:S(2)}, u32[]{:S(2)}) %collective-permute-start) | collective-permute-done | bytes 786464 | tf_op jit(solution)/shard_map/ppermute | solution.py:26
  21.1 0.2 collective-permute-start.4
  21.3 5.9 %collective-permute-start.1 = (bf16[256,1024]{1,0:T(8,128)(2,1)S(1)}, bf16[256,1024]{1,0:T(8,128)(2,1)S(1)}, u32[]{:S(2)}, u32[]{:S(2)}) collective-permute-start(bf16[256,1024]{1,0:T(8,128)(2,1)S(1)} %pad_maximum_fusion.1.refs_0_), channel_id=1, source_target_pairs={{0,4},{2,6},{4,0},{6,2},{1,5},{3,7},{5,1},{7,3},{8,12},{10,14},{12... | collective-permute-start | bytes 1572872 | tf_op jit(solution)/shard_map/ppermute | solution.py:448
  27.2 0.1 collective-permute-start.2
  27.3 2.6 %collective-permute-start.3 = (bf16[256,1024]{1,0:T(8,128)(2,1)S(1)}, bf16[256,1024]{1,0:T(8,128)(2,1)}, u32[]{:S(2)}, u32[]{:S(2)}) collective-permute-start(bf16[256,1024]{1,0:T(8,128)(2,1)S(1)} %pad_maximum_fusion.1.refs_0_), channel_id=1, source_target_pairs={{0,6},{2,0},{4,2},{6,4},{1,7},{3,1},{5,3},{7,5},{8,14},{10,8},{12,... | collective-permute-start | bytes 1572872 | tf_op jit(solution)/shard_map/ppermute | solution.py:448
  29.9 0.1 copy.10.ranges
  30.0 9.3 %collective-permute-done.1.refs_1_ = bf16[256,1024]{1,0:T(8,128)(2,1)S(1)} collective-permute-done((bf16[256,1024]{1,0:T(8,128)(2,1)S(1)}, bf16[256,1024]{1,0:T(8,128)(2,1)S(1)}, u32[]{:S(2)}, u32[]{:S(2)}) %collective-permute-start.1) | collective-permute-done | bytes 524320 | tf_op jit(solution)/shard_map/ppermute | solution.py:448
  39.2 11.7 %collective-permute-done.2.refs_2_ = bf16[256,1024]{1,0:T(8,128)(2,1)} collective-permute-done((bf16[256,1024]{1,0:T(8,128)(2,1)S(1)}, bf16[256,1024]{1,0:T(8,128)(2,1)}, u32[]{:S(2)}, u32[]{:S(2)}) %collective-permute-start.2) | collective-permute-done | bytes 524320 | tf_op jit(solution)/shard_map/ppermute | solution.py:448
  50.9 0.4 layer_norm.1
  51.3 0.9 collective-permute-start.5
  52.2 2.9 %collective-permute-start.6 = (bf16[128,2048]{1,0:T(8,128)(2,1)S(1)}, bf16[128,2048]{1,0:T(8,128)(2,1)S(1)}, u32[]{:S(2)}, u32[]{:S(2)}) collective-permute-start(bf16[128,2048]{1,0:T(8,128)(2,1)S(1)} %layer_norm.1), channel_id=1, source_target_pairs={{0,4},{2,6},{4,0},{6,2},{1,5},{3,7},{5,1},{7,3},{8,12},{10,14},{12... | collective-permute-start | bytes 1572872 | tf_op jit(solution)/shard_map/ppermute | solution.py:455
  55.1 1.2 copy-done.4
  56.3 19.3 %attend.1 = (bf16[256,1152]{1,0:T(8,128)(2,1)S(1)}, bf16[256,1152]{1,0:T(8,128)(2,1)}, bf16[256,1152]{1,0:T(8,128)(2,1)}, bf16[256,1152]{1,0:T(8,128)(2,1)S(1)}) custom-call(s32[3]{0:T(128)S(1)} %pad_add_fusion.place_ref.place, s32[16,2]{1,0:T(8,128)S(1)} %copy.10.ranges, bf16[256,1024]{1,0:T(8,128)(2,1)S(1)} %pad_maximum_fusion.1.refs_0_, ...), custom_call_target="tpu_custom_call" | custom-call | flops 9663676416 | bytes 16777216 | tf_op jit(solution)/shard_map/attend/pallas_call | solution.py:213
  75.6 2.3 %collective-permute-done.6 = bf16[128,2048]{1,0:T(8,128)(2,1)S(1)} collective-permute-done((bf16[128,2048]{1,0:T(8,128)(2,1)S(1)}, bf16[128,2048]{1,0:T(8,128)(2,1)S(1)}, u32[]{:S(2)}, u32[]{:S(2)}) %collective-permute-start.6) | collective-permute-done | bytes 524320 | tf_op jit(solution)/shard_map/ppermute | solution.py:455
  78.0 1.4 collective-permute-start.8
  79.5 0.8 collective-permute-start.10
  80.3 1.7 %collective-permute-start.11 = (bf16[256,1152]{1,0:T(8,128)(2,1)}, bf16[256,1152]{1,0:T(8,128)(2,1)S(1)}, u32[]{:S(2)}, u32[]{:S(2)}) collective-permute-start(bf16[256,1152]{1,0:T(8,128)(2,1)} %get-tuple-element.64), channel_id=1, source_target_pairs={{0,6},{2,0},{4,2},{6,4},{1,7},{3,1},{5,3},{7,5},{8,14},{10,8},{12,... | collective-permute-start | bytes 1769480 | tf_op jit(solution)/shard_map/ppermute | solution.py:458
  82.0 1.3 collective-permute-done.8.other_in
  83.4 13.3 %all-gather.3.cloned.1.call-done = bf16[2304,2048]{1,0:T(8,128)(2,1)} async-done(((bf16[144,2048]{1,0:T(8,128)(2,1)}), bf16[2304,2048]{1,0:T(8,128)(2,1)}) %all-gather.3.cloned.1.call-update) | async-done | bytes 9437200 | tf_op jit(solution)/shard_map/all_gather | solution.py:444
  96.7 8.7 %hidden_units.1 = (bf16[512,1024]{1,0:T(8,128)(2,1)S(1)}, bf16[512,1024]{1,0:T(8,128)(2,1)S(1)}) custom-call(bf16[512,2048]{1,0:T(8,128)(2,1)} %copy-done.7, bf16[512,2048]{1,0:T(8,128)(2,1)} %collective-permute-done.8.other_in, bf16[16,144,2048]{2,1,0:T(8,128)(2,1)} %bitcast.13), custom_call_target="tpu_custom_call" | custom-call | flops 4294967296 | bytes 8388608 | tf_op jit(solution)/shard_map/hidden_units/pallas_call | solution.py:308
  105.4 2.8 %collective-permute-done.11.c = bf16[256,1152]{1,0:T(8,128)(2,1)S(1)} collective-permute-done((bf16[256,1152]{1,0:T(8,128)(2,1)}, bf16[256,1152]{1,0:T(8,128)(2,1)S(1)}, u32[]{:S(2)}, u32[]{:S(2)}) %collective-permute-start.11) | collective-permute-done | bytes 589856 | tf_op jit(solution)/shard_map/ppermute | solution.py:458
  108.2 0.9 collective-permute-done.12.d
  109.1 1.7 %merge.1 = bf16[4,256,256]{2,1,0:T(8,128)(2,1)S(1)} custom-call(s32[3]{0:T(128)S(1)} %pad_add_fusion.place_ref.place, bf16[256,1152]{1,0:T(8,128)(2,1)S(1)} %get-tuple-element.62.a, bf16[256,1152]{1,0:T(8,128)(2,1)S(1)} %collective-permute-done.10.b, bf16[256,1152]{1,0:T(8,128)(2,1)S(1)} %collective-permute-done.11.c, ...), custom_call_target="tpu_custom_call" | custom-call | tf_op jit(solution)/shard_map/merge/pallas_call | solution.py:279
  110.8 0.3 collective-permute-start.13
  111.1 3.0 %collective-permute-start.14 = (bf16[256,256]{1,0:T(8,128)(2,1)S(1)}, bf16[256,256]{1,0:T(8,128)(2,1)S(1)}, u32[]{:S(2)}, u32[]{:S(2)}) collective-permute-start(bf16[256,256]{1,0:T(8,128)(2,1)S(1)} %get-tuple-element.84), channel_id=1, source_target_pairs={{0,4},{2,6},{4,0},{6,2},{1,5},{3,7},{5,1},{7,3},{8,12},{10,14},{12... | collective-permute-start | bytes 393224 | tf_op jit(solution)/shard_map/ppermute | solution.py:464
  114.1 5.9 %down_units.1 = (f32[512,2048]{1,0:T(8,128)S(1)}, f32[512,2048]{1,0:T(8,128)S(1)}) custom-call(bf16[512,1024]{1,0:T(8,128)(2,1)S(1)} %get-tuple-element.66.own_hidden, bf16[512,1024]{1,0:T(8,128)(2,1)S(1)} %get-tuple-element.67.other_hidden, bf16[16,144,2048]{2,1,0:T(8,128)(2,1)S(1)} %bitcast.16), custom_call_target="tpu_custom_call" | custom-call | flops 4294967296 | bytes 14680064 | tf_op jit(solution)/shard_map/down_units/pallas_call | solution.py:341
  120.0 1.8 %finish.2 = (bf16[128,2048]{1,0:T(8,128)(2,1)S(1)}, bf16[128,2048]{1,0:T(8,128)(2,1)S(1)}, bf16[128,2048]{1,0:T(8,128)(2,1)S(1)}, bf16[128,2048]{1,0:T(8,128)(2,1)S(1)}) custom-call(f32[512,2048]{1,0:T(8,128)S(1)} %get-tuple-element.69.partial, bf16[256,256]{1,0:T(8,128)(2,1)S(1)} %get-tuple-element.70.a0, bf16[256,256]{1,0:T(8,128)(2,1)S(1)} %collective-permute-done.13.a1, ...), custom_call_target="tpu_custom_call" | custom-call | flops 536870912 | bytes 9437184 | tf_op jit(solution)/shard_map/finish/pallas_call | solution.py:377
  121.7 1.5 collective-permute-start.17
  123.2 0.1 collective-permute-start.19
  123.3 0.4 collective-permute-start.21
  123.7 0.1 collective-permute-start.16
  123.8 1.9 %finish.3 = (f32[128,2048]{1,0:T(8,128)S(1)}, f32[128,2048]{1,0:T(8,128)S(1)}, f32[128,2048]{1,0:T(8,128)S(1)}, f32[128,2048]{1,0:T(8,128)S(1)}) custom-call(f32[512,2048]{1,0:T(8,128)S(1)} %get-tuple-element.78.partial, bf16[256,256]{1,0:T(8,128)(2,1)S(1)} %get-tuple-element.70.a0, bf16[256,256]{1,0:T(8,128)(2,1)S(1)} %collective-permute-done.13.a1, ...), custom_call_target="tpu_custom_call" | custom-call | flops 536870912 | bytes 9437184 | tf_op jit(solution)/shard_map/finish/pallas_call | solution.py:377
  125.7 0.1 add_convert_fusion.3
  125.8 1.9 %collective-permute-start.18 = (bf16[128,2048]{1,0:T(8,128)(2,1)S(1)}, bf16[128,2048]{1,0:T(8,128)(2,1)S(1)}, u32[]{:S(2)}, u32[]{:S(2)}) collective-permute-start(bf16[128,2048]{1,0:T(8,128)(2,1)S(1)} %add_convert_fusion.3), channel_id=1, source_target_pairs={{0,4},{2,6},{4,0},{6,2},{1,5},{3,7},{5,1},{7,3},{8,12},{10,14},{12... | collective-permute-start | bytes 1572872 | tf_op jit(solution)/shard_map/ppermute | solution.py:475
  127.7 0.1 add_convert_fusion.2
  127.9 2.0 %collective-permute-start.20 = (bf16[128,2048]{1,0:T(8,128)(2,1)S(1)}, bf16[128,2048]{1,0:T(8,128)(2,1)S(1)}, u32[]{:S(2)}, u32[]{:S(2)}) collective-permute-start(bf16[128,2048]{1,0:T(8,128)(2,1)S(1)} %add_convert_fusion.2), channel_id=1, source_target_pairs={{0,6},{2,0},{4,2},{6,4},{1,7},{3,1},{5,3},{7,5},{8,14},{10,8},{12,... | collective-permute-start | bytes 1572872 | tf_op jit(solution)/shard_map/ppermute | solution.py:475
  129.8 0.1 add_convert_fusion.1
  130.1 10.4 %collective-permute-done.18 = bf16[128,2048]{1,0:T(8,128)(2,1)S(1)} collective-permute-done((bf16[128,2048]{1,0:T(8,128)(2,1)S(1)}, bf16[128,2048]{1,0:T(8,128)(2,1)S(1)}, u32[]{:S(2)}, u32[]{:S(2)}) %collective-permute-start.18) | collective-permute-done | bytes 524320 | tf_op jit(solution)/shard_map/ppermute | solution.py:475
  140.5 11.2 %collective-permute-done.20 = bf16[128,2048]{1,0:T(8,128)(2,1)S(1)} collective-permute-done((bf16[128,2048]{1,0:T(8,128)(2,1)S(1)}, bf16[128,2048]{1,0:T(8,128)(2,1)S(1)}, u32[]{:S(2)}, u32[]{:S(2)}) %collective-permute-start.20) | collective-permute-done | bytes 524320 | tf_op jit(solution)/shard_map/ppermute | solution.py:475
  151.7 0.7 collective-permute-done.22
  152.5 1.3 add_convert_fusion
  (49 shorter events, 0.4 us)
Async XLA Ops:
  6.5 90.2 %all-gather.3.cloned.1.call-start = ((), (), s32[]{:S(2)}) async-start(), calls=%async_computation | async-start | bytes 10027008 | tf_op jit(solution)/shard_map/all_gather | solution.py:444
  6.5 11.2 %collective-permute-start.9 = (bf16[16,2048]{1,0:T(8,128)(2,1)}, bf16[16,2048]{1,0:T(8,128)(2,1)S(1)}, u32[]{:S(2)}, u32[]{:S(2)}) collective-permute-start(bf16[16,2048]{1,0:T(8,128)(2,1)} %param.15), channel_id=1, source_target_pairs={{0,0},{1,8},{2,16},{3,24},{4,32},{5,40},{6,48},{7,56},{8,64},{9,72... | collective-permute-start | bytes 196616 | tf_op jit(solution)/shard_map/ppermute | solution.py:438
  11.1 1.4 copy-start.1
  13.2 4.5 %copy-start.5 = (bf16[64,2048]{1,0:T(8,128)(2,1)S(1)}, bf16[64,2048]{1,0:T(8,128)(2,1)}, u32[]{:S(2)}) copy-start(bf16[64,2048]{1,0:T(8,128)(2,1)} %param.17) | copy-start | bytes 786436
  13.2 4.5 %copy-start.6 = (bf16[64,2048]{1,0:T(8,128)(2,1)S(1)}, bf16[64,2048]{1,0:T(8,128)(2,1)}, u32[]{:S(2)}) copy-start(bf16[64,2048]{1,0:T(8,128)(2,1)} %param.16) | copy-start | bytes 786436
  17.6 12.2 %copy-start.8 = (s32[16,2]{0,1:T(2,128)S(1)}, s32[16,2]{0,1:T(2,128)}, u32[]{:S(2)}) copy-start(s32[16,2]{0,1:T(2,128)} %param.13) | copy-start | bytes 388
  17.7 33.3 %copy-start = (bf16[128,2048]{1,0:T(8,128)(2,1)S(1)}, bf16[128,2048]{1,0:T(8,128)(2,1)}, u32[]{:S(2)}) copy-start(bf16[128,2048]{1,0:T(8,128)(2,1)} %stream.1) | copy-start | bytes 1572868
  17.7 33.3 %copy-start.2 = (f32[2048]{0:T(1024)S(1)}, f32[2048]{0:T(1024)}, u32[]{:S(2)}) copy-start(f32[2048]{0:T(1024)} %param.14) | copy-start | bytes 24580
  18.6 2.4 %collective-permute-start = (bf16[128,3072]{1,0:T(8,128)(2,1)S(1)}, bf16[128,3072]{1,0:T(8,128)(2,1)S(1)}, u32[]{:S(2)}, u32[]{:S(2)}) collective-permute-start(bf16[128,3072]{1,0:T(8,128)(2,1)S(1)} %get-tuple-element.45), channel_id=1, source_target_pairs={{0,1},{1,0},{2,3},{3,2},{4,5},{5,4},{6,7},{7,6},{8,9},{9,8},{10,11... | collective-permute-start | bytes 2359304 | tf_op jit(solution)/shard_map/ppermute | solution.py:26
  21.1 29.9 %collective-permute-start.4 = (bf16[2,1024,1024]{2,1,0:T(8,128)(2,1)}, bf16[2,1024,1024]{2,1,0:T(8,128)(2,1)}, u32[]{:S(2)}, u32[]{:S(2)}) collective-permute-start(bf16[2,1024,1024]{2,1,0:T(8,128)(2,1)} %pick_cache.1), channel_id=1, source_target_pairs={{0,1},{1,0},{2,3},{3,2},{4,5},{5,4},{6,7},{7,6},{8,9},{9,8},{10,11... | collective-permute-start | bytes 12582920 | tf_op jit(solution)/shard_map/ppermute | solution.py:26
  21.3 18.0 %collective-permute-start.1 = (bf16[256,1024]{1,0:T(8,128)(2,1)S(1)}, bf16[256,1024]{1,0:T(8,128)(2,1)S(1)}, u32[]{:S(2)}, u32[]{:S(2)}) collective-permute-start(bf16[256,1024]{1,0:T(8,128)(2,1)S(1)} %pad_maximum_fusion.1.refs_0_), channel_id=1, source_target_pairs={{0,4},{2,6},{4,0},{6,2},{1,5},{3,7},{5,1},{7,3},{8,12},{10,14},{12... | collective-permute-start | bytes 1572872 | tf_op jit(solution)/shard_map/ppermute | solution.py:448
  27.2 23.7 %collective-permute-start.2 = (bf16[256,1024]{1,0:T(8,128)(2,1)S(1)}, bf16[256,1024]{1,0:T(8,128)(2,1)}, u32[]{:S(2)}, u32[]{:S(2)}) collective-permute-start(bf16[256,1024]{1,0:T(8,128)(2,1)S(1)} %pad_maximum_fusion.1.refs_0_), channel_id=1, source_target_pairs={{0,2},{2,4},{4,6},{6,0},{1,3},{3,5},{5,7},{7,1},{8,10},{10,12},{12... | collective-permute-start | bytes 1572872 | tf_op jit(solution)/shard_map/ppermute | solution.py:448
  27.3 23.6 %collective-permute-start.3 = (bf16[256,1024]{1,0:T(8,128)(2,1)S(1)}, bf16[256,1024]{1,0:T(8,128)(2,1)}, u32[]{:S(2)}, u32[]{:S(2)}) collective-permute-start(bf16[256,1024]{1,0:T(8,128)(2,1)S(1)} %pad_maximum_fusion.1.refs_0_), channel_id=1, source_target_pairs={{0,6},{2,0},{4,2},{6,4},{1,7},{3,1},{5,3},{7,5},{8,14},{10,8},{12,... | collective-permute-start | bytes 1572872 | tf_op jit(solution)/shard_map/ppermute | solution.py:448
  39.2 15.8 %copy-start.3 = (bf16[256,1024]{1,0:T(8,128)(2,1)}, bf16[256,1024]{1,0:T(8,128)(2,1)S(1)}, u32[]{:S(2)}) copy-start(bf16[256,1024]{1,0:T(8,128)(2,1)S(1)} %collective-permute-done.1.refs_1_) | copy-start | bytes 1572868
  51.3 24.3 %collective-permute-start.5 = (bf16[128,2048]{1,0:T(8,128)(2,1)S(1)}, bf16[128,2048]{1,0:T(8,128)(2,1)S(1)}, u32[]{:S(2)}, u32[]{:S(2)}) collective-permute-start(bf16[128,2048]{1,0:T(8,128)(2,1)S(1)} %layer_norm.1), channel_id=1, source_target_pairs={{0,2},{2,4},{4,6},{6,0},{1,3},{3,5},{5,7},{7,1},{8,10},{10,12},{12... | collective-permute-start | bytes 1572872 | tf_op jit(solution)/shard_map/ppermute | solution.py:455
  52.2 25.6 %collective-permute-start.6 = (bf16[128,2048]{1,0:T(8,128)(2,1)S(1)}, bf16[128,2048]{1,0:T(8,128)(2,1)S(1)}, u32[]{:S(2)}, u32[]{:S(2)}) collective-permute-start(bf16[128,2048]{1,0:T(8,128)(2,1)S(1)} %layer_norm.1), channel_id=1, source_target_pairs={{0,4},{2,6},{4,0},{6,2},{1,5},{3,7},{5,1},{7,3},{8,12},{10,14},{12... | collective-permute-start | bytes 1572872 | tf_op jit(solution)/shard_map/ppermute | solution.py:455
  55.1 22.8 %collective-permute-start.7 = (bf16[128,2048]{1,0:T(8,128)(2,1)S(1)}, bf16[128,2048]{1,0:T(8,128)(2,1)S(1)}, u32[]{:S(2)}, u32[]{:S(2)}) collective-permute-start(bf16[128,2048]{1,0:T(8,128)(2,1)S(1)} %layer_norm.1), channel_id=1, source_target_pairs={{0,6},{2,0},{4,2},{6,4},{1,7},{3,1},{5,3},{7,5},{8,14},{10,8},{12,... | collective-permute-start | bytes 1572872 | tf_op jit(solution)/shard_map/ppermute | solution.py:455
  55.1 1.2 copy-start.4
  78.0 4.0 %copy-start.7 = (bf16[512,2048]{1,0:T(8,128)(2,1)}, bf16[512,2048]{1,0:T(8,128)(2,1)S(1)}, u32[]{:S(2)}) copy-start(bf16[512,2048]{1,0:T(8,128)(2,1)S(1)} %constant_dynamic-update-slice_fusion.own_in) | copy-start | bytes 6291460
  78.0 5.3 %collective-permute-start.8 = (bf16[512,2048]{1,0:T(8,128)(2,1)S(1)}, bf16[512,2048]{1,0:T(8,128)(2,1)}, u32[]{:S(2)}, u32[]{:S(2)}) collective-permute-start(bf16[512,2048]{1,0:T(8,128)(2,1)S(1)} %constant_dynamic-update-slice_fusion.own_in), channel_id=1, source_target_pairs={{0,1},{1,0},{2,3},{3,2},{4,5},{5,4},{6,7},{7,6},{8,9},{9,8},{10,11... | collective-permute-start | bytes 6291464 | tf_op jit(solution)/shard_map/ppermute | solution.py:26
  79.5 25.9 %collective-permute-start.10 = (bf16[256,1152]{1,0:T(8,128)(2,1)}, bf16[256,1152]{1,0:T(8,128)(2,1)S(1)}, u32[]{:S(2)}, u32[]{:S(2)}) collective-permute-start(bf16[256,1152]{1,0:T(8,128)(2,1)} %get-tuple-element.63), channel_id=1, source_target_pairs={{0,4},{2,6},{4,0},{6,2},{1,5},{3,7},{5,1},{7,3},{8,12},{10,14},{12... | collective-permute-start | bytes 1769480 | tf_op jit(solution)/shard_map/ppermute | solution.py:458
  80.3 27.9 %collective-permute-start.11 = (bf16[256,1152]{1,0:T(8,128)(2,1)}, bf16[256,1152]{1,0:T(8,128)(2,1)S(1)}, u32[]{:S(2)}, u32[]{:S(2)}) collective-permute-start(bf16[256,1152]{1,0:T(8,128)(2,1)} %get-tuple-element.64), channel_id=1, source_target_pairs={{0,6},{2,0},{4,2},{6,4},{1,7},{3,1},{5,3},{7,5},{8,14},{10,8},{12,... | collective-permute-start | bytes 1769480 | tf_op jit(solution)/shard_map/ppermute | solution.py:458
  82.0 27.0 %collective-permute-start.12 = (bf16[256,1152]{1,0:T(8,128)(2,1)S(1)}, bf16[256,1152]{1,0:T(8,128)(2,1)S(1)}, u32[]{:S(2)}, u32[]{:S(2)}) collective-permute-start(bf16[256,1152]{1,0:T(8,128)(2,1)S(1)} %get-tuple-element.65), channel_id=1, source_target_pairs={{0,2},{2,4},{4,6},{6,0},{1,3},{3,5},{5,7},{7,1},{8,10},{10,12},{12... | collective-permute-start | bytes 1769480 | tf_op jit(solution)/shard_map/ppermute | solution.py:458
  96.7 17.3 %slice-start = ((s8[9437184]{0:T(1024)(128)(4,1)}), s8[4194304]{0:T(1024)(128)(4,1)S(1)}, s32[]{:S(2)}) async-start(s8[9437184]{0:T(1024)(128)(4,1)} %bitcast.14), calls=%async_computation.1 | async-start | bytes 8388608
  96.7 17.3 %slice-start.1 = ((s8[9437184]{0:T(1024)(128)(4,1)}), s8[4194304]{0:T(1024)(128)(4,1)S(1)}, s32[]{:S(2)}) async-start(s8[9437184]{0:T(1024)(128)(4,1)} %bitcast.14), calls=%async_computation.2 | async-start | bytes 8388608
  96.7 17.3 %slice-start.2 = ((s8[9437184]{0:T(1024)(128)(4,1)}), s8[1048576]{0:T(1024)(128)(4,1)S(1)}, s32[]{:S(2)}) async-start(s8[9437184]{0:T(1024)(128)(4,1)} %bitcast.14), calls=%async_computation.3 | async-start | bytes 2097152
  110.8 9.1 %collective-permute-start.13 = (bf16[256,256]{1,0:T(8,128)(2,1)S(1)}, bf16[256,256]{1,0:T(8,128)(2,1)S(1)}, u32[]{:S(2)}, u32[]{:S(2)}) collective-permute-start(bf16[256,256]{1,0:T(8,128)(2,1)S(1)} %get-tuple-element.85), channel_id=1, source_target_pairs={{0,2},{2,4},{4,6},{6,0},{1,3},{3,5},{5,7},{7,1},{8,10},{10,12},{12... | collective-permute-start | bytes 393224 | tf_op jit(solution)/shard_map/ppermute | solution.py:464
  111.1 8.9 %collective-permute-start.14 = (bf16[256,256]{1,0:T(8,128)(2,1)S(1)}, bf16[256,256]{1,0:T(8,128)(2,1)S(1)}, u32[]{:S(2)}, u32[]{:S(2)}) collective-permute-start(bf16[256,256]{1,0:T(8,128)(2,1)S(1)} %get-tuple-element.84), channel_id=1, source_target_pairs={{0,4},{2,6},{4,0},{6,2},{1,5},{3,7},{5,1},{7,3},{8,12},{10,14},{12... | collective-permute-start | bytes 393224 | tf_op jit(solution)/shard_map/ppermute | solution.py:464
  114.0 5.9 %collective-permute-start.15 = (bf16[256,256]{1,0:T(8,128)(2,1)S(1)}, bf16[256,256]{1,0:T(8,128)(2,1)S(1)}, u32[]{:S(2)}, u32[]{:S(2)}) collective-permute-start(bf16[256,256]{1,0:T(8,128)(2,1)S(1)} %get-tuple-element.83), channel_id=1, source_target_pairs={{0,6},{2,0},{4,2},{6,4},{1,7},{3,1},{5,3},{7,5},{8,14},{10,8},{12,... | collective-permute-start | bytes 393224 | tf_op jit(solution)/shard_map/ppermute | solution.py:464
  121.7 3.9 %collective-permute-start.17 = (bf16[128,2048]{1,0:T(8,128)(2,1)S(1)}, bf16[128,2048]{1,0:T(8,128)(2,1)S(1)}, u32[]{:S(2)}, u32[]{:S(2)}) collective-permute-start(bf16[128,2048]{1,0:T(8,128)(2,1)S(1)} %get-tuple-element.76), channel_id=1, source_target_pairs={{0,1},{1,0},{2,3},{3,2},{4,5},{5,4},{6,7},{7,6},{8,9},{9,8},{10,11... | collective-permute-start | bytes 1572872 | tf_op jit(solution)/shard_map/ppermute | solution.py:26
  123.2 4.5 %collective-permute-start.19 = (bf16[128,2048]{1,0:T(8,128)(2,1)S(1)}, bf16[128,2048]{1,0:T(8,128)(2,1)S(1)}, u32[]{:S(2)}, u32[]{:S(2)}) collective-permute-start(bf16[128,2048]{1,0:T(8,128)(2,1)S(1)} %get-tuple-element.75), channel_id=1, source_target_pairs={{0,1},{1,0},{2,3},{3,2},{4,5},{5,4},{6,7},{7,6},{8,9},{9,8},{10,11... | collective-permute-start | bytes 1572872 | tf_op jit(solution)/shard_map/ppermute | solution.py:26
  123.3 6.6 %collective-permute-start.21 = (bf16[128,2048]{1,0:T(8,128)(2,1)S(1)}, bf16[128,2048]{1,0:T(8,128)(2,1)S(1)}, u32[]{:S(2)}, u32[]{:S(2)}) collective-permute-start(bf16[128,2048]{1,0:T(8,128)(2,1)S(1)} %get-tuple-element.77), channel_id=1, source_target_pairs={{0,1},{1,0},{2,3},{3,2},{4,5},{5,4},{6,7},{7,6},{8,9},{9,8},{10,11... | collective-permute-start | bytes 1572872 | tf_op jit(solution)/shard_map/ppermute | solution.py:26
  123.7 6.3 %collective-permute-start.16 = (bf16[128,2048]{1,0:T(8,128)(2,1)S(1)}, bf16[128,2048]{1,0:T(8,128)(2,1)S(1)}, u32[]{:S(2)}, u32[]{:S(2)}) collective-permute-start(bf16[128,2048]{1,0:T(8,128)(2,1)S(1)} %get-tuple-element.74), channel_id=1, source_target_pairs={{0,1},{1,0},{2,3},{3,2},{4,5},{5,4},{6,7},{7,6},{8,9},{9,8},{10,11... | collective-permute-start | bytes 1572872 | tf_op jit(solution)/shard_map/ppermute | solution.py:26
  125.8 14.7 %collective-permute-start.18 = (bf16[128,2048]{1,0:T(8,128)(2,1)S(1)}, bf16[128,2048]{1,0:T(8,128)(2,1)S(1)}, u32[]{:S(2)}, u32[]{:S(2)}) collective-permute-start(bf16[128,2048]{1,0:T(8,128)(2,1)S(1)} %add_convert_fusion.3), channel_id=1, source_target_pairs={{0,4},{2,6},{4,0},{6,2},{1,5},{3,7},{5,1},{7,3},{8,12},{10,14},{12... | collective-permute-start | bytes 1572872 | tf_op jit(solution)/shard_map/ppermute | solution.py:475
  127.9 23.9 %collective-permute-start.20 = (bf16[128,2048]{1,0:T(8,128)(2,1)S(1)}, bf16[128,2048]{1,0:T(8,128)(2,1)S(1)}, u32[]{:S(2)}, u32[]{:S(2)}) collective-permute-start(bf16[128,2048]{1,0:T(8,128)(2,1)S(1)} %add_convert_fusion.2), channel_id=1, source_target_pairs={{0,6},{2,0},{4,2},{6,4},{1,7},{3,1},{5,3},{7,5},{8,14},{10,8},{12,... | collective-permute-start | bytes 1572872 | tf_op jit(solution)/shard_map/ppermute | solution.py:475
  130.0 22.5 %collective-permute-start.22 = (bf16[128,2048]{1,0:T(8,128)(2,1)S(1)}, bf16[128,2048]{1,0:T(8,128)(2,1)S(1)}, u32[]{:S(2)}, u32[]{:S(2)}) collective-permute-start(bf16[128,2048]{1,0:T(8,128)(2,1)S(1)} %add_convert_fusion.1), channel_id=1, source_target_pairs={{0,2},{2,4},{4,6},{6,0},{1,3},{3,5},{5,7},{7,1},{8,10},{10,12},{12... | collective-permute-start | bytes 1572872 | tf_op jit(solution)/shard_map/ppermute | solution.py:475
Sparse Core Ops, SparseCore 0:
  18.7 77.9 all-gather.2

commit v9 on v6

--- a/solution.py
+++ b/solution.py
@@ -373,7 +373,7 @@
     shards, shard_rows, _ = weights.shape
     out_rows = shard_rows - 2 * unit_rows
     count = rows // len(heads)
-    columns = 512
+    columns = 1024
     return pl.pallas_call(
         finish_kernel,
         grid=(width // columns,),

time: 161 us -> 161 us (level)
  no operation moved by 1% of the time
where the time goes in v9:
time: 161 us; the launch traced here: 160 us
  waiting for transfers between devices  66.9 us (42%)
  Pallas kernels  44.4 us (28%)
  starting transfers between devices  30.4 us (19%)
  between operations  13.8 us (9%)
  other arithmetic  2.6 us (2%)
  local copies, waits for them, and re-layouts  1.78 us (1%)
    ppermute x3, waiting for transfers between devices, on_device(): summed = summed + lax.ppermute(both, 'z', ring(-k, nz)).astype(F32)  22.4 us
    ppermute x3, waiting for transfers between devices, on_device(): queries = [lax.ppermute(query, 'z', ring(k, nz)) for k in (2, 1, 3)]  20.9 us
    pallas_call x1, Pallas kernels, attend(): pl.pallas_call(functools.partial(attend_kernel, steps), grid_spec=pltpu.P...  19.7 us
    all_gather x1, waiting for transfers between devices, on_device(): lax.all_gather(jnp.concatenate([up_weight, down_weight, head_rows], 0), (...  13.4 us
    pallas_call x1, Pallas kernels, hidden_units(): pl.pallas_call(hidden_kernel, grid=(shards // chunk,), in_specs=[whole, w...  8.68 us
    ppermute x3, starting transfers between devices, on_device(): queries = [lax.ppermute(query, 'z', ring(k, nz)) for k in (2, 1, 3)]  8.6 us
    pallas_call x1, Pallas kernels, down_units(): pl.pallas_call(down_kernel, grid=(width // columns,), in_specs=[whole, wh...  5.88 us
    ppermute x1, starting transfers between devices, on_device(): lax.ppermute(out_weight, ('y', 'x', 'z', 'c'), head_owners(ny, nx, nz))  4.5 us
  transfers between devices with their start and end apart: 24, of which 11 were waited for; matrix products, arithmetic and copies ran while one was open for 0% of the time, Pallas kernels for 26%

profile of v9, /device:TPU:1, one launch (start us, length us, event | category | flops | bytes accessed | tf_op | source)
XLA Modules:
  0.0 159.9 jit_solution(17306270345646899051)
XLA Ops:
  6.5 4.5 %collective-permute-start.9 = (bf16[16,2048]{1,0:T(8,128)(2,1)}, bf16[16,2048]{1,0:T(8,128)(2,1)S(1)}, u32[]{:S(2)}, u32[]{:S(2)}) collective-permute-start(bf16[16,2048]{1,0:T(8,128)(2,1)} %param.15), channel_id=1, source_target_pairs={{0,0},{1,8},{2,16},{3,24},{4,32},{5,40},{6,48},{7,56},{8,64},{9,72... | collective-permute-start | bytes 196616 | tf_op jit(solution)/shard_map/ppermute | solution.py:438
  11.1 0.1 pad_add_fusion.place_ref.place
  11.1 1.4 copy-done.1
  12.5 0.7 pick_new.1
  13.3 4.4 %pick_cache.1 = bf16[2,1024,1024]{2,1,0:T(8,128)(2,1)} custom-call(s32[3]{0:T(128)S(1)} %pad_add_fusion.place_ref.place, bf16[1024,2048]{1,0:T(8,128)(2,1)} %refs_4_.1, bf16[1024,2048]{1,0:T(8,128)(2,1)} %refs_6_.1), custom_call_target="tpu_custom_call" | custom-call | tf_op jit(solution)/shard_map/pick_cache/pallas_call | solution.py:99
  17.7 0.9 pad_maximum_fusion
  18.6 0.1 collective-permute-start
  18.7 2.3 %collective-permute-done.refs_9_.refs_11_ = bf16[128,3072]{1,0:T(8,128)(2,1)S(1)} collective-permute-done((bf16[128,3072]{1,0:T(8,128)(2,1)S(1)}, bf16[128,3072]{1,0:T(8,128)(2,1)S(1)}, u32[]{:S(2)}, u32[]{:S(2)}) %collective-permute-start) | collective-permute-done | bytes 786464 | tf_op jit(solution)/shard_map/ppermute | solution.py:26
  21.1 0.2 collective-permute-start.4
  21.3 5.9 %collective-permute-start.1 = (bf16[256,1024]{1,0:T(8,128)(2,1)S(1)}, bf16[256,1024]{1,0:T(8,128)(2,1)S(1)}, u32[]{:S(2)}, u32[]{:S(2)}) collective-permute-start(bf16[256,1024]{1,0:T(8,128)(2,1)S(1)} %pad_maximum_fusion.1.refs_0_), channel_id=1, source_target_pairs={{0,4},{2,6},{4,0},{6,2},{1,5},{3,7},{5,1},{7,3},{8,12},{10,14},{12... | collective-permute-start | bytes 1572872 | tf_op jit(solution)/shard_map/ppermute | solution.py:448
  27.2 0.1 collective-permute-start.2
  27.3 2.6 %collective-permute-start.3 = (bf16[256,1024]{1,0:T(8,128)(2,1)S(1)}, bf16[256,1024]{1,0:T(8,128)(2,1)S(1)}, u32[]{:S(2)}, u32[]{:S(2)}) collective-permute-start(bf16[256,1024]{1,0:T(8,128)(2,1)S(1)} %pad_maximum_fusion.1.refs_0_), channel_id=1, source_target_pairs={{0,6},{2,0},{4,2},{6,4},{1,7},{3,1},{5,3},{7,5},{8,14},{10,8},{12,... | collective-permute-start | bytes 1572872 | tf_op jit(solution)/shard_map/ppermute | solution.py:448
  29.9 0.1 copy.10.ranges
  30.0 9.3 %collective-permute-done.1.refs_1_ = bf16[256,1024]{1,0:T(8,128)(2,1)S(1)} collective-permute-done((bf16[256,1024]{1,0:T(8,128)(2,1)S(1)}, bf16[256,1024]{1,0:T(8,128)(2,1)S(1)}, u32[]{:S(2)}, u32[]{:S(2)}) %collective-permute-start.1) | collective-permute-done | bytes 524320 | tf_op jit(solution)/shard_map/ppermute | solution.py:448
  39.2 11.6 %collective-permute-done.2.refs_2_ = bf16[256,1024]{1,0:T(8,128)(2,1)S(1)} collective-permute-done((bf16[256,1024]{1,0:T(8,128)(2,1)S(1)}, bf16[256,1024]{1,0:T(8,128)(2,1)S(1)}, u32[]{:S(2)}, u32[]{:S(2)}) %collective-permute-start.2) | collective-permute-done | bytes 524320 | tf_op jit(solution)/shard_map/ppermute | solution.py:448
  50.9 0.4 layer_norm.1
  51.2 0.9 collective-permute-start.5
  52.1 2.9 %collective-permute-start.6 = (bf16[128,2048]{1,0:T(8,128)(2,1)S(1)}, bf16[128,2048]{1,0:T(8,128)(2,1)S(1)}, u32[]{:S(2)}, u32[]{:S(2)}) collective-permute-start(bf16[128,2048]{1,0:T(8,128)(2,1)S(1)} %layer_norm.1), channel_id=1, source_target_pairs={{0,4},{2,6},{4,0},{6,2},{1,5},{3,7},{5,1},{7,3},{8,12},{10,14},{12... | collective-permute-start | bytes 1572872 | tf_op jit(solution)/shard_map/ppermute | solution.py:455
  55.0 19.7 %attend.1 = (bf16[256,1152]{1,0:T(8,128)(2,1)S(1)}, bf16[256,1152]{1,0:T(8,128)(2,1)}, bf16[256,1152]{1,0:T(8,128)(2,1)}, bf16[256,1152]{1,0:T(8,128)(2,1)S(1)}) custom-call(s32[3]{0:T(128)S(1)} %pad_add_fusion.place_ref.place, s32[16,2]{1,0:T(8,128)S(1)} %copy.10.ranges, bf16[256,1024]{1,0:T(8,128)(2,1)} %copy-done.3, bf16[256,1024]{1,0:T(8,128)(2,1)} %copy-done.8, ...), custom_call_target="tpu_custom_call" | custom-call | flops 9663676416 | bytes 16777216 | tf_op jit(solution)/shard_map/attend/pallas_call | solution.py:213
  74.7 3.0 %collective-permute-done.6 = bf16[128,2048]{1,0:T(8,128)(2,1)S(1)} collective-permute-done((bf16[128,2048]{1,0:T(8,128)(2,1)S(1)}, bf16[128,2048]{1,0:T(8,128)(2,1)S(1)}, u32[]{:S(2)}, u32[]{:S(2)}) %collective-permute-start.6) | collective-permute-done | bytes 524320 | tf_op jit(solution)/shard_map/ppermute | solution.py:455
  78.0 1.4 collective-permute-start.8
  79.4 0.8 collective-permute-start.10
  80.2 1.7 %collective-permute-start.11 = (bf16[256,1152]{1,0:T(8,128)(2,1)}, bf16[256,1152]{1,0:T(8,128)(2,1)S(1)}, u32[]{:S(2)}, u32[]{:S(2)}) collective-permute-start(bf16[256,1152]{1,0:T(8,128)(2,1)} %get-tuple-element.64), channel_id=1, source_target_pairs={{0,6},{2,0},{4,2},{6,4},{1,7},{3,1},{5,3},{7,5},{8,14},{10,8},{12,... | collective-permute-start | bytes 1769480 | tf_op jit(solution)/shard_map/ppermute | solution.py:458
  82.0 1.3 collective-permute-done.8.other_in
  83.3 13.4 %all-gather.3.cloned.1.call-done = bf16[2304,2048]{1,0:T(8,128)(2,1)} async-done(((bf16[144,2048]{1,0:T(8,128)(2,1)}), bf16[2304,2048]{1,0:T(8,128)(2,1)}) %all-gather.3.cloned.1.call-update) | async-done | bytes 9437200 | tf_op jit(solution)/shard_map/all_gather | solution.py:444
  96.7 8.7 %hidden_units.1 = (bf16[512,1024]{1,0:T(8,128)(2,1)S(1)}, bf16[512,1024]{1,0:T(8,128)(2,1)S(1)}) custom-call(bf16[512,2048]{1,0:T(8,128)(2,1)} %copy-done.6, bf16[512,2048]{1,0:T(8,128)(2,1)} %collective-permute-done.8.other_in, bf16[16,144,2048]{2,1,0:T(8,128)(2,1)} %bitcast.13), custom_call_target="tpu_custom_call" | custom-call | flops 4294967296 | bytes 8388608 | tf_op jit(solution)/shard_map/hidden_units/pallas_call | solution.py:308
  105.4 2.7 %collective-permute-done.11.c = bf16[256,1152]{1,0:T(8,128)(2,1)S(1)} collective-permute-done((bf16[256,1152]{1,0:T(8,128)(2,1)}, bf16[256,1152]{1,0:T(8,128)(2,1)S(1)}, u32[]{:S(2)}, u32[]{:S(2)}) %collective-permute-start.11) | collective-permute-done | bytes 589856 | tf_op jit(solution)/shard_map/ppermute | solution.py:458
  108.2 0.9 collective-permute-done.12.d
  109.0 1.7 %merge.1 = bf16[4,256,256]{2,1,0:T(8,128)(2,1)S(1)} custom-call(s32[3]{0:T(128)S(1)} %pad_add_fusion.place_ref.place, bf16[256,1152]{1,0:T(8,128)(2,1)S(1)} %get-tuple-element.62.a, bf16[256,1152]{1,0:T(8,128)(2,1)S(1)} %collective-permute-done.10.b, bf16[256,1152]{1,0:T(8,128)(2,1)S(1)} %collective-permute-done.11.c, ...), custom_call_target="tpu_custom_call" | custom-call | tf_op jit(solution)/shard_map/merge/pallas_call | solution.py:279
  110.7 0.3 collective-permute-start.13
  111.0 3.0 %collective-permute-start.14 = (bf16[256,256]{1,0:T(8,128)(2,1)S(1)}, bf16[256,256]{1,0:T(8,128)(2,1)S(1)}, u32[]{:S(2)}, u32[]{:S(2)}) collective-permute-start(bf16[256,256]{1,0:T(8,128)(2,1)S(1)} %get-tuple-element.84), channel_id=1, source_target_pairs={{0,4},{2,6},{4,0},{6,2},{1,5},{3,7},{5,1},{7,3},{8,12},{10,14},{12... | collective-permute-start | bytes 393224 | tf_op jit(solution)/shard_map/ppermute | solution.py:464
  114.0 5.9 %down_units.1 = (f32[512,2048]{1,0:T(8,128)S(1)}, f32[512,2048]{1,0:T(8,128)S(1)}) custom-call(bf16[512,1024]{1,0:T(8,128)(2,1)S(1)} %get-tuple-element.66.own_hidden, bf16[512,1024]{1,0:T(8,128)(2,1)S(1)} %get-tuple-element.67.other_hidden, bf16[16,144,2048]{2,1,0:T(8,128)(2,1)S(1)} %bitcast.16), custom_call_target="tpu_custom_call" | custom-call | flops 4294967296 | bytes 14680064 | tf_op jit(solution)/shard_map/down_units/pallas_call | solution.py:341
  119.9 1.4 finish.2
  121.3 1.5 collective-permute-start.17
  122.8 0.1 collective-permute-start.19
  122.9 0.4 collective-permute-start.21
  123.3 0.1 collective-permute-start.16
  123.4 1.5 finish.3
  125.0 0.1 add_convert_fusion.3
  125.1 1.9 %collective-permute-start.18 = (bf16[128,2048]{1,0:T(8,128)(2,1)S(1)}, bf16[128,2048]{1,0:T(8,128)(2,1)S(1)}, u32[]{:S(2)}, u32[]{:S(2)}) collective-permute-start(bf16[128,2048]{1,0:T(8,128)(2,1)S(1)} %add_convert_fusion.3), channel_id=1, source_target_pairs={{0,4},{2,6},{4,0},{6,2},{1,5},{3,7},{5,1},{7,3},{8,12},{10,14},{12... | collective-permute-start | bytes 1572872 | tf_op jit(solution)/shard_map/ppermute | solution.py:475
  127.0 0.1 add_convert_fusion.2
  127.1 2.0 %collective-permute-start.20 = (bf16[128,2048]{1,0:T(8,128)(2,1)S(1)}, bf16[128,2048]{1,0:T(8,128)(2,1)S(1)}, u32[]{:S(2)}, u32[]{:S(2)}) collective-permute-start(bf16[128,2048]{1,0:T(8,128)(2,1)S(1)} %add_convert_fusion.2), channel_id=1, source_target_pairs={{0,6},{2,0},{4,2},{6,4},{1,7},{3,1},{5,3},{7,5},{8,14},{10,8},{12,... | collective-permute-start | bytes 1572872 | tf_op jit(solution)/shard_map/ppermute | solution.py:475
  129.1 0.1 add_convert_fusion.1
  129.2 0.1 collective-permute-start.22
  129.3 10.5 %collective-permute-done.18 = bf16[128,2048]{1,0:T(8,128)(2,1)S(1)} collective-permute-done((bf16[128,2048]{1,0:T(8,128)(2,1)S(1)}, bf16[128,2048]{1,0:T(8,128)(2,1)S(1)}, u32[]{:S(2)}, u32[]{:S(2)}) %collective-permute-start.18) | collective-permute-done | bytes 524320 | tf_op jit(solution)/shard_map/ppermute | solution.py:475
  139.8 11.2 %collective-permute-done.20 = bf16[128,2048]{1,0:T(8,128)(2,1)S(1)} collective-permute-done((bf16[128,2048]{1,0:T(8,128)(2,1)S(1)}, bf16[128,2048]{1,0:T(8,128)(2,1)S(1)}, u32[]{:S(2)}, u32[]{:S(2)}) %collective-permute-start.20) | collective-permute-done | bytes 524320 | tf_op jit(solution)/shard_map/ppermute | solution.py:475
  151.0 0.7 collective-permute-done.22
  151.8 1.3 add_convert_fusion
  (53 shorter events, 0.4 us)
Async XLA Ops:
  6.5 90.2 %all-gather.3.cloned.1.call-start = ((), (), s32[]{:S(2)}) async-start(), calls=%async_computation | async-start | bytes 10027008 | tf_op jit(solution)/shard_map/all_gather | solution.py:444
  6.5 11.1 %collective-permute-start.9 = (bf16[16,2048]{1,0:T(8,128)(2,1)}, bf16[16,2048]{1,0:T(8,128)(2,1)S(1)}, u32[]{:S(2)}, u32[]{:S(2)}) collective-permute-start(bf16[16,2048]{1,0:T(8,128)(2,1)} %param.15), channel_id=1, source_target_pairs={{0,0},{1,8},{2,16},{3,24},{4,32},{5,40},{6,48},{7,56},{8,64},{9,72... | collective-permute-start | bytes 196616 | tf_op jit(solution)/shard_map/ppermute | solution.py:438
  11.1 1.4 copy-start.1
  13.2 4.5 %copy-start.4 = (bf16[64,2048]{1,0:T(8,128)(2,1)S(1)}, bf16[64,2048]{1,0:T(8,128)(2,1)}, u32[]{:S(2)}) copy-start(bf16[64,2048]{1,0:T(8,128)(2,1)} %param.17) | copy-start | bytes 786436
  13.2 4.5 %copy-start.5 = (bf16[64,2048]{1,0:T(8,128)(2,1)S(1)}, bf16[64,2048]{1,0:T(8,128)(2,1)}, u32[]{:S(2)}) copy-start(bf16[64,2048]{1,0:T(8,128)(2,1)} %param.16) | copy-start | bytes 786436
  17.6 12.2 %copy-start.7 = (s32[16,2]{0,1:T(2,128)S(1)}, s32[16,2]{0,1:T(2,128)}, u32[]{:S(2)}) copy-start(s32[16,2]{0,1:T(2,128)} %param.13) | copy-start | bytes 388
  17.7 33.2 %copy-start = (bf16[128,2048]{1,0:T(8,128)(2,1)S(1)}, bf16[128,2048]{1,0:T(8,128)(2,1)}, u32[]{:S(2)}) copy-start(bf16[128,2048]{1,0:T(8,128)(2,1)} %stream.1) | copy-start | bytes 1572868
  17.7 33.2 %copy-start.2 = (f32[2048]{0:T(1024)S(1)}, f32[2048]{0:T(1024)}, u32[]{:S(2)}) copy-start(f32[2048]{0:T(1024)} %param.14) | copy-start | bytes 24580
  18.6 2.4 %collective-permute-start = (bf16[128,3072]{1,0:T(8,128)(2,1)S(1)}, bf16[128,3072]{1,0:T(8,128)(2,1)S(1)}, u32[]{:S(2)}, u32[]{:S(2)}) collective-permute-start(bf16[128,3072]{1,0:T(8,128)(2,1)S(1)} %get-tuple-element.45), channel_id=1, source_target_pairs={{0,1},{1,0},{2,3},{3,2},{4,5},{5,4},{6,7},{7,6},{8,9},{9,8},{10,11... | collective-permute-start | bytes 2359304 | tf_op jit(solution)/shard_map/ppermute | solution.py:26
  21.1 33.9 %copy-start.3 = (bf16[256,1024]{1,0:T(8,128)(2,1)}, bf16[256,1024]{1,0:T(8,128)(2,1)S(1)}, u32[]{:S(2)}) copy-start(bf16[256,1024]{1,0:T(8,128)(2,1)S(1)} %pad_maximum_fusion.1.refs_0_) | copy-start | bytes 1572868
  21.1 29.8 %collective-permute-start.4 = (bf16[2,1024,1024]{2,1,0:T(8,128)(2,1)}, bf16[2,1024,1024]{2,1,0:T(8,128)(2,1)}, u32[]{:S(2)}, u32[]{:S(2)}) collective-permute-start(bf16[2,1024,1024]{2,1,0:T(8,128)(2,1)} %pick_cache.1), channel_id=1, source_target_pairs={{0,1},{1,0},{2,3},{3,2},{4,5},{5,4},{6,7},{7,6},{8,9},{9,8},{10,11... | collective-permute-start | bytes 12582920 | tf_op jit(solution)/shard_map/ppermute | solution.py:26
  21.3 18.0 %collective-permute-start.1 = (bf16[256,1024]{1,0:T(8,128)(2,1)S(1)}, bf16[256,1024]{1,0:T(8,128)(2,1)S(1)}, u32[]{:S(2)}, u32[]{:S(2)}) collective-permute-start(bf16[256,1024]{1,0:T(8,128)(2,1)S(1)} %pad_maximum_fusion.1.refs_0_), channel_id=1, source_target_pairs={{0,4},{2,6},{4,0},{6,2},{1,5},{3,7},{5,1},{7,3},{8,12},{10,14},{12... | collective-permute-start | bytes 1572872 | tf_op jit(solution)/shard_map/ppermute | solution.py:448
  27.2 23.6 %collective-permute-start.2 = (bf16[256,1024]{1,0:T(8,128)(2,1)S(1)}, bf16[256,1024]{1,0:T(8,128)(2,1)S(1)}, u32[]{:S(2)}, u32[]{:S(2)}) collective-permute-start(bf16[256,1024]{1,0:T(8,128)(2,1)S(1)} %pad_maximum_fusion.1.refs_0_), channel_id=1, source_target_pairs={{0,2},{2,4},{4,6},{6,0},{1,3},{3,5},{5,7},{7,1},{8,10},{10,12},{12... | collective-permute-start | bytes 1572872 | tf_op jit(solution)/shard_map/ppermute | solution.py:448
  27.3 23.5 %collective-permute-start.3 = (bf16[256,1024]{1,0:T(8,128)(2,1)S(1)}, bf16[256,1024]{1,0:T(8,128)(2,1)S(1)}, u32[]{:S(2)}, u32[]{:S(2)}) collective-permute-start(bf16[256,1024]{1,0:T(8,128)(2,1)S(1)} %pad_maximum_fusion.1.refs_0_), channel_id=1, source_target_pairs={{0,6},{2,0},{4,2},{6,4},{1,7},{3,1},{5,3},{7,5},{8,14},{10,8},{12,... | collective-permute-start | bytes 1572872 | tf_op jit(solution)/shard_map/ppermute | solution.py:448
  39.2 15.8 %copy-start.8 = (bf16[256,1024]{1,0:T(8,128)(2,1)}, bf16[256,1024]{1,0:T(8,128)(2,1)S(1)}, u32[]{:S(2)}) copy-start(bf16[256,1024]{1,0:T(8,128)(2,1)S(1)} %collective-permute-done.1.refs_1_) | copy-start | bytes 1572868
  50.8 4.2 %copy-start.9 = (bf16[256,1024]{1,0:T(8,128)(2,1)}, bf16[256,1024]{1,0:T(8,128)(2,1)S(1)}, u32[]{:S(2)}) copy-start(bf16[256,1024]{1,0:T(8,128)(2,1)S(1)} %collective-permute-done.2.refs_2_) | copy-start | bytes 1572868
  50.8 4.2 %copy-start.10 = (bf16[256,1024]{1,0:T(8,128)(2,1)}, bf16[256,1024]{1,0:T(8,128)(2,1)S(1)}, u32[]{:S(2)}) copy-start(bf16[256,1024]{1,0:T(8,128)(2,1)S(1)} %collective-permute-done.3.refs_3_) | copy-start | bytes 1572868
  51.2 23.5 %collective-permute-start.5 = (bf16[128,2048]{1,0:T(8,128)(2,1)S(1)}, bf16[128,2048]{1,0:T(8,128)(2,1)S(1)}, u32[]{:S(2)}, u32[]{:S(2)}) collective-permute-start(bf16[128,2048]{1,0:T(8,128)(2,1)S(1)} %layer_norm.1), channel_id=1, source_target_pairs={{0,2},{2,4},{4,6},{6,0},{1,3},{3,5},{5,7},{7,1},{8,10},{10,12},{12... | collective-permute-start | bytes 1572872 | tf_op jit(solution)/shard_map/ppermute | solution.py:455
  52.1 25.6 %collective-permute-start.6 = (bf16[128,2048]{1,0:T(8,128)(2,1)S(1)}, bf16[128,2048]{1,0:T(8,128)(2,1)S(1)}, u32[]{:S(2)}, u32[]{:S(2)}) collective-permute-start(bf16[128,2048]{1,0:T(8,128)(2,1)S(1)} %layer_norm.1), channel_id=1, source_target_pairs={{0,4},{2,6},{4,0},{6,2},{1,5},{3,7},{5,1},{7,3},{8,12},{10,14},{12... | collective-permute-start | bytes 1572872 | tf_op jit(solution)/shard_map/ppermute | solution.py:455
  55.0 22.8 %collective-permute-start.7 = (bf16[128,2048]{1,0:T(8,128)(2,1)S(1)}, bf16[128,2048]{1,0:T(8,128)(2,1)S(1)}, u32[]{:S(2)}, u32[]{:S(2)}) collective-permute-start(bf16[128,2048]{1,0:T(8,128)(2,1)S(1)} %layer_norm.1), channel_id=1, source_target_pairs={{0,6},{2,0},{4,2},{6,4},{1,7},{3,1},{5,3},{7,5},{8,14},{10,8},{12,... | collective-permute-start | bytes 1572872 | tf_op jit(solution)/shard_map/ppermute | solution.py:455
  78.0 4.0 %copy-start.6 = (bf16[512,2048]{1,0:T(8,128)(2,1)}, bf16[512,2048]{1,0:T(8,128)(2,1)S(1)}, u32[]{:S(2)}) copy-start(bf16[512,2048]{1,0:T(8,128)(2,1)S(1)} %constant_dynamic-update-slice_fusion.own_in) | copy-start | bytes 6291460
  78.0 5.3 %collective-permute-start.8 = (bf16[512,2048]{1,0:T(8,128)(2,1)S(1)}, bf16[512,2048]{1,0:T(8,128)(2,1)}, u32[]{:S(2)}, u32[]{:S(2)}) collective-permute-start(bf16[512,2048]{1,0:T(8,128)(2,1)S(1)} %constant_dynamic-update-slice_fusion.own_in), channel_id=1, source_target_pairs={{0,1},{1,0},{2,3},{3,2},{4,5},{5,4},{6,7},{7,6},{8,9},{9,8},{10,11... | collective-permute-start | bytes 6291464 | tf_op jit(solution)/shard_map/ppermute | solution.py:26
  79.4 26.0 %collective-permute-start.10 = (bf16[256,1152]{1,0:T(8,128)(2,1)}, bf16[256,1152]{1,0:T(8,128)(2,1)S(1)}, u32[]{:S(2)}, u32[]{:S(2)}) collective-permute-start(bf16[256,1152]{1,0:T(8,128)(2,1)} %get-tuple-element.63), channel_id=1, source_target_pairs={{0,4},{2,6},{4,0},{6,2},{1,5},{3,7},{5,1},{7,3},{8,12},{10,14},{12... | collective-permute-start | bytes 1769480 | tf_op jit(solution)/shard_map/ppermute | solution.py:458
  80.2 27.9 %collective-permute-start.11 = (bf16[256,1152]{1,0:T(8,128)(2,1)}, bf16[256,1152]{1,0:T(8,128)(2,1)S(1)}, u32[]{:S(2)}, u32[]{:S(2)}) collective-permute-start(bf16[256,1152]{1,0:T(8,128)(2,1)} %get-tuple-element.64), channel_id=1, source_target_pairs={{0,6},{2,0},{4,2},{6,4},{1,7},{3,1},{5,3},{7,5},{8,14},{10,8},{12,... | collective-permute-start | bytes 1769480 | tf_op jit(solution)/shard_map/ppermute | solution.py:458
  82.0 27.0 %collective-permute-start.12 = (bf16[256,1152]{1,0:T(8,128)(2,1)S(1)}, bf16[256,1152]{1,0:T(8,128)(2,1)S(1)}, u32[]{:S(2)}, u32[]{:S(2)}) collective-permute-start(bf16[256,1152]{1,0:T(8,128)(2,1)S(1)} %get-tuple-element.65), channel_id=1, source_target_pairs={{0,2},{2,4},{4,6},{6,0},{1,3},{3,5},{5,7},{7,1},{8,10},{10,12},{12... | collective-permute-start | bytes 1769480 | tf_op jit(solution)/shard_map/ppermute | solution.py:458
  96.7 17.2 %slice-start = ((s8[9437184]{0:T(1024)(128)(4,1)}), s8[4194304]{0:T(1024)(128)(4,1)S(1)}, s32[]{:S(2)}) async-start(s8[9437184]{0:T(1024)(128)(4,1)} %bitcast.14), calls=%async_computation.1 | async-start | bytes 8388608
  96.7 17.2 %slice-start.1 = ((s8[9437184]{0:T(1024)(128)(4,1)}), s8[4194304]{0:T(1024)(128)(4,1)S(1)}, s32[]{:S(2)}) async-start(s8[9437184]{0:T(1024)(128)(4,1)} %bitcast.14), calls=%async_computation.2 | async-start | bytes 8388608
  96.7 17.2 %slice-start.2 = ((s8[9437184]{0:T(1024)(128)(4,1)}), s8[1048576]{0:T(1024)(128)(4,1)S(1)}, s32[]{:S(2)}) async-start(s8[9437184]{0:T(1024)(128)(4,1)} %bitcast.14), calls=%async_computation.3 | async-start | bytes 2097152
  110.7 9.1 %collective-permute-start.13 = (bf16[256,256]{1,0:T(8,128)(2,1)S(1)}, bf16[256,256]{1,0:T(8,128)(2,1)S(1)}, u32[]{:S(2)}, u32[]{:S(2)}) collective-permute-start(bf16[256,256]{1,0:T(8,128)(2,1)S(1)} %get-tuple-element.85), channel_id=1, source_target_pairs={{0,2},{2,4},{4,6},{6,0},{1,3},{3,5},{5,7},{7,1},{8,10},{10,12},{12... | collective-permute-start | bytes 393224 | tf_op jit(solution)/shard_map/ppermute | solution.py:464
  111.0 8.9 %collective-permute-start.14 = (bf16[256,256]{1,0:T(8,128)(2,1)S(1)}, bf16[256,256]{1,0:T(8,128)(2,1)S(1)}, u32[]{:S(2)}, u32[]{:S(2)}) collective-permute-start(bf16[256,256]{1,0:T(8,128)(2,1)S(1)} %get-tuple-element.84), channel_id=1, source_target_pairs={{0,4},{2,6},{4,0},{6,2},{1,5},{3,7},{5,1},{7,3},{8,12},{10,14},{12... | collective-permute-start | bytes 393224 | tf_op jit(solution)/shard_map/ppermute | solution.py:464
  114.0 5.9 %collective-permute-start.15 = (bf16[256,256]{1,0:T(8,128)(2,1)S(1)}, bf16[256,256]{1,0:T(8,128)(2,1)S(1)}, u32[]{:S(2)}, u32[]{:S(2)}) collective-permute-start(bf16[256,256]{1,0:T(8,128)(2,1)S(1)} %get-tuple-element.83), channel_id=1, source_target_pairs={{0,6},{2,0},{4,2},{6,4},{1,7},{3,1},{5,3},{7,5},{8,14},{10,8},{12,... | collective-permute-start | bytes 393224 | tf_op jit(solution)/shard_map/ppermute | solution.py:464
  121.3 3.6 %collective-permute-start.17 = (bf16[128,2048]{1,0:T(8,128)(2,1)S(1)}, bf16[128,2048]{1,0:T(8,128)(2,1)S(1)}, u32[]{:S(2)}, u32[]{:S(2)}) collective-permute-start(bf16[128,2048]{1,0:T(8,128)(2,1)S(1)} %get-tuple-element.76), channel_id=1, source_target_pairs={{0,1},{1,0},{2,3},{3,2},{4,5},{5,4},{6,7},{7,6},{8,9},{9,8},{10,11... | collective-permute-start | bytes 1572872 | tf_op jit(solution)/shard_map/ppermute | solution.py:26
  122.8 4.2 %collective-permute-start.19 = (bf16[128,2048]{1,0:T(8,128)(2,1)S(1)}, bf16[128,2048]{1,0:T(8,128)(2,1)S(1)}, u32[]{:S(2)}, u32[]{:S(2)}) collective-permute-start(bf16[128,2048]{1,0:T(8,128)(2,1)S(1)} %get-tuple-element.75), channel_id=1, source_target_pairs={{0,1},{1,0},{2,3},{3,2},{4,5},{5,4},{6,7},{7,6},{8,9},{9,8},{10,11... | collective-permute-start | bytes 1572872 | tf_op jit(solution)/shard_map/ppermute | solution.py:26
  122.9 6.2 %collective-permute-start.21 = (bf16[128,2048]{1,0:T(8,128)(2,1)S(1)}, bf16[128,2048]{1,0:T(8,128)(2,1)S(1)}, u32[]{:S(2)}, u32[]{:S(2)}) collective-permute-start(bf16[128,2048]{1,0:T(8,128)(2,1)S(1)} %get-tuple-element.77), channel_id=1, source_target_pairs={{0,1},{1,0},{2,3},{3,2},{4,5},{5,4},{6,7},{7,6},{8,9},{9,8},{10,11... | collective-permute-start | bytes 1572872 | tf_op jit(solution)/shard_map/ppermute | solution.py:26
  123.3 6.0 %collective-permute-start.16 = (bf16[128,2048]{1,0:T(8,128)(2,1)S(1)}, bf16[128,2048]{1,0:T(8,128)(2,1)S(1)}, u32[]{:S(2)}, u32[]{:S(2)}) collective-permute-start(bf16[128,2048]{1,0:T(8,128)(2,1)S(1)} %get-tuple-element.74), channel_id=1, source_target_pairs={{0,1},{1,0},{2,3},{3,2},{4,5},{5,4},{6,7},{7,6},{8,9},{9,8},{10,11... | collective-permute-start | bytes 1572872 | tf_op jit(solution)/shard_map/ppermute | solution.py:26
  125.1 14.7 %collective-permute-start.18 = (bf16[128,2048]{1,0:T(8,128)(2,1)S(1)}, bf16[128,2048]{1,0:T(8,128)(2,1)S(1)}, u32[]{:S(2)}, u32[]{:S(2)}) collective-permute-start(bf16[128,2048]{1,0:T(8,128)(2,1)S(1)} %add_convert_fusion.3), channel_id=1, source_target_pairs={{0,4},{2,6},{4,0},{6,2},{1,5},{3,7},{5,1},{7,3},{8,12},{10,14},{12... | collective-permute-start | bytes 1572872 | tf_op jit(solution)/shard_map/ppermute | solution.py:475
  127.1 23.9 %collective-permute-start.20 = (bf16[128,2048]{1,0:T(8,128)(2,1)S(1)}, bf16[128,2048]{1,0:T(8,128)(2,1)S(1)}, u32[]{:S(2)}, u32[]{:S(2)}) collective-permute-start(bf16[128,2048]{1,0:T(8,128)(2,1)S(1)} %add_convert_fusion.2), channel_id=1, source_target_pairs={{0,6},{2,0},{4,2},{6,4},{1,7},{3,1},{5,3},{7,5},{8,14},{10,8},{12,... | collective-permute-start | bytes 1572872 | tf_op jit(solution)/shard_map/ppermute | solution.py:475
  129.2 22.5 %collective-permute-start.22 = (bf16[128,2048]{1,0:T(8,128)(2,1)S(1)}, bf16[128,2048]{1,0:T(8,128)(2,1)S(1)}, u32[]{:S(2)}, u32[]{:S(2)}) collective-permute-start(bf16[128,2048]{1,0:T(8,128)(2,1)S(1)} %add_convert_fusion.1), channel_id=1, source_target_pairs={{0,2},{2,4},{4,6},{6,0},{1,3},{3,5},{5,7},{7,1},{8,10},{10,12},{12... | collective-permute-start | bytes 1572872 | tf_op jit(solution)/shard_map/ppermute | solution.py:475
Sparse Core Ops, SparseCore 0:
  18.7 77.9 all-gather.2
